TPU v7x, 32 devices: a whole 2x2x4 slice. The times are simulated.
32 devices in a mesh: brick: 8 (over z, x), group: 4 (over y, core).
Axes of the slice: x: 2, y: 2, z: 4, core: 2. Of those that a mesh axis runs over, the one named last changes fastest.
Arguments:
- features: bfloat16 [32768, 96], P(('brick', 'group')), may hold values from -6 to 6
- order: int32 [32768], P(('brick', 'group')), may hold values from 0 to 1023, as said below
- face_list: int32 [8192], P(('brick', 'group')), may hold values from 0 to 1023, as said below
- face_count: int32 [64], P(('brick', 'group')), may hold values from 32 to 128, as said below
- kernel_map: int32 [27, 32768], P(None, ('brick', 'group')), may hold values from 0 to 1280, as said below
- weight: bfloat16 [27, 96, 256], replicated, may hold values from -0.15625 to 0.15625
- bias: float32 [256], replicated, may hold values from -3 to 3
- cotangent: bfloat16 [32768, 256], P(('brick', 'group')), may hold values from -6 to 6
Outputs:
- output: bfloat16 [32768, 256], P(('brick', 'group'))
- grad_in: bfloat16 [32768, 96], P(('brick', 'group'))
- weight_grad: float32 [27, 96, 256], replicated
Inputs may be any that keep to these rules, and one draw needn't show every extreme that they name: `order`: each device's 1024 entries are a permutation of 0 .. 1023. `face_list`: rows of the device's own brick. `face_count`: some list is full in every draw. `kernel_map`: the value 1024 + 2 * 128 names the zero row; offset 27 // 2 maps every voxel i to row i.
All inputs are finite; a program needn't handle non-finite values.
Results may differ from a plain program's by a relative error of at most 0.012.
Values may be sent and summed in bfloat16 or wider, within the bound.
No kernel may reach another device: no remote copies, remote signals or barrier semaphores. Data moves between devices by JAX's collectives and lax.ppermute only.
A program may use at most 64 MiB of HBM per device.

v0:
```python
import math

import jax
import jax.numpy as jnp
from jax import lax
from jax.sharding import PartitionSpec as P


def from_behind(array, axis, by):
    size = lax.axis_size(axis)
    pairs = [(i, i + by) for i in range(size) if 0 <= i + by < size]
    return lax.ppermute(array, axis, pairs)


def one_hot_rows(index, width):
    columns = jnp.arange(width, dtype=jnp.int32)
    return (index[:, None] == columns[None, :]).astype(jnp.bfloat16)


def pick_rows(selector, values):
    return jnp.dot(selector, values, preferred_element_type=jnp.float32).astype(jnp.bfloat16)


def spread_rows(selector, values):
    high_part = values.astype(jnp.bfloat16)
    low_part = (values - high_part.astype(jnp.float32)).astype(jnp.bfloat16)
    dims = (((0,), (0,)), ((), ()))
    first = lax.dot_general(selector, high_part, dims, preferred_element_type=jnp.float32)
    second = lax.dot_general(selector, low_part, dims, preferred_element_type=jnp.float32)
    return first + second


def on_device(features, order, face_list, face_count, kernel_map, weight, bias, cotangent):
    rows_here = features.shape[0]
    face_slots = face_list.shape[0] // 2
    order_pick = one_hot_rows(order, rows_here)
    sent_rows = pick_rows(order_pick, features)
    local_rows = lax.all_to_all(sent_rows, "brick", split_axis=0, concat_axis=0, tiled=True)
    slots = jnp.arange(face_slots, dtype=jnp.int32)
    lower_keep = (slots < face_count[0]).astype(jnp.bfloat16)[:, None]
    upper_keep = (slots < face_count[1]).astype(jnp.bfloat16)[:, None]
    lower_pick = one_hot_rows(face_list[:face_slots], rows_here) * lower_keep
    upper_pick = one_hot_rows(face_list[face_slots:], rows_here) * upper_keep
    lower_rows = pick_rows(lower_pick, local_rows)
    upper_rows = pick_rows(upper_pick, local_rows)
    prev_upper = from_behind(upper_rows, "brick", 1)
    next_lower = from_behind(lower_rows, "brick", -1)
    zero_row = jnp.zeros((1, local_rows.shape[1]), jnp.bfloat16)
    extended = jnp.concatenate([local_rows, prev_upper, next_lower, zero_row], 0)
    ext_count = extended.shape[0]

    def forward(summed, operands):
        map_row, kernel = operands
        gathered = pick_rows(one_hot_rows(map_row, ext_count), extended)
        return (summed + jnp.dot(gathered, kernel, preferred_element_type=jnp.float32), None)

    start = jnp.zeros((rows_here, weight.shape[2]), jnp.float32)
    pre, _ = lax.scan(forward, start, (kernel_map, weight))
    pre = pre + bias
    output = jnp.maximum(pre, 0.0).astype(jnp.bfloat16)
    pre_grad = jnp.where(pre > 0, cotangent, jnp.zeros_like(cotangent))

    def offset_grads(ext_grad, map_row, kernel):
        selector = one_hot_rows(map_row, ext_count)
        gathered = pick_rows(selector, extended)
        kernel_grad = lax.dot_general(
            gathered, pre_grad, (((0,), (0,)), ((), ())), preferred_element_type=jnp.float32
        )
        contrib = lax.dot_general(
            pre_grad, kernel, (((1,), (1,)), ((), ())), preferred_element_type=jnp.float32
        )
        return (ext_grad + spread_rows(selector, contrib), kernel_grad)

    zeros_grad = jnp.zeros((ext_count, extended.shape[1]), jnp.float32)

    def backward(ext_grad, operands):
        map_row, kernel = operands
        return offset_grads(ext_grad, map_row, kernel)

    ext_grad, kernel_grads = lax.scan(backward, zeros_grad, (kernel_map, weight))
    weight_sum = lax.psum(kernel_grads, ("brick", "group"))
    to_prev = ext_grad[rows_here : rows_here + face_slots]
    to_next = ext_grad[rows_here + face_slots : rows_here + 2 * face_slots]
    from_prev = from_behind(to_next.astype(jnp.bfloat16), "brick", 1).astype(to_next.dtype)
    from_next = from_behind(to_prev.astype(jnp.bfloat16), "brick", -1).astype(to_prev.dtype)
    local_grad = (
        ext_grad[:rows_here]
        + spread_rows(lower_pick, from_prev)
        + spread_rows(upper_pick, from_next)
    )
    brick_grad = local_grad.astype(jnp.bfloat16)
    returned = lax.all_to_all(brick_grad, "brick", split_axis=0, concat_axis=0, tiled=True)
    grad_in = lax.dot_general(
        order_pick, returned, (((0,), (0,)), ((), ())), preferred_element_type=jnp.float32
    ).astype(jnp.bfloat16)
    voxel_total = lax.axis_size("brick") * lax.axis_size("group") * rows_here
    weight_grad = weight_sum * jnp.float32(1.0 / math.sqrt(voxel_total))
    return (output, grad_in, weight_grad)


def solution(mesh):
    return jax.shard_map(
        on_device,
        mesh=mesh,
        in_specs=(
            P(("brick", "group"), None),
            P(("brick", "group")),
            P(("brick", "group")),
            P(("brick", "group")),
            P(None, ("brick", "group")),
            P(),
            P(),
            P(("brick", "group"), None),
        ),
        out_specs=(P(("brick", "group"), None), P(("brick", "group"), None), P()),
        check_vma=False,
    )
```

profile of v0, /device:TPU:0, one launch (start us, length us, event | category | flops | bytes accessed | tf_op | source)
XLA Modules:
  0.0 454.1 jit_solution(2190139345262719592)
XLA Ops:
  10.5 7.2 %all-to-all-start = ((bf16[8,128,96]{1,2,0:T(8,128)(2,1)}), bf16[8,128,96]{1,2,0:T(8,128)(2,1)S(1)}, u32[]{:S(2)}, u32[]{:S(2)}) async-start(bf16[8,128,96]{1,2,0:T(8,128)(2,1)} %bitcast.53), calls=%async_computation | async-start | bytes 393216 | tf_op jit(solution)/shard_map/all_to_all | solution.py:38
  21.3 4.4 all-to-all-done
  26.0 3.0 collective-permute-start
  30.6 4.4 collective-permute-done.1
  35.3 92.4 %while.24 = (s32[]{:T(128)}, f32[1024,256]{1,0:T(8,128)S(1)}, s32[27,1024]{1,0:T(8,128)}, bf16[1281,96]{1,0:T(8,128)(2,1)S(1)}, bf16[27,96,256]{2,1,0:T(8,128)(2,1)}, /*index=5*/s32[]{:T(128)}, s32[]{:T(128)}) while((s32[]{:T(128)}, f32[1024,256]{1,0:T(8,128)S(1)}, s32[27,1024]{1,0:T(8,128)}, bf16[1281,96]{1,0:T(8,128)(2,1)S(1)}, ...), condition=%wide.region_1.2_spmd.clone, body=%wide.region_0.1_spmd.clone.sunk | while | flops 304120832 | bytes 2404647 | solution.py:58
  36.2 2.6 convolution_add_fusion.4
  39.6 2.6 convolution_add_fusion.4
  43.0 2.6 convolution_add_fusion.4
  46.4 2.6 convolution_add_fusion.4
  49.8 2.6 convolution_add_fusion.4
  53.3 2.6 convolution_add_fusion.4
  56.7 2.6 convolution_add_fusion.4
  60.1 2.6 convolution_add_fusion.4
  63.5 2.6 convolution_add_fusion.4
  66.9 2.6 convolution_add_fusion.4
  70.4 2.6 convolution_add_fusion.4
  73.8 2.6 convolution_add_fusion.4
  77.2 2.6 convolution_add_fusion.4
  80.6 2.6 convolution_add_fusion.4
  84.0 2.6 convolution_add_fusion.4
  87.5 2.6 convolution_add_fusion.4
  90.9 2.6 convolution_add_fusion.4
  94.3 2.6 convolution_add_fusion.4
  97.7 2.6 convolution_add_fusion.4
  108.0 2.6 convolution_add_fusion.4
  118.2 2.6 convolution_add_fusion.4
  127.9 176.2 %while.25 = (s32[]{:T(128)}, f32[1281,96]{0,1:T(8,128)S(1)}, f32[27,96,256]{2,1,0:T(8,128)}, s32[27,1024]{1,0:T(8,128)}, bf16[27,96,256]{2,1,0:T(8,128)(2,1)}, /...) while((s32[]{:T(128)}, f32[1281,96]{0,1:T(8,128)S(1)}, ...), condition=%wide.region_3.4_spmd.clone, body=%wide.region_2.3_spmd.clone.sunk | while | flops 861121792 | bytes 4609851 | solution.py:80
  305.5 4.5 %collective-permute-start.2 = (bf16[128,96]{0,1:T(8,128)(2,1)S(1)}, bf16[128,96]{0,1:T(8,128)(2,1)S(1)}, u32[]{:S(2)}, u32[]{:S(2)}) collective-permute-start(bf16[128,96]{0,1:T(8,128)(2,1)S(1)} %get-tuple-element.149), channel_id=1, source_target_pairs={{0,4},{4,8},{8,12},{12,16},{16,20},{20,24},{24,28},{1,5},{5,9},{9,... | collective-permute-start | bytes 73736 | tf_op jit(solution)/shard_map/ppermute | solution.py:12
  313.2 6.1 %all-to-all-start.1 = ((bf16[8,128,96]{1,2,0:T(8,128)(2,1)}), bf16[8,128,96]{1,2,0:T(8,128)(2,1)S(1)}, u32[]{:S(2)}, u32[]{:S(2)}) async-start(bf16[8,128,96]{1,2,0:T(8,128)(2,1)} %bitcast.52), calls=%async_computation.1 | async-start | bytes 393216 | tf_op jit(solution)/shard_map/all_to_all | solution.py:92
  320.1 8.6 %all-to-all-done.1 = bf16[8,128,96]{1,2,0:T(8,128)(2,1)S(1)} async-done(((bf16[8,128,96]{1,2,0:T(8,128)(2,1)}), bf16[8,128,96]{1,2,0:T(8,128)(2,1)S(1)}, u32[]{:S(2)}, u32[]{:S(2)}) %all-to-all-start.1) | async-done | bytes 196640 | tf_op jit(solution)/shard_map/all_to_all | solution.py:92
  330.3 113.4 %all-reduce.2.cloned.1.call-done = f32[27,96,256]{2,1,0:T(8,128)} async-done(((f32[27,96,256]{2,1,0:T(8,128)}), f32[27,96,256]{2,1,0:T(8,128)}) %all-reduce.2.cloned.1.call-update) | async-done | bytes 2654224 | tf_op jit(solution)/shard_map/psum | solution.py:81
  443.7 3.6 broadcast_multiply_fusion
  (208 shorter events, 228.4 us)
Async XLA Ops:
  7.2 0.9 copy-start
  10.5 15.2 %all-to-all-start = ((bf16[8,128,96]{1,2,0:T(8,128)(2,1)}), bf16[8,128,96]{1,2,0:T(8,128)(2,1)S(1)}, u32[]{:S(2)}, u32[]{:S(2)}) async-start(bf16[8,128,96]{1,2,0:T(8,128)(2,1)} %bitcast.53), calls=%async_computation | async-start | bytes 393216 | tf_op jit(solution)/shard_map/all_to_all | solution.py:38
  17.8 425.9 %all-reduce.2.cloned.1.call-start = ((), (), s32[]{:S(2)}) async-start(), calls=%async_computation.2 | async-start | bytes 5308416 | tf_op jit(solution)/shard_map/psum | solution.py:81
  26.0 4.6 %collective-permute-start = (bf16[128,96]{0,1:T(8,128)(2,1)S(1)}, bf16[128,96]{0,1:T(8,128)(2,1)S(1)}, u32[]{:S(2)}, u32[]{:S(2)}) collective-permute-start(bf16[128,96]{0,1:T(8,128)(2,1)S(1)} %convolution_convert_fusion.1), channel_id=1, source_target_pairs={{0,4},{4,8},{8,12},{12,16},{16,20},{20,24},{24,28},{1,5},{5,9},{9,... | collective-permute-start | bytes 73736 | tf_op jit(solution)/shard_map/ppermute | solution.py:12
  29.3 5.7 %collective-permute-start.1 = (bf16[128,96]{0,1:T(8,128)(2,1)S(1)}, bf16[128,96]{0,1:T(8,128)(2,1)S(1)}, u32[]{:S(2)}, u32[]{:S(2)}) collective-permute-start(bf16[128,96]{0,1:T(8,128)(2,1)S(1)} %convolution_convert_fusion), channel_id=1, source_target_pairs={{4,0},{8,4},{12,8},{16,12},{20,16},{24,20},{28,24},{5,1},{9,5},{13... | collective-permute-start | bytes 73736 | tf_op jit(solution)/shard_map/ppermute | solution.py:12
  35.3 92.4 %copy-start.1 = (bf16[1024,256]{1,0:T(8,128)(2,1)S(1)}, bf16[1024,256]{1,0:T(8,128)(2,1)}, u32[]{:S(2)}) copy-start(bf16[1024,256]{1,0:T(8,128)(2,1)} %param.19) | copy-start | bytes 1572868
  35.3 92.4 %copy-start.2 = (f32[256]{0:T(256)S(1)}, f32[256]{0:T(256)}, u32[]{:S(2)}) copy-start(f32[256]{0:T(256)} %param.18) | copy-start | bytes 3076
  304.2 5.9 %collective-permute-start.3 = (bf16[128,96]{0,1:T(8,128)(2,1)S(1)}, bf16[128,96]{0,1:T(8,128)(2,1)S(1)}, u32[]{:S(2)}, u32[]{:S(2)}) collective-permute-start(bf16[128,96]{0,1:T(8,128)(2,1)S(1)} %get-tuple-element.150), channel_id=1, source_target_pairs={{4,0},{8,4},{12,8},{16,12},{20,16},{24,20},{28,24},{5,1},{9,5},{13... | collective-permute-start | bytes 73736 | tf_op jit(solution)/shard_map/ppermute | solution.py:12
  305.5 6.1 %collective-permute-start.2 = (bf16[128,96]{0,1:T(8,128)(2,1)S(1)}, bf16[128,96]{0,1:T(8,128)(2,1)S(1)}, u32[]{:S(2)}, u32[]{:S(2)}) collective-permute-start(bf16[128,96]{0,1:T(8,128)(2,1)S(1)} %get-tuple-element.149), channel_id=1, source_target_pairs={{0,4},{4,8},{8,12},{12,16},{16,20},{20,24},{24,28},{1,5},{5,9},{9,... | collective-permute-start | bytes 73736 | tf_op jit(solution)/shard_map/ppermute | solution.py:12
  310.4 18.4 %copy-start.3 = (s32[1024]{0:T(1024)S(1)}, s32[1024]{0:T(1024)}, u32[]{:S(2)}) copy-start(s32[1024]{0:T(1024)} %param.13) | copy-start | bytes 12292
  313.2 15.6 %all-to-all-start.1 = ((bf16[8,128,96]{1,2,0:T(8,128)(2,1)}), bf16[8,128,96]{1,2,0:T(8,128)(2,1)S(1)}, u32[]{:S(2)}, u32[]{:S(2)}) async-start(bf16[8,128,96]{1,2,0:T(8,128)(2,1)} %bitcast.52), calls=%async_computation.1 | async-start | bytes 393216 | tf_op jit(solution)/shard_map/all_to_all | solution.py:92
Sparse Core Ops, SparseCore 0:
  305.6 138.0 all-reduce.1
where the time goes:
time: 461 us; the launch traced here: 454 us
  matrix products  231 us (50%)
  waiting for transfers between devices  132 us (29%)
  local copies, waits for them, and re-layouts  46.2 us (10%)
  starting transfers between devices  23.5 us (5%)
  between operations  14.3 us (3%)
  other arithmetic  6.1 us (1%)
    psum x1, waiting for transfers between devices, on_device(): weight_sum = lax.psum(kernel_grads, ('brick', 'group'))  113 us
    dot_general x27, matrix products, forward(): jnp.dot(gathered, kernel, preferred_element_type=jnp.float32)  70.8 us
    dot_general x27, matrix products, offset_grads(): lax.dot_general(gathered, pre_grad, (((0,), (0,)), ((), ())), preferred_e...  57.3 us
    dynamic_slice x54, local copies, waits for them, and re-layouts, on_device(): pre, _ = lax.scan(forward, start, (kernel_map, weight))  41.5 us
    dot_general x29, matrix products, spread_rows(): lax.dot_general(selector, high_part, dims, preferred_element_type=jnp.flo...  35.7 us
    dot_general x29, matrix products, spread_rows(): lax.dot_general(selector, low_part, dims, preferred_element_type=jnp.floa...  34.1 us
    dot_general x27, matrix products, offset_grads(): lax.dot_general(pre_grad, kernel, (((1,), (1,)), ((), ())), preferred_ele...  29.2 us
    ppermute x4, starting transfers between devices, from_behind(): return lax.ppermute(array, axis, pairs)  10.1 us
  transfers between devices with their start and end apart: 7, of which 5 were waited for; matrix products, arithmetic and copies ran while one was open for 2% of the time, Pallas kernels for 0%

commit v1 on v0

v1 whole, which is shorter than its diff:
```python
import functools
import math

import jax
import jax.numpy as jnp
from jax import lax
from jax.experimental import pallas as pl
from jax.experimental.pallas import tpu as pltpu
from jax.sharding import PartitionSpec as P

BF = jnp.bfloat16
F32 = jnp.float32
LOW = 256
SHIFT = 8
VMEM_LIMIT = 48 << 20
AXES = ("brick", "group")


def dot(a, b, a_dim, b_dim):
    dims = (((a_dim,), (b_dim,)), ((), ()))
    return lax.dot_general(a, b, dims, preferred_element_type=F32)


def one_hot_rows(index, width):
    columns = jnp.arange(width, dtype=jnp.int32)
    return (index[:, None] == columns[None, :]).astype(BF)


def forward_kernel(x_ref, map_ref, wt_ref, bias_ref, cot_ref, out_ref, pg_ref, wg_ref, g_ref):
    offsets, voxels = map_ref.shape
    depth = wt_ref.shape[1]
    channels = depth // offsets
    blocks = x_ref.shape[0] // channels
    lanes = min(256, voxels)
    iota = lax.broadcasted_iota(jnp.int32, (LOW, lanes), 0).astype(BF)

    def offset(k, carry):
        row = map_ref[pl.ds(k, 1), :]
        low = (row & (LOW - 1)).astype(F32).astype(BF)
        high = lax.shift_right_logical(row, SHIFT)
        at = pl.ds(pl.multiple_of(k * channels, channels), channels)
        for n in range(voxels // lanes):
            sl = slice(n * lanes, (n + 1) * lanes)
            hit = iota == jnp.broadcast_to(low[:, sl], (LOW, lanes))
            hot = jnp.where(hit, jnp.ones((), BF), jnp.zeros((), BF))
            block = jnp.broadcast_to(high[:, sl], (channels, lanes))
            picked = jnp.zeros((channels, lanes), F32)
            for a in range(blocks):
                term = dot(x_ref[a * channels : (a + 1) * channels, :], hot, 1, 0)
                picked = jnp.where(block == a, term, picked)
            g_ref[at, sl] = picked.astype(BF)
        return carry

    lax.fori_loop(0, offsets, offset, 0)
    for n in range(voxels // lanes):
        sl = slice(n * lanes, (n + 1) * lanes)
        pre = dot(wt_ref[...], g_ref[:, sl], 1, 0).T + bias_ref[...]
        out_ref[sl, :] = jnp.maximum(pre, 0.0).astype(BF)
        pg_ref[sl, :] = jnp.where(pre > 0, cot_ref[sl, :].astype(F32), 0.0).astype(BF)
    step = depth // 9
    for m in range(9):
        sl = slice(m * step, (m + 1) * step)
        wg_ref[sl, :] = dot(g_ref[sl, :], pg_ref[...], 1, 0).astype(BF)
    wg_ref[depth:, :] = jnp.zeros((wg_ref.shape[0] - depth, wg_ref.shape[1]), BF)


def backward_kernel(pg_ref, map_ref, w_ref, acc_ref, c_ref):
    offsets, voxels = map_ref.shape
    depth = w_ref.shape[0]
    channels = depth // offsets
    blocks = acc_ref.shape[0] // channels
    step = depth // 9
    for m in range(9):
        sl = slice(m * step, (m + 1) * step)
        c_ref[sl, :] = dot(w_ref[sl, :], pg_ref[...], 1, 1).astype(BF)
    acc_ref[...] = jnp.zeros_like(acc_ref)
    iota = lax.broadcasted_iota(jnp.int32, (LOW, voxels), 0).astype(BF)

    def offset(k, carry):
        row = map_ref[pl.ds(k, 1), :]
        low = (row & (LOW - 1)).astype(F32).astype(BF)
        high = lax.shift_right_logical(row, SHIFT).astype(F32).astype(BF)
        hit = iota == jnp.broadcast_to(low, (LOW, voxels))
        hot = jnp.where(hit, jnp.ones((), BF), jnp.zeros((), BF))
        contrib = c_ref[pl.ds(pl.multiple_of(k * channels, channels), channels), :]
        block = jnp.broadcast_to(high, (channels, voxels))
        for a in range(blocks):
            part = jnp.where(block == jnp.array(a, BF), contrib, jnp.zeros((), BF))
            acc_ref[a * channels : (a + 1) * channels, :] += dot(part, hot, 1, 1)
        return carry

    lax.fori_loop(0, offsets, offset, 0)


def whole(count):
    return [pl.BlockSpec(memory_space=pltpu.VMEM)] * count


def forward(x, maps, wt, bias, cot, padded):
    offsets, voxels = maps.shape
    c_out, depth = wt.shape
    macs = voxels * depth * c_out * 2 + offsets * voxels * LOW * x.shape[0]
    return pl.pallas_call(
        forward_kernel,
        out_shape=(
            jax.ShapeDtypeStruct((voxels, c_out), BF),
            jax.ShapeDtypeStruct((voxels, c_out), BF),
            jax.ShapeDtypeStruct((padded, c_out), BF),
        ),
        in_specs=whole(5),
        out_specs=tuple(whole(3)),
        scratch_shapes=[pltpu.VMEM((depth, voxels), BF)],
        compiler_params=pltpu.CompilerParams(vmem_limit_bytes=VMEM_LIMIT),
        cost_estimate=pl.CostEstimate(flops=2 * macs, bytes_accessed=5 << 20, transcendentals=0),
    )(x, maps, wt, bias, cot)


def backward(pg, maps, w, rows):
    offsets, voxels = maps.shape
    depth, c_out = w.shape
    macs = voxels * depth * c_out + offsets * voxels * LOW * rows
    return pl.pallas_call(
        backward_kernel,
        out_shape=jax.ShapeDtypeStruct((rows, LOW), F32),
        in_specs=whole(3),
        out_specs=whole(1)[0],
        scratch_shapes=[pltpu.VMEM((depth, voxels), BF)],
        compiler_params=pltpu.CompilerParams(vmem_limit_bytes=VMEM_LIMIT),
        cost_estimate=pl.CostEstimate(flops=2 * macs, bytes_accessed=4 << 20, transcendentals=0),
    )(pg, maps, w)


def stages(count):
    plan, stride = [], 1
    while stride < count:
        left = count // stride
        radix = 4 if stride > 1 and left % 4 == 0 else 2
        if left % radix:
            radix = left
        plan.append((stride, radix))
        stride *= radix
    return plan


def swapped(array, count, stride, radix, delta):
    def partner(i):
        digit = i // stride % radix
        other = (digit ^ delta) if radix in (2, 4) else (delta - digit) % radix
        return i + (other - digit) * stride

    return lax.ppermute(array, AXES, [(i, partner(i)) for i in range(count)])


def other_digit(digit, delta, radix):
    return (digit ^ delta) if radix in (2, 4) else (delta - digit) % radix


def sum_over_all(x, count):
    flat = lax.axis_index("brick") * lax.axis_size("group") + lax.axis_index("group")
    plan = stages(count)
    for stride, radix in plan:
        digit = flat // stride % radix
        pieces = x.reshape((radix, x.shape[0] // radix) + x.shape[1:])
        got = []
        for delta in range(radix):
            other = other_digit(digit, delta, radix)
            piece = lax.dynamic_index_in_dim(pieces, other, 0, keepdims=False)
            if radix in (2, 4) and delta == 0:
                total = piece.astype(F32)
            else:
                got.append(swapped(piece, count, stride, radix, delta))
        if radix not in (2, 4):
            total = jnp.zeros(got[0].shape, F32)
        for piece in got:
            total = total + piece.astype(F32)
        x = total.astype(BF)
    for stride, radix in reversed(plan):
        digit = flat // stride % radix
        got = [x if radix in (2, 4) and d == 0 else swapped(x, count, stride, radix, d) for d in range(radix)]
        parts = []
        for place in range(radix):
            part = got[other_digit(place, 0, radix)]
            for d in range(1, radix):
                part = jnp.where(digit == d, got[other_digit(place, d, radix) if radix in (2, 4) else (place + d) % radix], part)
            parts.append(part)
        x = jnp.concatenate(parts, 0)
    return x


def meet(array_up, array_down):
    size = lax.axis_size("brick")
    odd = lax.axis_index("brick") % 2 == 1
    got = []
    for start in (0, 1):
        pairs = []
        for i in range(start, size - 1, 2):
            pairs += [(i, i + 1), (i + 1, i)]
        goes_up = ~odd if start == 0 else odd
        got.append(lax.ppermute(jnp.where(goes_up, array_up, array_down), "brick", pairs))
    return jnp.where(odd, got[0], got[1]), jnp.where(odd, got[1], got[0])


def on_device(features, order, face_list, face_count, kernel_map, weight, bias, cotangent):
    offsets, channels, c_out = weight.shape
    rows = features.shape[0]
    face = face_list.shape[0] // 2
    bricks = lax.axis_size("brick")
    count = bricks * lax.axis_size("group")
    per = rows // bricks
    depth = offsets * channels
    unit = 8 * count
    padded = -(-depth // unit) * unit
    blocks = rows // LOW

    w = weight.reshape(depth, c_out)
    wt = w.T
    order_pick = one_hot_rows(order, rows)
    sent = dot(order_pick, features, 1, 0).astype(BF)
    local = lax.all_to_all(sent, "brick", split_axis=0, concat_axis=0, tiled=True)

    slots = jnp.arange(face, dtype=jnp.int32)
    lower_pick = one_hot_rows(face_list[:face], rows) * (slots < face_count[0]).astype(BF)[:, None]
    upper_pick = one_hot_rows(face_list[face:], rows) * (slots < face_count[1]).astype(BF)[:, None]
    lower = dot(local, lower_pick, 0, 1).astype(BF)
    upper = dot(local, upper_pick, 0, 1).astype(BF)
    prev_upper, next_lower = meet(upper, lower)

    x_local = local.reshape(blocks, LOW, channels).transpose(0, 2, 1).reshape(blocks * channels, LOW)
    x = jnp.concatenate([x_local, jnp.concatenate([prev_upper, next_lower], 1)], 0)
    output, pre_grad, kernel_grads = forward(x, kernel_map, wt, bias[None], cotangent, padded)

    weight_sum = sum_over_all(kernel_grads, count)
    scale = jnp.float32(1.0 / math.sqrt(count * rows))
    weight_grad = (weight_sum[:depth].astype(F32) * scale).reshape(offsets, channels, c_out)

    acc = backward(pre_grad, kernel_map, w, x.shape[0])
    faces = acc[blocks * channels :].astype(BF)
    from_prev, from_next = meet(faces[:, face:], faces[:, :face])
    here = acc[: blocks * channels].reshape(blocks, channels, LOW).transpose(0, 2, 1).reshape(rows, channels)
    local_grad = here + dot(lower_pick, from_prev, 0, 1) + dot(upper_pick, from_next, 0, 1)
    returned = lax.all_to_all(local_grad.astype(BF), "brick", split_axis=0, concat_axis=0, tiled=True)
    grad_in = dot(order_pick, returned, 0, 0).astype(BF)
    return output, grad_in, weight_grad


def solution(mesh):
    return jax.shard_map(
        on_device,
        mesh=mesh,
        in_specs=(
            P(AXES, None),
            P(AXES),
            P(AXES),
            P(AXES),
            P(None, AXES),
            P(),
            P(),
            P(AXES, None),
        ),
        out_specs=(P(AXES, None), P(AXES, None), P()),
        check_vma=False,
    )
```

time: 461 us -> 133 us (0.29); the launches traced: 454 us -> 132 us
  matrix products: 231 us -> 5.03 us
  waiting for transfers between devices: 132 us -> 32.6 us
  Pallas kernels: 0 us -> 45.8 us
  local copies, waits for them, and re-layouts: 46.2 us -> 6.99 us
  between operations: 14.3 us -> 1.12 us
  starting transfers between devices: 23.5 us -> 33.6 us
    dot_general x143 -> x6, matrix products: 231 us -> 5.03 us  [dot(): return lax.dot_general(a, b, dims, preferred_element_type=F32)]
    psum x1 -> x0, waiting for transfers between devices: 113 us -> none  [on_device(): weight_sum = lax.psum(kernel_grads, ('brick', 'group'))]
    pallas_call x0 -> x2, Pallas kernels: none -> 45.8 us  [the longest x1 27 us: backward(): pl.pallas_call(backward_kernel, out_shape=jax.ShapeDtypeStruct((rows, LOW...]
    dynamic_slice x54 -> x0, local copies, waits for them, and re-layouts: 41.5 us -> none  [on_device(): pre, _ = lax.scan(forward, start, (kernel_map, weight))]
    ppermute x4 -> x18, waiting for transfers between devices: 5.59 us -> 17.9 us  [the longest x14 17.9 us: swapped(): return lax.ppermute(array, AXES, [(i, partner(i)) for i in range(count)])]
    ppermute x4 -> x18, starting transfers between devices: 10.1 us -> 22.4 us  [the longest x14 17.7 us: swapped(): return lax.ppermute(array, AXES, [(i, partner(i)) for i in range(count)])]
  transfers between devices with their start and end apart: 7 -> 20, of which waited for: 5 -> 10; matrix products, arithmetic and copies ran while one was open for 2% -> 5% of each run, Pallas kernels for 0% -> 20%
where the time goes in v1:
time: 133 us; the launch traced here: 132 us
  Pallas kernels  45.8 us (34%)
  starting transfers between devices  33.6 us (25%)
  waiting for transfers between devices  32.6 us (25%)
  other arithmetic  7 us (5%)
  local copies, waits for them, and re-layouts  6.99 us (5%)
  matrix products  5.03 us (4%)
    pallas_call x1, Pallas kernels, backward(): pl.pallas_call(backward_kernel, out_shape=jax.ShapeDtypeStruct((rows, LOW...  27 us
    pallas_call x1, Pallas kernels, forward(): pl.pallas_call(forward_kernel, out_shape=(jax.ShapeDtypeStruct((voxels, c...  18.7 us
    ppermute x14, waiting for transfers between devices, swapped(): return lax.ppermute(array, AXES, [(i, partner(i)) for i in range(count)])  17.9 us
    ppermute x14, starting transfers between devices, swapped(): return lax.ppermute(array, AXES, [(i, partner(i)) for i in range(count)])  17.7 us
    all_to_all x1, waiting for transfers between devices, on_device(): lax.all_to_all(local_grad.astype(BF), 'brick', split_axis=0, concat_axis=...  8.61 us
    all_to_all x1, starting transfers between devices, on_device(): lax.all_to_all(sent, 'brick', split_axis=0, concat_axis=0, tiled=True)  7.25 us
    all_to_all x1, waiting for transfers between devices, on_device(): lax.all_to_all(sent, 'brick', split_axis=0, concat_axis=0, tiled=True)  6 us
    dot_general x6, matrix products, dot(): return lax.dot_general(a, b, dims, preferred_element_type=F32)  5.03 us
  transfers between devices with their start and end apart: 20, of which 10 were waited for; matrix products, arithmetic and copies ran while one was open for 5% of the time, Pallas kernels for 20%

profile of v1, /device:TPU:0, one launch (start us, length us, event | category | flops | bytes accessed | tf_op | source)
XLA Modules:
  0.0 132.1 jit_solution(7219043177029149211)
XLA Ops:
  1.6 1.7 %fusion.10 = bf16[12,8,8,128]{3,2,1,0:T(8,128)(2,1)S(1)} fusion(bf16[1024,96]{0,1:T(8,128)(2,1)S(1)} %copy-done, s32[1024]{0:T(1024)} %param.9), kind=kOutput, calls=%fused_computation.15 | convolution fusion | flops 202473472 | bytes 397312 | tf_op jit(solution)/shard_map/dot_general | solution.py:21
  4.0 7.3 %all-to-all-start = ((bf16[8,128,96]{1,2,0:T(8,128)(2,1)}), bf16[8,128,96]{1,2,0:T(8,128)(2,1)S(1)}, u32[]{:S(2)}, u32[]{:S(2)}) async-start(bf16[8,128,96]{1,2,0:T(8,128)(2,1)} %bitcast.73), calls=%async_computation | async-start | bytes 393216 | tf_op jit(solution)/shard_map/all_to_all | solution.py:219
  13.2 6.0 %all-to-all-done = bf16[8,128,96]{1,2,0:T(8,128)(2,1)S(1)} async-done(((bf16[8,128,96]{1,2,0:T(8,128)(2,1)}), bf16[8,128,96]{1,2,0:T(8,128)(2,1)S(1)}, u32[]{:S(2)}, u32[]{:S(2)}) %all-to-all-start) | async-done | bytes 196640 | tf_op jit(solution)/shard_map/all_to_all | solution.py:219
  19.5 0.9 broadcast_select_fusion.3
  20.4 1.1 collective-permute-start
  21.5 1.2 collective-permute-start.1
  22.8 0.9 copy.26.wt_ref
  23.7 1.1 copy.23
  26.7 18.7 %shard_map.103 = (bf16[1024,256]{1,0:T(8,128)(2,1)}, bf16[1024,256]{1,0:T(8,128)(2,1)S(1)}, bf16[2816,256]{1,0:T(8,128)(2,1)S(1)}) custom-call(bf16[480,256]{1,0:T(8,128)(2,1)S(1)} %maximum_maximum_fusion.x_ref, s32[27,1024]{1,0:T(8,128)S(1)} %copy-done.4, bf16[256,2592]{1,0:T(8,128)(2,1)S(1)} %copy.26.wt_ref, f32[1,256]{1,0:T(1,128)S(1)} %bitcast.78, ...), custom_call_target="tpu_custom_call" | custom-call | flops 9512681472 | bytes 5242880 | tf_op jit(solution)/shard_map/pallas_call | solution.py:103
  46.4 2.3 %collective-permute-done.4 = bf16[1408,256]{1,0:T(8,128)(2,1)} collective-permute-done((bf16[1408,256]{1,0:T(8,128)(2,1)S(1)}, bf16[1408,256]{1,0:T(8,128)(2,1)}, u32[]{:S(2)}, u32[]{:S(2)}) %collective-permute-start.4) | collective-permute-done | bytes 720928 | tf_op jit(solution)/shard_map/ppermute | solution.py:151
  48.7 1.3 fusion.4
  50.1 1.6 %collective-permute-start.5 = (bf16[352,256]{1,0:T(8,128)(2,1)S(1)}, bf16[352,256]{1,0:T(8,128)(2,1)}, u32[]{:S(2)}, u32[]{:S(2)}) collective-permute-start(bf16[352,256]{1,0:T(8,128)(2,1)S(1)} %get-tuple-element.14), channel_id=1, source_target_pairs={{0,2},{1,3},{2,0},{3,1},{4,6},{5,7},{6,4},{7,5},{8,10},{9,11},{10,... | collective-permute-start | bytes 540680 | tf_op jit(solution)/shard_map/ppermute | solution.py:151
  51.7 4.3 %collective-permute-start.7 = (bf16[352,256]{1,0:T(8,128)(2,1)S(1)}, bf16[352,256]{1,0:T(8,128)(2,1)}, u32[]{:S(2)}, u32[]{:S(2)}) collective-permute-start(bf16[352,256]{1,0:T(8,128)(2,1)S(1)} %get-tuple-element.15), channel_id=1, source_target_pairs={{0,6},{1,7},{2,4},{3,5},{4,2},{5,3},{6,0},{7,1},{8,14},{9,15},{10,... | collective-permute-start | bytes 540680 | tf_op jit(solution)/shard_map/ppermute | solution.py:151
  56.9 4.6 %collective-permute-done.7 = bf16[352,256]{1,0:T(8,128)(2,1)} collective-permute-done((bf16[352,256]{1,0:T(8,128)(2,1)S(1)}, bf16[352,256]{1,0:T(8,128)(2,1)}, u32[]{:S(2)}, u32[]{:S(2)}) %collective-permute-start.7) | collective-permute-done | bytes 180256 | tf_op jit(solution)/shard_map/ppermute | solution.py:151
  61.5 3.1 %collective-permute-done.6 = bf16[352,256]{1,0:T(8,128)(2,1)} collective-permute-done((bf16[352,256]{1,0:T(8,128)(2,1)S(1)}, bf16[352,256]{1,0:T(8,128)(2,1)}, u32[]{:S(2)}, u32[]{:S(2)}) %collective-permute-start.6) | collective-permute-done | bytes 180256 | tf_op jit(solution)/shard_map/ppermute | solution.py:151
  64.6 1.2 fusion.15
  65.8 1.2 collective-permute-start.8
  67.0 1.1 collective-permute-start.10
  68.1 1.3 collective-permute-start.9
  69.4 27.0 %shard_map.104 = f32[480,256]{1,0:T(8,128)S(1)} custom-call(bf16[1024,256]{1,0:T(8,128)(2,1)S(1)} %copy-done.8, s32[27,1024]{1,0:T(8,128)S(1)} %copy-done.5, bf16[2592,256]{1,0:T(8,128)(2,1)S(1)} %bitcast.77), custom_call_target="tpu_custom_call" | custom-call | flops 8153726976 | bytes 4194304 | tf_op jit(solution)/shard_map/pallas_call | solution.py:122
  96.5 2.1 %collective-permute-start.13 = (bf16[88,256]{1,0:T(8,128)(2,1)S(1)}, bf16[88,256]{1,0:T(8,128)(2,1)S(1)}, u32[]{:S(2)}, u32[]{:S(2)}) collective-permute-start(bf16[88,256]{1,0:T(8,128)(2,1)S(1)} %fusion.41), channel_id=1, source_target_pairs={{0,8},{1,9},{2,10},{3,11},{4,12},{5,13},{6,14},{7,15},{8,0},{9,1},... | collective-permute-start | bytes 135176 | tf_op jit(solution)/shard_map/ppermute | solution.py:151
  99.3 1.7 %collective-permute-start.11 = (bf16[88,256]{1,0:T(8,128)(2,1)S(1)}, bf16[88,256]{1,0:T(8,128)(2,1)S(1)}, u32[]{:S(2)}, u32[]{:S(2)}) collective-permute-start(bf16[88,256]{1,0:T(8,128)(2,1)S(1)} %fusion.41), channel_id=1, source_target_pairs={{0,24},{1,25},{2,26},{3,27},{4,28},{5,29},{6,30},{7,31},{8,16},{9,... | collective-permute-start | bytes 135176 | tf_op jit(solution)/shard_map/ppermute | solution.py:151
  101.1 1.7 %collective-permute-start.2 = (bf16[96,128]{1,0:T(8,128)(2,1)S(1)}, bf16[96,128]{1,0:T(8,128)(2,1)S(1)}, u32[]{:S(2)}, u32[]{:S(2)}) collective-permute-start(bf16[96,128]{1,0:T(8,128)(2,1)S(1)} %get-tuple-element.17), channel_id=1, source_target_pairs={{0,4},{4,0},{8,12},{12,8},{16,20},{20,16},{24,28},{28,24},{1,5},{5... | collective-permute-start | bytes 73736 | tf_op jit(solution)/shard_map/ppermute | solution.py:199
  103.5 1.9 %collective-permute-done.11 = bf16[88,256]{1,0:T(8,128)(2,1)S(1)} collective-permute-done((bf16[88,256]{1,0:T(8,128)(2,1)S(1)}, bf16[88,256]{1,0:T(8,128)(2,1)S(1)}, u32[]{:S(2)}, u32[]{:S(2)}) %collective-permute-start.11) | collective-permute-done | bytes 45088 | tf_op jit(solution)/shard_map/ppermute | solution.py:151
  105.5 1.6 %collective-permute-start.16 = (bf16[352,256]{1,0:T(8,128)(2,1)S(1)}, bf16[352,256]{1,0:T(8,128)(2,1)S(1)}, u32[]{:S(2)}, u32[]{:S(2)}) collective-permute-start(bf16[352,256]{1,0:T(8,128)(2,1)S(1)} %pad_maximum_fusion.2), channel_id=1, source_target_pairs={{0,2},{1,3},{2,0},{3,1},{4,6},{5,7},{6,4},{7,5},{8,10},{9,11},{10,... | collective-permute-start | bytes 540680 | tf_op jit(solution)/shard_map/ppermute | solution.py:151
  107.1 1.1 collective-permute-start.15
  109.3 2.5 %collective-permute-done.16 = bf16[352,256]{1,0:T(8,128)(2,1)S(1)} collective-permute-done((bf16[352,256]{1,0:T(8,128)(2,1)S(1)}, bf16[352,256]{1,0:T(8,128)(2,1)S(1)}, u32[]{:S(2)}, u32[]{:S(2)}) %collective-permute-start.16) | collective-permute-done | bytes 180256 | tf_op jit(solution)/shard_map/ppermute | solution.py:151
  112.5 2.0 %collective-permute-done.14 = bf16[352,256]{1,0:T(8,128)(2,1)S(1)} collective-permute-done((bf16[352,256]{1,0:T(8,128)(2,1)S(1)}, bf16[352,256]{1,0:T(8,128)(2,1)S(1)}, u32[]{:S(2)}, u32[]{:S(2)}) %collective-permute-start.14) | collective-permute-done | bytes 180256 | tf_op jit(solution)/shard_map/ppermute | solution.py:151
  116.0 3.9 %all-to-all-start.1 = ((bf16[8,128,96]{1,2,0:T(8,128)(2,1)}), bf16[8,128,96]{1,2,0:T(8,128)(2,1)S(1)}, u32[]{:S(2)}, u32[]{:S(2)}) async-start(bf16[8,128,96]{1,2,0:T(8,128)(2,1)} %bitcast.72), calls=%async_computation.1 | async-start | bytes 393216 | tf_op jit(solution)/shard_map/all_to_all | solution.py:241
  119.9 8.6 %all-to-all-done.1 = bf16[8,128,96]{1,2,0:T(8,128)(2,1)S(1)} async-done(((bf16[8,128,96]{1,2,0:T(8,128)(2,1)}), bf16[8,128,96]{1,2,0:T(8,128)(2,1)S(1)}, u32[]{:S(2)}, u32[]{:S(2)}) %all-to-all-start.1) | async-done | bytes 196640 | tf_op jit(solution)/shard_map/all_to_all | solution.py:241
  128.6 1.5 %fusion.7 = bf16[1024,96]{0,1:T(8,128)(2,1)} fusion(s32[1024]{0:T(1024)S(1)} %copy-done.12, bf16[8,128,96]{1,2,0:T(8,128)(2,1)S(1)} %all-to-all-done.1), kind=kOutput, calls=%fused_computation.12 | convolution fusion | flops 202473472 | bytes 397312 | tf_op jit(solution)/shard_map/dot_general | solution.py:21
  130.4 1.7 %convert_multiply_fusion = f32[2592,256]{1,0:T(8,128)} fusion(bf16[1408,256]{1,0:T(8,128)(2,1)S(1)} %get-tuple-element.10, bf16[1408,256]{1,0:T(8,128)(2,1)S(1)} %get-tuple-element.9), kind=kLoop, calls=%fused_computation.3 | loop fusion | flops 3317760 | bytes 4096000 | tf_op jit(solution)/shard_map/mul | solution.py:234
  (75 shorter events, 12.6 us)
Async XLA Ops:
  0.6 10.6 %copy-start.10 = (s32[2]{0:T(128)S(1)}, s32[2]{0:T(128)}, u32[]{:S(2)}) copy-start(s32[2]{0:T(128)} %param.11) | copy-start | bytes 28
  0.7 12.5 %copy-start.11 = (s32[256]{0:T(256)S(1)}, s32[256]{0:T(256)}, u32[]{:S(2)}) copy-start(s32[256]{0:T(256)} %param.10) | copy-start | bytes 3076
  3.3 19.5 %copy-start.1 = (bf16[27,96,256]{2,1,0:T(8,128)(2,1)S(1)}, bf16[27,96,256]{2,1,0:T(8,128)(2,1)}, u32[]{:S(2)}) copy-start(bf16[27,96,256]{2,1,0:T(8,128)(2,1)} %param.13) | copy-start | bytes 3981316
  4.0 15.2 %all-to-all-start = ((bf16[8,128,96]{1,2,0:T(8,128)(2,1)}), bf16[8,128,96]{1,2,0:T(8,128)(2,1)S(1)}, u32[]{:S(2)}, u32[]{:S(2)}) async-start(bf16[8,128,96]{1,2,0:T(8,128)(2,1)} %bitcast.73), calls=%async_computation | async-start | bytes 393216 | tf_op jit(solution)/shard_map/all_to_all | solution.py:219
  13.2 9.6 %copy-start.13 = (bf16[128]{0:T(256)(128)(2,1)}, bf16[128]{0:T(256)(128)(2,1)S(1)}, u32[]{:S(2)}) copy-start(bf16[128]{0:T(256)(128)(2,1)S(1)} %compare_convert_fusion.1) | copy-start | bytes 772
  19.2 3.5 %copy-start.9 = (bf16[8,128,96]{1,2,0:T(8,128)(2,1)}, bf16[8,128,96]{1,2,0:T(8,128)(2,1)S(1)}, u32[]{:S(2)}) copy-start(bf16[8,128,96]{1,2,0:T(8,128)(2,1)S(1)} %all-to-all-done) | copy-start | bytes 589828
  20.4 4.5 %collective-permute-start = (bf16[96,128]{1,0:T(8,128)(2,1)}, bf16[96,128]{1,0:T(8,128)(2,1)}, u32[]{:S(2)}, u32[]{:S(2)}) collective-permute-start(bf16[96,128]{1,0:T(8,128)(2,1)} %get-tuple-element.28), channel_id=1, source_target_pairs={{0,4},{4,0},{8,12},{12,8},{16,20},{20,16},{24,28},{28,24},{1,5},{5... | collective-permute-start | bytes 73736 | tf_op jit(solution)/shard_map/ppermute | solution.py:199
  21.5 3.5 %collective-permute-start.1 = (bf16[96,128]{1,0:T(8,128)(2,1)}, bf16[96,128]{1,0:T(8,128)(2,1)}, u32[]{:S(2)}, u32[]{:S(2)}) collective-permute-start(bf16[96,128]{1,0:T(8,128)(2,1)} %get-tuple-element.29), channel_id=1, source_target_pairs={{4,8},{8,4},{12,16},{16,12},{20,24},{24,20},{5,9},{9,5},{13,17},{1... | collective-permute-start | bytes 73736 | tf_op jit(solution)/shard_map/ppermute | solution.py:199
  23.7 2.1 %copy-start.3 = (bf16[1024,256]{1,0:T(8,128)(2,1)S(1)}, bf16[1024,256]{1,0:T(8,128)(2,1)}, u32[]{:S(2)}) copy-start(bf16[1024,256]{1,0:T(8,128)(2,1)} %cot_ref.1) | copy-start | bytes 1572868
  23.7 2.1 %copy-start.6 = (f32[256]{0:T(256)S(1)}, f32[256]{0:T(256)}, u32[]{:S(2)}) copy-start(f32[256]{0:T(256)} %param.14) | copy-start | bytes 3076
  46.3 2.4 %collective-permute-start.4 = (bf16[1408,256]{1,0:T(8,128)(2,1)S(1)}, bf16[1408,256]{1,0:T(8,128)(2,1)}, u32[]{:S(2)}, u32[]{:S(2)}) collective-permute-start(bf16[1408,256]{1,0:T(8,128)(2,1)S(1)} %dynamic-slice_bitcast_fusion), channel_id=1, source_target_pairs={{0,1},{1,0},{2,3},{3,2},{4,5},{5,4},{6,7},{7,6},{8,9},{9,8},{10,11... | collective-permute-start | bytes 2162696 | tf_op jit(solution)/shard_map/ppermute | solution.py:151
  50.0 19.4 %copy-start.2 = (bf16[27,96,256]{2,1,0:T(8,128)(2,1)S(1)}, bf16[27,96,256]{2,1,0:T(8,128)(2,1)}, u32[]{:S(2)}) copy-start(bf16[27,96,256]{2,1,0:T(8,128)(2,1)} %param.13) | copy-start | bytes 3981316
  50.0 19.4 %copy-start.5 = (s32[27,1024]{1,0:T(8,128)S(1)}, s32[27,1024]{1,0:T(8,128)}, u32[]{:S(2)}) copy-start(s32[27,1024]{1,0:T(8,128)} %map_ref.3) | copy-start | bytes 331780
  50.0 19.4 %copy-start.8 = (bf16[1024,256]{1,0:T(8,128)(2,1)S(1)}, bf16[1024,256]{1,0:T(8,128)(2,1)}, u32[]{:S(2)}) copy-start(bf16[1024,256]{1,0:T(8,128)(2,1)} %copy-done.7) | copy-start | bytes 1572868
  50.1 6.8 %collective-permute-start.5 = (bf16[352,256]{1,0:T(8,128)(2,1)S(1)}, bf16[352,256]{1,0:T(8,128)(2,1)}, u32[]{:S(2)}, u32[]{:S(2)}) collective-permute-start(bf16[352,256]{1,0:T(8,128)(2,1)S(1)} %get-tuple-element.14), channel_id=1, source_target_pairs={{0,2},{1,3},{2,0},{3,1},{4,6},{5,7},{6,4},{7,5},{8,10},{9,11},{10,... | collective-permute-start | bytes 540680 | tf_op jit(solution)/shard_map/ppermute | solution.py:151
  51.7 9.8 %collective-permute-start.7 = (bf16[352,256]{1,0:T(8,128)(2,1)S(1)}, bf16[352,256]{1,0:T(8,128)(2,1)}, u32[]{:S(2)}, u32[]{:S(2)}) collective-permute-start(bf16[352,256]{1,0:T(8,128)(2,1)S(1)} %get-tuple-element.15), channel_id=1, source_target_pairs={{0,6},{1,7},{2,4},{3,5},{4,2},{5,3},{6,0},{7,1},{8,14},{9,15},{10,... | collective-permute-start | bytes 540680 | tf_op jit(solution)/shard_map/ppermute | solution.py:151
  56.0 8.6 %collective-permute-start.6 = (bf16[352,256]{1,0:T(8,128)(2,1)S(1)}, bf16[352,256]{1,0:T(8,128)(2,1)}, u32[]{:S(2)}, u32[]{:S(2)}) collective-permute-start(bf16[352,256]{1,0:T(8,128)(2,1)S(1)} %get-tuple-element.16), channel_id=1, source_target_pairs={{0,4},{1,5},{2,6},{3,7},{4,0},{5,1},{6,2},{7,3},{8,12},{9,13},{10,... | collective-permute-start | bytes 540680 | tf_op jit(solution)/shard_map/ppermute | solution.py:151
  65.8 30.6 %collective-permute-start.8 = (bf16[88,256]{1,0:T(8,128)(2,1)S(1)}, bf16[88,256]{1,0:T(8,128)(2,1)S(1)}, u32[]{:S(2)}, u32[]{:S(2)}) collective-permute-start(bf16[88,256]{1,0:T(8,128)(2,1)S(1)} %get-tuple-element.23), channel_id=1, source_target_pairs={{0,8},{1,9},{2,10},{3,11},{4,12},{5,13},{6,14},{7,15},{8,0},{9,1},... | collective-permute-start | bytes 135176 | tf_op jit(solution)/shard_map/ppermute | solution.py:151
  67.0 29.5 %collective-permute-start.10 = (bf16[88,256]{1,0:T(8,128)(2,1)S(1)}, bf16[88,256]{1,0:T(8,128)(2,1)S(1)}, u32[]{:S(2)}, u32[]{:S(2)}) collective-permute-start(bf16[88,256]{1,0:T(8,128)(2,1)S(1)} %get-tuple-element.24), channel_id=1, source_target_pairs={{0,24},{1,25},{2,26},{3,27},{4,28},{5,29},{6,30},{7,31},{8,16},{9,... | collective-permute-start | bytes 135176 | tf_op jit(solution)/shard_map/ppermute | solution.py:151
  68.1 28.4 %collective-permute-start.9 = (bf16[88,256]{1,0:T(8,128)(2,1)S(1)}, bf16[88,256]{1,0:T(8,128)(2,1)S(1)}, u32[]{:S(2)}, u32[]{:S(2)}) collective-permute-start(bf16[88,256]{1,0:T(8,128)(2,1)S(1)} %get-tuple-element.25), channel_id=1, source_target_pairs={{0,16},{1,17},{2,18},{3,19},{4,20},{5,21},{6,22},{7,23},{8,24},{9,... | collective-permute-start | bytes 135176 | tf_op jit(solution)/shard_map/ppermute | solution.py:151
  96.4 12.6 %copy-start.14 = (bf16[128]{0:T(256)(128)(2,1)S(1)}, bf16[128]{0:T(256)(128)(2,1)}, u32[]{:S(2)}) copy-start(bf16[128]{0:T(256)(128)(2,1)} %copy-done.13) | copy-start | bytes 772
  96.5 7.0 %collective-permute-start.13 = (bf16[88,256]{1,0:T(8,128)(2,1)S(1)}, bf16[88,256]{1,0:T(8,128)(2,1)S(1)}, u32[]{:S(2)}, u32[]{:S(2)}) collective-permute-start(bf16[88,256]{1,0:T(8,128)(2,1)S(1)} %fusion.41), channel_id=1, source_target_pairs={{0,8},{1,9},{2,10},{3,11},{4,12},{5,13},{6,14},{7,15},{8,0},{9,1},... | collective-permute-start | bytes 135176 | tf_op jit(solution)/shard_map/ppermute | solution.py:151
  98.6 4.9 %collective-permute-start.12 = (bf16[88,256]{1,0:T(8,128)(2,1)S(1)}, bf16[88,256]{1,0:T(8,128)(2,1)S(1)}, u32[]{:S(2)}, u32[]{:S(2)}) collective-permute-start(bf16[88,256]{1,0:T(8,128)(2,1)S(1)} %fusion.41), channel_id=1, source_target_pairs={{0,16},{1,17},{2,18},{3,19},{4,20},{5,21},{6,22},{7,23},{8,24},{9,... | collective-permute-start | bytes 135176 | tf_op jit(solution)/shard_map/ppermute | solution.py:151
  99.3 6.1 %collective-permute-start.11 = (bf16[88,256]{1,0:T(8,128)(2,1)S(1)}, bf16[88,256]{1,0:T(8,128)(2,1)S(1)}, u32[]{:S(2)}, u32[]{:S(2)}) collective-permute-start(bf16[88,256]{1,0:T(8,128)(2,1)S(1)} %fusion.41), channel_id=1, source_target_pairs={{0,24},{1,25},{2,26},{3,27},{4,28},{5,29},{6,30},{7,31},{8,16},{9,... | collective-permute-start | bytes 135176 | tf_op jit(solution)/shard_map/ppermute | solution.py:151
  101.1 7.9 %collective-permute-start.2 = (bf16[96,128]{1,0:T(8,128)(2,1)S(1)}, bf16[96,128]{1,0:T(8,128)(2,1)S(1)}, u32[]{:S(2)}, u32[]{:S(2)}) collective-permute-start(bf16[96,128]{1,0:T(8,128)(2,1)S(1)} %get-tuple-element.17), channel_id=1, source_target_pairs={{0,4},{4,0},{8,12},{12,8},{16,20},{20,16},{24,28},{28,24},{1,5},{5... | collective-permute-start | bytes 73736 | tf_op jit(solution)/shard_map/ppermute | solution.py:199
  102.9 6.2 %collective-permute-start.3 = (bf16[96,128]{1,0:T(8,128)(2,1)S(1)}, bf16[96,128]{1,0:T(8,128)(2,1)S(1)}, u32[]{:S(2)}, u32[]{:S(2)}) collective-permute-start(bf16[96,128]{1,0:T(8,128)(2,1)S(1)} %get-tuple-element.18), channel_id=1, source_target_pairs={{4,8},{8,4},{12,16},{16,12},{20,24},{24,20},{5,9},{9,5},{13,17},{1... | collective-permute-start | bytes 73736 | tf_op jit(solution)/shard_map/ppermute | solution.py:199
  105.5 6.4 %collective-permute-start.16 = (bf16[352,256]{1,0:T(8,128)(2,1)S(1)}, bf16[352,256]{1,0:T(8,128)(2,1)S(1)}, u32[]{:S(2)}, u32[]{:S(2)}) collective-permute-start(bf16[352,256]{1,0:T(8,128)(2,1)S(1)} %pad_maximum_fusion.2), channel_id=1, source_target_pairs={{0,2},{1,3},{2,0},{3,1},{4,6},{5,7},{6,4},{7,5},{8,10},{9,11},{10,... | collective-permute-start | bytes 540680 | tf_op jit(solution)/shard_map/ppermute | solution.py:151
  107.1 5.5 %collective-permute-start.15 = (bf16[352,256]{1,0:T(8,128)(2,1)S(1)}, bf16[352,256]{1,0:T(8,128)(2,1)S(1)}, u32[]{:S(2)}, u32[]{:S(2)}) collective-permute-start(bf16[352,256]{1,0:T(8,128)(2,1)S(1)} %pad_maximum_fusion.2), channel_id=1, source_target_pairs={{0,4},{1,5},{2,6},{3,7},{4,0},{5,1},{6,2},{7,3},{8,12},{9,13},{10,... | collective-permute-start | bytes 540680 | tf_op jit(solution)/shard_map/ppermute | solution.py:151
  108.2 6.4 %collective-permute-start.14 = (bf16[352,256]{1,0:T(8,128)(2,1)S(1)}, bf16[352,256]{1,0:T(8,128)(2,1)S(1)}, u32[]{:S(2)}, u32[]{:S(2)}) collective-permute-start(bf16[352,256]{1,0:T(8,128)(2,1)S(1)} %pad_maximum_fusion.2), channel_id=1, source_target_pairs={{0,6},{1,7},{2,4},{3,5},{4,2},{5,3},{6,0},{7,1},{8,14},{9,15},{10,... | collective-permute-start | bytes 540680 | tf_op jit(solution)/shard_map/ppermute | solution.py:151
  114.9 13.7 %copy-start.12 = (s32[1024]{0:T(1024)S(1)}, s32[1024]{0:T(1024)}, u32[]{:S(2)}) copy-start(s32[1024]{0:T(1024)} %param.9) | copy-start | bytes 12292
  114.9 15.2 %collective-permute-start.17 = (bf16[1408,256]{1,0:T(8,128)(2,1)S(1)}, bf16[1408,256]{1,0:T(8,128)(2,1)S(1)}, u32[]{:S(2)}, u32[]{:S(2)}) collective-permute-start(bf16[1408,256]{1,0:T(8,128)(2,1)S(1)} %pad_maximum_fusion.1), channel_id=1, source_target_pairs={{0,1},{1,0},{2,3},{3,2},{4,5},{5,4},{6,7},{7,6},{8,9},{9,8},{10,11... | collective-permute-start | bytes 2162696 | tf_op jit(solution)/shard_map/ppermute | solution.py:151
  116.0 12.5 %all-to-all-start.1 = ((bf16[8,128,96]{1,2,0:T(8,128)(2,1)}), bf16[8,128,96]{1,2,0:T(8,128)(2,1)S(1)}, u32[]{:S(2)}, u32[]{:S(2)}) async-start(bf16[8,128,96]{1,2,0:T(8,128)(2,1)} %bitcast.72), calls=%async_computation.1 | async-start | bytes 393216 | tf_op jit(solution)/shard_map/all_to_all | solution.py:241
  (3 other events, 2.6 us)

commit v2 on v1

--- a/solution.py
+++ b/solution.py
@@ -12,7 +12,7 @@
 F32 = jnp.float32
 LOW = 256
 SHIFT = 8
-VMEM_LIMIT = 48 << 20
+VMEM_LIMIT = 32 << 20
 AXES = ("brick", "group")
 
 
@@ -26,34 +26,44 @@
     return (index[:, None] == columns[None, :]).astype(BF)
 
 
-def forward_kernel(x_ref, map_ref, wt_ref, bias_ref, cot_ref, out_ref, pg_ref, wg_ref, g_ref):
+def one_hot_low(row, lanes):
+    low = (row & (LOW - 1)).astype(F32).astype(BF)
+    iota = lax.broadcasted_iota(jnp.int32, (LOW, lanes), 0).astype(BF)
+    hit = iota == jnp.broadcast_to(low, (LOW, lanes))
+    return jnp.where(hit, jnp.ones((), BF), jnp.zeros((), BF))
+
+
+def forward_kernel(local_ref, prev_ref, next_ref, map_ref, w_ref, bias_ref, cot_ref, out_ref, pg_ref, wg_ref, g_ref, x_ref, wt_ref):
     offsets, voxels = map_ref.shape
-    depth = wt_ref.shape[1]
+    depth, c_out = w_ref.shape
     channels = depth // offsets
+    here = voxels // LOW
     blocks = x_ref.shape[0] // channels
-    lanes = min(256, voxels)
-    iota = lax.broadcasted_iota(jnp.int32, (LOW, lanes), 0).astype(BF)
-
-    def offset(k, carry):
-        row = map_ref[pl.ds(k, 1), :]
-        low = (row & (LOW - 1)).astype(F32).astype(BF)
+    center = offsets // 2
+    for a in range(here):
+        x_ref[a * channels : (a + 1) * channels, :] = local_ref[a * LOW : (a + 1) * LOW, :].T
+    half = prev_ref.shape[1]
+    x_ref[here * channels :, :half] = prev_ref[...]
+    x_ref[here * channels :, half:] = next_ref[...]
+    for k in range(offsets):
+        wt_ref[:, k * channels : (k + 1) * channels] = w_ref[k * channels : (k + 1) * channels, :].T
+        at = slice(k * channels, (k + 1) * channels)
+        if k == center:
+            for a in range(here):
+                g_ref[at, a * LOW : (a + 1) * LOW] = x_ref[a * channels : (a + 1) * channels, :]
+            continue
+        row = map_ref[k : k + 1, :]
         high = lax.shift_right_logical(row, SHIFT)
-        at = pl.ds(pl.multiple_of(k * channels, channels), channels)
-        for n in range(voxels // lanes):
-            sl = slice(n * lanes, (n + 1) * lanes)
-            hit = iota == jnp.broadcast_to(low[:, sl], (LOW, lanes))
-            hot = jnp.where(hit, jnp.ones((), BF), jnp.zeros((), BF))
-            block = jnp.broadcast_to(high[:, sl], (channels, lanes))
-            picked = jnp.zeros((channels, lanes), F32)
+        for n in range(here):
+            sl = slice(n * LOW, (n + 1) * LOW)
+            terms = dot(x_ref[...], one_hot_low(row[:, sl], LOW), 1, 0)
+            block = jnp.broadcast_to(high[:, sl], (channels, LOW))
+            picked = jnp.zeros((channels, LOW), F32)
             for a in range(blocks):
-                term = dot(x_ref[a * channels : (a + 1) * channels, :], hot, 1, 0)
-                picked = jnp.where(block == a, term, picked)
+                picked = jnp.where(block == a, terms[a * channels : (a + 1) * channels], picked)
             g_ref[at, sl] = picked.astype(BF)
-        return carry
-
-    lax.fori_loop(0, offsets, offset, 0)
-    for n in range(voxels // lanes):
-        sl = slice(n * lanes, (n + 1) * lanes)
+    for n in range(here):
+        sl = slice(n * LOW, (n + 1) * LOW)
         pre = dot(wt_ref[...], g_ref[:, sl], 1, 0).T + bias_ref[...]
         out_ref[sl, :] = jnp.maximum(pre, 0.0).astype(BF)
         pg_ref[sl, :] = jnp.where(pre > 0, cot_ref[sl, :].astype(F32), 0.0).astype(BF)
@@ -61,45 +71,39 @@
     for m in range(9):
         sl = slice(m * step, (m + 1) * step)
         wg_ref[sl, :] = dot(g_ref[sl, :], pg_ref[...], 1, 0).astype(BF)
-    wg_ref[depth:, :] = jnp.zeros((wg_ref.shape[0] - depth, wg_ref.shape[1]), BF)
-
-
-def backward_kernel(pg_ref, map_ref, w_ref, acc_ref, c_ref):
+    wg_ref[depth:, :] = jnp.zeros((wg_ref.shape[0] - depth, c_out), BF)
+
+
+def backward_kernel(first, last, pg_ref, map_ref, w_ref, *refs):
+    in_ref, acc_ref = refs if len(refs) == 2 else (None, refs[0])
     offsets, voxels = map_ref.shape
-    depth = w_ref.shape[0]
-    channels = depth // offsets
+    channels = w_ref.shape[0] // offsets
+    here = voxels // LOW
     blocks = acc_ref.shape[0] // channels
-    step = depth // 9
-    for m in range(9):
-        sl = slice(m * step, (m + 1) * step)
-        c_ref[sl, :] = dot(w_ref[sl, :], pg_ref[...], 1, 1).astype(BF)
-    acc_ref[...] = jnp.zeros_like(acc_ref)
-    iota = lax.broadcasted_iota(jnp.int32, (LOW, voxels), 0).astype(BF)
-
-    def offset(k, carry):
-        row = map_ref[pl.ds(k, 1), :]
-        low = (row & (LOW - 1)).astype(F32).astype(BF)
+    acc_ref[...] = jnp.zeros_like(acc_ref) if in_ref is None else in_ref[...]
+    for k in range(first, last):
+        contrib = dot(w_ref[k * channels : (k + 1) * channels, :], pg_ref[...], 1, 1)
+        if k == offsets // 2:
+            for a in range(here):
+                acc_ref[a * channels : (a + 1) * channels, :] += contrib[:, a * LOW : (a + 1) * LOW]
+            continue
+        contrib = contrib.astype(BF)
+        row = map_ref[k : k + 1, :]
         high = lax.shift_right_logical(row, SHIFT).astype(F32).astype(BF)
-        hit = iota == jnp.broadcast_to(low, (LOW, voxels))
-        hot = jnp.where(hit, jnp.ones((), BF), jnp.zeros((), BF))
-        contrib = c_ref[pl.ds(pl.multiple_of(k * channels, channels), channels), :]
         block = jnp.broadcast_to(high, (channels, voxels))
-        for a in range(blocks):
-            part = jnp.where(block == jnp.array(a, BF), contrib, jnp.zeros((), BF))
-            acc_ref[a * channels : (a + 1) * channels, :] += dot(part, hot, 1, 1)
-        return carry
-
-    lax.fori_loop(0, offsets, offset, 0)
+        parts = [jnp.where(block == jnp.array(a, BF), contrib, jnp.zeros((), BF)) for a in range(blocks)]
+        acc_ref[...] += dot(jnp.concatenate(parts, 0), one_hot_low(row, voxels), 1, 1)
 
 
 def whole(count):
     return [pl.BlockSpec(memory_space=pltpu.VMEM)] * count
 
 
-def forward(x, maps, wt, bias, cot, padded):
+def forward(local, prev_upper, next_lower, maps, w, bias, cot, padded):
     offsets, voxels = maps.shape
-    c_out, depth = wt.shape
-    macs = voxels * depth * c_out * 2 + offsets * voxels * LOW * x.shape[0]
+    depth, c_out = w.shape
+    rows = depth // offsets * (voxels // LOW + 1)
+    macs = voxels * depth * c_out * 2 + offsets * voxels * LOW * rows
     return pl.pallas_call(
         forward_kernel,
         out_shape=(
@@ -107,27 +111,27 @@
             jax.ShapeDtypeStruct((voxels, c_out), BF),
             jax.ShapeDtypeStruct((padded, c_out), BF),
         ),
-        in_specs=whole(5),
+        in_specs=whole(7),
         out_specs=tuple(whole(3)),
-        scratch_shapes=[pltpu.VMEM((depth, voxels), BF)],
+        scratch_shapes=[pltpu.VMEM((depth, voxels), BF), pltpu.VMEM((rows, LOW), BF), pltpu.VMEM((c_out, depth), BF)],
         compiler_params=pltpu.CompilerParams(vmem_limit_bytes=VMEM_LIMIT),
         cost_estimate=pl.CostEstimate(flops=2 * macs, bytes_accessed=5 << 20, transcendentals=0),
-    )(x, maps, wt, bias, cot)
-
-
-def backward(pg, maps, w, rows):
+    )(local, prev_upper, next_lower, maps, w, bias, cot)
+
+
+def backward(first, last, pg, maps, w, acc, rows):
     offsets, voxels = maps.shape
     depth, c_out = w.shape
-    macs = voxels * depth * c_out + offsets * voxels * LOW * rows
+    macs = (voxels * depth * c_out + offsets * voxels * LOW * rows) * (last - first) // offsets
+    args = (pg, maps, w) if acc is None else (pg, maps, w, acc)
     return pl.pallas_call(
-        backward_kernel,
+        functools.partial(backward_kernel, first, last),
         out_shape=jax.ShapeDtypeStruct((rows, LOW), F32),
-        in_specs=whole(3),
+        in_specs=whole(len(args)),
         out_specs=whole(1)[0],
-        scratch_shapes=[pltpu.VMEM((depth, voxels), BF)],
         compiler_params=pltpu.CompilerParams(vmem_limit_bytes=VMEM_LIMIT),
-        cost_estimate=pl.CostEstimate(flops=2 * macs, bytes_accessed=4 << 20, transcendentals=0),
-    )(pg, maps, w)
+        cost_estimate=pl.CostEstimate(flops=2 * macs, bytes_accessed=3 << 20, transcendentals=0),
+    )(*args)
 
 
 def stages(count):
@@ -213,7 +217,6 @@
     blocks = rows // LOW
 
     w = weight.reshape(depth, c_out)
-    wt = w.T
     order_pick = one_hot_rows(order, rows)
     sent = dot(order_pick, features, 1, 0).astype(BF)
     local = lax.all_to_all(sent, "brick", split_axis=0, concat_axis=0, tiled=True)
@@ -225,15 +228,17 @@
     upper = dot(local, upper_pick, 0, 1).astype(BF)
     prev_upper, next_lower = meet(upper, lower)
 
-    x_local = local.reshape(blocks, LOW, channels).transpose(0, 2, 1).reshape(blocks * channels, LOW)
-    x = jnp.concatenate([x_local, jnp.concatenate([prev_upper, next_lower], 1)], 0)
-    output, pre_grad, kernel_grads = forward(x, kernel_map, wt, bias[None], cotangent, padded)
+    output, pre_grad, kernel_grads = forward(
+        local, prev_upper, next_lower, kernel_map, w, bias[None], cotangent, padded
+    )
 
     weight_sum = sum_over_all(kernel_grads, count)
     scale = jnp.float32(1.0 / math.sqrt(count * rows))
     weight_grad = (weight_sum[:depth].astype(F32) * scale).reshape(offsets, channels, c_out)
 
-    acc = backward(pre_grad, kernel_map, w, x.shape[0])
+    acc = None
+    for first, last in ((0, offsets // 3), (offsets // 3, 2 * offsets // 3), (2 * offsets // 3, offsets)):
+        acc = backward(first, last, pre_grad, kernel_map, w, acc, (blocks + 1) * channels)
     faces = acc[blocks * channels :].astype(BF)
     from_prev, from_next = meet(faces[:, face:], faces[:, :face])
     here = acc[: blocks * channels].reshape(blocks, channels, LOW).transpose(0, 2, 1).reshape(rows, channels)

time: 133 us -> 105 us (0.79)
  Pallas kernels: 45.8 us -> 25.9 us
  waiting for transfers between devices: 32.6 us -> 27.9 us
  other arithmetic: 7 us -> 5.14 us
    pallas_call x1 -> x3, Pallas kernels: 27 us -> 15.9 us  [backward(): pl.pallas_call(functools.partial(backward_kernel, first, last), out_shape...]
    pallas_call x1, Pallas kernels: 18.7 us -> 10 us  [forward(): pl.pallas_call(forward_kernel, out_shape=(jax.ShapeDtypeStruct((voxels, c...]
    ppermute x14, waiting for transfers between devices: 17.9 us -> 11.5 us  [swapped(): return lax.ppermute(array, AXES, [(i, partner(i)) for i in range(count)])]
    ppermute x4, waiting for transfers between devices: 0.01 us -> 1.81 us  [meet(): lax.ppermute(jnp.where(goes_up, array_up, array_down), 'brick', pairs)]
    unnamed x30 -> x20, local copies, waits for them, and re-layouts: 2.66 us -> 3.8 us
  transfers between devices with their start and end apart: 20 -> 20, of which waited for: 10 -> 9; matrix products, arithmetic and copies ran while one was open for 5% -> 5% of each run, Pallas kernels for 20% -> 15%
where the time goes in v2:
time: 105 us; the launch traced here: 104 us
  starting transfers between devices  32.9 us (31%)
  waiting for transfers between devices  27.9 us (27%)
  Pallas kernels  25.9 us (25%)
  local copies, waits for them, and re-layouts  7.02 us (7%)
  other arithmetic  5.14 us (5%)
  matrix products  4.44 us (4%)
    ppermute x14, starting transfers between devices, swapped(): return lax.ppermute(array, AXES, [(i, partner(i)) for i in range(count)])  16.7 us
    pallas_call x3, Pallas kernels, backward(): pl.pallas_call(functools.partial(backward_kernel, first, last), out_shape...  15.9 us
    ppermute x14, waiting for transfers between devices, swapped(): return lax.ppermute(array, AXES, [(i, partner(i)) for i in range(count)])  11.5 us
    pallas_call x1, Pallas kernels, forward(): pl.pallas_call(forward_kernel, out_shape=(jax.ShapeDtypeStruct((voxels, c...  10 us
    all_to_all x1, waiting for transfers between devices, on_device(): lax.all_to_all(local_grad.astype(BF), 'brick', split_axis=0, concat_axis=...  8.61 us
    all_to_all x1, starting transfers between devices, on_device(): lax.all_to_all(sent, 'brick', split_axis=0, concat_axis=0, tiled=True)  7.25 us
    all_to_all x1, waiting for transfers between devices, on_device(): lax.all_to_all(sent, 'brick', split_axis=0, concat_axis=0, tiled=True)  6.01 us
    ppermute x4, starting transfers between devices, meet(): lax.ppermute(jnp.where(goes_up, array_up, array_down), 'brick', pairs)  4.97 us
  transfers between devices with their start and end apart: 20, of which 9 were waited for; matrix products, arithmetic and copies ran while one was open for 5% of the time, Pallas kernels for 15%

profile of v2, /device:TPU:0, one launch (start us, length us, event | category | flops | bytes accessed | tf_op | source)
XLA Modules:
  0.0 104.3 jit_solution(13664947453581969083)
XLA Ops:
  0.7 0.9 copy-done
  1.6 1.7 %fusion.10 = bf16[12,8,8,128]{3,2,1,0:T(8,128)(2,1)S(1)} fusion(bf16[1024,96]{0,1:T(8,128)(2,1)S(1)} %copy-done, s32[1024]{0:T(1024)} %param.9), kind=kOutput, calls=%fused_computation.15 | convolution fusion | flops 202473472 | bytes 397312 | tf_op jit(solution)/shard_map/dot_general | solution.py:21
  4.0 7.3 %all-to-all-start = ((bf16[8,128,96]{1,2,0:T(8,128)(2,1)}), bf16[8,128,96]{1,2,0:T(8,128)(2,1)S(1)}, u32[]{:S(2)}, u32[]{:S(2)}) async-start(bf16[8,128,96]{1,2,0:T(8,128)(2,1)} %bitcast.56), calls=%async_computation | async-start | bytes 393216 | tf_op jit(solution)/shard_map/all_to_all | solution.py:222
  13.2 6.0 %all-to-all-done = bf16[8,128,96]{1,2,0:T(8,128)(2,1)S(1)} async-done(((bf16[8,128,96]{1,2,0:T(8,128)(2,1)}), bf16[8,128,96]{1,2,0:T(8,128)(2,1)S(1)}, u32[]{:S(2)}, u32[]{:S(2)}) %all-to-all-start) | async-done | bytes 196640 | tf_op jit(solution)/shard_map/all_to_all | solution.py:222
  20.7 3.1 %collective-permute-start = (bf16[96,128]{1,0:T(8,128)(2,1)S(1)}, bf16[96,128]{1,0:T(8,128)(2,1)S(1)}, u32[]{:S(2)}, u32[]{:S(2)}) collective-permute-start(bf16[96,128]{1,0:T(8,128)(2,1)S(1)} %get-tuple-element.29), channel_id=1, source_target_pairs={{0,4},{4,0},{8,12},{12,8},{16,20},{20,16},{24,28},{28,24},{1,5},{5... | collective-permute-start | bytes 73736 | tf_op jit(solution)/shard_map/ppermute | solution.py:203
  23.8 1.8 %collective-permute-done = bf16[96,128]{1,0:T(8,128)(2,1)S(1)} collective-permute-done((bf16[96,128]{1,0:T(8,128)(2,1)S(1)}, bf16[96,128]{1,0:T(8,128)(2,1)S(1)}, u32[]{:S(2)}, u32[]{:S(2)}) %collective-permute-start) | collective-permute-done | bytes 24608 | tf_op jit(solution)/shard_map/ppermute | solution.py:203
  25.6 1.0 copy-done.2
  26.7 10.0 %shard_map.103 = (bf16[1024,256]{1,0:T(8,128)(2,1)}, bf16[1024,256]{1,0:T(8,128)(2,1)S(1)}, bf16[2816,256]{1,0:T(8,128)(2,1)S(1)}) custom-call(bf16[1024,96]{1,0:T(8,128)(2,1)S(1)} %bitcast.61, bf16[96,128]{1,0:T(8,128)(2,1)S(1)} %get-tuple-element.27.prev_ref, bf16[96,128]{1,0:T(8,128)(2,1)S(1)} %get-tuple-element.26.next_ref, s32[27,1024]{1,0:T(8,128)S(1)} %copy-done.3, ...), custom_call_target="tpu_custom_call" | custom-call | flops 9512681472 | bytes 5242880 | tf_op jit(solution)/shard_map/pallas_call | solution.py:107
  37.5 0.9 dynamic-slice_bitcast_fusion
  38.4 1.0 copy-done.6
  39.5 5.5 %shard_map.104.refs_0_ = f32[480,256]{1,0:T(8,128)S(1)} custom-call(bf16[1024,256]{1,0:T(8,128)(2,1)S(1)} %copy-done.6, s32[27,1024]{1,0:T(8,128)S(1)} %copy-done.3, bf16[2592,256]{1,0:T(8,128)(2,1)S(1)} %bitcast.63), custom_call_target="tpu_custom_call" | custom-call | flops 2717908992 | bytes 3145728 | tf_op jit(solution)/shard_map/pallas_call | solution.py:127
  45.0 1.3 %fusion.4 = bf16[1408,256]{1,0:T(8,128)(2,1)S(1)} fusion(bf16[1408,256]{1,0:T(8,128)(2,1)} %collective-permute-done.4, bf16[2,1408,256]{2,1,0:T(8,128)(2,1)S(1)} %bitcast.58, s32[]{:T(128)S(6)} %select_n.252), kind=kLoop, calls=%fused_computation.7 | loop fusion | flops 1441792 | bytes 2162692 | tf_op jit(solution)/shard_map/convert_element_type | solution.py:180
  46.4 1.6 %collective-permute-start.5 = (bf16[352,256]{1,0:T(8,128)(2,1)S(1)}, bf16[352,256]{1,0:T(8,128)(2,1)S(1)}, u32[]{:S(2)}, u32[]{:S(2)}) collective-permute-start(bf16[352,256]{1,0:T(8,128)(2,1)S(1)} %get-tuple-element.14), channel_id=1, source_target_pairs={{0,2},{1,3},{2,0},{3,1},{4,6},{5,7},{6,4},{7,5},{8,10},{9,11},{10,... | collective-permute-start | bytes 540680 | tf_op jit(solution)/shard_map/ppermute | solution.py:155
  48.0 2.2 %collective-permute-start.7 = (bf16[352,256]{1,0:T(8,128)(2,1)S(1)}, bf16[352,256]{1,0:T(8,128)(2,1)S(1)}, u32[]{:S(2)}, u32[]{:S(2)}) collective-permute-start(bf16[352,256]{1,0:T(8,128)(2,1)S(1)} %get-tuple-element.15), channel_id=1, source_target_pairs={{0,6},{1,7},{2,4},{3,5},{4,2},{5,3},{6,0},{7,1},{8,14},{9,15},{10,... | collective-permute-start | bytes 540680 | tf_op jit(solution)/shard_map/ppermute | solution.py:155
  50.3 5.0 %shard_map.105.refs_0_ = f32[480,256]{1,0:T(8,128)S(1)} custom-call(bf16[1024,256]{1,0:T(8,128)(2,1)S(1)} %copy-done.6, s32[27,1024]{1,0:T(8,128)S(1)} %copy-done.3, bf16[2592,256]{1,0:T(8,128)(2,1)S(1)} %bitcast.64, f32[480,256]{1,0:T(8,128)S(1)} %shard_map.104.refs_0_), custom_call_target="tpu_custom_call" | custom-call | flops 2717908992 | bytes 3145728 | tf_op jit(solution)/shard_map/pallas_call | solution.py:127
  55.3 2.0 %collective-permute-done.5 = bf16[352,256]{1,0:T(8,128)(2,1)S(1)} collective-permute-done((bf16[352,256]{1,0:T(8,128)(2,1)S(1)}, bf16[352,256]{1,0:T(8,128)(2,1)S(1)}, u32[]{:S(2)}, u32[]{:S(2)}) %collective-permute-start.5) | collective-permute-done | bytes 180256 | tf_op jit(solution)/shard_map/ppermute | solution.py:155
  57.3 1.8 %collective-permute-done.6 = bf16[352,256]{1,0:T(8,128)(2,1)S(1)} collective-permute-done((bf16[352,256]{1,0:T(8,128)(2,1)S(1)}, bf16[352,256]{1,0:T(8,128)(2,1)S(1)}, u32[]{:S(2)}, u32[]{:S(2)}) %collective-permute-start.6) | collective-permute-done | bytes 180256 | tf_op jit(solution)/shard_map/ppermute | solution.py:155
  59.2 2.3 %collective-permute-start.8 = (bf16[88,256]{1,0:T(8,128)(2,1)S(1)}, bf16[88,256]{1,0:T(8,128)(2,1)S(1)}, u32[]{:S(2)}, u32[]{:S(2)}) collective-permute-start(bf16[88,256]{1,0:T(8,128)(2,1)S(1)} %get-tuple-element.23), channel_id=1, source_target_pairs={{0,8},{1,9},{2,10},{3,11},{4,12},{5,13},{6,14},{7,15},{8,0},{9,1},... | collective-permute-start | bytes 135176 | tf_op jit(solution)/shard_map/ppermute | solution.py:155
  61.5 1.2 %collective-permute-start.10 = (bf16[88,256]{1,0:T(8,128)(2,1)S(1)}, bf16[88,256]{1,0:T(8,128)(2,1)S(1)}, u32[]{:S(2)}, u32[]{:S(2)}) collective-permute-start(bf16[88,256]{1,0:T(8,128)(2,1)S(1)} %get-tuple-element.24), channel_id=1, source_target_pairs={{0,24},{1,25},{2,26},{3,27},{4,28},{5,29},{6,30},{7,31},{8,16},{9,... | collective-permute-start | bytes 135176 | tf_op jit(solution)/shard_map/ppermute | solution.py:155
  63.0 5.4 %shard_map.106 = f32[480,256]{1,0:T(8,128)S(1)} custom-call(bf16[1024,256]{1,0:T(8,128)(2,1)S(1)} %copy-done.6, s32[27,1024]{1,0:T(8,128)S(1)} %copy-done.3, bf16[2592,256]{1,0:T(8,128)(2,1)S(1)} %bitcast.65, f32[480,256]{1,0:T(8,128)S(1)} %shard_map.105.refs_0_), custom_call_target="tpu_custom_call" | custom-call | flops 2717908992 | bytes 3145728 | tf_op jit(solution)/shard_map/pallas_call | solution.py:127
  68.5 2.9 %collective-permute-start.13 = (bf16[88,256]{1,0:T(8,128)(2,1)S(1)}, bf16[88,256]{1,0:T(8,128)(2,1)S(1)}, u32[]{:S(2)}, u32[]{:S(2)}) collective-permute-start(bf16[88,256]{1,0:T(8,128)(2,1)S(1)} %fusion.37), channel_id=1, source_target_pairs={{0,8},{1,9},{2,10},{3,11},{4,12},{5,13},{6,14},{7,15},{8,0},{9,1},... | collective-permute-start | bytes 135176 | tf_op jit(solution)/shard_map/ppermute | solution.py:155
  71.4 2.4 %collective-permute-start.11 = (bf16[88,256]{1,0:T(8,128)(2,1)S(1)}, bf16[88,256]{1,0:T(8,128)(2,1)S(1)}, u32[]{:S(2)}, u32[]{:S(2)}) collective-permute-start(bf16[88,256]{1,0:T(8,128)(2,1)S(1)} %fusion.37), channel_id=1, source_target_pairs={{0,24},{1,25},{2,26},{3,27},{4,28},{5,29},{6,30},{7,31},{8,16},{9,... | collective-permute-start | bytes 135176 | tf_op jit(solution)/shard_map/ppermute | solution.py:155
  75.2 1.2 %collective-permute-done.12 = bf16[88,256]{1,0:T(8,128)(2,1)S(1)} collective-permute-done((bf16[88,256]{1,0:T(8,128)(2,1)S(1)}, bf16[88,256]{1,0:T(8,128)(2,1)S(1)}, u32[]{:S(2)}, u32[]{:S(2)}) %collective-permute-start.12) | collective-permute-done | bytes 45088 | tf_op jit(solution)/shard_map/ppermute | solution.py:155
  76.4 1.0 collective-permute-done.11
  77.4 1.6 %collective-permute-start.16 = (bf16[352,256]{1,0:T(8,128)(2,1)S(1)}, bf16[352,256]{1,0:T(8,128)(2,1)S(1)}, u32[]{:S(2)}, u32[]{:S(2)}) collective-permute-start(bf16[352,256]{1,0:T(8,128)(2,1)S(1)} %pad_maximum_fusion.2), channel_id=1, source_target_pairs={{0,2},{1,3},{2,0},{3,1},{4,6},{5,7},{6,4},{7,5},{8,10},{9,11},{10,... | collective-permute-start | bytes 540680 | tf_op jit(solution)/shard_map/ppermute | solution.py:155
  79.0 1.3 %collective-permute-start.15 = (bf16[352,256]{1,0:T(8,128)(2,1)S(1)}, bf16[352,256]{1,0:T(8,128)(2,1)S(1)}, u32[]{:S(2)}, u32[]{:S(2)}) collective-permute-start(bf16[352,256]{1,0:T(8,128)(2,1)S(1)} %pad_maximum_fusion.2), channel_id=1, source_target_pairs={{0,4},{1,5},{2,6},{3,7},{4,0},{5,1},{6,2},{7,3},{8,12},{9,13},{10,... | collective-permute-start | bytes 540680 | tf_op jit(solution)/shard_map/ppermute | solution.py:155
  81.2 3.4 %collective-permute-done.16 = bf16[352,256]{1,0:T(8,128)(2,1)S(1)} collective-permute-done((bf16[352,256]{1,0:T(8,128)(2,1)S(1)}, bf16[352,256]{1,0:T(8,128)(2,1)S(1)}, u32[]{:S(2)}, u32[]{:S(2)}) %collective-permute-start.16) | collective-permute-done | bytes 180256 | tf_op jit(solution)/shard_map/ppermute | solution.py:155
  84.6 2.1 %collective-permute-done.14 = bf16[352,256]{1,0:T(8,128)(2,1)S(1)} collective-permute-done((bf16[352,256]{1,0:T(8,128)(2,1)S(1)}, bf16[352,256]{1,0:T(8,128)(2,1)S(1)}, u32[]{:S(2)}, u32[]{:S(2)}) %collective-permute-start.14) | collective-permute-done | bytes 180256 | tf_op jit(solution)/shard_map/ppermute | solution.py:155
  88.2 4.0 %all-to-all-start.1 = ((bf16[8,128,96]{1,2,0:T(8,128)(2,1)}), bf16[8,128,96]{1,2,0:T(8,128)(2,1)S(1)}, u32[]{:S(2)}, u32[]{:S(2)}) async-start(bf16[8,128,96]{1,2,0:T(8,128)(2,1)} %bitcast.55), calls=%async_computation.1 | async-start | bytes 393216 | tf_op jit(solution)/shard_map/all_to_all | solution.py:246
  92.2 8.6 %all-to-all-done.1 = bf16[8,128,96]{1,2,0:T(8,128)(2,1)S(1)} async-done(((bf16[8,128,96]{1,2,0:T(8,128)(2,1)}), bf16[8,128,96]{1,2,0:T(8,128)(2,1)S(1)}, u32[]{:S(2)}, u32[]{:S(2)}) %all-to-all-start.1) | async-done | bytes 196640 | tf_op jit(solution)/shard_map/all_to_all | solution.py:246
  100.8 1.5 %fusion.7 = bf16[1024,96]{0,1:T(8,128)(2,1)} fusion(s32[1024]{0:T(1024)S(1)} %copy-done.9, bf16[8,128,96]{1,2,0:T(8,128)(2,1)S(1)} %all-to-all-done.1), kind=kOutput, calls=%fused_computation.12 | convolution fusion | flops 202473472 | bytes 397312 | tf_op jit(solution)/shard_map/dot_general | solution.py:21
  102.6 1.7 %convert_multiply_fusion = f32[2592,256]{1,0:T(8,128)} fusion(bf16[1408,256]{1,0:T(8,128)(2,1)S(1)} %get-tuple-element.10, bf16[1408,256]{1,0:T(8,128)(2,1)S(1)} %get-tuple-element.9), kind=kLoop, calls=%fused_computation.3 | loop fusion | flops 3317760 | bytes 4096000 | tf_op jit(solution)/shard_map/mul | solution.py:237
  (63 shorter events, 9.5 us)
Async XLA Ops:
  0.6 0.9 copy-start
  0.6 10.6 %copy-start.7 = (s32[2]{0:T(128)S(1)}, s32[2]{0:T(128)}, u32[]{:S(2)}) copy-start(s32[2]{0:T(128)} %param.11) | copy-start | bytes 28
  0.7 12.6 %copy-start.8 = (s32[256]{0:T(256)S(1)}, s32[256]{0:T(256)}, u32[]{:S(2)}) copy-start(s32[256]{0:T(256)} %param.10) | copy-start | bytes 3076
  3.3 22.3 %copy-start.1 = (bf16[27,96,256]{2,1,0:T(8,128)(2,1)S(1)}, bf16[27,96,256]{2,1,0:T(8,128)(2,1)}, u32[]{:S(2)}) copy-start(bf16[27,96,256]{2,1,0:T(8,128)(2,1)} %param.13) | copy-start | bytes 3981316
  3.3 22.3 %copy-start.3 = (s32[27,1024]{1,0:T(8,128)S(1)}, s32[27,1024]{1,0:T(8,128)}, u32[]{:S(2)}) copy-start(s32[27,1024]{1,0:T(8,128)} %map_ref.7) | copy-start | bytes 331780
  3.3 22.3 %copy-start.4 = (f32[256]{0:T(256)S(1)}, f32[256]{0:T(256)}, u32[]{:S(2)}) copy-start(f32[256]{0:T(256)} %param.14) | copy-start | bytes 3076
  4.0 15.2 %all-to-all-start = ((bf16[8,128,96]{1,2,0:T(8,128)(2,1)}), bf16[8,128,96]{1,2,0:T(8,128)(2,1)S(1)}, u32[]{:S(2)}, u32[]{:S(2)}) async-start(bf16[8,128,96]{1,2,0:T(8,128)(2,1)} %bitcast.56), calls=%async_computation | async-start | bytes 393216 | tf_op jit(solution)/shard_map/all_to_all | solution.py:222
  20.1 3.7 %collective-permute-start.1 = (bf16[96,128]{1,0:T(8,128)(2,1)S(1)}, bf16[96,128]{1,0:T(8,128)(2,1)S(1)}, u32[]{:S(2)}, u32[]{:S(2)}) collective-permute-start(bf16[96,128]{1,0:T(8,128)(2,1)S(1)} %get-tuple-element.28), channel_id=1, source_target_pairs={{4,8},{8,4},{12,16},{16,12},{20,24},{24,20},{5,9},{9,5},{13,17},{1... | collective-permute-start | bytes 73736 | tf_op jit(solution)/shard_map/ppermute | solution.py:203
  20.7 4.9 %collective-permute-start = (bf16[96,128]{1,0:T(8,128)(2,1)S(1)}, bf16[96,128]{1,0:T(8,128)(2,1)S(1)}, u32[]{:S(2)}, u32[]{:S(2)}) collective-permute-start(bf16[96,128]{1,0:T(8,128)(2,1)S(1)} %get-tuple-element.29), channel_id=1, source_target_pairs={{0,4},{4,0},{8,12},{12,8},{16,20},{20,16},{24,28},{28,24},{1,5},{5... | collective-permute-start | bytes 73736 | tf_op jit(solution)/shard_map/ppermute | solution.py:203
  25.6 1.0 %copy-start.2 = (bf16[1024,256]{1,0:T(8,128)(2,1)S(1)}, bf16[1024,256]{1,0:T(8,128)(2,1)}, u32[]{:S(2)}) copy-start(bf16[1024,256]{1,0:T(8,128)(2,1)} %cot_ref.1) | copy-start | bytes 1572868
  36.7 0.8 copy-start.5
  38.4 6.6 %collective-permute-start.4 = (bf16[1408,256]{1,0:T(8,128)(2,1)}, bf16[1408,256]{1,0:T(8,128)(2,1)}, u32[]{:S(2)}, u32[]{:S(2)}) collective-permute-start(bf16[1408,256]{1,0:T(8,128)(2,1)} %dynamic-slice_bitcast_fusion), channel_id=1, source_target_pairs={{0,1},{1,0},{2,3},{3,2},{4,5},{5,4},{6,7},{7,6},{8,9},{9,8},{10,11... | collective-permute-start | bytes 2162696 | tf_op jit(solution)/shard_map/ppermute | solution.py:155
  38.4 1.0 copy-start.6
  46.4 10.9 %collective-permute-start.5 = (bf16[352,256]{1,0:T(8,128)(2,1)S(1)}, bf16[352,256]{1,0:T(8,128)(2,1)S(1)}, u32[]{:S(2)}, u32[]{:S(2)}) collective-permute-start(bf16[352,256]{1,0:T(8,128)(2,1)S(1)} %get-tuple-element.14), channel_id=1, source_target_pairs={{0,2},{1,3},{2,0},{3,1},{4,6},{5,7},{6,4},{7,5},{8,10},{9,11},{10,... | collective-permute-start | bytes 540680 | tf_op jit(solution)/shard_map/ppermute | solution.py:155
  48.0 9.3 %collective-permute-start.7 = (bf16[352,256]{1,0:T(8,128)(2,1)S(1)}, bf16[352,256]{1,0:T(8,128)(2,1)S(1)}, u32[]{:S(2)}, u32[]{:S(2)}) collective-permute-start(bf16[352,256]{1,0:T(8,128)(2,1)S(1)} %get-tuple-element.15), channel_id=1, source_target_pairs={{0,6},{1,7},{2,4},{3,5},{4,2},{5,3},{6,0},{7,1},{8,14},{9,15},{10,... | collective-permute-start | bytes 540680 | tf_op jit(solution)/shard_map/ppermute | solution.py:155
  50.2 8.9 %collective-permute-start.6 = (bf16[352,256]{1,0:T(8,128)(2,1)S(1)}, bf16[352,256]{1,0:T(8,128)(2,1)S(1)}, u32[]{:S(2)}, u32[]{:S(2)}) collective-permute-start(bf16[352,256]{1,0:T(8,128)(2,1)S(1)} %get-tuple-element.16), channel_id=1, source_target_pairs={{0,4},{1,5},{2,6},{3,7},{4,0},{5,1},{6,2},{7,3},{8,12},{9,13},{10,... | collective-permute-start | bytes 540680 | tf_op jit(solution)/shard_map/ppermute | solution.py:155
  59.2 9.2 %collective-permute-start.8 = (bf16[88,256]{1,0:T(8,128)(2,1)S(1)}, bf16[88,256]{1,0:T(8,128)(2,1)S(1)}, u32[]{:S(2)}, u32[]{:S(2)}) collective-permute-start(bf16[88,256]{1,0:T(8,128)(2,1)S(1)} %get-tuple-element.23), channel_id=1, source_target_pairs={{0,8},{1,9},{2,10},{3,11},{4,12},{5,13},{6,14},{7,15},{8,0},{9,1},... | collective-permute-start | bytes 135176 | tf_op jit(solution)/shard_map/ppermute | solution.py:155
  61.5 7.0 %collective-permute-start.10 = (bf16[88,256]{1,0:T(8,128)(2,1)S(1)}, bf16[88,256]{1,0:T(8,128)(2,1)S(1)}, u32[]{:S(2)}, u32[]{:S(2)}) collective-permute-start(bf16[88,256]{1,0:T(8,128)(2,1)S(1)} %get-tuple-element.24), channel_id=1, source_target_pairs={{0,24},{1,25},{2,26},{3,27},{4,28},{5,29},{6,30},{7,31},{8,16},{9,... | collective-permute-start | bytes 135176 | tf_op jit(solution)/shard_map/ppermute | solution.py:155
  62.7 5.7 %collective-permute-start.9 = (bf16[88,256]{1,0:T(8,128)(2,1)S(1)}, bf16[88,256]{1,0:T(8,128)(2,1)S(1)}, u32[]{:S(2)}, u32[]{:S(2)}) collective-permute-start(bf16[88,256]{1,0:T(8,128)(2,1)S(1)} %get-tuple-element.25), channel_id=1, source_target_pairs={{0,16},{1,17},{2,18},{3,19},{4,20},{5,21},{6,22},{7,23},{8,24},{9,... | collective-permute-start | bytes 135176 | tf_op jit(solution)/shard_map/ppermute | solution.py:155
  68.5 6.7 %collective-permute-start.13 = (bf16[88,256]{1,0:T(8,128)(2,1)S(1)}, bf16[88,256]{1,0:T(8,128)(2,1)S(1)}, u32[]{:S(2)}, u32[]{:S(2)}) collective-permute-start(bf16[88,256]{1,0:T(8,128)(2,1)S(1)} %fusion.37), channel_id=1, source_target_pairs={{0,8},{1,9},{2,10},{3,11},{4,12},{5,13},{6,14},{7,15},{8,0},{9,1},... | collective-permute-start | bytes 135176 | tf_op jit(solution)/shard_map/ppermute | solution.py:155
  71.4 4.9 %collective-permute-start.12 = (bf16[88,256]{1,0:T(8,128)(2,1)S(1)}, bf16[88,256]{1,0:T(8,128)(2,1)S(1)}, u32[]{:S(2)}, u32[]{:S(2)}) collective-permute-start(bf16[88,256]{1,0:T(8,128)(2,1)S(1)} %fusion.37), channel_id=1, source_target_pairs={{0,16},{1,17},{2,18},{3,19},{4,20},{5,21},{6,22},{7,23},{8,24},{9,... | collective-permute-start | bytes 135176 | tf_op jit(solution)/shard_map/ppermute | solution.py:155
  71.4 5.9 %collective-permute-start.11 = (bf16[88,256]{1,0:T(8,128)(2,1)S(1)}, bf16[88,256]{1,0:T(8,128)(2,1)S(1)}, u32[]{:S(2)}, u32[]{:S(2)}) collective-permute-start(bf16[88,256]{1,0:T(8,128)(2,1)S(1)} %fusion.37), channel_id=1, source_target_pairs={{0,24},{1,25},{2,26},{3,27},{4,28},{5,29},{6,30},{7,31},{8,16},{9,... | collective-permute-start | bytes 135176 | tf_op jit(solution)/shard_map/ppermute | solution.py:155
  74.0 7.0 %collective-permute-start.2 = (bf16[96,128]{1,0:T(8,128)(2,1)S(1)}, bf16[96,128]{1,0:T(8,128)(2,1)S(1)}, u32[]{:S(2)}, u32[]{:S(2)}) collective-permute-start(bf16[96,128]{1,0:T(8,128)(2,1)S(1)} %get-tuple-element.17), channel_id=1, source_target_pairs={{0,4},{4,0},{8,12},{12,8},{16,20},{20,16},{24,28},{28,24},{1,5},{5... | collective-permute-start | bytes 73736 | tf_op jit(solution)/shard_map/ppermute | solution.py:203
  74.6 6.4 %collective-permute-start.3 = (bf16[96,128]{1,0:T(8,128)(2,1)S(1)}, bf16[96,128]{1,0:T(8,128)(2,1)S(1)}, u32[]{:S(2)}, u32[]{:S(2)}) collective-permute-start(bf16[96,128]{1,0:T(8,128)(2,1)S(1)} %get-tuple-element.18), channel_id=1, source_target_pairs={{4,8},{8,4},{12,16},{16,12},{20,24},{24,20},{5,9},{9,5},{13,17},{1... | collective-permute-start | bytes 73736 | tf_op jit(solution)/shard_map/ppermute | solution.py:203
  77.4 7.2 %collective-permute-start.16 = (bf16[352,256]{1,0:T(8,128)(2,1)S(1)}, bf16[352,256]{1,0:T(8,128)(2,1)S(1)}, u32[]{:S(2)}, u32[]{:S(2)}) collective-permute-start(bf16[352,256]{1,0:T(8,128)(2,1)S(1)} %pad_maximum_fusion.2), channel_id=1, source_target_pairs={{0,2},{1,3},{2,0},{3,1},{4,6},{5,7},{6,4},{7,5},{8,10},{9,11},{10,... | collective-permute-start | bytes 540680 | tf_op jit(solution)/shard_map/ppermute | solution.py:155
  79.0 5.6 %collective-permute-start.15 = (bf16[352,256]{1,0:T(8,128)(2,1)S(1)}, bf16[352,256]{1,0:T(8,128)(2,1)S(1)}, u32[]{:S(2)}, u32[]{:S(2)}) collective-permute-start(bf16[352,256]{1,0:T(8,128)(2,1)S(1)} %pad_maximum_fusion.2), channel_id=1, source_target_pairs={{0,4},{1,5},{2,6},{3,7},{4,0},{5,1},{6,2},{7,3},{8,12},{9,13},{10,... | collective-permute-start | bytes 540680 | tf_op jit(solution)/shard_map/ppermute | solution.py:155
  80.3 6.4 %collective-permute-start.14 = (bf16[352,256]{1,0:T(8,128)(2,1)S(1)}, bf16[352,256]{1,0:T(8,128)(2,1)S(1)}, u32[]{:S(2)}, u32[]{:S(2)}) collective-permute-start(bf16[352,256]{1,0:T(8,128)(2,1)S(1)} %pad_maximum_fusion.2), channel_id=1, source_target_pairs={{0,6},{1,7},{2,4},{3,5},{4,2},{5,3},{6,0},{7,1},{8,14},{9,15},{10,... | collective-permute-start | bytes 540680 | tf_op jit(solution)/shard_map/ppermute | solution.py:155
  87.0 13.8 %copy-start.9 = (s32[1024]{0:T(1024)S(1)}, s32[1024]{0:T(1024)}, u32[]{:S(2)}) copy-start(s32[1024]{0:T(1024)} %param.9) | copy-start | bytes 12292
  87.1 15.2 %collective-permute-start.17 = (bf16[1408,256]{1,0:T(8,128)(2,1)S(1)}, bf16[1408,256]{1,0:T(8,128)(2,1)S(1)}, u32[]{:S(2)}, u32[]{:S(2)}) collective-permute-start(bf16[1408,256]{1,0:T(8,128)(2,1)S(1)} %pad_maximum_fusion.1), channel_id=1, source_target_pairs={{0,1},{1,0},{2,3},{3,2},{4,5},{5,4},{6,7},{7,6},{8,9},{9,8},{10,11... | collective-permute-start | bytes 2162696 | tf_op jit(solution)/shard_map/ppermute | solution.py:155
  88.2 12.6 %all-to-all-start.1 = ((bf16[8,128,96]{1,2,0:T(8,128)(2,1)}), bf16[8,128,96]{1,2,0:T(8,128)(2,1)S(1)}, u32[]{:S(2)}, u32[]{:S(2)}) async-start(bf16[8,128,96]{1,2,0:T(8,128)(2,1)} %bitcast.55), calls=%async_computation.1 | async-start | bytes 393216 | tf_op jit(solution)/shard_map/all_to_all | solution.py:246

commit v3 on v2

v3 whole, which is shorter than its diff:
```python
import functools
import math

import jax
import jax.numpy as jnp
from jax import lax
from jax.experimental import pallas as pl
from jax.experimental.pallas import tpu as pltpu
from jax.sharding import PartitionSpec as P

BF = jnp.bfloat16
F32 = jnp.float32
LOW = 256
SHIFT = 8
VMEM_LIMIT = 20 << 20
AXES = ("brick", "group")


def dot(a, b, a_dim, b_dim):
    dims = (((a_dim,), (b_dim,)), ((), ()))
    return lax.dot_general(a, b, dims, preferred_element_type=F32)


def one_hot_rows(index, width):
    columns = jnp.arange(width, dtype=jnp.int32)
    return (index[:, None] == columns[None, :]).astype(BF)


def one_hot_low(row, lanes):
    low = (row & (LOW - 1)).astype(F32).astype(BF)
    iota = lax.broadcasted_iota(jnp.int32, (LOW, lanes), 0).astype(BF)
    hit = iota == jnp.broadcast_to(low, (LOW, lanes))
    return jnp.where(hit, jnp.ones((), BF), jnp.zeros((), BF))


def send_kernel(feat_ref, order_ref, out_ref):
    channels, rows = feat_ref.shape
    per = out_ref.shape[2]
    for n in range(rows // LOW):
        row = order_ref[:, n * LOW : (n + 1) * LOW]
        hot = one_hot_low(row, LOW)
        block = jnp.broadcast_to(lax.shift_right_logical(row, SHIFT), (channels, LOW))
        picked = jnp.zeros((channels, LOW), F32)
        for a in range(rows // LOW):
            picked = jnp.where(block == a, dot(feat_ref[:, a * LOW : (a + 1) * LOW], hot, 1, 0), picked)
        picked = picked.astype(BF)
        for p in range(LOW // per):
            out_ref[n * (LOW // per) + p] = picked[:, p * per : (p + 1) * per]


def forward_kernel(
    half_ref, got_ref, prev_ref, next_ref, map_ref, w_ref, bias_ref, cot_hbm, out_hbm, pg_hbm, send_ref, keep_ref,
    g_ref, x_ref, wt_ref, cot_ref, out_ref, pg_ref, cot_sem, out_sem, pg_sem,
):
    fetch = pltpu.make_async_copy(cot_hbm, cot_ref, cot_sem)
    fetch.start()
    offsets, voxels = map_ref.shape
    depth, c_out = w_ref.shape
    channels = depth // offsets
    here = voxels // LOW
    blocks = x_ref.shape[0] // channels
    center = offsets // 2
    per = got_ref.shape[2]
    for a in range(here):
        for p in range(LOW // per):
            x_ref[a * channels : (a + 1) * channels, p * per : (p + 1) * per] = got_ref[a * (LOW // per) + p]
    face = prev_ref.shape[1]
    x_ref[here * channels :, :face] = prev_ref[...]
    x_ref[here * channels :, face:] = next_ref[...]
    for k in range(offsets):
        wt_ref[:, k * channels : (k + 1) * channels] = w_ref[k * channels : (k + 1) * channels, :].T
        at = slice(k * channels, (k + 1) * channels)
        if k == center:
            for a in range(here):
                g_ref[at, a * LOW : (a + 1) * LOW] = x_ref[a * channels : (a + 1) * channels, :]
            continue
        row = map_ref[k : k + 1, :]
        high = lax.shift_right_logical(row, SHIFT)
        for n in range(here):
            sl = slice(n * LOW, (n + 1) * LOW)
            terms = dot(x_ref[...], one_hot_low(row[:, sl], LOW), 1, 0)
            block = jnp.broadcast_to(high[:, sl], (channels, LOW))
            picked = jnp.zeros((channels, LOW), F32)
            for a in range(blocks):
                picked = jnp.where(block == a, terms[a * channels : (a + 1) * channels], picked)
            g_ref[at, sl] = picked.astype(BF)
    fetch.wait()
    copies = []
    for n in range(here):
        sl = slice(n * LOW, (n + 1) * LOW)
        pre = dot(wt_ref[...], g_ref[:, sl], 1, 0).T + bias_ref[...]
        out_ref[sl, :] = jnp.maximum(pre, 0.0).astype(BF)
        pg_ref[sl, :] = jnp.where(pre > 0, cot_ref[sl, :].astype(F32), 0.0).astype(BF)
    copies.append(pltpu.make_async_copy(out_ref, out_hbm, out_sem))
    copies.append(pltpu.make_async_copy(pg_ref, pg_hbm, pg_sem))
    for copy in copies:
        copy.start()
    half = half_ref[0]
    count = depth // 2
    step = count // 9
    for ref, which in ((send_ref, 1 - half), (keep_ref, half)):
        for m in range(9):
            at = pl.ds(pl.multiple_of(which * count + m * step, 16), step)
            ref[m * step : (m + 1) * step, :] = dot(g_ref[at, :], pg_ref[...], 1, 0).astype(ref.dtype)
        ref[count:, :] = jnp.zeros((ref.shape[0] - count, c_out), ref.dtype)
    for copy in copies:
        copy.wait()


def backward_kernel(pg_ref, map_ref, w_ref, here_ref, faces_ref, c_ref, acc_ref):
    offsets, voxels = map_ref.shape
    depth = w_ref.shape[0]
    channels = depth // offsets
    here = voxels // LOW
    blocks = acc_ref.shape[0] // channels
    step = depth // 9
    for m in range(9):
        sl = slice(m * step, (m + 1) * step)
        c_ref[sl, :] = dot(w_ref[sl, :], pg_ref[...], 1, 1).astype(BF)
    center = offsets // 2
    for a in range(here):
        at = slice(a * channels, (a + 1) * channels)
        acc_ref[at, :] = c_ref[center * channels : (center + 1) * channels, a * LOW : (a + 1) * LOW].astype(F32)
    acc_ref[here * channels :, :] = jnp.zeros((channels * (blocks - here), LOW), F32)
    for k in range(offsets):
        if k == center:
            continue
        contrib = c_ref[k * channels : (k + 1) * channels, :]
        row = map_ref[k : k + 1, :]
        high = lax.shift_right_logical(row, SHIFT).astype(F32).astype(BF)
        block = jnp.broadcast_to(high, (channels, voxels))
        parts = [jnp.where(block == jnp.array(a, BF), contrib, jnp.zeros((), BF)) for a in range(blocks)]
        acc_ref[...] += dot(jnp.concatenate(parts, 0), one_hot_low(row, voxels), 1, 1)
    per = here_ref.shape[2]
    for a in range(here):
        for p in range(LOW // per):
            here_ref[a * (LOW // per) + p] = acc_ref[a * channels : (a + 1) * channels, p * per : (p + 1) * per]
    faces_ref[...] = acc_ref[here * channels :, :].astype(BF)


def whole(count):
    return [pl.BlockSpec(memory_space=pltpu.VMEM)] * count


def send_blocks(features, order, bricks):
    channels, rows = features.shape
    return pl.pallas_call(
        send_kernel,
        out_shape=jax.ShapeDtypeStruct((bricks, channels, rows // bricks), BF),
        in_specs=whole(2),
        out_specs=whole(1)[0],
        cost_estimate=pl.CostEstimate(flops=2 * rows * rows * channels, bytes_accessed=1 << 19, transcendentals=0),
    )(features, order)


def forward(half, got, prev_upper, next_lower, maps, w, bias, cot, padded):
    offsets, voxels = maps.shape
    depth, c_out = w.shape
    rows = depth // offsets * (voxels // LOW + 1)
    macs = voxels * depth * c_out * 2 + offsets * voxels * LOW * rows
    hbm = pl.BlockSpec(memory_space=pltpu.HBM)
    return pl.pallas_call(
        forward_kernel,
        out_shape=(
            jax.ShapeDtypeStruct((voxels, c_out), BF),
            jax.ShapeDtypeStruct((voxels, c_out), BF),
            jax.ShapeDtypeStruct((padded // 2, c_out), BF),
            jax.ShapeDtypeStruct((padded // 2, c_out), F32),
        ),
        in_specs=[pl.BlockSpec(memory_space=pltpu.SMEM)] + whole(6) + [hbm],
        out_specs=(hbm, hbm) + tuple(whole(2)),
        scratch_shapes=[
            pltpu.VMEM((depth, voxels), BF),
            pltpu.VMEM((rows, LOW), BF),
            pltpu.VMEM((c_out, depth), BF),
            pltpu.VMEM((voxels, c_out), BF),
            pltpu.VMEM((voxels, c_out), BF),
            pltpu.VMEM((voxels, c_out), BF),
            pltpu.SemaphoreType.DMA,
            pltpu.SemaphoreType.DMA,
            pltpu.SemaphoreType.DMA,
        ],
        compiler_params=pltpu.CompilerParams(vmem_limit_bytes=VMEM_LIMIT),
        cost_estimate=pl.CostEstimate(flops=2 * macs, bytes_accessed=5 << 20, transcendentals=0),
    )(half, got, prev_upper, next_lower, maps, w, bias, cot)


def backward(pg, maps, w, bricks):
    offsets, voxels = maps.shape
    depth, c_out = w.shape
    channels = depth // offsets
    rows = channels * (voxels // LOW + 1)
    macs = voxels * depth * c_out + offsets * voxels * LOW * rows
    return pl.pallas_call(
        backward_kernel,
        out_shape=(
            jax.ShapeDtypeStruct((bricks, channels, voxels // bricks), F32),
            jax.ShapeDtypeStruct((channels, LOW), BF),
        ),
        in_specs=whole(3),
        out_specs=tuple(whole(2)),
        scratch_shapes=[pltpu.VMEM((depth, voxels), BF), pltpu.VMEM((rows, LOW), F32)],
        compiler_params=pltpu.CompilerParams(vmem_limit_bytes=VMEM_LIMIT),
        cost_estimate=pl.CostEstimate(flops=2 * macs, bytes_accessed=3 << 20, transcendentals=0),
    )(pg, maps, w)


def stages(count):
    plan, stride = [], 1
    while stride < count:
        left = count // stride
        radix = 4 if stride > 1 and left % 4 == 0 else 2
        if left % radix:
            radix = left
        plan.append((stride, radix))
        stride *= radix
    return plan


def swapped(array, count, stride, radix, delta):
    def partner(i):
        digit = i // stride % radix
        other = (digit ^ delta) if radix in (2, 4) else (delta - digit) % radix
        return i + (other - digit) * stride

    return lax.ppermute(array, AXES, [(i, partner(i)) for i in range(count)])


def other_digit(digit, delta, radix):
    return (digit ^ delta) if radix in (2, 4) else (delta - digit) % radix


def reduce_stage(x, flat, count, stride, radix):
    digit = flat // stride % radix
    pieces = x.reshape((radix, x.shape[0] // radix) + x.shape[1:])
    total = None
    for delta in range(radix):
        piece = lax.dynamic_index_in_dim(pieces, other_digit(digit, delta, radix), 0, keepdims=False)
        if radix not in (2, 4) or delta:
            piece = swapped(piece, count, stride, radix, delta)
        total = piece.astype(F32) if total is None else total + piece.astype(F32)
    return total.astype(BF)


def gather_stage(x, flat, count, stride, radix):
    digit = flat // stride % radix
    got = [x if radix in (2, 4) and d == 0 else swapped(x, count, stride, radix, d) for d in range(radix)]
    parts = []
    for place in range(radix):
        part = got[0]
        for d in range(radix):
            where = (place ^ d) if radix in (2, 4) else (place + d) % radix
            part = jnp.where(digit == d, got[where], part)
        parts.append(part)
    return jnp.concatenate(parts, 0)


def meet(array_up, array_down):
    size = lax.axis_size("brick")
    odd = lax.axis_index("brick") % 2 == 1
    got = []
    for start in (0, 1):
        pairs = []
        for i in range(start, size - 1, 2):
            pairs += [(i, i + 1), (i + 1, i)]
        goes_up = ~odd if start == 0 else odd
        got.append(lax.ppermute(jnp.where(goes_up, array_up, array_down), "brick", pairs))
    return jnp.where(odd, got[0], got[1]), jnp.where(odd, got[1], got[0])


def on_device(features, order, face_list, face_count, kernel_map, weight, bias, cotangent):
    offsets, channels, c_out = weight.shape
    rows = features.shape[0]
    face = face_list.shape[0] // 2
    bricks = lax.axis_size("brick")
    count = bricks * lax.axis_size("group")
    per = rows // bricks
    depth = offsets * channels
    unit = 8 * count
    padded = -(-depth // unit) * unit

    w = weight.reshape(depth, c_out)
    flat = lax.axis_index("brick") * lax.axis_size("group") + lax.axis_index("group")
    send = send_blocks(features.T, order[None], bricks)
    got = lax.all_to_all(send, "brick", split_axis=0, concat_axis=0)
    local = got.transpose(1, 0, 2).reshape(channels, rows)

    slots = jnp.arange(face, dtype=jnp.int32)
    lower_pick = one_hot_rows(face_list[:face], rows) * (slots < face_count[0]).astype(BF)[:, None]
    upper_pick = one_hot_rows(face_list[face:], rows) * (slots < face_count[1]).astype(BF)[:, None]
    lower = dot(local, lower_pick, 1, 1).astype(BF)
    upper = dot(local, upper_pick, 1, 1).astype(BF)
    prev_upper, next_lower = meet(upper, lower)

    half = (flat % 2).astype(jnp.int32)[None]
    output, pre_grad, give, keep = forward(
        half, got, prev_upper, next_lower, kernel_map, w, bias[None], cotangent, padded
    )
    plan = stages(count)[1:]
    total = (keep + swapped(give, count, 1, 2, 1).astype(F32)).astype(BF)
    total = reduce_stage(total, flat, count, *plan[0])
    here, faces = backward(pre_grad, kernel_map, w, bricks)
    total, faces = lax.optimization_barrier((total, faces))
    from_prev, from_next = meet(faces[:, face:], faces[:, :face])
    for stride, radix in plan[1:]:
        total = reduce_stage(total, flat, count, stride, radix)

    added = dot(from_prev, lower_pick, 1, 0) + dot(from_next, upper_pick, 1, 0)
    local_grad = (here + added.reshape(channels, bricks, per).transpose(1, 0, 2)).astype(BF)
    total, local_grad = lax.optimization_barrier((total, local_grad))
    returned = lax.all_to_all(local_grad, "brick", split_axis=0, concat_axis=0)
    returned = returned.transpose(1, 0, 2).reshape(channels, rows)
    order_pick = one_hot_rows(order, rows)

    for stride, radix in reversed(plan):
        total = gather_stage(total, flat, count, stride, radix)
    total, returned = lax.optimization_barrier((total, returned))
    grad_in = dot(returned, order_pick, 1, 0).astype(BF).T
    other = swapped(total, count, 1, 2, 1)
    low = jnp.where(flat % 2 == 0, total, other)[: depth // 2]
    high = jnp.where(flat % 2 == 0, other, total)[: depth // 2]
    scale = jnp.float32(1.0 / math.sqrt(count * rows))
    weight_grad = (jnp.concatenate([low, high], 0).astype(F32) * scale).reshape(offsets, channels, c_out)
    return output, grad_in, weight_grad


def solution(mesh):
    return jax.shard_map(
        on_device,
        mesh=mesh,
        in_specs=(
            P(AXES, None),
            P(AXES),
            P(AXES),
            P(AXES),
            P(None, AXES),
            P(),
            P(),
            P(AXES, None),
        ),
        out_specs=(P(AXES, None), P(AXES, None), P()),
        check_vma=False,
    )
```

time: 105 us -> 95 us (0.905)
  Pallas kernels: 25.9 us -> 21.8 us
  waiting for transfers between devices: 27.9 us -> 24.5 us
  local copies, waits for them, and re-layouts: 7.02 us -> 3.87 us
  starting transfers between devices: 32.9 us -> 35 us
  matrix products: 4.44 us -> 2.69 us
    all_to_all x2, waiting for transfers between devices: 14.6 us -> 8.94 us  [the longest x1 4.54 us: on_device(): got = lax.all_to_all(send, 'brick', split_axis=0, concat_axis=0)]
    pallas_call x3 -> x2, Pallas kernels: 15.9 us -> 10.4 us  [the longest x1 8.16 us: backward(): pl.pallas_call(backward_kernel, out_shape=(jax.ShapeDtypeStruct((bricks,...]
    ppermute x14, waiting for transfers between devices: 11.5 us -> 13.7 us  [swapped(): return lax.ppermute(array, AXES, [(i, partner(i)) for i in range(count)])]
    unnamed x20 -> x16, local copies, waits for them, and re-layouts: 3.8 us -> 1.72 us
    dot_general x6 -> x5, matrix products: 4.44 us -> 2.69 us  [dot(): return lax.dot_general(a, b, dims, preferred_element_type=F32)]
    all_to_all x3 -> x0, local copies, waits for them, and re-layouts: 1.6 us -> none  [the longest x2 0.89 us: on_device(): lax.all_to_all(sent, 'brick', split_axis=0, concat_axis=0, tiled=True)]
    ppermute x14, starting transfers between devices: 16.7 us -> 18.2 us  [swapped(): return lax.ppermute(array, AXES, [(i, partner(i)) for i in range(count)])]
    pallas_call x1, Pallas kernels: 10 us -> 11.5 us  [forward(): pl.pallas_call(forward_kernel, out_shape=(jax.ShapeDtypeStruct((voxels, c...]
  transfers between devices with their start and end apart: 20 -> 20, of which waited for: 9 -> 12; matrix products, arithmetic and copies ran while one was open for 5% -> 7% of each run, Pallas kernels for 15% -> 9%
where the time goes in v3:
time: 95 us; the launch traced here: 94.6 us
  starting transfers between devices  35 us (37%)
  waiting for transfers between devices  24.5 us (26%)
  Pallas kernels  21.8 us (23%)
  other arithmetic  5.74 us (6%)
  local copies, waits for them, and re-layouts  3.87 us (4%)
  matrix products  2.69 us (3%)
    ppermute x14, starting transfers between devices, swapped(): return lax.ppermute(array, AXES, [(i, partner(i)) for i in range(count)])  18.2 us
    ppermute x14, waiting for transfers between devices, swapped(): return lax.ppermute(array, AXES, [(i, partner(i)) for i in range(count)])  13.7 us
    pallas_call x1, Pallas kernels, forward(): pl.pallas_call(forward_kernel, out_shape=(jax.ShapeDtypeStruct((voxels, c...  11.5 us
    pallas_call x1, Pallas kernels, backward(): pl.pallas_call(backward_kernel, out_shape=(jax.ShapeDtypeStruct((bricks,...  8.16 us
    all_to_all x1, starting transfers between devices, on_device(): got = lax.all_to_all(send, 'brick', split_axis=0, concat_axis=0)  7.25 us
    ppermute x4, starting transfers between devices, meet(): lax.ppermute(jnp.where(goes_up, array_up, array_down), 'brick', pairs)  6.13 us
    all_to_all x1, waiting for transfers between devices, on_device(): got = lax.all_to_all(send, 'brick', split_axis=0, concat_axis=0)  4.54 us
    all_to_all x1, waiting for transfers between devices, on_device(): returned = lax.all_to_all(local_grad, 'brick', split_axis=0, concat_axis=0)  4.39 us
  transfers between devices with their start and end apart: 20, of which 12 were waited for; matrix products, arithmetic and copies ran while one was open for 7% of the time, Pallas kernels for 9%

profile of v3, /device:TPU:0, one launch (start us, length us, event | category | flops | bytes accessed | tf_op | source)
XLA Modules:
  0.0 94.6 jit_solution(16523540399981902957)
XLA Ops:
  0.7 2.2 %shard_map.103 = bf16[8,96,128]{2,1,0:T(8,128)(2,1)} custom-call(bf16[96,1024]{1,0:T(8,128)(2,1)} %bitcast.72, s32[1,1024]{1,0:T(1,128)} %bitcast.73), custom_call_target="tpu_custom_call" | custom-call | flops 201326592 | bytes 524288 | tf_op jit(solution)/shard_map/pallas_call | solution.py:147
  2.9 7.2 %all-to-all-start = ((bf16[8,96,128]{2,1,0:T(8,128)(2,1)}), bf16[8,96,128]{2,1,0:T(8,128)(2,1)S(1)}, u32[]{:S(2)}, u32[]{:S(2)}) async-start(bf16[8,96,128]{2,1,0:T(8,128)(2,1)} %shard_map.103), calls=%async_computation | async-start | bytes 393216 | tf_op jit(solution)/shard_map/all_to_all | solution.py:285
  10.1 1.3 %fusion.48 = (s32[1]{0:T(128)}, s32[1]{0:T(128)}) fusion(s32[2]{0:T(128)} %param.11), kind=kLoop, calls=%fused_computation.82 | loop fusion | bytes 16 | tf_op jit(solution)/shard_map/slice | solution.py:289
  12.8 0.8 fusion.47
  13.5 4.5 %all-to-all-done.got_ref = bf16[8,96,128]{2,1,0:T(8,128)(2,1)S(1)} async-done(((bf16[8,96,128]{2,1,0:T(8,128)(2,1)}), bf16[8,96,128]{2,1,0:T(8,128)(2,1)S(1)}, u32[]{:S(2)}, u32[]{:S(2)}) %all-to-all-start) | async-done | bytes 196640 | tf_op jit(solution)/shard_map/all_to_all | solution.py:285
  19.3 3.1 %collective-permute-start = (bf16[96,128]{1,0:T(8,128)(2,1)S(1)}, bf16[96,128]{1,0:T(8,128)(2,1)S(1)}, u32[]{:S(2)}, u32[]{:S(2)}) collective-permute-start(bf16[96,128]{1,0:T(8,128)(2,1)S(1)} %get-tuple-element.47), channel_id=1, source_target_pairs={{0,4},{4,0},{8,12},{12,8},{16,20},{20,16},{24,28},{28,24},{1,5},{5... | collective-permute-start | bytes 73736 | tf_op jit(solution)/shard_map/ppermute | solution.py:267
  22.4 1.8 %collective-permute-done = bf16[96,128]{1,0:T(8,128)(2,1)S(1)} collective-permute-done((bf16[96,128]{1,0:T(8,128)(2,1)S(1)}, bf16[96,128]{1,0:T(8,128)(2,1)S(1)}, u32[]{:S(2)}, u32[]{:S(2)}) %collective-permute-start) | collective-permute-done | bytes 24608 | tf_op jit(solution)/shard_map/ppermute | solution.py:267
  24.3 0.9 copy-done.2
  25.2 11.5 %shard_map.104 = (bf16[1024,256]{1,0:T(8,128)(2,1)}, bf16[1024,256]{1,0:T(8,128)(2,1)S(1)}, bf16[1408,256]{1,0:T(8,128)(2,1)}, f32[1408,256]{1,0:T(8,128)S(1)}) custom-call(s32[1]{0:T(128)} %bitcast.half_ref, bf16[8,96,128]{2,1,0:T(8,128)(2,1)S(1)} %all-to-all-done.got_ref, bf16[96,128]{1,0:T(8,128)(2,1)S(1)} %get-tuple-element.45.prev_ref, ...), custom_call_target="tpu_custom_call" | custom-call | flops 9512681472 | bytes 5242880 | tf_op jit(solution)/shard_map/pallas_call | solution.py:162
  36.6 0.8 copy-done.5
  37.4 2.5 %collective-permute-done.2 = bf16[1408,256]{1,0:T(8,128)(2,1)} collective-permute-done((bf16[1408,256]{1,0:T(8,128)(2,1)}, bf16[1408,256]{1,0:T(8,128)(2,1)}, u32[]{:S(2)}, u32[]{:S(2)}) %collective-permute-start.2) | collective-permute-done | bytes 720928 | tf_op jit(solution)/shard_map/ppermute | solution.py:226
  40.0 1.3 %add_convert_fusion = bf16[1408,256]{1,0:T(8,128)(2,1)S(1)} fusion(f32[1408,256]{1,0:T(8,128)S(1)} %get-tuple-element.16, bf16[1408,256]{1,0:T(8,128)(2,1)} %collective-permute-done.2), kind=kLoop, calls=%fused_computation.4 | loop fusion | flops 1081344 | bytes 2883584 | tf_op jit(solution)/shard_map/convert_element_type | solution.py:300
  41.4 1.6 %collective-permute-start.3 = (bf16[352,256]{1,0:T(8,128)(2,1)S(1)}, bf16[352,256]{1,0:T(8,128)(2,1)S(1)}, u32[]{:S(2)}, u32[]{:S(2)}) collective-permute-start(bf16[352,256]{1,0:T(8,128)(2,1)S(1)} %get-tuple-element.32), channel_id=1, source_target_pairs={{0,2},{1,3},{2,0},{3,1},{4,6},{5,7},{6,4},{7,5},{8,10},{9,11},{10,... | collective-permute-start | bytes 540680 | tf_op jit(solution)/shard_map/ppermute | solution.py:226
  42.9 2.2 %collective-permute-start.5 = (bf16[352,256]{1,0:T(8,128)(2,1)S(1)}, bf16[352,256]{1,0:T(8,128)(2,1)S(1)}, u32[]{:S(2)}, u32[]{:S(2)}) collective-permute-start(bf16[352,256]{1,0:T(8,128)(2,1)S(1)} %get-tuple-element.33), channel_id=1, source_target_pairs={{0,6},{1,7},{2,4},{3,5},{4,2},{5,3},{6,0},{7,1},{8,14},{9,15},{10,... | collective-permute-start | bytes 540680 | tf_op jit(solution)/shard_map/ppermute | solution.py:226
  45.2 8.2 %shard_map.105 = (f32[8,96,128]{2,1,0:T(8,128)S(1)}, bf16[96,256]{1,0:T(8,128)(2,1)S(1)}) custom-call(bf16[1024,256]{1,0:T(8,128)(2,1)S(1)} %copy-done.6, s32[27,1024]{1,0:T(8,128)S(1)} %copy-done.3, bf16[2592,256]{1,0:T(8,128)(2,1)S(1)} %bitcast.65), custom_call_target="tpu_custom_call" | custom-call | flops 8153726976 | bytes 3145728 | tf_op jit(solution)/shard_map/pallas_call | solution.py:194
  53.8 1.8 %collective-permute-start.9 = (bf16[96,128]{1,0:T(8,128)(2,1)S(1)}, bf16[96,128]{1,0:T(8,128)(2,1)S(1)}, u32[]{:S(2)}, u32[]{:S(2)}) collective-permute-start(bf16[96,128]{1,0:T(8,128)(2,1)S(1)} %get-tuple-element.42), channel_id=1, source_target_pairs={{0,4},{4,0},{8,12},{12,8},{16,20},{20,16},{24,28},{28,24},{1,5},{5... | collective-permute-start | bytes 73736 | tf_op jit(solution)/shard_map/ppermute | solution.py:267
  56.3 3.1 %collective-permute-start.6 = (bf16[88,256]{1,0:T(8,128)(2,1)S(1)}, bf16[88,256]{1,0:T(8,128)(2,1)S(1)}, u32[]{:S(2)}, u32[]{:S(2)}) collective-permute-start(bf16[88,256]{1,0:T(8,128)(2,1)S(1)} %get-tuple-element.39), channel_id=1, source_target_pairs={{0,8},{1,9},{2,10},{3,11},{4,12},{5,13},{6,14},{7,15},{8,0},{9,1},... | collective-permute-start | bytes 135176 | tf_op jit(solution)/shard_map/ppermute | solution.py:226
  59.4 3.1 %collective-permute-start.8 = (bf16[88,256]{1,0:T(8,128)(2,1)S(1)}, bf16[88,256]{1,0:T(8,128)(2,1)S(1)}, u32[]{:S(2)}, u32[]{:S(2)}) collective-permute-start(bf16[88,256]{1,0:T(8,128)(2,1)S(1)} %get-tuple-element.40), channel_id=1, source_target_pairs={{0,24},{1,25},{2,26},{3,27},{4,28},{5,29},{6,30},{7,31},{8,16},{9,... | collective-permute-start | bytes 135176 | tf_op jit(solution)/shard_map/ppermute | solution.py:226
  63.1 0.7 fusion.7
  63.8 1.4 %collective-permute-done.8 = bf16[88,256]{1,0:T(8,128)(2,1)S(1)} collective-permute-done((bf16[88,256]{1,0:T(8,128)(2,1)S(1)}, bf16[88,256]{1,0:T(8,128)(2,1)S(1)}, u32[]{:S(2)}, u32[]{:S(2)}) %collective-permute-start.8) | collective-permute-done | bytes 45088 | tf_op jit(solution)/shard_map/ppermute | solution.py:226
  65.2 2.2 %collective-permute-done.7 = bf16[88,256]{1,0:T(8,128)(2,1)S(1)} collective-permute-done((bf16[88,256]{1,0:T(8,128)(2,1)S(1)}, bf16[88,256]{1,0:T(8,128)(2,1)S(1)}, u32[]{:S(2)}, u32[]{:S(2)}) %collective-permute-start.7) | collective-permute-done | bytes 45088 | tf_op jit(solution)/shard_map/ppermute | solution.py:226
  67.6 2.2 %collective-permute-start.12 = (bf16[88,256]{1,0:T(8,128)(2,1)S(1)}, bf16[88,256]{1,0:T(8,128)(2,1)S(1)}, u32[]{:S(2)}, u32[]{:S(2)}) collective-permute-start(bf16[88,256]{1,0:T(8,128)(2,1)S(1)} %fusion.36), channel_id=1, source_target_pairs={{0,16},{1,17},{2,18},{3,19},{4,20},{5,21},{6,22},{7,23},{8,24},{9,... | collective-permute-start | bytes 135176 | tf_op jit(solution)/shard_map/ppermute | solution.py:226
  69.8 2.2 %collective-permute-start.11 = (bf16[88,256]{1,0:T(8,128)(2,1)S(1)}, bf16[88,256]{1,0:T(8,128)(2,1)S(1)}, u32[]{:S(2)}, u32[]{:S(2)}) collective-permute-start(bf16[88,256]{1,0:T(8,128)(2,1)S(1)} %fusion.36), channel_id=1, source_target_pairs={{0,24},{1,25},{2,26},{3,27},{4,28},{5,29},{6,30},{7,31},{8,16},{9,... | collective-permute-start | bytes 135176 | tf_op jit(solution)/shard_map/ppermute | solution.py:226
  72.6 3.0 %collective-permute-done.11 = bf16[88,256]{1,0:T(8,128)(2,1)S(1)} collective-permute-done((bf16[88,256]{1,0:T(8,128)(2,1)S(1)}, bf16[88,256]{1,0:T(8,128)(2,1)S(1)}, u32[]{:S(2)}, u32[]{:S(2)}) %collective-permute-start.11) | collective-permute-done | bytes 45088 | tf_op jit(solution)/shard_map/ppermute | solution.py:226
  75.7 0.8 collective-permute-start.16
  76.5 1.2 %collective-permute-start.15 = (bf16[352,256]{1,0:T(8,128)(2,1)S(1)}, bf16[352,256]{1,0:T(8,128)(2,1)S(1)}, u32[]{:S(2)}, u32[]{:S(2)}) collective-permute-start(bf16[352,256]{1,0:T(8,128)(2,1)S(1)} %pad_maximum_fusion.1), channel_id=1, source_target_pairs={{0,4},{1,5},{2,6},{3,7},{4,0},{5,1},{6,2},{7,3},{8,12},{9,13},{10,... | collective-permute-start | bytes 540680 | tf_op jit(solution)/shard_map/ppermute | solution.py:226
  77.7 1.5 %collective-permute-start.14 = (bf16[352,256]{1,0:T(8,128)(2,1)S(1)}, bf16[352,256]{1,0:T(8,128)(2,1)S(1)}, u32[]{:S(2)}, u32[]{:S(2)}) collective-permute-start(bf16[352,256]{1,0:T(8,128)(2,1)S(1)} %pad_maximum_fusion.1), channel_id=1, source_target_pairs={{0,6},{1,7},{2,4},{3,5},{4,2},{5,3},{6,0},{7,1},{8,14},{9,15},{10,... | collective-permute-start | bytes 540680 | tf_op jit(solution)/shard_map/ppermute | solution.py:226
  79.2 3.5 %all-to-all-start.1 = ((bf16[8,96,128]{2,1,0:T(8,128)(2,1)}), bf16[8,96,128]{2,1,0:T(8,128)(2,1)S(1)}, u32[]{:S(2)}, u32[]{:S(2)}) async-start(bf16[8,96,128]{2,1,0:T(8,128)(2,1)} %fusion.7), calls=%async_computation.1 | async-start | bytes 393216 | tf_op jit(solution)/shard_map/all_to_all | solution.py:311
  82.8 2.9 %collective-permute-done.14 = bf16[352,256]{1,0:T(8,128)(2,1)S(1)} collective-permute-done((bf16[352,256]{1,0:T(8,128)(2,1)S(1)}, bf16[352,256]{1,0:T(8,128)(2,1)S(1)}, u32[]{:S(2)}, u32[]{:S(2)}) %collective-permute-start.14) | collective-permute-done | bytes 180256 | tf_op jit(solution)/shard_map/ppermute | solution.py:226
  86.1 4.4 %all-to-all-done.1 = bf16[8,96,128]{2,1,0:T(8,128)(2,1)S(1)} async-done(((bf16[8,96,128]{2,1,0:T(8,128)(2,1)}), bf16[8,96,128]{2,1,0:T(8,128)(2,1)S(1)}, u32[]{:S(2)}, u32[]{:S(2)}) %all-to-all-start.1) | async-done | bytes 196640 | tf_op jit(solution)/shard_map/all_to_all | solution.py:311
  90.6 1.5 %fusion.3 = bf16[1024,96]{0,1:T(8,128)(2,1)} fusion(bf16[96,1024]{1,0:T(8,128)(2,1)S(1)} %copy_bitcast_fusion, s32[1024]{0:T(1024)S(1)} %copy-done.7), kind=kOutput, calls=%fused_computation.7 | convolution fusion | flops 202473472 | bytes 397312 | tf_op jit(solution)/shard_map/dot_general | solution.py:21
  92.8 1.7 %convert_multiply_fusion = f32[2592,256]{1,0:T(8,128)} fusion(bf16[1296,256]{1,0:T(8,128)(2,1)S(1)} %get-tuple-element.28, bf16[1296,256]{1,0:T(8,128)(2,1)S(1)} %get-tuple-element.27), kind=kLoop, calls=%fused_computation.2 | loop fusion | flops 3317760 | bytes 3981312 | tf_op jit(solution)/shard_map/mul | solution.py:323
  (52 shorter events, 6.4 us)
Async XLA Ops:
  0.6 23.6 %copy-start = (bf16[27,96,256]{2,1,0:T(8,128)(2,1)S(1)}, bf16[27,96,256]{2,1,0:T(8,128)(2,1)}, u32[]{:S(2)}) copy-start(bf16[27,96,256]{2,1,0:T(8,128)(2,1)} %param.13) | copy-start | bytes 3981316
  0.6 23.6 %copy-start.1 = (bf16[1024,256]{1,0:T(8,128)(2,1)S(1)}, bf16[1024,256]{1,0:T(8,128)(2,1)}, u32[]{:S(2)}) copy-start(bf16[1024,256]{1,0:T(8,128)(2,1)} %cot_hbm.1) | copy-start | bytes 1572868
  0.7 23.6 %copy-start.4 = (f32[256]{0:T(256)S(1)}, f32[256]{0:T(256)}, u32[]{:S(2)}) copy-start(f32[256]{0:T(256)} %param.14) | copy-start | bytes 3076
  2.9 15.2 %all-to-all-start = ((bf16[8,96,128]{2,1,0:T(8,128)(2,1)}), bf16[8,96,128]{2,1,0:T(8,128)(2,1)S(1)}, u32[]{:S(2)}, u32[]{:S(2)}) async-start(bf16[8,96,128]{2,1,0:T(8,128)(2,1)} %shard_map.103), calls=%async_computation | async-start | bytes 393216 | tf_op jit(solution)/shard_map/all_to_all | solution.py:285
  18.7 3.7 %collective-permute-start.1 = (bf16[96,128]{1,0:T(8,128)(2,1)S(1)}, bf16[96,128]{1,0:T(8,128)(2,1)S(1)}, u32[]{:S(2)}, u32[]{:S(2)}) collective-permute-start(bf16[96,128]{1,0:T(8,128)(2,1)S(1)} %get-tuple-element.46), channel_id=1, source_target_pairs={{4,8},{8,4},{12,16},{16,12},{20,24},{24,20},{5,9},{9,5},{13,17},{1... | collective-permute-start | bytes 73736 | tf_op jit(solution)/shard_map/ppermute | solution.py:267
  19.3 4.9 %collective-permute-start = (bf16[96,128]{1,0:T(8,128)(2,1)S(1)}, bf16[96,128]{1,0:T(8,128)(2,1)S(1)}, u32[]{:S(2)}, u32[]{:S(2)}) collective-permute-start(bf16[96,128]{1,0:T(8,128)(2,1)S(1)} %get-tuple-element.47), channel_id=1, source_target_pairs={{0,4},{4,0},{8,12},{12,8},{16,20},{20,16},{24,28},{28,24},{1,5},{5... | collective-permute-start | bytes 73736 | tf_op jit(solution)/shard_map/ppermute | solution.py:267
  24.2 0.9 copy-start.2
  36.6 0.8 copy-start.5
  37.4 2.5 %collective-permute-start.2 = (bf16[1408,256]{1,0:T(8,128)(2,1)}, bf16[1408,256]{1,0:T(8,128)(2,1)}, u32[]{:S(2)}, u32[]{:S(2)}) collective-permute-start(bf16[1408,256]{1,0:T(8,128)(2,1)} %get-tuple-element.17), channel_id=1, source_target_pairs={{0,1},{1,0},{2,3},{3,2},{4,5},{5,4},{6,7},{7,6},{8,9},{9,8},{10,11... | collective-permute-start | bytes 2162696 | tf_op jit(solution)/shard_map/ppermute | solution.py:226
  40.0 5.3 %copy-start.3 = (s32[27,1024]{1,0:T(8,128)S(1)}, s32[27,1024]{1,0:T(8,128)}, u32[]{:S(2)}) copy-start(s32[27,1024]{1,0:T(8,128)} %map_ref.3) | copy-start | bytes 331780
  40.0 5.3 %copy-start.6 = (bf16[1024,256]{1,0:T(8,128)(2,1)S(1)}, bf16[1024,256]{1,0:T(8,128)(2,1)}, u32[]{:S(2)}) copy-start(bf16[1024,256]{1,0:T(8,128)(2,1)} %copy-done.5) | copy-start | bytes 1572868
  41.4 12.1 %collective-permute-start.3 = (bf16[352,256]{1,0:T(8,128)(2,1)S(1)}, bf16[352,256]{1,0:T(8,128)(2,1)S(1)}, u32[]{:S(2)}, u32[]{:S(2)}) collective-permute-start(bf16[352,256]{1,0:T(8,128)(2,1)S(1)} %get-tuple-element.32), channel_id=1, source_target_pairs={{0,2},{1,3},{2,0},{3,1},{4,6},{5,7},{6,4},{7,5},{8,10},{9,11},{10,... | collective-permute-start | bytes 540680 | tf_op jit(solution)/shard_map/ppermute | solution.py:226
  42.9 10.5 %collective-permute-start.5 = (bf16[352,256]{1,0:T(8,128)(2,1)S(1)}, bf16[352,256]{1,0:T(8,128)(2,1)S(1)}, u32[]{:S(2)}, u32[]{:S(2)}) collective-permute-start(bf16[352,256]{1,0:T(8,128)(2,1)S(1)} %get-tuple-element.33), channel_id=1, source_target_pairs={{0,6},{1,7},{2,4},{3,5},{4,2},{5,3},{6,0},{7,1},{8,14},{9,15},{10,... | collective-permute-start | bytes 540680 | tf_op jit(solution)/shard_map/ppermute | solution.py:226
  45.2 8.5 %collective-permute-start.4 = (bf16[352,256]{1,0:T(8,128)(2,1)S(1)}, bf16[352,256]{1,0:T(8,128)(2,1)S(1)}, u32[]{:S(2)}, u32[]{:S(2)}) collective-permute-start(bf16[352,256]{1,0:T(8,128)(2,1)S(1)} %get-tuple-element.34), channel_id=1, source_target_pairs={{0,4},{1,5},{2,6},{3,7},{4,0},{5,1},{6,2},{7,3},{8,12},{9,13},{10,... | collective-permute-start | bytes 540680 | tf_op jit(solution)/shard_map/ppermute | solution.py:226
  53.8 8.7 %collective-permute-start.9 = (bf16[96,128]{1,0:T(8,128)(2,1)S(1)}, bf16[96,128]{1,0:T(8,128)(2,1)S(1)}, u32[]{:S(2)}, u32[]{:S(2)}) collective-permute-start(bf16[96,128]{1,0:T(8,128)(2,1)S(1)} %get-tuple-element.42), channel_id=1, source_target_pairs={{0,4},{4,0},{8,12},{12,8},{16,20},{20,16},{24,28},{28,24},{1,5},{5... | collective-permute-start | bytes 73736 | tf_op jit(solution)/shard_map/ppermute | solution.py:267
  55.6 6.9 %collective-permute-start.10 = (bf16[96,128]{1,0:T(8,128)(2,1)S(1)}, bf16[96,128]{1,0:T(8,128)(2,1)S(1)}, u32[]{:S(2)}, u32[]{:S(2)}) collective-permute-start(bf16[96,128]{1,0:T(8,128)(2,1)S(1)} %get-tuple-element.43), channel_id=1, source_target_pairs={{4,8},{8,4},{12,16},{16,12},{20,24},{24,20},{5,9},{9,5},{13,17},{1... | collective-permute-start | bytes 73736 | tf_op jit(solution)/shard_map/ppermute | solution.py:267
  56.3 7.5 %collective-permute-start.6 = (bf16[88,256]{1,0:T(8,128)(2,1)S(1)}, bf16[88,256]{1,0:T(8,128)(2,1)S(1)}, u32[]{:S(2)}, u32[]{:S(2)}) collective-permute-start(bf16[88,256]{1,0:T(8,128)(2,1)S(1)} %get-tuple-element.39), channel_id=1, source_target_pairs={{0,8},{1,9},{2,10},{3,11},{4,12},{5,13},{6,14},{7,15},{8,0},{9,1},... | collective-permute-start | bytes 135176 | tf_op jit(solution)/shard_map/ppermute | solution.py:226
  59.4 5.8 %collective-permute-start.8 = (bf16[88,256]{1,0:T(8,128)(2,1)S(1)}, bf16[88,256]{1,0:T(8,128)(2,1)S(1)}, u32[]{:S(2)}, u32[]{:S(2)}) collective-permute-start(bf16[88,256]{1,0:T(8,128)(2,1)S(1)} %get-tuple-element.40), channel_id=1, source_target_pairs={{0,24},{1,25},{2,26},{3,27},{4,28},{5,29},{6,30},{7,31},{8,16},{9,... | collective-permute-start | bytes 135176 | tf_op jit(solution)/shard_map/ppermute | solution.py:226
  62.5 5.0 %collective-permute-start.7 = (bf16[88,256]{1,0:T(8,128)(2,1)S(1)}, bf16[88,256]{1,0:T(8,128)(2,1)S(1)}, u32[]{:S(2)}, u32[]{:S(2)}) collective-permute-start(bf16[88,256]{1,0:T(8,128)(2,1)S(1)} %get-tuple-element.41), channel_id=1, source_target_pairs={{0,16},{1,17},{2,18},{3,19},{4,20},{5,21},{6,22},{7,23},{8,24},{9,... | collective-permute-start | bytes 135176 | tf_op jit(solution)/shard_map/ppermute | solution.py:226
  67.5 4.5 %collective-permute-start.13 = (bf16[88,256]{1,0:T(8,128)(2,1)S(1)}, bf16[88,256]{1,0:T(8,128)(2,1)S(1)}, u32[]{:S(2)}, u32[]{:S(2)}) collective-permute-start(bf16[88,256]{1,0:T(8,128)(2,1)S(1)} %fusion.36), channel_id=1, source_target_pairs={{0,8},{1,9},{2,10},{3,11},{4,12},{5,13},{6,14},{7,15},{8,0},{9,1},... | collective-permute-start | bytes 135176 | tf_op jit(solution)/shard_map/ppermute | solution.py:226
  67.6 5.0 %collective-permute-start.12 = (bf16[88,256]{1,0:T(8,128)(2,1)S(1)}, bf16[88,256]{1,0:T(8,128)(2,1)S(1)}, u32[]{:S(2)}, u32[]{:S(2)}) collective-permute-start(bf16[88,256]{1,0:T(8,128)(2,1)S(1)} %fusion.36), channel_id=1, source_target_pairs={{0,16},{1,17},{2,18},{3,19},{4,20},{5,21},{6,22},{7,23},{8,24},{9,... | collective-permute-start | bytes 135176 | tf_op jit(solution)/shard_map/ppermute | solution.py:226
  69.8 5.8 %collective-permute-start.11 = (bf16[88,256]{1,0:T(8,128)(2,1)S(1)}, bf16[88,256]{1,0:T(8,128)(2,1)S(1)}, u32[]{:S(2)}, u32[]{:S(2)}) collective-permute-start(bf16[88,256]{1,0:T(8,128)(2,1)S(1)} %fusion.36), channel_id=1, source_target_pairs={{0,24},{1,25},{2,26},{3,27},{4,28},{5,29},{6,30},{7,31},{8,16},{9,... | collective-permute-start | bytes 135176 | tf_op jit(solution)/shard_map/ppermute | solution.py:226
  75.7 7.0 %collective-permute-start.16 = (bf16[352,256]{1,0:T(8,128)(2,1)S(1)}, bf16[352,256]{1,0:T(8,128)(2,1)S(1)}, u32[]{:S(2)}, u32[]{:S(2)}) collective-permute-start(bf16[352,256]{1,0:T(8,128)(2,1)S(1)} %pad_maximum_fusion.1), channel_id=1, source_target_pairs={{0,2},{1,3},{2,0},{3,1},{4,6},{5,7},{6,4},{7,5},{8,10},{9,11},{10,... | collective-permute-start | bytes 540680 | tf_op jit(solution)/shard_map/ppermute | solution.py:226
  76.5 6.3 %collective-permute-start.15 = (bf16[352,256]{1,0:T(8,128)(2,1)S(1)}, bf16[352,256]{1,0:T(8,128)(2,1)S(1)}, u32[]{:S(2)}, u32[]{:S(2)}) collective-permute-start(bf16[352,256]{1,0:T(8,128)(2,1)S(1)} %pad_maximum_fusion.1), channel_id=1, source_target_pairs={{0,4},{1,5},{2,6},{3,7},{4,0},{5,1},{6,2},{7,3},{8,12},{9,13},{10,... | collective-permute-start | bytes 540680 | tf_op jit(solution)/shard_map/ppermute | solution.py:226
  77.7 7.9 %collective-permute-start.14 = (bf16[352,256]{1,0:T(8,128)(2,1)S(1)}, bf16[352,256]{1,0:T(8,128)(2,1)S(1)}, u32[]{:S(2)}, u32[]{:S(2)}) collective-permute-start(bf16[352,256]{1,0:T(8,128)(2,1)S(1)} %pad_maximum_fusion.1), channel_id=1, source_target_pairs={{0,6},{1,7},{2,4},{3,5},{4,2},{5,3},{6,0},{7,1},{8,14},{9,15},{10,... | collective-permute-start | bytes 540680 | tf_op jit(solution)/shard_map/ppermute | solution.py:226
  79.2 11.2 %all-to-all-start.1 = ((bf16[8,96,128]{2,1,0:T(8,128)(2,1)}), bf16[8,96,128]{2,1,0:T(8,128)(2,1)S(1)}, u32[]{:S(2)}, u32[]{:S(2)}) async-start(bf16[8,96,128]{2,1,0:T(8,128)(2,1)} %fusion.7), calls=%async_computation.1 | async-start | bytes 393216 | tf_op jit(solution)/shard_map/all_to_all | solution.py:311
  85.9 4.7 %copy-start.7 = (s32[1024]{0:T(1024)S(1)}, s32[1024]{0:T(1024)}, u32[]{:S(2)}) copy-start(s32[1024]{0:T(1024)} %param.9) | copy-start | bytes 12292
  90.5 2.3 %collective-permute-start.17 = (bf16[1408,256]{1,0:T(8,128)(2,1)S(1)}, bf16[1408,256]{1,0:T(8,128)(2,1)S(1)}, u32[]{:S(2)}, u32[]{:S(2)}) collective-permute-start(bf16[1408,256]{1,0:T(8,128)(2,1)S(1)} %pad_maximum_fusion), channel_id=1, source_target_pairs={{0,1},{1,0},{2,3},{3,2},{4,5},{5,4},{6,7},{7,6},{8,9},{9,8},{10,11... | collective-permute-start | bytes 2162696 | tf_op jit(solution)/shard_map/ppermute | solution.py:226

commit v4 on v3

v4 whole, which is shorter than its diff:
```python
import functools
import math

import jax
import jax.numpy as jnp
from jax import lax
from jax.experimental import pallas as pl
from jax.experimental.pallas import tpu as pltpu
from jax.sharding import PartitionSpec as P

BF = jnp.bfloat16
F32 = jnp.float32
LOW = 256
SHIFT = 8
VMEM_LIMIT = 20 << 20
SMALL_LIMIT = 6 << 20
FULL_LIMIT = 58 << 20
AXES = ("brick", "group")


def dot(a, b, a_dim, b_dim):
    dims = (((a_dim,), (b_dim,)), ((), ()))
    return lax.dot_general(a, b, dims, preferred_element_type=F32)


def one_hot_rows(index, width):
    columns = jnp.arange(width, dtype=jnp.int32)
    return (index[:, None] == columns[None, :]).astype(BF)


def one_hot_low(low, lanes):
    iota = lax.broadcasted_iota(jnp.int32, (LOW, lanes), 0).astype(BF)
    hit = iota == jnp.broadcast_to(low.astype(BF), (LOW, lanes))
    return jnp.where(hit, jnp.ones((), BF), jnp.zeros((), BF))


def send_kernel(feat_ref, order_ref, out_ref, x_ref):
    channels, rows = feat_ref.shape
    per = out_ref.shape[2]
    for a in range(rows // LOW):
        x_ref[a * channels : (a + 1) * channels, :] = feat_ref[:, a * LOW : (a + 1) * LOW]
    for n in range(rows // LOW):
        row = order_ref[:, n * LOW : (n + 1) * LOW]
        terms = dot(x_ref[...], one_hot_low((row & (LOW - 1)).astype(F32), LOW), 1, 0)
        block = jnp.broadcast_to(lax.shift_right_logical(row, SHIFT), (channels, LOW))
        picked = terms[:channels]
        for a in range(1, rows // LOW):
            picked = jnp.where(block == a, terms[a * channels : (a + 1) * channels], picked)
        picked = picked.astype(BF)
        for p in range(LOW // per):
            out_ref[n * (LOW // per) + p] = picked[:, p * per : (p + 1) * per]


def forward_kernel(
    half_ref, got_ref, prev_ref, next_ref, low_ref, high_ref, w_hbm, bias_ref, cot_hbm, out_hbm, send_ref, keep_ref,
    g_ref, x_ref, wt_ref, w_ref, cot_ref, out_ref, pg_ref, w_sem, cot_sem, out_sem,
):
    fetch_w = pltpu.make_async_copy(w_hbm, w_ref, w_sem)
    fetch_w.start()
    fetch_cot = pltpu.make_async_copy(cot_hbm, cot_ref, cot_sem)
    fetch_cot.start()
    offsets, voxels = low_ref.shape
    depth, c_out = w_ref.shape
    channels = depth // offsets
    here = voxels // LOW
    blocks = x_ref.shape[0] // channels
    center = offsets // 2
    per = got_ref.shape[2]
    for a in range(here):
        for p in range(LOW // per):
            x_ref[a * channels : (a + 1) * channels, p * per : (p + 1) * per] = got_ref[a * (LOW // per) + p]
    face = prev_ref.shape[1]
    x_ref[here * channels :, :face] = prev_ref[...]
    x_ref[here * channels :, face:] = next_ref[...]
    ready = offsets // 3
    for k in range(offsets):
        if k == ready:
            fetch_w.wait()
            fetch_cot.wait()
        for j in range(2 * (k - ready), min(2 * (k - ready + 1), offsets)) if k >= ready else ():
            wt_ref[:, j * channels : (j + 1) * channels] = w_ref[j * channels : (j + 1) * channels, :].T
        at = slice(k * channels, (k + 1) * channels)
        if k == center:
            for a in range(here):
                g_ref[at, a * LOW : (a + 1) * LOW] = x_ref[a * channels : (a + 1) * channels, :]
            continue
        low, high = low_ref[k : k + 1, :], high_ref[k : k + 1, :]
        for n in range(here):
            sl = slice(n * LOW, (n + 1) * LOW)
            terms = dot(x_ref[...], one_hot_low(low[:, sl], LOW), 1, 0)
            block = jnp.broadcast_to(high[:, sl], (channels, LOW))
            picked = jnp.zeros((channels, LOW), F32)
            for a in range(blocks):
                picked = jnp.where(block == a, terms[a * channels : (a + 1) * channels], picked)
            g_ref[at, sl] = picked.astype(BF)
    for n in range(here):
        sl = slice(n * LOW, (n + 1) * LOW)
        pre = dot(wt_ref[...], g_ref[:, sl], 1, 0).T + bias_ref[0:1, :]
        out_ref[sl, :] = jnp.maximum(pre, 0.0).astype(BF)
        pg_ref[sl, :] = jnp.where(pre > 0, cot_ref[sl, :].astype(F32), 0.0).astype(BF)
    store = pltpu.make_async_copy(out_ref, out_hbm, out_sem)
    store.start()
    half = half_ref[0]
    count = depth // 2
    step = count // 3
    for ref, which in ((send_ref, 1 - half), (keep_ref, half)):
        for m in range(3):
            at = pl.ds(pl.multiple_of(which * count + m * step, 16), step)
            ref[m * step : (m + 1) * step, :] = dot(g_ref[at, :], pg_ref[...], 1, 0).astype(ref.dtype)
        ref[count:, :] = jnp.zeros((ref.shape[0] - count, c_out), ref.dtype)
    store.wait()


def backward_kernel(
    packed, out_hbm, cot_hbm, low_ref, high_ref, w_ref, here_ref, faces_ref,
    c_ref, acc_ref, pg_ref, out_ref, cot_ref, out_sem, cot_sem,
):
    fetch_out = pltpu.make_async_copy(out_hbm, out_ref, out_sem)
    fetch_out.start()
    fetch_cot = pltpu.make_async_copy(cot_hbm, cot_ref, cot_sem)
    fetch_cot.start()
    offsets, voxels = low_ref.shape
    depth = w_ref.shape[0]
    channels = depth // offsets
    here = voxels // LOW
    blocks = acc_ref.shape[0] // channels
    fetch_out.wait()
    fetch_cot.wait()
    pg_ref[...] = jnp.where(out_ref[...] > 0, cot_ref[...], jnp.zeros((), BF))
    step = depth // 3
    for m in range(3):
        sl = slice(m * step, (m + 1) * step)
        c_ref[sl, :] = dot(w_ref[sl, :], pg_ref[...], 1, 1).astype(BF)
    center = offsets // 2
    for a in range(here):
        at = slice(a * channels, (a + 1) * channels)
        acc_ref[at, :] = c_ref[center * channels : (center + 1) * channels, a * LOW : (a + 1) * LOW].astype(F32)
    acc_ref[here * channels :, :] = jnp.zeros((channels * (blocks - here), LOW), F32)
    for k in range(offsets):
        if k == center:
            continue
        contrib = c_ref[k * channels : (k + 1) * channels, :]
        low, high = low_ref[k : k + 1, :], high_ref[k : k + 1, :]
        block = jnp.broadcast_to(high.astype(BF), (channels, voxels))
        parts = [jnp.where(block == jnp.array(a, BF), contrib, jnp.zeros((), BF)) for a in range(blocks)]
        acc_ref[...] += dot(jnp.concatenate(parts, 0), one_hot_low(low, voxels), 1, 1)
    if packed:
        part, per = channels // 2, LOW // 2
        for a in range(here):
            for p in range(2):
                for h in range(2):
                    at = slice(a * channels + h * part, a * channels + (h + 1) * part)
                    to = slice((2 * a + p) * part, (2 * a + p + 1) * part)
                    here_ref[to, h * per : (h + 1) * per] = acc_ref[at, p * per : (p + 1) * per]
    else:
        here_ref[...] = acc_ref[: here * channels, :]
    faces_ref[...] = acc_ref[here * channels :, :].astype(BF)


def finish_kernel(packed, here_ref, prev_ref, next_ref, pick_ref, out_ref, from_ref):
    channels, face = prev_ref.shape
    blocks = here_ref.shape[0] // channels
    from_ref[:, :face] = prev_ref[...]
    from_ref[:, face:] = next_ref[...]
    part, per = channels // 2, LOW // 2
    for a in range(blocks):
        added = dot(from_ref[...], pick_ref[:, a * LOW : (a + 1) * LOW], 1, 0)
        if not packed:
            at = slice(a * channels, (a + 1) * channels)
            out_ref[at, :] = (here_ref[at, :] + added).astype(BF)
            continue
        for p in range(2):
            at = slice((2 * a + p) * part, (2 * a + p + 1) * part)
            for h in range(2):
                lanes = slice(h * per, (h + 1) * per)
                term = added[h * part : (h + 1) * part, p * per : (p + 1) * per]
                out_ref[at, lanes] = (here_ref[at, lanes] + term).astype(BF)


def place_kernel(side_ref, keep_ref, came_ref, order_ref, out_ref, back_ref):
    channels, rows = out_ref.shape
    part, per = channels // 2, LOW // 2
    side = side_ref[0]
    for z in range(rows // LOW):
        at = slice(z * part, (z + 1) * part)
        for p in range(2):
            block = jnp.where(side == p, keep_ref[at, :].astype(F32), came_ref[at, :].astype(F32)).astype(BF)
            lanes = slice((2 * z + p) * per, (2 * z + p + 1) * per)
            for h in range(2):
                back_ref[h * part : (h + 1) * part, lanes] = block[:, h * per : (h + 1) * per]
    row = order_ref[...]
    block = jnp.broadcast_to(lax.shift_right_logical(row, SHIFT).astype(F32).astype(BF), (channels, rows))
    back = back_ref[...]
    parts = [jnp.where(block == jnp.array(a, BF), back, jnp.zeros((), BF)) for a in range(rows // LOW)]
    placed = dot(jnp.concatenate(parts, 0), one_hot_low((row & (LOW - 1)).astype(F32), rows), 1, 1)
    for a in range(rows // LOW):
        out_ref[:, a * LOW : (a + 1) * LOW] = placed[a * channels : (a + 1) * channels].astype(BF)


def whole(count):
    return [pl.BlockSpec(memory_space=pltpu.VMEM)] * count


def send_blocks(features, order, bricks):
    channels, rows = features.shape
    return pl.pallas_call(
        send_kernel,
        out_shape=jax.ShapeDtypeStruct((bricks, channels, rows // bricks), BF),
        in_specs=whole(2),
        out_specs=whole(1)[0],
        scratch_shapes=[pltpu.VMEM((channels * rows // LOW, LOW), BF)],
        compiler_params=pltpu.CompilerParams(vmem_limit_bytes=SMALL_LIMIT),
        cost_estimate=pl.CostEstimate(flops=2 * rows * rows * channels, bytes_accessed=1 << 19, transcendentals=0),
    )(features, order)


def forward(half, got, prev_upper, next_lower, low, high, w, bias, cot, padded):
    offsets, voxels = low.shape
    depth, c_out = w.shape
    rows = depth // offsets * (voxels // LOW + 1)
    macs = voxels * depth * c_out * 2 + offsets * voxels * LOW * rows
    hbm = pl.BlockSpec(memory_space=pltpu.HBM)
    return pl.pallas_call(
        forward_kernel,
        out_shape=(
            jax.ShapeDtypeStruct((voxels, c_out), BF),
            jax.ShapeDtypeStruct((padded // 2, c_out), BF),
            jax.ShapeDtypeStruct((padded // 2, c_out), F32),
        ),
        in_specs=[pl.BlockSpec(memory_space=pltpu.SMEM)] + whole(5) + [hbm] + whole(1) + [hbm],
        out_specs=(hbm,) + tuple(whole(2)),
        scratch_shapes=[
            pltpu.VMEM((depth, voxels), BF),
            pltpu.VMEM((rows, LOW), BF),
            pltpu.VMEM((c_out, depth), BF),
            pltpu.VMEM((depth, c_out), BF),
            pltpu.VMEM((voxels, c_out), BF),
            pltpu.VMEM((voxels, c_out), BF),
            pltpu.VMEM((voxels, c_out), BF),
            pltpu.SemaphoreType.DMA,
            pltpu.SemaphoreType.DMA,
            pltpu.SemaphoreType.DMA,
        ],
        compiler_params=pltpu.CompilerParams(vmem_limit_bytes=FULL_LIMIT),
        cost_estimate=pl.CostEstimate(flops=2 * macs, bytes_accessed=5 << 20, transcendentals=0),
    )(half, got, prev_upper, next_lower, low, high, w, bias, cot)


def backward(packed, out, cot, low, high, w):
    hbm = pl.BlockSpec(memory_space=pltpu.HBM)
    offsets, voxels = low.shape
    depth, c_out = w.shape
    channels = depth // offsets
    rows = channels * (voxels // LOW + 1)
    macs = voxels * depth * c_out + offsets * voxels * LOW * rows
    return pl.pallas_call(
        functools.partial(backward_kernel, packed),
        out_shape=(
            jax.ShapeDtypeStruct((voxels // LOW * channels, LOW), F32),
            jax.ShapeDtypeStruct((channels, LOW), BF),
        ),
        in_specs=[hbm, hbm] + whole(3),
        out_specs=tuple(whole(2)),
        scratch_shapes=[
            pltpu.VMEM((depth, voxels), BF),
            pltpu.VMEM((rows, LOW), F32),
            pltpu.VMEM((voxels, c_out), BF),
            pltpu.VMEM((voxels, c_out), BF),
            pltpu.VMEM((voxels, c_out), BF),
            pltpu.SemaphoreType.DMA,
            pltpu.SemaphoreType.DMA,
        ],
        compiler_params=pltpu.CompilerParams(vmem_limit_bytes=VMEM_LIMIT),
        cost_estimate=pl.CostEstimate(flops=2 * macs, bytes_accessed=3 << 20, transcendentals=0),
    )(out, cot, low, high, w)


def finish(packed, here, from_prev, from_next, pick):
    rows, _ = here.shape
    channels, face = from_prev.shape
    return pl.pallas_call(
        functools.partial(finish_kernel, packed),
        out_shape=jax.ShapeDtypeStruct((rows, LOW), BF),
        in_specs=whole(4),
        out_specs=whole(1)[0],
        scratch_shapes=[pltpu.VMEM((channels, 2 * face), BF)],
        compiler_params=pltpu.CompilerParams(vmem_limit_bytes=SMALL_LIMIT),
        cost_estimate=pl.CostEstimate(flops=4 * rows * LOW * face, bytes_accessed=1 << 20, transcendentals=0),
    )(here, from_prev, from_next, pick)


def place(side, keep, came, order, channels):
    rows = order.shape[1]
    return pl.pallas_call(
        place_kernel,
        out_shape=jax.ShapeDtypeStruct((channels, rows), BF),
        in_specs=[pl.BlockSpec(memory_space=pltpu.SMEM)] + whole(3),
        out_specs=whole(1)[0],
        scratch_shapes=[pltpu.VMEM((channels, rows), BF)],
        compiler_params=pltpu.CompilerParams(vmem_limit_bytes=SMALL_LIMIT),
        cost_estimate=pl.CostEstimate(flops=2 * rows * rows * channels, bytes_accessed=1 << 20, transcendentals=0),
    )(side, keep, came, order)


def stages(count):
    plan, stride = [], 1
    while stride < count:
        left = count // stride
        radix = 4 if stride > 1 and left % 4 == 0 else 2
        if left % radix:
            radix = left
        plan.append((stride, radix))
        stride *= radix
    return plan


def swapped(array, count, stride, radix, delta):
    def partner(i):
        digit = i // stride % radix
        other = (digit ^ delta) if radix in (2, 4) else (delta - digit) % radix
        return i + (other - digit) * stride

    return lax.ppermute(array, AXES, [(i, partner(i)) for i in range(count)])


def other_digit(digit, delta, radix):
    return (digit ^ delta) if radix in (2, 4) else (delta - digit) % radix


def reduce_stage(x, flat, count, stride, radix):
    digit = flat // stride % radix
    pieces = x.reshape((radix, x.shape[0] // radix) + x.shape[1:])
    total = None
    for delta in range(radix):
        piece = lax.dynamic_index_in_dim(pieces, other_digit(digit, delta, radix), 0, keepdims=False)
        if radix not in (2, 4) or delta:
            piece = swapped(piece, count, stride, radix, delta)
        total = piece.astype(F32) if total is None else total + piece.astype(F32)
    return total.astype(BF)


def by_digit(got, digit, radix):
    parts = []
    for place in range(radix):
        part = got[0]
        for d in range(radix):
            where = (place ^ d) if radix in (2, 4) else (place + d) % radix
            part = jnp.where(digit == d, got[where], part)
        parts.append(part)
    return parts


def joined(parts):
    return parts[0] if len(parts) == 1 else jnp.concatenate(parts, 0)


def gather_stage(parts, flat, count, stride, radix, cargo=lambda delta: None):
    digit = flat // stride % radix
    rows = sum(part.shape[0] for part in parts)
    got, brought = [], {}
    for d in range(radix):
        if radix in (2, 4) and d == 0:
            got.append(joined(parts))
            continue
        extra = cargo(d)
        piece = swapped(joined(parts if extra is None else parts + [extra]), count, stride, radix, d)
        got.append(piece[:rows])
        brought[d] = piece[rows:]
    return by_digit(got, digit, radix), brought


def meet(array_up, array_down):
    size = lax.axis_size("brick")
    odd = lax.axis_index("brick") % 2 == 1
    got = []
    for start in (0, 1):
        pairs = []
        for i in range(start, size - 1, 2):
            pairs += [(i, i + 1), (i + 1, i)]
        goes_up = ~odd if start == 0 else odd
        got.append(lax.ppermute(jnp.where(goes_up, array_up, array_down), "brick", pairs))
    return jnp.where(odd, got[0], got[1]), jnp.where(odd, got[1], got[0])


def on_device(features, order, face_list, face_count, kernel_map, weight, bias, cotangent):
    offsets, channels, c_out = weight.shape
    rows = features.shape[0]
    face = face_list.shape[0] // 2
    bricks = lax.axis_size("brick")
    count = bricks * lax.axis_size("group")
    per = rows // bricks
    depth = offsets * channels
    unit = 8 * count
    padded = -(-depth // unit) * unit

    w = weight.reshape(depth, c_out)
    flat = lax.axis_index("brick") * lax.axis_size("group") + lax.axis_index("group")
    send = send_blocks(features.T, order[None], bricks)
    got = lax.all_to_all(send, "brick", split_axis=0, concat_axis=0)

    slots = jnp.arange(2 * face, dtype=jnp.int32)
    live = jnp.where(slots < face, slots < face_count[0], slots - face < face_count[1])
    pick = one_hot_rows(jnp.where(live, face_list, -1), rows)
    pick, got = lax.optimization_barrier((pick, got))
    local = got.transpose(1, 0, 2).reshape(channels, rows)
    shown = dot(local, pick, 1, 1).astype(BF)
    prev_upper, next_lower = meet(shown[:, face:], shown[:, :face])

    half = (flat % 2).astype(jnp.int32)[None]
    low = (kernel_map & (LOW - 1)).astype(F32)
    high = lax.shift_right_logical(kernel_map, SHIFT).astype(F32)
    tall_bias = jnp.broadcast_to(bias, (8, c_out))
    output, give, keep = forward(half, got, prev_upper, next_lower, low, high, w, tall_bias, cotangent, padded)
    packed = (bricks, count) == (8, 32) and per * 2 == LOW and channels % 16 == 0
    plan = stages(count)[1:]
    total = (keep + swapped(give, count, 1, 2, 1).astype(F32)).astype(BF)
    total = reduce_stage(total, flat, count, *plan[0])
    here, faces = backward(packed, output, cotangent, low, high, w)
    total, faces = lax.optimization_barrier((total, faces))
    from_prev, from_next = meet(faces[:, face:], faces[:, :face])
    for stride, radix in plan[1:]:
        total = reduce_stage(total, flat, count, stride, radix)

    local_grad = finish(packed, here, from_prev, from_next, pick)
    if packed:
        part = channels // 2
        total, local_grad = lax.optimization_barrier((total, local_grad))
        local_grad = local_grad.reshape(bricks // 2, channels, LOW)
        z, x = flat // 8, flat // 4 % 2
        cargo = lambda d: lax.dynamic_index_in_dim(local_grad, z ^ d, 0, keepdims=False)
        parts, brought = gather_stage([total], flat, count, 8, 4, cargo)
        mine = jnp.stack(by_digit([cargo(0)] + [brought[d] for d in (1, 2, 3)], z, 4))
        mine = mine.reshape(bricks // 2, 2, part, LOW)
        give = jnp.where(x == 0, mine[:, 1], mine[:, 0]).reshape(-1, LOW)
        keep = jnp.where(x == 0, mine[:, 0], mine[:, 1]).reshape(-1, LOW)
        parts, brought = gather_stage(parts, flat, count, 2, 4, lambda d: give if d == 2 else None)
        came = brought[2]
    else:
        blocks = rows // LOW
        send = local_grad.reshape(blocks, channels, LOW // per, per).transpose(0, 2, 1, 3)
        came = lax.all_to_all(send.reshape(bricks, channels, per), "brick", split_axis=0, concat_axis=0)
        parts = [total]
        for stride, radix in reversed(plan):
            parts, _ = gather_stage(parts, flat, count, stride, radix)
    total = joined(parts)
    total, came = lax.optimization_barrier((total, came))
    if packed:
        grad_in = place(x.astype(jnp.int32)[None], keep, came, order[None], channels).T
    else:
        returned = came.transpose(1, 0, 2).reshape(channels, rows)
        grad_in = dot(returned, one_hot_rows(order, rows), 1, 0).astype(BF).T
    other = swapped(total, count, 1, 2, 1)
    low = jnp.where(flat % 2 == 0, total, other)[: depth // 2]
    high = jnp.where(flat % 2 == 0, other, total)[: depth // 2]
    scale = jnp.float32(1.0 / math.sqrt(count * rows))
    weight_grad = (jnp.concatenate([low, high], 0).astype(F32) * scale).reshape(offsets, channels, c_out)
    return output, grad_in, weight_grad


def solution(mesh):
    return jax.shard_map(
        on_device,
        mesh=mesh,
        in_specs=(
            P(AXES, None),
            P(AXES),
            P(AXES),
            P(AXES),
            P(None, AXES),
            P(),
            P(),
            P(AXES, None),
        ),
        out_specs=(P(AXES, None), P(AXES, None), P()),
        check_vma=False,
    )
```

time: 95 us -> 95.7 us (level)
  Pallas kernels: 21.8 us -> 24.7 us
  starting transfers between devices: 35 us -> 32.5 us
  matrix products: 2.69 us -> 0.29 us
  other arithmetic: 5.74 us -> 7.78 us
    ppermute x14, waiting for transfers between devices: 13.7 us -> 19.3 us  [swapped(): return lax.ppermute(array, AXES, [(i, partner(i)) for i in range(count)])]
    all_to_all x1 -> x0, waiting for transfers between devices: 4.39 us -> none  [on_device(): returned = lax.all_to_all(local_grad, 'brick', split_axis=0, concat_axis=0)]
    ppermute x4, starting transfers between devices: 6.13 us -> 9.64 us  [meet(): lax.ppermute(jnp.where(goes_up, array_up, array_down), 'brick', pairs)]
    all_to_all x1 -> x0, starting transfers between devices: 3.46 us -> none  [on_device(): returned = lax.all_to_all(local_grad, 'brick', split_axis=0, concat_axis=0)]
    pallas_call x1 -> x3, Pallas kernels: 8.16 us -> 11.3 us  [the longest x1 9.94 us: backward(): pl.pallas_call(functools.partial(backward_kernel, packed), out_shape=(jax...]
    ppermute x14, starting transfers between devices: 18.2 us -> 15.6 us  [swapped(): return lax.ppermute(array, AXES, [(i, partner(i)) for i in range(count)])]
    dot_general x5 -> x1, matrix products: 2.69 us -> 0.29 us  [dot(): return lax.dot_general(a, b, dims, preferred_element_type=F32)]
    select_n x3 -> x5, other arithmetic: 0.35 us -> 2.36 us  [the longest x1 1.98 us: on_device(): pick = one_hot_rows(jnp.where(live, face_list, -1), rows)]
  transfers between devices with their start and end apart: 20 -> 19, of which waited for: 12 -> 11; matrix products, arithmetic and copies ran while one was open for 7% -> 4% of each run, Pallas kernels for 9% -> 12%
where the time goes in v4:
time: 95.7 us; the launch traced here: 95.3 us
  starting transfers between devices  32.5 us (34%)
  waiting for transfers between devices  24.9 us (26%)
  Pallas kernels  24.7 us (26%)
  other arithmetic  7.78 us (8%)
  local copies, waits for them, and re-layouts  4 us (4%)
  between operations  1.04 us (1%)
    ppermute x14, waiting for transfers between devices, swapped(): return lax.ppermute(array, AXES, [(i, partner(i)) for i in range(count)])  19.3 us
    ppermute x14, starting transfers between devices, swapped(): return lax.ppermute(array, AXES, [(i, partner(i)) for i in range(count)])  15.6 us
    pallas_call x1, Pallas kernels, forward(): pl.pallas_call(forward_kernel, out_shape=(jax.ShapeDtypeStruct((voxels, c...  12.4 us
    pallas_call x1, Pallas kernels, backward(): pl.pallas_call(functools.partial(backward_kernel, packed), out_shape=(jax...  9.94 us
    ppermute x4, starting transfers between devices, meet(): lax.ppermute(jnp.where(goes_up, array_up, array_down), 'brick', pairs)  9.64 us
    all_to_all x1, starting transfers between devices, on_device(): got = lax.all_to_all(send, 'brick', split_axis=0, concat_axis=0)  7.25 us
    all_to_all x1, waiting for transfers between devices, on_device(): got = lax.all_to_all(send, 'brick', split_axis=0, concat_axis=0)  4.5 us
    unnamed x22, local copies, waits for them, and re-layouts  1.99 us
  transfers between devices with their start and end apart: 19, of which 11 were waited for; matrix products, arithmetic and copies ran while one was open for 4% of the time, Pallas kernels for 12%

profile of v4, /device:TPU:0, one launch (start us, length us, event | category | flops | bytes accessed | tf_op | source)
XLA Modules:
  0.0 95.3 jit_solution(9008248311757481312)
XLA Ops:
  0.6 0.9 copy-done.4
  2.2 1.1 %shard_map.103 = bf16[8,96,128]{2,1,0:T(8,128)(2,1)} custom-call(bf16[96,1024]{1,0:T(8,128)(2,1)S(1)} %bitcast.79, s32[1,1024]{1,0:T(1,128)S(1)} %bitcast.80), custom_call_target="tpu_custom_call" | custom-call | flops 201326592 | bytes 524288 | tf_op jit(solution)/shard_map/pallas_call | solution.py:206
  3.3 7.3 %all-to-all-start = ((bf16[8,96,128]{2,1,0:T(8,128)(2,1)}), bf16[8,96,128]{2,1,0:T(8,128)(2,1)S(1)}, u32[]{:S(2)}, u32[]{:S(2)}) async-start(bf16[8,96,128]{2,1,0:T(8,128)(2,1)} %shard_map.103), calls=%async_computation | async-start | bytes 393216 | tf_op jit(solution)/shard_map/all_to_all | solution.py:399
  10.6 1.3 %fusion.22 = (s32[1]{0:T(128)}, s32[1]{0:T(128)}) fusion(s32[2]{0:T(128)} %param.11), kind=kLoop, calls=%fused_computation.76 | loop fusion | bytes 16 | tf_op jit(solution)/shard_map/slice | solution.py:402
  11.9 2.0 %select_select_fusion.9 = s32[256]{0:T(256)S(1)} fusion(s32[256]{0:T(256)} %param.10, s32[]{:T(128)} %bitcast.2, s32[]{:T(128)} %bitcast.1), kind=kLoop, calls=%fused_computation.75 | loop fusion | flops 1536 | bytes 2056 | tf_op jit(solution)/shard_map/jit(_where)/select_n | solution.py:403
  14.0 4.5 %all-to-all-done.got_ref = bf16[8,96,128]{2,1,0:T(8,128)(2,1)S(1)} async-done(((bf16[8,96,128]{2,1,0:T(8,128)(2,1)}), bf16[8,96,128]{2,1,0:T(8,128)(2,1)S(1)}, u32[]{:S(2)}, u32[]{:S(2)}) %all-to-all-start) | async-done | bytes 196640 | tf_op jit(solution)/shard_map/all_to_all | solution.py:399
  19.5 3.0 %collective-permute-start = (bf16[96,128]{1,0:T(8,128)(2,1)S(1)}, bf16[96,128]{1,0:T(8,128)(2,1)S(1)}, u32[]{:S(2)}, u32[]{:S(2)}) collective-permute-start(bf16[96,128]{1,0:T(8,128)(2,1)S(1)} %get-tuple-element.67), channel_id=1, source_target_pairs={{0,4},{4,0},{8,12},{12,8},{16,20},{20,16},{24,28},{28,24},{1,5},{5... | collective-permute-start | bytes 73736 | tf_op jit(solution)/shard_map/ppermute | solution.py:381
  22.6 0.7 shift-right-logical_convert_fusion
  23.3 1.1 %collective-permute-done = bf16[96,128]{1,0:T(8,128)(2,1)S(1)} collective-permute-done((bf16[96,128]{1,0:T(8,128)(2,1)S(1)}, bf16[96,128]{1,0:T(8,128)(2,1)S(1)}, u32[]{:S(2)}, u32[]{:S(2)}) %collective-permute-start) | collective-permute-done | bytes 24608 | tf_op jit(solution)/shard_map/ppermute | solution.py:381
  25.6 12.4 %shard_map.104 = (bf16[1024,256]{1,0:T(8,128)(2,1)}, bf16[1408,256]{1,0:T(8,128)(2,1)}, f32[1408,256]{1,0:T(8,128)}) custom-call(s32[1]{0:T(128)} %bitcast.half_ref, bf16[8,96,128]{2,1,0:T(8,128)(2,1)} %copy-done.8, bf16[96,128]{1,0:T(8,128)(2,1)} %get-tuple-element.65.prev_ref, bf16[96,128]{1,0:T(8,128)(2,1)} %get-tuple-element.64.next_ref, ...), custom_call_target="tpu_custom_call" | custom-call | flops 9512681472 | bytes 5242880 | tf_op jit(solution)/shard_map/pallas_call | solution.py:223
  38.2 2.3 %collective-permute-done.2 = bf16[1408,256]{1,0:T(8,128)(2,1)S(1)} collective-permute-done((bf16[1408,256]{1,0:T(8,128)(2,1)}, bf16[1408,256]{1,0:T(8,128)(2,1)S(1)}, u32[]{:S(2)}, u32[]{:S(2)}) %collective-permute-start.2) | collective-permute-done | bytes 720928 | tf_op jit(solution)/shard_map/ppermute | solution.py:323
  40.5 1.7 %add_convert_fusion = bf16[1408,256]{1,0:T(8,128)(2,1)S(1)} fusion(f32[1408,256]{1,0:T(8,128)} %get-tuple-element.19, bf16[1408,256]{1,0:T(8,128)(2,1)S(1)} %collective-permute-done.2), kind=kLoop, calls=%fused_computation.1 | loop fusion | flops 1081344 | bytes 2883584 | tf_op jit(solution)/shard_map/convert_element_type | solution.py:416
  42.2 1.6 %collective-permute-start.3 = (bf16[352,256]{1,0:T(8,128)(2,1)S(1)}, bf16[352,256]{1,0:T(8,128)(2,1)S(1)}, u32[]{:S(2)}, u32[]{:S(2)}) collective-permute-start(bf16[352,256]{1,0:T(8,128)(2,1)S(1)} %get-tuple-element.43), channel_id=1, source_target_pairs={{0,2},{1,3},{2,0},{3,1},{4,6},{5,7},{6,4},{7,5},{8,10},{9,11},{10,... | collective-permute-start | bytes 540680 | tf_op jit(solution)/shard_map/ppermute | solution.py:323
  43.8 2.2 %collective-permute-start.5 = (bf16[352,256]{1,0:T(8,128)(2,1)S(1)}, bf16[352,256]{1,0:T(8,128)(2,1)S(1)}, u32[]{:S(2)}, u32[]{:S(2)}) collective-permute-start(bf16[352,256]{1,0:T(8,128)(2,1)S(1)} %get-tuple-element.44), channel_id=1, source_target_pairs={{0,6},{1,7},{2,4},{3,5},{4,2},{5,3},{6,0},{7,1},{8,14},{9,15},{10,... | collective-permute-start | bytes 540680 | tf_op jit(solution)/shard_map/ppermute | solution.py:323
  46.1 9.9 %shard_map.105 = (f32[384,256]{1,0:T(8,128)S(1)}, bf16[96,256]{1,0:T(8,128)(2,1)S(1)}) custom-call(bf16[1024,256]{1,0:T(8,128)(2,1)S(1)} %copy-done.7, bf16[1024,256]{1,0:T(8,128)(2,1)S(1)} %copy-done.3, f32[27,1024]{1,0:T(8,128)S(1)} %copy-done.1, f32[27,1024]{1,0:T(8,128)S(1)} %copy-done, bf16[2592,256]{1,0:T(8,128)(2,1)S(1)} %bitcast.78), custom_call_target="tpu_custom_call" | custom-call | flops 8153726976 | bytes 3145728 | tf_op jit(solution)/shard_map/pallas_call | solution.py:256
  56.9 5.3 %collective-permute-start.9 = (bf16[96,128]{1,0:T(8,128)(2,1)S(1)}, bf16[96,128]{1,0:T(8,128)(2,1)S(1)}, u32[]{:S(2)}, u32[]{:S(2)}) collective-permute-start(bf16[96,128]{1,0:T(8,128)(2,1)S(1)} %get-tuple-element.63), channel_id=1, source_target_pairs={{0,4},{4,0},{8,12},{12,8},{16,20},{20,16},{24,28},{28,24},{1,5},{5... | collective-permute-start | bytes 73736 | tf_op jit(solution)/shard_map/ppermute | solution.py:381
  62.6 1.1 %collective-permute-start.8 = (bf16[88,256]{1,0:T(8,128)(2,1)S(1)}, bf16[88,256]{1,0:T(8,128)(2,1)S(1)}, u32[]{:S(2)}, u32[]{:S(2)}) collective-permute-start(bf16[88,256]{1,0:T(8,128)(2,1)S(1)} %get-tuple-element.56), channel_id=1, source_target_pairs={{0,24},{1,25},{2,26},{3,27},{4,28},{5,29},{6,30},{7,31},{8,16},{9,... | collective-permute-start | bytes 135176 | tf_op jit(solution)/shard_map/ppermute | solution.py:323
  63.7 2.1 %collective-permute-start.7 = (bf16[88,256]{1,0:T(8,128)(2,1)S(1)}, bf16[88,256]{1,0:T(8,128)(2,1)S(1)}, u32[]{:S(2)}, u32[]{:S(2)}) collective-permute-start(bf16[88,256]{1,0:T(8,128)(2,1)S(1)} %get-tuple-element.57), channel_id=1, source_target_pairs={{0,16},{1,17},{2,18},{3,19},{4,20},{5,21},{6,22},{7,23},{8,24},{9,... | collective-permute-start | bytes 135176 | tf_op jit(solution)/shard_map/ppermute | solution.py:323
  66.0 0.8 collective-permute-done.6
  66.8 1.7 %collective-permute-done.8 = bf16[88,256]{1,0:T(8,128)(2,1)S(1)} collective-permute-done((bf16[88,256]{1,0:T(8,128)(2,1)S(1)}, bf16[88,256]{1,0:T(8,128)(2,1)S(1)}, u32[]{:S(2)}, u32[]{:S(2)}) %collective-permute-start.8) | collective-permute-done | bytes 45088 | tf_op jit(solution)/shard_map/ppermute | solution.py:323
  68.4 0.9 collective-permute-done.7
  69.5 2.7 %collective-permute-start.11 = (bf16[184,256]{1,0:T(8,128)(2,1)S(1)}, bf16[184,256]{1,0:T(8,128)(2,1)S(1)}, u32[]{:S(2)}, u32[]{:S(2)}) collective-permute-start(bf16[184,256]{1,0:T(8,128)(2,1)S(1)} %get-tuple-element.68), channel_id=1, source_target_pairs={{0,24},{1,25},{2,26},{3,27},{4,28},{5,29},{6,30},{7,31},{8,16},{9,... | collective-permute-start | bytes 282632 | tf_op jit(solution)/shard_map/ppermute | solution.py:323
  72.2 1.8 %collective-permute-start.13 = (bf16[184,256]{1,0:T(8,128)(2,1)S(1)}, bf16[184,256]{1,0:T(8,128)(2,1)S(1)}, u32[]{:S(2)}, u32[]{:S(2)}) collective-permute-start(bf16[184,256]{1,0:T(8,128)(2,1)S(1)} %get-tuple-element.70), channel_id=1, source_target_pairs={{0,8},{1,9},{2,10},{3,11},{4,12},{5,13},{6,14},{7,15},{8,0},{9,1},... | collective-permute-start | bytes 282632 | tf_op jit(solution)/shard_map/ppermute | solution.py:323
  73.9 2.5 %collective-permute-done.11 = bf16[184,256]{1,0:T(8,128)(2,1)S(1)} collective-permute-done((bf16[184,256]{1,0:T(8,128)(2,1)S(1)}, bf16[184,256]{1,0:T(8,128)(2,1)S(1)}, u32[]{:S(2)}, u32[]{:S(2)}) %collective-permute-start.11) | collective-permute-done | bytes 94240 | tf_op jit(solution)/shard_map/ppermute | solution.py:323
  76.4 2.0 %collective-permute-done.12 = bf16[184,256]{1,0:T(8,128)(2,1)S(1)} collective-permute-done((bf16[184,256]{1,0:T(8,128)(2,1)S(1)}, bf16[184,256]{1,0:T(8,128)(2,1)S(1)}, u32[]{:S(2)}, u32[]{:S(2)}) %collective-permute-start.12) | collective-permute-done | bytes 94240 | tf_op jit(solution)/shard_map/ppermute | solution.py:323
  78.6 1.7 %collective-permute-start.15 = (bf16[544,256]{1,0:T(8,128)(2,1)S(1)}, bf16[544,256]{1,0:T(8,128)(2,1)S(1)}, u32[]{:S(2)}, u32[]{:S(2)}) collective-permute-start(bf16[544,256]{1,0:T(8,128)(2,1)S(1)} %constant_dynamic-update-slice_fusion), channel_id=1, source_target_pairs={{0,4},{1,5},{2,6},{3,7},{4,0},{5,1},{6,2},{7,3},{8,12},{9,13},{10,... | collective-permute-start | bytes 835592 | tf_op jit(solution)/shard_map/ppermute | solution.py:323
  80.4 1.5 %collective-permute-start.16 = (bf16[352,256]{1,0:T(8,128)(2,1)S(1)}, bf16[352,256]{1,0:T(8,128)(2,1)S(1)}, u32[]{:S(2)}, u32[]{:S(2)}) collective-permute-start(bf16[352,256]{1,0:T(8,128)(2,1)S(1)} %pad_maximum_fusion.2), channel_id=1, source_target_pairs={{0,2},{1,3},{2,0},{3,1},{4,6},{5,7},{6,4},{7,5},{8,10},{9,11},{10,... | collective-permute-start | bytes 540680 | tf_op jit(solution)/shard_map/ppermute | solution.py:323
  82.3 5.1 %collective-permute-done.16 = bf16[352,256]{1,0:T(8,128)(2,1)S(1)} collective-permute-done((bf16[352,256]{1,0:T(8,128)(2,1)S(1)}, bf16[352,256]{1,0:T(8,128)(2,1)S(1)}, u32[]{:S(2)}, u32[]{:S(2)}) %collective-permute-start.16) | collective-permute-done | bytes 180256 | tf_op jit(solution)/shard_map/ppermute | solution.py:323
  87.3 3.4 %collective-permute-done.14 = bf16[352,256]{1,0:T(8,128)(2,1)S(1)} collective-permute-done((bf16[352,256]{1,0:T(8,128)(2,1)S(1)}, bf16[352,256]{1,0:T(8,128)(2,1)S(1)}, u32[]{:S(2)}, u32[]{:S(2)}) %collective-permute-start.14) | collective-permute-done | bytes 180256 | tf_op jit(solution)/shard_map/ppermute | solution.py:323
  91.6 1.1 %shard_map.107 = bf16[96,1024]{1,0:T(8,128)(2,1)} custom-call(s32[1]{0:T(128)} %bitcast.7.side_ref, bf16[192,256]{1,0:T(8,128)(2,1)S(1)} %bitcast.76, bf16[192,256]{1,0:T(8,128)(2,1)S(1)} %slice.85.came_ref, s32[1,1024]{1,0:T(1,128)S(1)} %bitcast.81), custom_call_target="tpu_custom_call" | custom-call | flops 201326592 | bytes 1048576 | tf_op jit(solution)/shard_map/pallas_call | solution.py:294
  92.7 0.7 collective-permute-done.17
  93.5 1.7 %convert_multiply_fusion = f32[2592,256]{1,0:T(8,128)} fusion(bf16[1296,256]{1,0:T(8,128)(2,1)S(1)} %get-tuple-element.38, bf16[1296,256]{1,0:T(8,128)(2,1)S(1)} %get-tuple-element.37), kind=kLoop, calls=%fused_computation | loop fusion | flops 3317760 | bytes 3981312 | tf_op jit(solution)/shard_map/mul | solution.py:456
  (65 shorter events, 6.2 us)
Async XLA Ops:
  0.6 0.9 copy-start.4
  1.6 0.7 copy-start.5
  2.2 20.3 %copy-start.9 = (s32[27,1024]{1,0:T(8,128)S(1)}, s32[27,1024]{1,0:T(8,128)}, u32[]{:S(2)}) copy-start(s32[27,1024]{1,0:T(8,128)} %param.12) | copy-start | bytes 331780
  2.2 22.7 %copy-start.10 = (f32[256]{0:T(256)S(1)}, f32[256]{0:T(256)}, u32[]{:S(2)}) copy-start(f32[256]{0:T(256)} %param.14) | copy-start | bytes 3076
  3.3 15.2 %all-to-all-start = ((bf16[8,96,128]{2,1,0:T(8,128)(2,1)}), bf16[8,96,128]{2,1,0:T(8,128)(2,1)S(1)}, u32[]{:S(2)}, u32[]{:S(2)}) async-start(bf16[8,96,128]{2,1,0:T(8,128)(2,1)} %shard_map.103), calls=%async_computation | async-start | bytes 393216 | tf_op jit(solution)/shard_map/all_to_all | solution.py:399
  18.5 7.1 %copy-start.8 = (bf16[8,96,128]{2,1,0:T(8,128)(2,1)}, bf16[8,96,128]{2,1,0:T(8,128)(2,1)S(1)}, u32[]{:S(2)}) copy-start(bf16[8,96,128]{2,1,0:T(8,128)(2,1)S(1)} %all-to-all-done.got_ref) | copy-start | bytes 589828
  18.8 4.4 %collective-permute-start.1 = (bf16[96,128]{1,0:T(8,128)(2,1)S(1)}, bf16[96,128]{1,0:T(8,128)(2,1)S(1)}, u32[]{:S(2)}, u32[]{:S(2)}) collective-permute-start(bf16[96,128]{1,0:T(8,128)(2,1)S(1)} %get-tuple-element.66), channel_id=1, source_target_pairs={{4,8},{8,4},{12,16},{16,12},{20,24},{24,20},{5,9},{9,5},{13,17},{1... | collective-permute-start | bytes 73736 | tf_op jit(solution)/shard_map/ppermute | solution.py:381
  19.5 4.9 %collective-permute-start = (bf16[96,128]{1,0:T(8,128)(2,1)S(1)}, bf16[96,128]{1,0:T(8,128)(2,1)S(1)}, u32[]{:S(2)}, u32[]{:S(2)}) collective-permute-start(bf16[96,128]{1,0:T(8,128)(2,1)S(1)} %get-tuple-element.67), channel_id=1, source_target_pairs={{0,4},{4,0},{8,12},{12,8},{16,20},{20,16},{24,28},{28,24},{1,5},{5... | collective-permute-start | bytes 73736 | tf_op jit(solution)/shard_map/ppermute | solution.py:381
  38.0 2.5 %collective-permute-start.2 = (bf16[1408,256]{1,0:T(8,128)(2,1)}, bf16[1408,256]{1,0:T(8,128)(2,1)S(1)}, u32[]{:S(2)}, u32[]{:S(2)}) collective-permute-start(bf16[1408,256]{1,0:T(8,128)(2,1)} %get-tuple-element.20), channel_id=1, source_target_pairs={{0,1},{1,0},{2,3},{3,2},{4,5},{5,4},{6,7},{7,6},{8,9},{9,8},{10,11... | collective-permute-start | bytes 2162696 | tf_op jit(solution)/shard_map/ppermute | solution.py:323
  40.5 5.6 %copy-start = (f32[27,1024]{1,0:T(8,128)S(1)}, f32[27,1024]{1,0:T(8,128)}, u32[]{:S(2)}) copy-start(f32[27,1024]{1,0:T(8,128)} %get-tuple-element.58.high_ref) | copy-start | bytes 331780
  40.5 5.6 %copy-start.1 = (f32[27,1024]{1,0:T(8,128)S(1)}, f32[27,1024]{1,0:T(8,128)}, u32[]{:S(2)}) copy-start(f32[27,1024]{1,0:T(8,128)} %get-tuple-element.59.low_ref) | copy-start | bytes 331780
  40.5 5.6 %copy-start.2 = (bf16[27,96,256]{2,1,0:T(8,128)(2,1)S(1)}, bf16[27,96,256]{2,1,0:T(8,128)(2,1)}, u32[]{:S(2)}) copy-start(bf16[27,96,256]{2,1,0:T(8,128)(2,1)} %param.13) | copy-start | bytes 3981316
  40.5 5.6 %copy-start.3 = (bf16[1024,256]{1,0:T(8,128)(2,1)S(1)}, bf16[1024,256]{1,0:T(8,128)(2,1)}, u32[]{:S(2)}) copy-start(bf16[1024,256]{1,0:T(8,128)(2,1)} %cot_hbm.3) | copy-start | bytes 1572868
  40.5 5.6 %copy-start.7 = (bf16[1024,256]{1,0:T(8,128)(2,1)S(1)}, bf16[1024,256]{1,0:T(8,128)(2,1)}, u32[]{:S(2)}) copy-start(bf16[1024,256]{1,0:T(8,128)(2,1)} %get-tuple-element.13.out_hbm) | copy-start | bytes 1572868
  42.2 13.9 %collective-permute-start.3 = (bf16[352,256]{1,0:T(8,128)(2,1)S(1)}, bf16[352,256]{1,0:T(8,128)(2,1)S(1)}, u32[]{:S(2)}, u32[]{:S(2)}) collective-permute-start(bf16[352,256]{1,0:T(8,128)(2,1)S(1)} %get-tuple-element.43), channel_id=1, source_target_pairs={{0,2},{1,3},{2,0},{3,1},{4,6},{5,7},{6,4},{7,5},{8,10},{9,11},{10,... | collective-permute-start | bytes 540680 | tf_op jit(solution)/shard_map/ppermute | solution.py:323
  43.8 12.3 %collective-permute-start.5 = (bf16[352,256]{1,0:T(8,128)(2,1)S(1)}, bf16[352,256]{1,0:T(8,128)(2,1)S(1)}, u32[]{:S(2)}, u32[]{:S(2)}) collective-permute-start(bf16[352,256]{1,0:T(8,128)(2,1)S(1)} %get-tuple-element.44), channel_id=1, source_target_pairs={{0,6},{1,7},{2,4},{3,5},{4,2},{5,3},{6,0},{7,1},{8,14},{9,15},{10,... | collective-permute-start | bytes 540680 | tf_op jit(solution)/shard_map/ppermute | solution.py:323
  46.0 10.1 %collective-permute-start.4 = (bf16[352,256]{1,0:T(8,128)(2,1)S(1)}, bf16[352,256]{1,0:T(8,128)(2,1)S(1)}, u32[]{:S(2)}, u32[]{:S(2)}) collective-permute-start(bf16[352,256]{1,0:T(8,128)(2,1)S(1)} %get-tuple-element.45), channel_id=1, source_target_pairs={{0,4},{1,5},{2,6},{3,7},{4,0},{5,1},{6,2},{7,3},{8,12},{9,13},{10,... | collective-permute-start | bytes 540680 | tf_op jit(solution)/shard_map/ppermute | solution.py:323
  56.2 9.5 %collective-permute-start.10 = (bf16[96,128]{1,0:T(8,128)(2,1)S(1)}, bf16[96,128]{1,0:T(8,128)(2,1)S(1)}, u32[]{:S(2)}, u32[]{:S(2)}) collective-permute-start(bf16[96,128]{1,0:T(8,128)(2,1)S(1)} %get-tuple-element.62), channel_id=1, source_target_pairs={{4,8},{8,4},{12,16},{16,12},{20,24},{24,20},{5,9},{9,5},{13,17},{1... | collective-permute-start | bytes 73736 | tf_op jit(solution)/shard_map/ppermute | solution.py:381
  56.9 8.8 %collective-permute-start.9 = (bf16[96,128]{1,0:T(8,128)(2,1)S(1)}, bf16[96,128]{1,0:T(8,128)(2,1)S(1)}, u32[]{:S(2)}, u32[]{:S(2)}) collective-permute-start(bf16[96,128]{1,0:T(8,128)(2,1)S(1)} %get-tuple-element.63), channel_id=1, source_target_pairs={{0,4},{4,0},{8,12},{12,8},{16,20},{20,16},{24,28},{28,24},{1,5},{5... | collective-permute-start | bytes 73736 | tf_op jit(solution)/shard_map/ppermute | solution.py:381
  62.2 4.6 %collective-permute-start.6 = (bf16[88,256]{1,0:T(8,128)(2,1)S(1)}, bf16[88,256]{1,0:T(8,128)(2,1)S(1)}, u32[]{:S(2)}, u32[]{:S(2)}) collective-permute-start(bf16[88,256]{1,0:T(8,128)(2,1)S(1)} %get-tuple-element.55), channel_id=1, source_target_pairs={{0,8},{1,9},{2,10},{3,11},{4,12},{5,13},{6,14},{7,15},{8,0},{9,1},... | collective-permute-start | bytes 135176 | tf_op jit(solution)/shard_map/ppermute | solution.py:323
  62.6 5.9 %collective-permute-start.8 = (bf16[88,256]{1,0:T(8,128)(2,1)S(1)}, bf16[88,256]{1,0:T(8,128)(2,1)S(1)}, u32[]{:S(2)}, u32[]{:S(2)}) collective-permute-start(bf16[88,256]{1,0:T(8,128)(2,1)S(1)} %get-tuple-element.56), channel_id=1, source_target_pairs={{0,24},{1,25},{2,26},{3,27},{4,28},{5,29},{6,30},{7,31},{8,16},{9,... | collective-permute-start | bytes 135176 | tf_op jit(solution)/shard_map/ppermute | solution.py:323
  63.7 5.7 %collective-permute-start.7 = (bf16[88,256]{1,0:T(8,128)(2,1)S(1)}, bf16[88,256]{1,0:T(8,128)(2,1)S(1)}, u32[]{:S(2)}, u32[]{:S(2)}) collective-permute-start(bf16[88,256]{1,0:T(8,128)(2,1)S(1)} %get-tuple-element.57), channel_id=1, source_target_pairs={{0,16},{1,17},{2,18},{3,19},{4,20},{5,21},{6,22},{7,23},{8,24},{9,... | collective-permute-start | bytes 135176 | tf_op jit(solution)/shard_map/ppermute | solution.py:323
  69.5 6.9 %collective-permute-start.11 = (bf16[184,256]{1,0:T(8,128)(2,1)S(1)}, bf16[184,256]{1,0:T(8,128)(2,1)S(1)}, u32[]{:S(2)}, u32[]{:S(2)}) collective-permute-start(bf16[184,256]{1,0:T(8,128)(2,1)S(1)} %get-tuple-element.68), channel_id=1, source_target_pairs={{0,24},{1,25},{2,26},{3,27},{4,28},{5,29},{6,30},{7,31},{8,16},{9,... | collective-permute-start | bytes 282632 | tf_op jit(solution)/shard_map/ppermute | solution.py:323
  72.1 6.2 %collective-permute-start.12 = (bf16[184,256]{1,0:T(8,128)(2,1)S(1)}, bf16[184,256]{1,0:T(8,128)(2,1)S(1)}, u32[]{:S(2)}, u32[]{:S(2)}) collective-permute-start(bf16[184,256]{1,0:T(8,128)(2,1)S(1)} %get-tuple-element.69), channel_id=1, source_target_pairs={{0,16},{1,17},{2,18},{3,19},{4,20},{5,21},{6,22},{7,23},{8,24},{9,... | collective-permute-start | bytes 282632 | tf_op jit(solution)/shard_map/ppermute | solution.py:323
  72.2 6.2 %collective-permute-start.13 = (bf16[184,256]{1,0:T(8,128)(2,1)S(1)}, bf16[184,256]{1,0:T(8,128)(2,1)S(1)}, u32[]{:S(2)}, u32[]{:S(2)}) collective-permute-start(bf16[184,256]{1,0:T(8,128)(2,1)S(1)} %get-tuple-element.70), channel_id=1, source_target_pairs={{0,8},{1,9},{2,10},{3,11},{4,12},{5,13},{6,14},{7,15},{8,0},{9,1},... | collective-permute-start | bytes 282632 | tf_op jit(solution)/shard_map/ppermute | solution.py:323
  78.6 12.1 %collective-permute-start.15 = (bf16[544,256]{1,0:T(8,128)(2,1)S(1)}, bf16[544,256]{1,0:T(8,128)(2,1)S(1)}, u32[]{:S(2)}, u32[]{:S(2)}) collective-permute-start(bf16[544,256]{1,0:T(8,128)(2,1)S(1)} %constant_dynamic-update-slice_fusion), channel_id=1, source_target_pairs={{0,4},{1,5},{2,6},{3,7},{4,0},{5,1},{6,2},{7,3},{8,12},{9,13},{10,... | collective-permute-start | bytes 835592 | tf_op jit(solution)/shard_map/ppermute | solution.py:323
  80.4 7.0 %collective-permute-start.16 = (bf16[352,256]{1,0:T(8,128)(2,1)S(1)}, bf16[352,256]{1,0:T(8,128)(2,1)S(1)}, u32[]{:S(2)}, u32[]{:S(2)}) collective-permute-start(bf16[352,256]{1,0:T(8,128)(2,1)S(1)} %pad_maximum_fusion.2), channel_id=1, source_target_pairs={{0,2},{1,3},{2,0},{3,1},{4,6},{5,7},{6,4},{7,5},{8,10},{9,11},{10,... | collective-permute-start | bytes 540680 | tf_op jit(solution)/shard_map/ppermute | solution.py:323
  81.9 8.8 %collective-permute-start.14 = (bf16[352,256]{1,0:T(8,128)(2,1)S(1)}, bf16[352,256]{1,0:T(8,128)(2,1)S(1)}, u32[]{:S(2)}, u32[]{:S(2)}) collective-permute-start(bf16[352,256]{1,0:T(8,128)(2,1)S(1)} %pad_maximum_fusion.2), channel_id=1, source_target_pairs={{0,6},{1,7},{2,4},{3,5},{4,2},{5,3},{6,0},{7,1},{8,14},{9,15},{10,... | collective-permute-start | bytes 540680 | tf_op jit(solution)/shard_map/ppermute | solution.py:323
  90.9 0.7 copy-start.6
  91.2 2.3 %collective-permute-start.17 = (bf16[1408,256]{1,0:T(8,128)(2,1)S(1)}, bf16[1408,256]{1,0:T(8,128)(2,1)S(1)}, u32[]{:S(2)}, u32[]{:S(2)}) collective-permute-start(bf16[1408,256]{1,0:T(8,128)(2,1)S(1)} %pad_maximum_fusion), channel_id=1, source_target_pairs={{0,1},{1,0},{2,3},{3,2},{4,5},{5,4},{6,7},{7,6},{8,9},{9,8},{10,11... | collective-permute-start | bytes 2162696 | tf_op jit(solution)/shard_map/ppermute | solution.py:323

commit v5 on v4

--- a/solution.py
+++ b/solution.py
@@ -14,7 +14,8 @@
 SHIFT = 8
 VMEM_LIMIT = 20 << 20
 SMALL_LIMIT = 6 << 20
-FULL_LIMIT = 58 << 20
+FULL_LIMIT = 52 << 20
+ALL_LIMIT = 60 << 20
 AXES = ("brick", "group")
 
 
@@ -34,9 +35,15 @@
     return jnp.where(hit, jnp.ones((), BF), jnp.zeros((), BF))
 
 
-def send_kernel(feat_ref, order_ref, out_ref, x_ref):
+def send_kernel(feat_hbm, order_hbm, out_ref, feat_ref, order_ref, x_ref, feat_sem, order_sem):
+    fetch_feat = pltpu.make_async_copy(feat_hbm, feat_ref, feat_sem)
+    fetch_feat.start()
+    fetch_order = pltpu.make_async_copy(order_hbm, order_ref, order_sem)
+    fetch_order.start()
     channels, rows = feat_ref.shape
     per = out_ref.shape[2]
+    fetch_feat.wait()
+    fetch_order.wait()
     for a in range(rows // LOW):
         x_ref[a * channels : (a + 1) * channels, :] = feat_ref[:, a * LOW : (a + 1) * LOW]
     for n in range(rows // LOW):
@@ -51,8 +58,15 @@
             out_ref[n * (LOW // per) + p] = picked[:, p * per : (p + 1) * per]
 
 
+def sides(odd, first_ref, second_ref):
+    first, second = first_ref[...].astype(F32), second_ref[...].astype(F32)
+    low = jnp.where(odd == 1, first, second)
+    high = jnp.where(odd == 1, second, first)
+    return low.astype(BF), high.astype(BF)
+
+
 def forward_kernel(
-    half_ref, got_ref, prev_ref, next_ref, low_ref, high_ref, w_hbm, bias_ref, cot_hbm, out_hbm, send_ref, keep_ref,
+    flag_ref, got_ref, even_ref, odd_ref, low_ref, high_ref, w_hbm, bias_ref, cot_hbm, out_hbm, send_ref, keep_ref,
     g_ref, x_ref, wt_ref, w_ref, cot_ref, out_ref, pg_ref, w_sem, cot_sem, out_sem,
 ):
     fetch_w = pltpu.make_async_copy(w_hbm, w_ref, w_sem)
@@ -69,9 +83,10 @@
     for a in range(here):
         for p in range(LOW // per):
             x_ref[a * channels : (a + 1) * channels, p * per : (p + 1) * per] = got_ref[a * (LOW // per) + p]
-    face = prev_ref.shape[1]
-    x_ref[here * channels :, :face] = prev_ref[...]
-    x_ref[here * channels :, face:] = next_ref[...]
+    face = even_ref.shape[1]
+    prev, after = sides(flag_ref[1], even_ref, odd_ref)
+    x_ref[here * channels :, :face] = prev
+    x_ref[here * channels :, face:] = after
     ready = offsets // 3
     for k in range(offsets):
         if k == ready:
@@ -95,24 +110,24 @@
             g_ref[at, sl] = picked.astype(BF)
     for n in range(here):
         sl = slice(n * LOW, (n + 1) * LOW)
-        pre = dot(wt_ref[...], g_ref[:, sl], 1, 0).T + bias_ref[0:1, :]
+        pre = dot(wt_ref[...], g_ref[:, sl], 1, 0).T + bias_ref[...]
         out_ref[sl, :] = jnp.maximum(pre, 0.0).astype(BF)
         pg_ref[sl, :] = jnp.where(pre > 0, cot_ref[sl, :].astype(F32), 0.0).astype(BF)
     store = pltpu.make_async_copy(out_ref, out_hbm, out_sem)
     store.start()
-    half = half_ref[0]
+    half = flag_ref[0]
     count = depth // 2
-    step = count // 3
     for ref, which in ((send_ref, 1 - half), (keep_ref, half)):
-        for m in range(3):
-            at = pl.ds(pl.multiple_of(which * count + m * step, 16), step)
-            ref[m * step : (m + 1) * step, :] = dot(g_ref[at, :], pg_ref[...], 1, 0).astype(ref.dtype)
+        for m in range(0, count, 288):
+            step = min(288, count - m)
+            at = pl.ds(pl.multiple_of(which * count + m, 16), step)
+            ref[m : m + step, :] = dot(g_ref[at, :], pg_ref[...], 1, 0).astype(ref.dtype)
         ref[count:, :] = jnp.zeros((ref.shape[0] - count, c_out), ref.dtype)
     store.wait()
 
 
 def backward_kernel(
-    packed, out_hbm, cot_hbm, low_ref, high_ref, w_ref, here_ref, faces_ref,
+    packed, flag_ref, out_hbm, cot_hbm, low_ref, high_ref, w_ref, here_ref, first_ref, second_ref,
     c_ref, acc_ref, pg_ref, out_ref, cot_ref, out_sem, cot_sem,
 ):
     fetch_out = pltpu.make_async_copy(out_hbm, out_ref, out_sem)
@@ -127,8 +142,8 @@
     fetch_out.wait()
     fetch_cot.wait()
     pg_ref[...] = jnp.where(out_ref[...] > 0, cot_ref[...], jnp.zeros((), BF))
-    step = depth // 3
-    for m in range(3):
+    step = depth // 9
+    for m in range(9):
         sl = slice(m * step, (m + 1) * step)
         c_ref[sl, :] = dot(w_ref[sl, :], pg_ref[...], 1, 1).astype(BF)
     center = offsets // 2
@@ -154,14 +169,19 @@
                     here_ref[to, h * per : (h + 1) * per] = acc_ref[at, p * per : (p + 1) * per]
     else:
         here_ref[...] = acc_ref[: here * channels, :]
-    faces_ref[...] = acc_ref[here * channels :, :].astype(BF)
-
-
-def finish_kernel(packed, here_ref, prev_ref, next_ref, pick_ref, out_ref, from_ref):
-    channels, face = prev_ref.shape
+    face = first_ref.shape[1]
+    down, up = acc_ref[here * channels :, :face], acc_ref[here * channels :, face:]
+    odd = flag_ref[1]
+    first_ref[...] = jnp.where(odd == 1, down, up).astype(BF)
+    second_ref[...] = jnp.where(odd == 1, up, down).astype(BF)
+
+
+def finish_kernel(packed, flag_ref, here_ref, first_ref, second_ref, pick_ref, out_ref, from_ref):
+    channels, face = first_ref.shape
     blocks = here_ref.shape[0] // channels
-    from_ref[:, :face] = prev_ref[...]
-    from_ref[:, face:] = next_ref[...]
+    prev, after = sides(flag_ref[1], first_ref, second_ref)
+    from_ref[:, :face] = prev
+    from_ref[:, face:] = after
     part, per = channels // 2, LOW // 2
     for a in range(blocks):
         added = dot(from_ref[...], pick_ref[:, a * LOW : (a + 1) * LOW], 1, 0)
@@ -203,18 +223,25 @@
 
 def send_blocks(features, order, bricks):
     channels, rows = features.shape
+    hbm = pl.BlockSpec(memory_space=pltpu.HBM)
     return pl.pallas_call(
         send_kernel,
         out_shape=jax.ShapeDtypeStruct((bricks, channels, rows // bricks), BF),
-        in_specs=whole(2),
+        in_specs=[hbm, hbm],
         out_specs=whole(1)[0],
-        scratch_shapes=[pltpu.VMEM((channels * rows // LOW, LOW), BF)],
-        compiler_params=pltpu.CompilerParams(vmem_limit_bytes=SMALL_LIMIT),
+        scratch_shapes=[
+            pltpu.VMEM((channels, rows), BF),
+            pltpu.VMEM((1, rows), jnp.int32),
+            pltpu.VMEM((channels * rows // LOW, LOW), BF),
+            pltpu.SemaphoreType.DMA,
+            pltpu.SemaphoreType.DMA,
+        ],
+        compiler_params=pltpu.CompilerParams(vmem_limit_bytes=ALL_LIMIT),
         cost_estimate=pl.CostEstimate(flops=2 * rows * rows * channels, bytes_accessed=1 << 19, transcendentals=0),
     )(features, order)
 
 
-def forward(half, got, prev_upper, next_lower, low, high, w, bias, cot, padded):
+def forward(flags, got, first, second, low, high, w, bias, cot, padded):
     offsets, voxels = low.shape
     depth, c_out = w.shape
     rows = depth // offsets * (voxels // LOW + 1)
@@ -243,10 +270,10 @@
         ],
         compiler_params=pltpu.CompilerParams(vmem_limit_bytes=FULL_LIMIT),
         cost_estimate=pl.CostEstimate(flops=2 * macs, bytes_accessed=5 << 20, transcendentals=0),
-    )(half, got, prev_upper, next_lower, low, high, w, bias, cot)
-
-
-def backward(packed, out, cot, low, high, w):
+    )(flags, got, first, second, low, high, w, bias, cot)
+
+
+def backward(packed, flags, out, cot, low, high, w, face):
     hbm = pl.BlockSpec(memory_space=pltpu.HBM)
     offsets, voxels = low.shape
     depth, c_out = w.shape
@@ -257,10 +284,11 @@
         functools.partial(backward_kernel, packed),
         out_shape=(
             jax.ShapeDtypeStruct((voxels // LOW * channels, LOW), F32),
-            jax.ShapeDtypeStruct((channels, LOW), BF),
+            jax.ShapeDtypeStruct((channels, face), BF),
+            jax.ShapeDtypeStruct((channels, face), BF),
         ),
-        in_specs=[hbm, hbm] + whole(3),
-        out_specs=tuple(whole(2)),
+        in_specs=[pl.BlockSpec(memory_space=pltpu.SMEM), hbm, hbm] + whole(3),
+        out_specs=tuple(whole(3)),
         scratch_shapes=[
             pltpu.VMEM((depth, voxels), BF),
             pltpu.VMEM((rows, LOW), F32),
@@ -272,21 +300,21 @@
         ],
         compiler_params=pltpu.CompilerParams(vmem_limit_bytes=VMEM_LIMIT),
         cost_estimate=pl.CostEstimate(flops=2 * macs, bytes_accessed=3 << 20, transcendentals=0),
-    )(out, cot, low, high, w)
-
-
-def finish(packed, here, from_prev, from_next, pick):
+    )(flags, out, cot, low, high, w)
+
+
+def finish(packed, flags, here, first, second, pick):
     rows, _ = here.shape
-    channels, face = from_prev.shape
+    channels, face = first.shape
     return pl.pallas_call(
         functools.partial(finish_kernel, packed),
         out_shape=jax.ShapeDtypeStruct((rows, LOW), BF),
-        in_specs=whole(4),
+        in_specs=[pl.BlockSpec(memory_space=pltpu.SMEM)] + whole(4),
         out_specs=whole(1)[0],
         scratch_shapes=[pltpu.VMEM((channels, 2 * face), BF)],
         compiler_params=pltpu.CompilerParams(vmem_limit_bytes=SMALL_LIMIT),
         cost_estimate=pl.CostEstimate(flops=4 * rows * LOW * face, bytes_accessed=1 << 20, transcendentals=0),
-    )(here, from_prev, from_next, pick)
+    )(flags, here, first, second, pick)
 
 
 def place(side, keep, came, order, channels):
@@ -369,17 +397,15 @@
     return by_digit(got, digit, radix), brought
 
 
-def meet(array_up, array_down):
+def meet(first, second):
     size = lax.axis_size("brick")
-    odd = lax.axis_index("brick") % 2 == 1
     got = []
-    for start in (0, 1):
+    for start, array in ((0, first), (1, second)):
         pairs = []
         for i in range(start, size - 1, 2):
             pairs += [(i, i + 1), (i + 1, i)]
-        goes_up = ~odd if start == 0 else odd
-        got.append(lax.ppermute(jnp.where(goes_up, array_up, array_down), "brick", pairs))
-    return jnp.where(odd, got[0], got[1]), jnp.where(odd, got[1], got[0])
+        got.append(lax.ppermute(array, "brick", pairs))
+    return got
 
 
 def on_device(features, order, face_list, face_count, kernel_map, weight, bias, cotangent):
@@ -404,24 +430,25 @@
     pick, got = lax.optimization_barrier((pick, got))
     local = got.transpose(1, 0, 2).reshape(channels, rows)
     shown = dot(local, pick, 1, 1).astype(BF)
-    prev_upper, next_lower = meet(shown[:, face:], shown[:, :face])
-
-    half = (flat % 2).astype(jnp.int32)[None]
+    odd = lax.axis_index("brick") % 2
+    down, up = shown[:, :face], shown[:, face:]
+    first, second = meet(jnp.where(odd == 1, down, up), jnp.where(odd == 1, up, down))
+
+    flags = jnp.stack([flat % 2, odd]).astype(jnp.int32)
     low = (kernel_map & (LOW - 1)).astype(F32)
     high = lax.shift_right_logical(kernel_map, SHIFT).astype(F32)
-    tall_bias = jnp.broadcast_to(bias, (8, c_out))
-    output, give, keep = forward(half, got, prev_upper, next_lower, low, high, w, tall_bias, cotangent, padded)
+    output, give, keep = forward(flags, got, first, second, low, high, w, bias[None], cotangent, padded)
     packed = (bricks, count) == (8, 32) and per * 2 == LOW and channels % 16 == 0
     plan = stages(count)[1:]
     total = (keep + swapped(give, count, 1, 2, 1).astype(F32)).astype(BF)
     total = reduce_stage(total, flat, count, *plan[0])
-    here, faces = backward(packed, output, cotangent, low, high, w)
-    total, faces = lax.optimization_barrier((total, faces))
-    from_prev, from_next = meet(faces[:, face:], faces[:, :face])
+    here, first, second = backward(packed, flags, output, cotangent, low, high, w, face)
+    total, first, second = lax.optimization_barrier((total, first, second))
+    first, second = meet(first, second)
     for stride, radix in plan[1:]:
         total = reduce_stage(total, flat, count, stride, radix)
 
-    local_grad = finish(packed, here, from_prev, from_next, pick)
+    local_grad = finish(packed, flags, here, first, second, pick)
     if packed:
         part = channels // 2
         total, local_grad = lax.optimization_barrier((total, local_grad))

time: 95.7 us -> 90 us (0.940)
  local copies, waits for them, and re-layouts: 4 us -> 1.8 us
  waiting for transfers between devices: 24.9 us -> 22.9 us
  other arithmetic: 7.78 us -> 6.75 us
    ppermute x14, waiting for transfers between devices: 19.3 us -> 15.2 us  [swapped(): return lax.ppermute(array, AXES, [(i, partner(i)) for i in range(count)])]
    ppermute x4, starting transfers between devices: 9.64 us -> 5.79 us  [meet(): got.append(lax.ppermute(array, 'brick', pairs))]
    ppermute x14, starting transfers between devices: 15.6 us -> 19.1 us  [swapped(): return lax.ppermute(array, AXES, [(i, partner(i)) for i in range(count)])]
    ppermute x4, waiting for transfers between devices: 1.09 us -> 3.45 us  [meet(): got.append(lax.ppermute(array, 'brick', pairs))]
    unnamed x22 -> x12, local copies, waits for them, and re-layouts: 1.99 us -> 0.38 us
    pallas_call x1, Pallas kernels: 1.06 us -> 2.06 us  [send_blocks(): pl.pallas_call(send_kernel, out_shape=jax.ShapeDtypeStruct((bricks, chann...]
where the time goes in v5:
time: 90 us; the launch traced here: 89.7 us
  starting transfers between devices  32.2 us (36%)
  Pallas kernels  24.7 us (27%)
  waiting for transfers between devices  22.9 us (25%)
  other arithmetic  6.75 us (8%)
  local copies, waits for them, and re-layouts  1.8 us (2%)
  between operations  1.09 us (1%)
    ppermute x14, starting transfers between devices, swapped(): return lax.ppermute(array, AXES, [(i, partner(i)) for i in range(count)])  19.1 us
    ppermute x14, waiting for transfers between devices, swapped(): return lax.ppermute(array, AXES, [(i, partner(i)) for i in range(count)])  15.2 us
    pallas_call x1, Pallas kernels, forward(): pl.pallas_call(forward_kernel, out_shape=(jax.ShapeDtypeStruct((voxels, c...  11.8 us
    pallas_call x1, Pallas kernels, backward(): pl.pallas_call(functools.partial(backward_kernel, packed), out_shape=(jax...  9.02 us
    all_to_all x1, starting transfers between devices, on_device(): got = lax.all_to_all(send, 'brick', split_axis=0, concat_axis=0)  7.27 us
    ppermute x4, starting transfers between devices, meet(): got.append(lax.ppermute(array, 'brick', pairs))  5.79 us
    all_to_all x1, waiting for transfers between devices, on_device(): got = lax.all_to_all(send, 'brick', split_axis=0, concat_axis=0)  4.21 us
    ppermute x4, waiting for transfers between devices, meet(): got.append(lax.ppermute(array, 'brick', pairs))  3.45 us
  transfers between devices with their start and end apart: 19, of which 11 were waited for; matrix products, arithmetic and copies ran while one was open for 4% of the time, Pallas kernels for 12%

profile of v5, /device:TPU:0, one launch (start us, length us, event | category | flops | bytes accessed | tf_op | source)
XLA Modules:
  0.0 89.7 jit_solution(3027690906998024883)
XLA Ops:
  0.7 2.1 %shard_map.103 = bf16[8,96,128]{2,1,0:T(8,128)(2,1)} custom-call(bf16[96,1024]{1,0:T(8,128)(2,1)} %bitcast.94, s32[1,1024]{1,0:T(1,128)} %bitcast.81), custom_call_target="tpu_custom_call" | custom-call | flops 201326592 | bytes 524288 | tf_op jit(solution)/shard_map/pallas_call | solution.py:227
  2.7 7.3 %all-to-all-start = ((bf16[8,96,128]{2,1,0:T(8,128)(2,1)}), bf16[8,96,128]{2,1,0:T(8,128)(2,1)S(1)}, u32[]{:S(2)}, u32[]{:S(2)}) async-start(bf16[8,96,128]{2,1,0:T(8,128)(2,1)} %shard_map.103), calls=%async_computation | async-start | bytes 393216 | tf_op jit(solution)/shard_map/all_to_all | solution.py:425
  10.0 1.3 %fusion.22 = (s32[1]{0:T(128)}, s32[1]{0:T(128)}) fusion(s32[2]{0:T(128)} %param.11), kind=kLoop, calls=%fused_computation.71 | loop fusion | bytes 16 | tf_op jit(solution)/shard_map/slice | solution.py:428
  11.3 0.9 %shift-right-logical_convert_fusion = (f32[27,1024]{1,0:T(8,128)S(1)}, f32[27,1024]{1,0:T(8,128)S(1)}) fusion(s32[27,1024]{1,0:T(8,128)} %param.12), kind=kLoop, calls=%fused_computation.25 | loop fusion | flops 110592 | bytes 331776 | tf_op jit(solution)/shard_map/convert_element_type | solution.py:439
  12.2 1.3 %select_select_fusion.9 = s32[256]{0:T(256)S(1)} fusion(s32[256]{0:T(256)S(1)} %copy-done.5, s32[]{:T(128)} %bitcast.3, s32[]{:T(128)} %bitcast.2), kind=kLoop, calls=%fused_computation.69 | loop fusion | flops 1536 | bytes 2056 | tf_op jit(solution)/shard_map/jit(_where)/select_n | solution.py:429
  13.7 4.2 %all-to-all-done.got_ref = bf16[8,96,128]{2,1,0:T(8,128)(2,1)S(1)} async-done(((bf16[8,96,128]{2,1,0:T(8,128)(2,1)}), bf16[8,96,128]{2,1,0:T(8,128)(2,1)S(1)}, u32[]{:S(2)}, u32[]{:S(2)}) %all-to-all-start) | async-done | bytes 196640 | tf_op jit(solution)/shard_map/all_to_all | solution.py:425
  18.3 0.7 collective-permute-start.1
  18.9 3.1 %collective-permute-start = (bf16[96,128]{1,0:T(8,128)(2,1)S(1)}, bf16[96,128]{1,0:T(8,128)(2,1)S(1)}, u32[]{:S(2)}, u32[]{:S(2)}) collective-permute-start(bf16[96,128]{1,0:T(8,128)(2,1)S(1)} %get-tuple-element.65), channel_id=1, source_target_pairs={{0,4},{4,0},{8,12},{12,8},{16,20},{20,16},{24,28},{28,24},{1,5},{5... | collective-permute-start | bytes 73736 | tf_op jit(solution)/shard_map/ppermute | solution.py:407
  22.1 1.7 %collective-permute-done.even_ref = bf16[96,128]{1,0:T(8,128)(2,1)S(1)} collective-permute-done((bf16[96,128]{1,0:T(8,128)(2,1)S(1)}, bf16[96,128]{1,0:T(8,128)(2,1)S(1)}, u32[]{:S(2)}, u32[]{:S(2)}) %collective-permute-start) | collective-permute-done | bytes 24608 | tf_op jit(solution)/shard_map/ppermute | solution.py:407
  23.8 11.8 %shard_map.104 = (bf16[1024,256]{1,0:T(8,128)(2,1)}, bf16[1408,256]{1,0:T(8,128)(2,1)S(1)}, f32[1408,256]{1,0:T(8,128)}) custom-call(s32[2]{0:T(128)S(1)} %pad_add_fusion.flag_ref, bf16[8,96,128]{2,1,0:T(8,128)(2,1)S(1)} %all-to-all-done.got_ref, bf16[96,128]{1,0:T(8,128)(2,1)S(1)} %collective-permute-done.even_ref, ...), custom_call_target="tpu_custom_call" | custom-call | flops 9512681472 | bytes 5242880 | tf_op jit(solution)/shard_map/pallas_call | solution.py:250
  35.7 2.1 %collective-permute-done.2 = bf16[1408,256]{1,0:T(8,128)(2,1)S(1)} collective-permute-done((bf16[1408,256]{1,0:T(8,128)(2,1)S(1)}, bf16[1408,256]{1,0:T(8,128)(2,1)S(1)}, u32[]{:S(2)}, u32[]{:S(2)}) %collective-permute-start.2) | collective-permute-done | bytes 720928 | tf_op jit(solution)/shard_map/ppermute | solution.py:351
  37.8 1.7 %add_convert_fusion = bf16[1408,256]{1,0:T(8,128)(2,1)S(1)} fusion(f32[1408,256]{1,0:T(8,128)} %get-tuple-element.21, bf16[1408,256]{1,0:T(8,128)(2,1)S(1)} %collective-permute-done.2), kind=kLoop, calls=%fused_computation.1 | loop fusion | flops 1081344 | bytes 2883584 | tf_op jit(solution)/shard_map/convert_element_type | solution.py:443
  39.6 1.6 %collective-permute-start.3 = (bf16[352,256]{1,0:T(8,128)(2,1)S(1)}, bf16[352,256]{1,0:T(8,128)(2,1)S(1)}, u32[]{:S(2)}, u32[]{:S(2)}) collective-permute-start(bf16[352,256]{1,0:T(8,128)(2,1)S(1)} %get-tuple-element.47), channel_id=1, source_target_pairs={{0,2},{1,3},{2,0},{3,1},{4,6},{5,7},{6,4},{7,5},{8,10},{9,11},{10,... | collective-permute-start | bytes 540680 | tf_op jit(solution)/shard_map/ppermute | solution.py:351
  41.2 2.2 %collective-permute-start.5 = (bf16[352,256]{1,0:T(8,128)(2,1)S(1)}, bf16[352,256]{1,0:T(8,128)(2,1)S(1)}, u32[]{:S(2)}, u32[]{:S(2)}) collective-permute-start(bf16[352,256]{1,0:T(8,128)(2,1)S(1)} %get-tuple-element.48), channel_id=1, source_target_pairs={{0,6},{1,7},{2,4},{3,5},{4,2},{5,3},{6,0},{7,1},{8,14},{9,15},{10,... | collective-permute-start | bytes 540680 | tf_op jit(solution)/shard_map/ppermute | solution.py:351
  43.5 9.0 %shard_map.105 = (f32[384,256]{1,0:T(8,128)S(1)}, bf16[96,128]{1,0:T(8,128)(2,1)S(1)}, bf16[96,128]{1,0:T(8,128)(2,1)S(1)}) custom-call(s32[2]{0:T(128)S(1)} %pad_add_fusion.flag_ref, bf16[1024,256]{1,0:T(8,128)(2,1)S(1)} %copy-done.4, bf16[1024,256]{1,0:T(8,128)(2,1)S(1)} %copy-done.1, f32[27,1024]{1,0:T(8,128)S(1)} %get-tuple-element.63.low_ref, ...), custom_call_target="tpu_custom_call" | custom-call | flops 8153726976 | bytes 3145728 | tf_op jit(solution)/shard_map/pallas_call | solution.py:283
  52.7 2.6 %collective-permute-start.6 = (bf16[88,256]{1,0:T(8,128)(2,1)S(1)}, bf16[88,256]{1,0:T(8,128)(2,1)S(1)}, u32[]{:S(2)}, u32[]{:S(2)}) collective-permute-start(bf16[88,256]{1,0:T(8,128)(2,1)S(1)} %get-tuple-element.59), channel_id=1, source_target_pairs={{0,8},{1,9},{2,10},{3,11},{4,12},{5,13},{6,14},{7,15},{8,0},{9,1},... | collective-permute-start | bytes 135176 | tf_op jit(solution)/shard_map/ppermute | solution.py:351
  55.2 1.2 %collective-permute-start.8 = (bf16[88,256]{1,0:T(8,128)(2,1)S(1)}, bf16[88,256]{1,0:T(8,128)(2,1)S(1)}, u32[]{:S(2)}, u32[]{:S(2)}) collective-permute-start(bf16[88,256]{1,0:T(8,128)(2,1)S(1)} %get-tuple-element.60), channel_id=1, source_target_pairs={{0,24},{1,25},{2,26},{3,27},{4,28},{5,29},{6,30},{7,31},{8,16},{9,... | collective-permute-start | bytes 135176 | tf_op jit(solution)/shard_map/ppermute | solution.py:351
  56.8 1.4 %collective-permute-start.9 = (bf16[96,128]{1,0:T(8,128)(2,1)S(1)}, bf16[96,128]{1,0:T(8,128)(2,1)S(1)}, u32[]{:S(2)}, u32[]{:S(2)}) collective-permute-start(bf16[96,128]{1,0:T(8,128)(2,1)S(1)} %get-tuple-element.27), channel_id=1, source_target_pairs={{0,4},{4,0},{8,12},{12,8},{16,20},{20,16},{24,28},{28,24},{1,5},{5... | collective-permute-start | bytes 73736 | tf_op jit(solution)/shard_map/ppermute | solution.py:407
  58.2 0.7 collective-permute-start.10
  58.9 1.7 %collective-permute-done.9.first_ref = bf16[96,128]{1,0:T(8,128)(2,1)S(1)} collective-permute-done((bf16[96,128]{1,0:T(8,128)(2,1)S(1)}, bf16[96,128]{1,0:T(8,128)(2,1)S(1)}, u32[]{:S(2)}, u32[]{:S(2)}) %collective-permute-start.9) | collective-permute-done | bytes 24608 | tf_op jit(solution)/shard_map/ppermute | solution.py:407
  60.6 0.8 shard_map.106
  62.1 4.8 %collective-permute-start.11 = (bf16[184,256]{1,0:T(8,128)(2,1)S(1)}, bf16[184,256]{1,0:T(8,128)(2,1)S(1)}, u32[]{:S(2)}, u32[]{:S(2)}) collective-permute-start(bf16[184,256]{1,0:T(8,128)(2,1)S(1)} %get-tuple-element.66), channel_id=1, source_target_pairs={{0,24},{1,25},{2,26},{3,27},{4,28},{5,29},{6,30},{7,31},{8,16},{9,... | collective-permute-start | bytes 282632 | tf_op jit(solution)/shard_map/ppermute | solution.py:351
  67.0 2.2 %collective-permute-start.12 = (bf16[184,256]{1,0:T(8,128)(2,1)S(1)}, bf16[184,256]{1,0:T(8,128)(2,1)S(1)}, u32[]{:S(2)}, u32[]{:S(2)}) collective-permute-start(bf16[184,256]{1,0:T(8,128)(2,1)S(1)} %get-tuple-element.67), channel_id=1, source_target_pairs={{0,16},{1,17},{2,18},{3,19},{4,20},{5,21},{6,22},{7,23},{8,24},{9,... | collective-permute-start | bytes 282632 | tf_op jit(solution)/shard_map/ppermute | solution.py:351
  69.1 1.5 %collective-permute-done.11 = bf16[184,256]{1,0:T(8,128)(2,1)S(1)} collective-permute-done((bf16[184,256]{1,0:T(8,128)(2,1)S(1)}, bf16[184,256]{1,0:T(8,128)(2,1)S(1)}, u32[]{:S(2)}, u32[]{:S(2)}) %collective-permute-start.11) | collective-permute-done | bytes 94240 | tf_op jit(solution)/shard_map/ppermute | solution.py:351
  70.6 3.5 %collective-permute-done.12 = bf16[184,256]{1,0:T(8,128)(2,1)S(1)} collective-permute-done((bf16[184,256]{1,0:T(8,128)(2,1)S(1)}, bf16[184,256]{1,0:T(8,128)(2,1)S(1)}, u32[]{:S(2)}, u32[]{:S(2)}) %collective-permute-start.12) | collective-permute-done | bytes 94240 | tf_op jit(solution)/shard_map/ppermute | solution.py:351
  74.8 2.5 %collective-permute-start.15 = (bf16[544,256]{1,0:T(8,128)(2,1)S(1)}, bf16[544,256]{1,0:T(8,128)(2,1)S(1)}, u32[]{:S(2)}, u32[]{:S(2)}) collective-permute-start(bf16[544,256]{1,0:T(8,128)(2,1)S(1)} %constant_dynamic-update-slice_fusion), channel_id=1, source_target_pairs={{0,4},{1,5},{2,6},{3,7},{4,0},{5,1},{6,2},{7,3},{8,12},{9,13},{10,... | collective-permute-start | bytes 835592 | tf_op jit(solution)/shard_map/ppermute | solution.py:351
  77.3 1.3 %collective-permute-start.16 = (bf16[352,256]{1,0:T(8,128)(2,1)S(1)}, bf16[352,256]{1,0:T(8,128)(2,1)S(1)}, u32[]{:S(2)}, u32[]{:S(2)}) collective-permute-start(bf16[352,256]{1,0:T(8,128)(2,1)S(1)} %pad_maximum_fusion.2), channel_id=1, source_target_pairs={{0,2},{1,3},{2,0},{3,1},{4,6},{5,7},{6,4},{7,5},{8,10},{9,11},{10,... | collective-permute-start | bytes 540680 | tf_op jit(solution)/shard_map/ppermute | solution.py:351
  78.8 4.1 %collective-permute-done.16 = bf16[352,256]{1,0:T(8,128)(2,1)S(1)} collective-permute-done((bf16[352,256]{1,0:T(8,128)(2,1)S(1)}, bf16[352,256]{1,0:T(8,128)(2,1)S(1)}, u32[]{:S(2)}, u32[]{:S(2)}) %collective-permute-start.16) | collective-permute-done | bytes 180256 | tf_op jit(solution)/shard_map/ppermute | solution.py:351
  82.9 2.3 %collective-permute-done.14 = bf16[352,256]{1,0:T(8,128)(2,1)S(1)} collective-permute-done((bf16[352,256]{1,0:T(8,128)(2,1)S(1)}, bf16[352,256]{1,0:T(8,128)(2,1)S(1)}, u32[]{:S(2)}, u32[]{:S(2)}) %collective-permute-start.14) | collective-permute-done | bytes 180256 | tf_op jit(solution)/shard_map/ppermute | solution.py:351
  86.0 1.1 %shard_map.107 = bf16[96,1024]{1,0:T(8,128)(2,1)} custom-call(s32[1]{0:T(128)} %bitcast.9.side_ref, bf16[192,256]{1,0:T(8,128)(2,1)S(1)} %bitcast.78, bf16[192,256]{1,0:T(8,128)(2,1)S(1)} %slice.77.came_ref, s32[1,1024]{1,0:T(1,128)S(1)} %bitcast.82), custom_call_target="tpu_custom_call" | custom-call | flops 201326592 | bytes 1048576 | tf_op jit(solution)/shard_map/pallas_call | solution.py:322
  87.1 0.7 collective-permute-done.17
  88.0 1.7 %convert_multiply_fusion = f32[2592,256]{1,0:T(8,128)} fusion(bf16[1296,256]{1,0:T(8,128)(2,1)S(1)} %get-tuple-element.42, bf16[1296,256]{1,0:T(8,128)(2,1)S(1)} %get-tuple-element.41), kind=kLoop, calls=%fused_computation | loop fusion | flops 3317760 | bytes 3981312 | tf_op jit(solution)/shard_map/mul | solution.py:483
  (52 shorter events, 3.8 us)
Async XLA Ops:
  0.6 11.6 %copy-start.5 = (s32[256]{0:T(256)S(1)}, s32[256]{0:T(256)}, u32[]{:S(2)}) copy-start(s32[256]{0:T(256)} %param.10) | copy-start | bytes 3076
  0.6 23.2 %copy-start.1 = (bf16[1024,256]{1,0:T(8,128)(2,1)S(1)}, bf16[1024,256]{1,0:T(8,128)(2,1)}, u32[]{:S(2)}) copy-start(bf16[1024,256]{1,0:T(8,128)(2,1)} %cot_hbm.3) | copy-start | bytes 1572868
  0.7 23.2 %copy-start.3 = (f32[256]{0:T(256)S(1)}, f32[256]{0:T(256)}, u32[]{:S(2)}) copy-start(f32[256]{0:T(256)} %param.14) | copy-start | bytes 3076
  2.7 15.2 %all-to-all-start = ((bf16[8,96,128]{2,1,0:T(8,128)(2,1)}), bf16[8,96,128]{2,1,0:T(8,128)(2,1)S(1)}, u32[]{:S(2)}, u32[]{:S(2)}) async-start(bf16[8,96,128]{2,1,0:T(8,128)(2,1)} %shard_map.103), calls=%async_computation | async-start | bytes 393216 | tf_op jit(solution)/shard_map/all_to_all | solution.py:425
  18.3 3.8 %collective-permute-start.1 = (bf16[96,128]{1,0:T(8,128)(2,1)S(1)}, bf16[96,128]{1,0:T(8,128)(2,1)S(1)}, u32[]{:S(2)}, u32[]{:S(2)}) collective-permute-start(bf16[96,128]{1,0:T(8,128)(2,1)S(1)} %get-tuple-element.64), channel_id=1, source_target_pairs={{4,8},{8,4},{12,16},{16,12},{20,24},{24,20},{5,9},{9,5},{13,17},{1... | collective-permute-start | bytes 73736 | tf_op jit(solution)/shard_map/ppermute | solution.py:407
  18.9 4.9 %collective-permute-start = (bf16[96,128]{1,0:T(8,128)(2,1)S(1)}, bf16[96,128]{1,0:T(8,128)(2,1)S(1)}, u32[]{:S(2)}, u32[]{:S(2)}) collective-permute-start(bf16[96,128]{1,0:T(8,128)(2,1)S(1)} %get-tuple-element.65), channel_id=1, source_target_pairs={{0,4},{4,0},{8,12},{12,8},{16,20},{20,16},{24,28},{28,24},{1,5},{5... | collective-permute-start | bytes 73736 | tf_op jit(solution)/shard_map/ppermute | solution.py:407
  35.6 2.3 %collective-permute-start.2 = (bf16[1408,256]{1,0:T(8,128)(2,1)S(1)}, bf16[1408,256]{1,0:T(8,128)(2,1)S(1)}, u32[]{:S(2)}, u32[]{:S(2)}) collective-permute-start(bf16[1408,256]{1,0:T(8,128)(2,1)S(1)} %get-tuple-element.22), channel_id=1, source_target_pairs={{0,1},{1,0},{2,3},{3,2},{4,5},{5,4},{6,7},{7,6},{8,9},{9,8},{10,11... | collective-permute-start | bytes 2162696 | tf_op jit(solution)/shard_map/ppermute | solution.py:351
  37.8 5.6 %copy-start = (bf16[27,96,256]{2,1,0:T(8,128)(2,1)S(1)}, bf16[27,96,256]{2,1,0:T(8,128)(2,1)}, u32[]{:S(2)}) copy-start(bf16[27,96,256]{2,1,0:T(8,128)(2,1)} %param.13) | copy-start | bytes 3981316
  37.8 5.6 %copy-start.4 = (bf16[1024,256]{1,0:T(8,128)(2,1)S(1)}, bf16[1024,256]{1,0:T(8,128)(2,1)}, u32[]{:S(2)}) copy-start(bf16[1024,256]{1,0:T(8,128)(2,1)} %get-tuple-element.15.out_hbm) | copy-start | bytes 1572868
  39.6 12.9 %collective-permute-start.3 = (bf16[352,256]{1,0:T(8,128)(2,1)S(1)}, bf16[352,256]{1,0:T(8,128)(2,1)S(1)}, u32[]{:S(2)}, u32[]{:S(2)}) collective-permute-start(bf16[352,256]{1,0:T(8,128)(2,1)S(1)} %get-tuple-element.47), channel_id=1, source_target_pairs={{0,2},{1,3},{2,0},{3,1},{4,6},{5,7},{6,4},{7,5},{8,10},{9,11},{10,... | collective-permute-start | bytes 540680 | tf_op jit(solution)/shard_map/ppermute | solution.py:351
  41.2 11.3 %collective-permute-start.5 = (bf16[352,256]{1,0:T(8,128)(2,1)S(1)}, bf16[352,256]{1,0:T(8,128)(2,1)S(1)}, u32[]{:S(2)}, u32[]{:S(2)}) collective-permute-start(bf16[352,256]{1,0:T(8,128)(2,1)S(1)} %get-tuple-element.48), channel_id=1, source_target_pairs={{0,6},{1,7},{2,4},{3,5},{4,2},{5,3},{6,0},{7,1},{8,14},{9,15},{10,... | collective-permute-start | bytes 540680 | tf_op jit(solution)/shard_map/ppermute | solution.py:351
  43.4 9.1 %collective-permute-start.4 = (bf16[352,256]{1,0:T(8,128)(2,1)S(1)}, bf16[352,256]{1,0:T(8,128)(2,1)S(1)}, u32[]{:S(2)}, u32[]{:S(2)}) collective-permute-start(bf16[352,256]{1,0:T(8,128)(2,1)S(1)} %get-tuple-element.49), channel_id=1, source_target_pairs={{0,4},{1,5},{2,6},{3,7},{4,0},{5,1},{6,2},{7,3},{8,12},{9,13},{10,... | collective-permute-start | bytes 540680 | tf_op jit(solution)/shard_map/ppermute | solution.py:351
  52.7 8.7 %collective-permute-start.6 = (bf16[88,256]{1,0:T(8,128)(2,1)S(1)}, bf16[88,256]{1,0:T(8,128)(2,1)S(1)}, u32[]{:S(2)}, u32[]{:S(2)}) collective-permute-start(bf16[88,256]{1,0:T(8,128)(2,1)S(1)} %get-tuple-element.59), channel_id=1, source_target_pairs={{0,8},{1,9},{2,10},{3,11},{4,12},{5,13},{6,14},{7,15},{8,0},{9,1},... | collective-permute-start | bytes 135176 | tf_op jit(solution)/shard_map/ppermute | solution.py:351
  55.2 6.2 %collective-permute-start.8 = (bf16[88,256]{1,0:T(8,128)(2,1)S(1)}, bf16[88,256]{1,0:T(8,128)(2,1)S(1)}, u32[]{:S(2)}, u32[]{:S(2)}) collective-permute-start(bf16[88,256]{1,0:T(8,128)(2,1)S(1)} %get-tuple-element.60), channel_id=1, source_target_pairs={{0,24},{1,25},{2,26},{3,27},{4,28},{5,29},{6,30},{7,31},{8,16},{9,... | collective-permute-start | bytes 135176 | tf_op jit(solution)/shard_map/ppermute | solution.py:351
  56.4 5.6 %collective-permute-start.7 = (bf16[88,256]{1,0:T(8,128)(2,1)S(1)}, bf16[88,256]{1,0:T(8,128)(2,1)S(1)}, u32[]{:S(2)}, u32[]{:S(2)}) collective-permute-start(bf16[88,256]{1,0:T(8,128)(2,1)S(1)} %get-tuple-element.61), channel_id=1, source_target_pairs={{0,16},{1,17},{2,18},{3,19},{4,20},{5,21},{6,22},{7,23},{8,24},{9,... | collective-permute-start | bytes 135176 | tf_op jit(solution)/shard_map/ppermute | solution.py:351
  56.8 3.8 %collective-permute-start.9 = (bf16[96,128]{1,0:T(8,128)(2,1)S(1)}, bf16[96,128]{1,0:T(8,128)(2,1)S(1)}, u32[]{:S(2)}, u32[]{:S(2)}) collective-permute-start(bf16[96,128]{1,0:T(8,128)(2,1)S(1)} %get-tuple-element.27), channel_id=1, source_target_pairs={{0,4},{4,0},{8,12},{12,8},{16,20},{20,16},{24,28},{28,24},{1,5},{5... | collective-permute-start | bytes 73736 | tf_op jit(solution)/shard_map/ppermute | solution.py:407
  58.2 2.4 %collective-permute-start.10 = (bf16[96,128]{1,0:T(8,128)(2,1)S(1)}, bf16[96,128]{1,0:T(8,128)(2,1)S(1)}, u32[]{:S(2)}, u32[]{:S(2)}) collective-permute-start(bf16[96,128]{1,0:T(8,128)(2,1)S(1)} %get-tuple-element.28), channel_id=1, source_target_pairs={{4,8},{8,4},{12,16},{16,12},{20,24},{24,20},{5,9},{9,5},{13,17},{1... | collective-permute-start | bytes 73736 | tf_op jit(solution)/shard_map/ppermute | solution.py:407
  62.1 8.4 %collective-permute-start.11 = (bf16[184,256]{1,0:T(8,128)(2,1)S(1)}, bf16[184,256]{1,0:T(8,128)(2,1)S(1)}, u32[]{:S(2)}, u32[]{:S(2)}) collective-permute-start(bf16[184,256]{1,0:T(8,128)(2,1)S(1)} %get-tuple-element.66), channel_id=1, source_target_pairs={{0,24},{1,25},{2,26},{3,27},{4,28},{5,29},{6,30},{7,31},{8,16},{9,... | collective-permute-start | bytes 282632 | tf_op jit(solution)/shard_map/ppermute | solution.py:351
  67.0 7.1 %collective-permute-start.12 = (bf16[184,256]{1,0:T(8,128)(2,1)S(1)}, bf16[184,256]{1,0:T(8,128)(2,1)S(1)}, u32[]{:S(2)}, u32[]{:S(2)}) collective-permute-start(bf16[184,256]{1,0:T(8,128)(2,1)S(1)} %get-tuple-element.67), channel_id=1, source_target_pairs={{0,16},{1,17},{2,18},{3,19},{4,20},{5,21},{6,22},{7,23},{8,24},{9,... | collective-permute-start | bytes 282632 | tf_op jit(solution)/shard_map/ppermute | solution.py:351
  69.1 5.4 %collective-permute-start.13 = (bf16[184,256]{1,0:T(8,128)(2,1)S(1)}, bf16[184,256]{1,0:T(8,128)(2,1)S(1)}, u32[]{:S(2)}, u32[]{:S(2)}) collective-permute-start(bf16[184,256]{1,0:T(8,128)(2,1)S(1)} %get-tuple-element.68), channel_id=1, source_target_pairs={{0,8},{1,9},{2,10},{3,11},{4,12},{5,13},{6,14},{7,15},{8,0},{9,1},... | collective-permute-start | bytes 282632 | tf_op jit(solution)/shard_map/ppermute | solution.py:351
  74.8 10.4 %collective-permute-start.15 = (bf16[544,256]{1,0:T(8,128)(2,1)S(1)}, bf16[544,256]{1,0:T(8,128)(2,1)S(1)}, u32[]{:S(2)}, u32[]{:S(2)}) collective-permute-start(bf16[544,256]{1,0:T(8,128)(2,1)S(1)} %constant_dynamic-update-slice_fusion), channel_id=1, source_target_pairs={{0,4},{1,5},{2,6},{3,7},{4,0},{5,1},{6,2},{7,3},{8,12},{9,13},{10,... | collective-permute-start | bytes 835592 | tf_op jit(solution)/shard_map/ppermute | solution.py:351
  77.3 5.6 %collective-permute-start.16 = (bf16[352,256]{1,0:T(8,128)(2,1)S(1)}, bf16[352,256]{1,0:T(8,128)(2,1)S(1)}, u32[]{:S(2)}, u32[]{:S(2)}) collective-permute-start(bf16[352,256]{1,0:T(8,128)(2,1)S(1)} %pad_maximum_fusion.2), channel_id=1, source_target_pairs={{0,2},{1,3},{2,0},{3,1},{4,6},{5,7},{6,4},{7,5},{8,10},{9,11},{10,... | collective-permute-start | bytes 540680 | tf_op jit(solution)/shard_map/ppermute | solution.py:351
  78.6 6.6 %collective-permute-start.14 = (bf16[352,256]{1,0:T(8,128)(2,1)S(1)}, bf16[352,256]{1,0:T(8,128)(2,1)S(1)}, u32[]{:S(2)}, u32[]{:S(2)}) collective-permute-start(bf16[352,256]{1,0:T(8,128)(2,1)S(1)} %pad_maximum_fusion.2), channel_id=1, source_target_pairs={{0,6},{1,7},{2,4},{3,5},{4,2},{5,3},{6,0},{7,1},{8,14},{9,15},{10,... | collective-permute-start | bytes 540680 | tf_op jit(solution)/shard_map/ppermute | solution.py:351
  85.4 0.7 copy-start.2
  85.6 2.3 %collective-permute-start.17 = (bf16[1408,256]{1,0:T(8,128)(2,1)S(1)}, bf16[1408,256]{1,0:T(8,128)(2,1)S(1)}, u32[]{:S(2)}, u32[]{:S(2)}) collective-permute-start(bf16[1408,256]{1,0:T(8,128)(2,1)S(1)} %pad_maximum_fusion), channel_id=1, source_target_pairs={{0,1},{1,0},{2,3},{3,2},{4,5},{5,4},{6,7},{7,6},{8,9},{9,8},{10,11... | collective-permute-start | bytes 2162696 | tf_op jit(solution)/shard_map/ppermute | solution.py:351

commit v6 on v5

--- a/solution.py
+++ b/solution.py
@@ -66,8 +66,8 @@
 
 
 def forward_kernel(
-    flag_ref, got_ref, even_ref, odd_ref, low_ref, high_ref, w_hbm, bias_ref, cot_hbm, out_hbm, send_ref, keep_ref,
-    g_ref, x_ref, wt_ref, w_ref, cot_ref, out_ref, pg_ref, w_sem, cot_sem, out_sem,
+    flag_ref, got_ref, even_ref, odd_ref, low_ref, high_ref, w_hbm, bias_ref, cot_hbm, out_hbm, send_hbm, keep_hbm,
+    g_ref, x_ref, wt_ref, w_ref, cot_ref, out_ref, pg_ref, send_ref, keep_ref, w_sem, cot_sem, out_sem, grad_sems,
 ):
     fetch_w = pltpu.make_async_copy(w_hbm, w_ref, w_sem)
     fetch_w.start()
@@ -117,30 +117,29 @@
     store.start()
     half = flag_ref[0]
     count = depth // 2
-    for ref, which in ((send_ref, 1 - half), (keep_ref, half)):
+    stores = [store]
+    for ref, to, which in ((send_ref, send_hbm, 1 - half), (keep_ref, keep_hbm, half)):
+        ref[count:, :] = jnp.zeros((ref.shape[0] - count, c_out), ref.dtype)
         for m in range(0, count, 288):
             step = min(288, count - m)
             at = pl.ds(pl.multiple_of(which * count + m, 16), step)
             ref[m : m + step, :] = dot(g_ref[at, :], pg_ref[...], 1, 0).astype(ref.dtype)
-        ref[count:, :] = jnp.zeros((ref.shape[0] - count, c_out), ref.dtype)
-    store.wait()
+            end = ref.shape[0] if m + step == count else m + step
+            store = pltpu.make_async_copy(ref.at[m:end, :], to.at[m:end, :], grad_sems.at[len(stores) - 1])
+            store.start()
+            stores.append(store)
+    for store in stores:
+        store.wait()
 
 
 def backward_kernel(
-    packed, flag_ref, out_hbm, cot_hbm, low_ref, high_ref, w_ref, here_ref, first_ref, second_ref,
-    c_ref, acc_ref, pg_ref, out_ref, cot_ref, out_sem, cot_sem,
+    packed, flag_ref, out_ref, cot_ref, low_ref, high_ref, w_ref, here_ref, first_ref, second_ref, c_ref, acc_ref, pg_ref
 ):
-    fetch_out = pltpu.make_async_copy(out_hbm, out_ref, out_sem)
-    fetch_out.start()
-    fetch_cot = pltpu.make_async_copy(cot_hbm, cot_ref, cot_sem)
-    fetch_cot.start()
     offsets, voxels = low_ref.shape
     depth = w_ref.shape[0]
     channels = depth // offsets
     here = voxels // LOW
     blocks = acc_ref.shape[0] // channels
-    fetch_out.wait()
-    fetch_cot.wait()
     pg_ref[...] = jnp.where(out_ref[...] > 0, cot_ref[...], jnp.zeros((), BF))
     step = depth // 9
     for m in range(9):
@@ -197,17 +196,16 @@
                 out_ref[at, lanes] = (here_ref[at, lanes] + term).astype(BF)
 
 
-def place_kernel(side_ref, keep_ref, came_ref, order_ref, out_ref, back_ref):
+def place_kernel(z_ref, *refs):
+    came_refs, (order_ref, out_ref, back_ref) = refs[:-3], refs[-3:]
     channels, rows = out_ref.shape
     part, per = channels // 2, LOW // 2
-    side = side_ref[0]
-    for z in range(rows // LOW):
-        at = slice(z * part, (z + 1) * part)
+    for d, came_ref in enumerate(came_refs):
+        base = (z_ref[0] ^ d) * LOW
         for p in range(2):
-            block = jnp.where(side == p, keep_ref[at, :].astype(F32), came_ref[at, :].astype(F32)).astype(BF)
-            lanes = slice((2 * z + p) * per, (2 * z + p + 1) * per)
+            lanes = pl.ds(pl.multiple_of(base + p * per, per), per)
             for h in range(2):
-                back_ref[h * part : (h + 1) * part, lanes] = block[:, h * per : (h + 1) * per]
+                back_ref[h * part : (h + 1) * part, lanes] = came_ref[p * part : (p + 1) * part, h * per : (h + 1) * per]
     row = order_ref[...]
     block = jnp.broadcast_to(lax.shift_right_logical(row, SHIFT).astype(F32).astype(BF), (channels, rows))
     back = back_ref[...]
@@ -255,7 +253,7 @@
             jax.ShapeDtypeStruct((padded // 2, c_out), F32),
         ),
         in_specs=[pl.BlockSpec(memory_space=pltpu.SMEM)] + whole(5) + [hbm] + whole(1) + [hbm],
-        out_specs=(hbm,) + tuple(whole(2)),
+        out_specs=(hbm, hbm, hbm),
         scratch_shapes=[
             pltpu.VMEM((depth, voxels), BF),
             pltpu.VMEM((rows, LOW), BF),
@@ -264,9 +262,12 @@
             pltpu.VMEM((voxels, c_out), BF),
             pltpu.VMEM((voxels, c_out), BF),
             pltpu.VMEM((voxels, c_out), BF),
+            pltpu.VMEM((padded // 2, c_out), BF),
+            pltpu.VMEM((padded // 2, c_out), F32),
             pltpu.SemaphoreType.DMA,
             pltpu.SemaphoreType.DMA,
             pltpu.SemaphoreType.DMA,
+            pltpu.SemaphoreType.DMA((2 * pl.cdiv(depth // 2, 288),)),
         ],
         compiler_params=pltpu.CompilerParams(vmem_limit_bytes=FULL_LIMIT),
         cost_estimate=pl.CostEstimate(flops=2 * macs, bytes_accessed=5 << 20, transcendentals=0),
@@ -274,7 +275,6 @@
 
 
 def backward(packed, flags, out, cot, low, high, w, face):
-    hbm = pl.BlockSpec(memory_space=pltpu.HBM)
     offsets, voxels = low.shape
     depth, c_out = w.shape
     channels = depth // offsets
@@ -287,16 +287,12 @@
             jax.ShapeDtypeStruct((channels, face), BF),
             jax.ShapeDtypeStruct((channels, face), BF),
         ),
-        in_specs=[pl.BlockSpec(memory_space=pltpu.SMEM), hbm, hbm] + whole(3),
+        in_specs=[pl.BlockSpec(memory_space=pltpu.SMEM)] + whole(5),
         out_specs=tuple(whole(3)),
         scratch_shapes=[
             pltpu.VMEM((depth, voxels), BF),
             pltpu.VMEM((rows, LOW), F32),
             pltpu.VMEM((voxels, c_out), BF),
-            pltpu.VMEM((voxels, c_out), BF),
-            pltpu.VMEM((voxels, c_out), BF),
-            pltpu.SemaphoreType.DMA,
-            pltpu.SemaphoreType.DMA,
         ],
         compiler_params=pltpu.CompilerParams(vmem_limit_bytes=VMEM_LIMIT),
         cost_estimate=pl.CostEstimate(flops=2 * macs, bytes_accessed=3 << 20, transcendentals=0),
@@ -317,17 +313,17 @@
     )(flags, here, first, second, pick)
 
 
-def place(side, keep, came, order, channels):
+def place(z, came, order, channels):
     rows = order.shape[1]
     return pl.pallas_call(
         place_kernel,
         out_shape=jax.ShapeDtypeStruct((channels, rows), BF),
-        in_specs=[pl.BlockSpec(memory_space=pltpu.SMEM)] + whole(3),
+        in_specs=[pl.BlockSpec(memory_space=pltpu.SMEM)] + whole(len(came) + 1),
         out_specs=whole(1)[0],
         scratch_shapes=[pltpu.VMEM((channels, rows), BF)],
         compiler_params=pltpu.CompilerParams(vmem_limit_bytes=SMALL_LIMIT),
         cost_estimate=pl.CostEstimate(flops=2 * rows * rows * channels, bytes_accessed=1 << 20, transcendentals=0),
-    )(side, keep, came, order)
+    )(z, *came, order)
 
 
 def stages(count):
@@ -382,19 +378,10 @@
     return parts[0] if len(parts) == 1 else jnp.concatenate(parts, 0)
 
 
-def gather_stage(parts, flat, count, stride, radix, cargo=lambda delta: None):
+def gather_stage(x, flat, count, stride, radix):
     digit = flat // stride % radix
-    rows = sum(part.shape[0] for part in parts)
-    got, brought = [], {}
-    for d in range(radix):
-        if radix in (2, 4) and d == 0:
-            got.append(joined(parts))
-            continue
-        extra = cargo(d)
-        piece = swapped(joined(parts if extra is None else parts + [extra]), count, stride, radix, d)
-        got.append(piece[:rows])
-        brought[d] = piece[rows:]
-    return by_digit(got, digit, radix), brought
+    got = [x if radix in (2, 4) and d == 0 else swapped(x, count, stride, radix, d) for d in range(radix)]
+    return by_digit(got, digit, radix)
 
 
 def meet(first, second):
@@ -452,27 +439,29 @@
     if packed:
         part = channels // 2
         total, local_grad = lax.optimization_barrier((total, local_grad))
-        local_grad = local_grad.reshape(bricks // 2, channels, LOW)
         z, x = flat // 8, flat // 4 % 2
-        cargo = lambda d: lax.dynamic_index_in_dim(local_grad, z ^ d, 0, keepdims=False)
-        parts, brought = gather_stage([total], flat, count, 8, 4, cargo)
-        mine = jnp.stack(by_digit([cargo(0)] + [brought[d] for d in (1, 2, 3)], z, 4))
-        mine = mine.reshape(bricks // 2, 2, part, LOW)
-        give = jnp.where(x == 0, mine[:, 1], mine[:, 0]).reshape(-1, LOW)
-        keep = jnp.where(x == 0, mine[:, 0], mine[:, 1]).reshape(-1, LOW)
-        parts, brought = gather_stage(parts, flat, count, 2, 4, lambda d: give if d == 2 else None)
-        came = brought[2]
+        cargo = local_grad.reshape(bricks // 2, 2, part, LOW)
+        keep = jnp.where(x == 0, cargo[:, 0], cargo[:, 1])
+        give = jnp.where(x == 0, cargo[:, 1], cargo[:, 0])
+        came = swapped(give.reshape(-1, LOW), count, 4, 2, 1).reshape(keep.shape)
+        cargo = jnp.stack([jnp.where(x == 0, keep, came), jnp.where(x == 0, came, keep)], 1)
+        cargo = cargo.reshape(bricks // 2, channels, LOW)
+        parts = gather_stage(total, flat, count, 8, 4)
+        total, cargo = lax.optimization_barrier((joined(parts), cargo))
+        came = [lax.dynamic_index_in_dim(cargo, z ^ d, 0, keepdims=False) for d in range(4)]
+        came = came[:1] + [swapped(came[d], count, 8, 4, d) for d in (1, 2, 3)]
+        parts = gather_stage(total, flat, count, 2, 4)
     else:
         blocks = rows // LOW
         send = local_grad.reshape(blocks, channels, LOW // per, per).transpose(0, 2, 1, 3)
         came = lax.all_to_all(send.reshape(bricks, channels, per), "brick", split_axis=0, concat_axis=0)
         parts = [total]
         for stride, radix in reversed(plan):
-            parts, _ = gather_stage(parts, flat, count, stride, radix)
+            parts = gather_stage(joined(parts), flat, count, stride, radix)
     total = joined(parts)
     total, came = lax.optimization_barrier((total, came))
     if packed:
-        grad_in = place(x.astype(jnp.int32)[None], keep, came, order[None], channels).T
+        grad_in = place(z.astype(jnp.int32)[None], came, order[None], channels).T
     else:
         returned = came.transpose(1, 0, 2).reshape(channels, rows)
         grad_in = dot(returned, one_hot_rows(order, rows), 1, 0).astype(BF).T

time: 90 us -> 92.5 us (1.028)
  starting transfers between devices: 32.2 us -> 38.9 us
  waiting for transfers between devices: 22.9 us -> 17.5 us
  Pallas kernels: 24.7 us -> 26.7 us
    ppermute x14 -> x18, starting transfers between devices: 19.1 us -> 25.8 us  [swapped(): return lax.ppermute(array, AXES, [(i, partner(i)) for i in range(count)])]
    ppermute x14 -> x18, waiting for transfers between devices: 15.2 us -> 9.87 us  [swapped(): return lax.ppermute(array, AXES, [(i, partner(i)) for i in range(count)])]
    pallas_call x1, Pallas kernels: 11.8 us -> 14 us  [forward(): pl.pallas_call(forward_kernel, out_shape=(jax.ShapeDtypeStruct((voxels, c...]
  transfers between devices with their start and end apart: 19 -> 23, of which waited for: 11 -> 12; matrix products, arithmetic and copies ran while one was open for 4% -> 4% of each run, Pallas kernels for 12% -> 12%
where the time goes in v6:
time: 92.5 us; the launch traced here: 92.2 us
  starting transfers between devices  38.9 us (42%)
  Pallas kernels  26.7 us (29%)
  waiting for transfers between devices  17.5 us (19%)
  other arithmetic  6.37 us (7%)
  local copies, waits for them, and re-layouts  1.42 us (2%)
  between operations  1.05 us (1%)
    ppermute x18, starting transfers between devices, swapped(): return lax.ppermute(array, AXES, [(i, partner(i)) for i in range(count)])  25.8 us
    pallas_call x1, Pallas kernels, forward(): pl.pallas_call(forward_kernel, out_shape=(jax.ShapeDtypeStruct((voxels, c...  14 us
    ppermute x18, waiting for transfers between devices, swapped(): return lax.ppermute(array, AXES, [(i, partner(i)) for i in range(count)])  9.87 us
    pallas_call x1, Pallas kernels, backward(): pl.pallas_call(functools.partial(backward_kernel, packed), out_shape=(jax...  8.74 us
    all_to_all x1, starting transfers between devices, on_device(): got = lax.all_to_all(send, 'brick', split_axis=0, concat_axis=0)  7.27 us
    ppermute x4, starting transfers between devices, meet(): got.append(lax.ppermute(array, 'brick', pairs))  5.79 us
    all_to_all x1, waiting for transfers between devices, on_device(): got = lax.all_to_all(send, 'brick', split_axis=0, concat_axis=0)  4.21 us
    ppermute x4, waiting for transfers between devices, meet(): got.append(lax.ppermute(array, 'brick', pairs))  3.43 us
  transfers between devices with their start and end apart: 23, of which 12 were waited for; matrix products, arithmetic and copies ran while one was open for 4% of the time, Pallas kernels for 12%

profile of v6, /device:TPU:0, one launch (start us, length us, event | category | flops | bytes accessed | tf_op | source)
XLA Modules:
  0.0 92.2 jit_solution(242015444399374055)
XLA Ops:
  0.7 2.1 %shard_map.103 = bf16[8,96,128]{2,1,0:T(8,128)(2,1)} custom-call(bf16[96,1024]{1,0:T(8,128)(2,1)} %bitcast.67, s32[1,1024]{1,0:T(1,128)} %bitcast.56), custom_call_target="tpu_custom_call" | custom-call | flops 201326592 | bytes 524288 | tf_op jit(solution)/shard_map/pallas_call | solution.py:225
  2.7 7.3 %all-to-all-start = ((bf16[8,96,128]{2,1,0:T(8,128)(2,1)}), bf16[8,96,128]{2,1,0:T(8,128)(2,1)S(1)}, u32[]{:S(2)}, u32[]{:S(2)}) async-start(bf16[8,96,128]{2,1,0:T(8,128)(2,1)} %shard_map.103), calls=%async_computation | async-start | bytes 393216 | tf_op jit(solution)/shard_map/all_to_all | solution.py:412
  10.0 1.3 %fusion.13 = (s32[1]{0:T(128)}, s32[1]{0:T(128)}) fusion(s32[2]{0:T(128)} %param.11), kind=kLoop, calls=%fused_computation.52 | loop fusion | bytes 16 | tf_op jit(solution)/shard_map/slice | solution.py:415
  11.3 0.9 %shift-right-logical_convert_fusion = (f32[27,1024]{1,0:T(8,128)S(1)}, f32[27,1024]{1,0:T(8,128)S(1)}) fusion(s32[27,1024]{1,0:T(8,128)} %param.12), kind=kLoop, calls=%fused_computation.25 | loop fusion | flops 110592 | bytes 331776 | tf_op jit(solution)/shard_map/convert_element_type | solution.py:426
  12.2 1.3 %select_select_fusion.8 = s32[256]{0:T(256)S(1)} fusion(s32[256]{0:T(256)S(1)} %copy-done.5, s32[]{:T(128)} %bitcast.3, s32[]{:T(128)} %bitcast.2), kind=kLoop, calls=%fused_computation.50 | loop fusion | flops 1536 | bytes 2056 | tf_op jit(solution)/shard_map/jit(_where)/select_n | solution.py:416
  13.7 4.2 %all-to-all-done.got_ref = bf16[8,96,128]{2,1,0:T(8,128)(2,1)S(1)} async-done(((bf16[8,96,128]{2,1,0:T(8,128)(2,1)}), bf16[8,96,128]{2,1,0:T(8,128)(2,1)S(1)}, u32[]{:S(2)}, u32[]{:S(2)}) %all-to-all-start) | async-done | bytes 196640 | tf_op jit(solution)/shard_map/all_to_all | solution.py:412
  18.9 3.1 %collective-permute-start = (bf16[96,128]{1,0:T(8,128)(2,1)S(1)}, bf16[96,128]{1,0:T(8,128)(2,1)S(1)}, u32[]{:S(2)}, u32[]{:S(2)}) collective-permute-start(bf16[96,128]{1,0:T(8,128)(2,1)S(1)} %get-tuple-element.68), channel_id=1, source_target_pairs={{0,4},{4,0},{8,12},{12,8},{16,20},{20,16},{24,28},{28,24},{1,5},{5... | collective-permute-start | bytes 73736 | tf_op jit(solution)/shard_map/ppermute | solution.py:394
  22.1 1.7 %collective-permute-done.even_ref = bf16[96,128]{1,0:T(8,128)(2,1)S(1)} collective-permute-done((bf16[96,128]{1,0:T(8,128)(2,1)S(1)}, bf16[96,128]{1,0:T(8,128)(2,1)S(1)}, u32[]{:S(2)}, u32[]{:S(2)}) %collective-permute-start) | collective-permute-done | bytes 24608 | tf_op jit(solution)/shard_map/ppermute | solution.py:394
  23.8 14.0 %shard_map.104 = (bf16[1024,256]{1,0:T(8,128)(2,1)}, bf16[1408,256]{1,0:T(8,128)(2,1)S(1)}, f32[1408,256]{1,0:T(8,128)}) custom-call(s32[2]{0:T(128)S(1)} %pad_add_fusion.flag_ref, bf16[8,96,128]{2,1,0:T(8,128)(2,1)S(1)} %all-to-all-done.got_ref, bf16[96,128]{1,0:T(8,128)(2,1)S(1)} %collective-permute-done.even_ref, ...), custom_call_target="tpu_custom_call" | custom-call | flops 9512681472 | bytes 5242880 | tf_op jit(solution)/shard_map/pallas_call | solution.py:248
  38.0 2.1 %collective-permute-done.2 = bf16[1408,256]{1,0:T(8,128)(2,1)S(1)} collective-permute-done((bf16[1408,256]{1,0:T(8,128)(2,1)S(1)}, bf16[1408,256]{1,0:T(8,128)(2,1)S(1)}, u32[]{:S(2)}, u32[]{:S(2)}) %collective-permute-start.2) | collective-permute-done | bytes 720928 | tf_op jit(solution)/shard_map/ppermute | solution.py:347
  40.1 1.7 %add_convert_fusion = bf16[1408,256]{1,0:T(8,128)(2,1)S(1)} fusion(f32[1408,256]{1,0:T(8,128)} %get-tuple-element.26, bf16[1408,256]{1,0:T(8,128)(2,1)S(1)} %collective-permute-done.2), kind=kLoop, calls=%fused_computation.1 | loop fusion | flops 1081344 | bytes 2883584 | tf_op jit(solution)/shard_map/convert_element_type | solution.py:430
  41.9 1.6 %collective-permute-start.3 = (bf16[352,256]{1,0:T(8,128)(2,1)S(1)}, bf16[352,256]{1,0:T(8,128)(2,1)S(1)}, u32[]{:S(2)}, u32[]{:S(2)}) collective-permute-start(bf16[352,256]{1,0:T(8,128)(2,1)S(1)} %get-tuple-element.49), channel_id=1, source_target_pairs={{0,2},{1,3},{2,0},{3,1},{4,6},{5,7},{6,4},{7,5},{8,10},{9,11},{10,... | collective-permute-start | bytes 540680 | tf_op jit(solution)/shard_map/ppermute | solution.py:347
  43.5 2.2 %collective-permute-start.5 = (bf16[352,256]{1,0:T(8,128)(2,1)S(1)}, bf16[352,256]{1,0:T(8,128)(2,1)S(1)}, u32[]{:S(2)}, u32[]{:S(2)}) collective-permute-start(bf16[352,256]{1,0:T(8,128)(2,1)S(1)} %get-tuple-element.50), channel_id=1, source_target_pairs={{0,6},{1,7},{2,4},{3,5},{4,2},{5,3},{6,0},{7,1},{8,14},{9,15},{10,... | collective-permute-start | bytes 540680 | tf_op jit(solution)/shard_map/ppermute | solution.py:347
  45.8 8.7 %shard_map.105 = (f32[384,256]{1,0:T(8,128)S(1)}, bf16[96,128]{1,0:T(8,128)(2,1)S(1)}, bf16[96,128]{1,0:T(8,128)(2,1)S(1)}) custom-call(s32[2]{0:T(128)S(1)} %pad_add_fusion.flag_ref, bf16[1024,256]{1,0:T(8,128)(2,1)S(1)} %copy-done.4, bf16[1024,256]{1,0:T(8,128)(2,1)S(1)} %copy-done.1, f32[27,1024]{1,0:T(8,128)S(1)} %get-tuple-element.66.low_ref, ...), custom_call_target="tpu_custom_call" | custom-call | flops 8153726976 | bytes 3145728 | tf_op jit(solution)/shard_map/pallas_call | solution.py:283
  54.7 2.6 %collective-permute-start.6 = (bf16[88,256]{1,0:T(8,128)(2,1)S(1)}, bf16[88,256]{1,0:T(8,128)(2,1)S(1)}, u32[]{:S(2)}, u32[]{:S(2)}) collective-permute-start(bf16[88,256]{1,0:T(8,128)(2,1)S(1)} %get-tuple-element.62), channel_id=1, source_target_pairs={{0,8},{1,9},{2,10},{3,11},{4,12},{5,13},{6,14},{7,15},{8,0},{9,1},... | collective-permute-start | bytes 135176 | tf_op jit(solution)/shard_map/ppermute | solution.py:347
  57.2 1.2 %collective-permute-start.8 = (bf16[88,256]{1,0:T(8,128)(2,1)S(1)}, bf16[88,256]{1,0:T(8,128)(2,1)S(1)}, u32[]{:S(2)}, u32[]{:S(2)}) collective-permute-start(bf16[88,256]{1,0:T(8,128)(2,1)S(1)} %get-tuple-element.63), channel_id=1, source_target_pairs={{0,24},{1,25},{2,26},{3,27},{4,28},{5,29},{6,30},{7,31},{8,16},{9,... | collective-permute-start | bytes 135176 | tf_op jit(solution)/shard_map/ppermute | solution.py:347
  58.8 1.4 %collective-permute-start.9 = (bf16[96,128]{1,0:T(8,128)(2,1)S(1)}, bf16[96,128]{1,0:T(8,128)(2,1)S(1)}, u32[]{:S(2)}, u32[]{:S(2)}) collective-permute-start(bf16[96,128]{1,0:T(8,128)(2,1)S(1)} %get-tuple-element.32), channel_id=1, source_target_pairs={{0,4},{4,0},{8,12},{12,8},{16,20},{20,16},{24,28},{28,24},{1,5},{5... | collective-permute-start | bytes 73736 | tf_op jit(solution)/shard_map/ppermute | solution.py:394
  60.9 1.7 %collective-permute-done.9.first_ref = bf16[96,128]{1,0:T(8,128)(2,1)S(1)} collective-permute-done((bf16[96,128]{1,0:T(8,128)(2,1)S(1)}, bf16[96,128]{1,0:T(8,128)(2,1)S(1)}, u32[]{:S(2)}, u32[]{:S(2)}) %collective-permute-start.9) | collective-permute-done | bytes 24608 | tf_op jit(solution)/shard_map/ppermute | solution.py:394
  64.1 5.3 %collective-permute-start.13 = (bf16[88,256]{1,0:T(8,128)(2,1)S(1)}, bf16[88,256]{1,0:T(8,128)(2,1)S(1)}, u32[]{:S(2)}, u32[]{:S(2)}) collective-permute-start(bf16[88,256]{1,0:T(8,128)(2,1)S(1)} %fusion.10), channel_id=1, source_target_pairs={{0,8},{1,9},{2,10},{3,11},{4,12},{5,13},{6,14},{7,15},{8,0},{9,1},... | collective-permute-start | bytes 135176 | tf_op jit(solution)/shard_map/ppermute | solution.py:347
  69.6 2.2 %collective-permute-start.11 = (bf16[88,256]{1,0:T(8,128)(2,1)S(1)}, bf16[88,256]{1,0:T(8,128)(2,1)S(1)}, u32[]{:S(2)}, u32[]{:S(2)}) collective-permute-start(bf16[88,256]{1,0:T(8,128)(2,1)S(1)} %fusion.10), channel_id=1, source_target_pairs={{0,24},{1,25},{2,26},{3,27},{4,28},{5,29},{6,30},{7,31},{8,16},{9,... | collective-permute-start | bytes 135176 | tf_op jit(solution)/shard_map/ppermute | solution.py:347
  71.8 1.9 %collective-permute-start.14 = (bf16[192,256]{1,0:T(8,128)(2,1)S(1)}, bf16[192,256]{1,0:T(8,128)(2,1)S(1)}, u32[]{:S(2)}, u32[]{:S(2)}) collective-permute-start(bf16[192,256]{1,0:T(8,128)(2,1)S(1)} %bitcast.66), channel_id=1, source_target_pairs={{0,4},{1,5},{2,6},{3,7},{4,0},{5,1},{6,2},{7,3},{8,12},{9,13},{10,... | collective-permute-start | bytes 294920 | tf_op jit(solution)/shard_map/ppermute | solution.py:347
  74.3 1.2 %collective-permute-done.11 = bf16[88,256]{1,0:T(8,128)(2,1)S(1)} collective-permute-done((bf16[88,256]{1,0:T(8,128)(2,1)S(1)}, bf16[88,256]{1,0:T(8,128)(2,1)S(1)}, u32[]{:S(2)}, u32[]{:S(2)}) %collective-permute-start.11) | collective-permute-done | bytes 45088 | tf_op jit(solution)/shard_map/ppermute | solution.py:347
  75.5 1.6 %collective-permute-done.14 = bf16[192,256]{1,0:T(8,128)(2,1)S(1)} collective-permute-done((bf16[192,256]{1,0:T(8,128)(2,1)S(1)}, bf16[192,256]{1,0:T(8,128)(2,1)S(1)}, u32[]{:S(2)}, u32[]{:S(2)}) %collective-permute-start.14) | collective-permute-done | bytes 98336 | tf_op jit(solution)/shard_map/ppermute | solution.py:347
  77.2 1.9 %collective-permute-start.17 = (bf16[352,256]{1,0:T(8,128)(2,1)S(1)}, bf16[352,256]{1,0:T(8,128)(2,1)S(1)}, u32[]{:S(2)}, u32[]{:S(2)}) collective-permute-start(bf16[352,256]{1,0:T(8,128)(2,1)S(1)} %pad_maximum_fusion.2), channel_id=1, source_target_pairs={{0,2},{1,3},{2,0},{3,1},{4,6},{5,7},{6,4},{7,5},{8,10},{9,11},{10,... | collective-permute-start | bytes 540680 | tf_op jit(solution)/shard_map/ppermute | solution.py:347
  79.1 1.9 %collective-permute-start.16 = (bf16[352,256]{1,0:T(8,128)(2,1)S(1)}, bf16[352,256]{1,0:T(8,128)(2,1)S(1)}, u32[]{:S(2)}, u32[]{:S(2)}) collective-permute-start(bf16[352,256]{1,0:T(8,128)(2,1)S(1)} %pad_maximum_fusion.2), channel_id=1, source_target_pairs={{0,4},{1,5},{2,6},{3,7},{4,0},{5,1},{6,2},{7,3},{8,12},{9,13},{10,... | collective-permute-start | bytes 540680 | tf_op jit(solution)/shard_map/ppermute | solution.py:347
  81.0 1.5 %collective-permute-start.20 = (bf16[96,256]{1,0:T(8,128)(2,1)S(1)}, bf16[96,256]{1,0:T(8,128)(2,1)S(1)}, u32[]{:S(2)}, u32[]{:S(2)}) collective-permute-start(bf16[96,256]{1,0:T(8,128)(2,1)S(1)} %get-tuple-element.54), channel_id=1, source_target_pairs={{0,24},{1,25},{2,26},{3,27},{4,28},{5,29},{6,30},{7,31},{8,16},{9,... | collective-permute-start | bytes 147464 | tf_op jit(solution)/shard_map/ppermute | solution.py:347
  82.5 1.1 %collective-permute-start.19 = (bf16[96,256]{1,0:T(8,128)(2,1)S(1)}, bf16[96,256]{1,0:T(8,128)(2,1)S(1)}, u32[]{:S(2)}, u32[]{:S(2)}) collective-permute-start(bf16[96,256]{1,0:T(8,128)(2,1)S(1)} %get-tuple-element.55), channel_id=1, source_target_pairs={{0,16},{1,17},{2,18},{3,19},{4,20},{5,21},{6,22},{7,23},{8,24},{9,... | collective-permute-start | bytes 147464 | tf_op jit(solution)/shard_map/ppermute | solution.py:347
  83.6 1.8 %collective-permute-start.18 = (bf16[96,256]{1,0:T(8,128)(2,1)S(1)}, bf16[96,256]{1,0:T(8,128)(2,1)S(1)}, u32[]{:S(2)}, u32[]{:S(2)}) collective-permute-start(bf16[96,256]{1,0:T(8,128)(2,1)S(1)} %get-tuple-element.56), channel_id=1, source_target_pairs={{0,8},{1,9},{2,10},{3,11},{4,12},{5,13},{6,14},{7,15},{8,0},{9,1},... | collective-permute-start | bytes 147464 | tf_op jit(solution)/shard_map/ppermute | solution.py:347
  85.4 1.9 %collective-permute-done.15 = bf16[352,256]{1,0:T(8,128)(2,1)S(1)} collective-permute-done((bf16[352,256]{1,0:T(8,128)(2,1)S(1)}, bf16[352,256]{1,0:T(8,128)(2,1)S(1)}, u32[]{:S(2)}, u32[]{:S(2)}) %collective-permute-start.15) | collective-permute-done | bytes 180256 | tf_op jit(solution)/shard_map/ppermute | solution.py:347
  88.2 1.1 %shard_map.107 = bf16[96,1024]{1,0:T(8,128)(2,1)} custom-call(s32[1]{0:T(128)} %bitcast.9.z_ref, bf16[96,256]{1,0:T(8,128)(2,1)S(1)} %get-tuple-element.38.refs_0_, bf16[96,256]{1,0:T(8,128)(2,1)S(1)} %collective-permute-done.18.refs_1_, bf16[96,256]{1,0:T(8,128)(2,1)S(1)} %collective-permute-done.19.refs_2_, ...), custom_call_target="tpu_custom_call" | custom-call | flops 201326592 | bytes 1048576 | tf_op jit(solution)/shard_map/pallas_call | solution.py:318
  89.3 1.1 %collective-permute-done.21 = bf16[1408,256]{1,0:T(8,128)(2,1)S(1)} collective-permute-done((bf16[1408,256]{1,0:T(8,128)(2,1)S(1)}, bf16[1408,256]{1,0:T(8,128)(2,1)S(1)}, u32[]{:S(2)}, u32[]{:S(2)}) %collective-permute-start.21) | collective-permute-done | bytes 720928 | tf_op jit(solution)/shard_map/ppermute | solution.py:347
  90.5 1.7 %convert_multiply_fusion = f32[2592,256]{1,0:T(8,128)} fusion(bf16[1296,256]{1,0:T(8,128)(2,1)S(1)} %get-tuple-element.44, bf16[1296,256]{1,0:T(8,128)(2,1)S(1)} %get-tuple-element.43), kind=kLoop, calls=%fused_computation | loop fusion | flops 3317760 | bytes 3981312 | tf_op jit(solution)/shard_map/mul | solution.py:472
  (53 shorter events, 5.8 us)
Async XLA Ops:
  0.6 11.6 %copy-start.5 = (s32[256]{0:T(256)S(1)}, s32[256]{0:T(256)}, u32[]{:S(2)}) copy-start(s32[256]{0:T(256)} %param.10) | copy-start | bytes 3076
  0.6 23.2 %copy-start.1 = (bf16[1024,256]{1,0:T(8,128)(2,1)S(1)}, bf16[1024,256]{1,0:T(8,128)(2,1)}, u32[]{:S(2)}) copy-start(bf16[1024,256]{1,0:T(8,128)(2,1)} %cot_ref.1) | copy-start | bytes 1572868
  0.7 23.2 %copy-start.3 = (f32[256]{0:T(256)S(1)}, f32[256]{0:T(256)}, u32[]{:S(2)}) copy-start(f32[256]{0:T(256)} %param.14) | copy-start | bytes 3076
  2.7 15.2 %all-to-all-start = ((bf16[8,96,128]{2,1,0:T(8,128)(2,1)}), bf16[8,96,128]{2,1,0:T(8,128)(2,1)S(1)}, u32[]{:S(2)}, u32[]{:S(2)}) async-start(bf16[8,96,128]{2,1,0:T(8,128)(2,1)} %shard_map.103), calls=%async_computation | async-start | bytes 393216 | tf_op jit(solution)/shard_map/all_to_all | solution.py:412
  18.3 3.8 %collective-permute-start.1 = (bf16[96,128]{1,0:T(8,128)(2,1)S(1)}, bf16[96,128]{1,0:T(8,128)(2,1)S(1)}, u32[]{:S(2)}, u32[]{:S(2)}) collective-permute-start(bf16[96,128]{1,0:T(8,128)(2,1)S(1)} %get-tuple-element.67), channel_id=1, source_target_pairs={{4,8},{8,4},{12,16},{16,12},{20,24},{24,20},{5,9},{9,5},{13,17},{1... | collective-permute-start | bytes 73736 | tf_op jit(solution)/shard_map/ppermute | solution.py:394
  18.9 4.9 %collective-permute-start = (bf16[96,128]{1,0:T(8,128)(2,1)S(1)}, bf16[96,128]{1,0:T(8,128)(2,1)S(1)}, u32[]{:S(2)}, u32[]{:S(2)}) collective-permute-start(bf16[96,128]{1,0:T(8,128)(2,1)S(1)} %get-tuple-element.68), channel_id=1, source_target_pairs={{0,4},{4,0},{8,12},{12,8},{16,20},{20,16},{24,28},{28,24},{1,5},{5... | collective-permute-start | bytes 73736 | tf_op jit(solution)/shard_map/ppermute | solution.py:394
  37.9 2.3 %collective-permute-start.2 = (bf16[1408,256]{1,0:T(8,128)(2,1)S(1)}, bf16[1408,256]{1,0:T(8,128)(2,1)S(1)}, u32[]{:S(2)}, u32[]{:S(2)}) collective-permute-start(bf16[1408,256]{1,0:T(8,128)(2,1)S(1)} %get-tuple-element.27), channel_id=1, source_target_pairs={{0,1},{1,0},{2,3},{3,2},{4,5},{5,4},{6,7},{7,6},{8,9},{9,8},{10,11... | collective-permute-start | bytes 2162696 | tf_op jit(solution)/shard_map/ppermute | solution.py:347
  40.1 5.6 %copy-start = (bf16[27,96,256]{2,1,0:T(8,128)(2,1)S(1)}, bf16[27,96,256]{2,1,0:T(8,128)(2,1)}, u32[]{:S(2)}) copy-start(bf16[27,96,256]{2,1,0:T(8,128)(2,1)} %param.13) | copy-start | bytes 3981316
  40.1 5.6 %copy-start.4 = (bf16[1024,256]{1,0:T(8,128)(2,1)S(1)}, bf16[1024,256]{1,0:T(8,128)(2,1)}, u32[]{:S(2)}) copy-start(bf16[1024,256]{1,0:T(8,128)(2,1)} %get-tuple-element.20.out_ref) | copy-start | bytes 1572868
  41.9 12.6 %collective-permute-start.3 = (bf16[352,256]{1,0:T(8,128)(2,1)S(1)}, bf16[352,256]{1,0:T(8,128)(2,1)S(1)}, u32[]{:S(2)}, u32[]{:S(2)}) collective-permute-start(bf16[352,256]{1,0:T(8,128)(2,1)S(1)} %get-tuple-element.49), channel_id=1, source_target_pairs={{0,2},{1,3},{2,0},{3,1},{4,6},{5,7},{6,4},{7,5},{8,10},{9,11},{10,... | collective-permute-start | bytes 540680 | tf_op jit(solution)/shard_map/ppermute | solution.py:347
  43.5 11.0 %collective-permute-start.5 = (bf16[352,256]{1,0:T(8,128)(2,1)S(1)}, bf16[352,256]{1,0:T(8,128)(2,1)S(1)}, u32[]{:S(2)}, u32[]{:S(2)}) collective-permute-start(bf16[352,256]{1,0:T(8,128)(2,1)S(1)} %get-tuple-element.50), channel_id=1, source_target_pairs={{0,6},{1,7},{2,4},{3,5},{4,2},{5,3},{6,0},{7,1},{8,14},{9,15},{10,... | collective-permute-start | bytes 540680 | tf_op jit(solution)/shard_map/ppermute | solution.py:347
  45.7 8.8 %collective-permute-start.4 = (bf16[352,256]{1,0:T(8,128)(2,1)S(1)}, bf16[352,256]{1,0:T(8,128)(2,1)S(1)}, u32[]{:S(2)}, u32[]{:S(2)}) collective-permute-start(bf16[352,256]{1,0:T(8,128)(2,1)S(1)} %get-tuple-element.51), channel_id=1, source_target_pairs={{0,4},{1,5},{2,6},{3,7},{4,0},{5,1},{6,2},{7,3},{8,12},{9,13},{10,... | collective-permute-start | bytes 540680 | tf_op jit(solution)/shard_map/ppermute | solution.py:347
  54.7 8.7 %collective-permute-start.6 = (bf16[88,256]{1,0:T(8,128)(2,1)S(1)}, bf16[88,256]{1,0:T(8,128)(2,1)S(1)}, u32[]{:S(2)}, u32[]{:S(2)}) collective-permute-start(bf16[88,256]{1,0:T(8,128)(2,1)S(1)} %get-tuple-element.62), channel_id=1, source_target_pairs={{0,8},{1,9},{2,10},{3,11},{4,12},{5,13},{6,14},{7,15},{8,0},{9,1},... | collective-permute-start | bytes 135176 | tf_op jit(solution)/shard_map/ppermute | solution.py:347
  57.2 6.2 %collective-permute-start.8 = (bf16[88,256]{1,0:T(8,128)(2,1)S(1)}, bf16[88,256]{1,0:T(8,128)(2,1)S(1)}, u32[]{:S(2)}, u32[]{:S(2)}) collective-permute-start(bf16[88,256]{1,0:T(8,128)(2,1)S(1)} %get-tuple-element.63), channel_id=1, source_target_pairs={{0,24},{1,25},{2,26},{3,27},{4,28},{5,29},{6,30},{7,31},{8,16},{9,... | collective-permute-start | bytes 135176 | tf_op jit(solution)/shard_map/ppermute | solution.py:347
  58.4 5.6 %collective-permute-start.7 = (bf16[88,256]{1,0:T(8,128)(2,1)S(1)}, bf16[88,256]{1,0:T(8,128)(2,1)S(1)}, u32[]{:S(2)}, u32[]{:S(2)}) collective-permute-start(bf16[88,256]{1,0:T(8,128)(2,1)S(1)} %get-tuple-element.64), channel_id=1, source_target_pairs={{0,16},{1,17},{2,18},{3,19},{4,20},{5,21},{6,22},{7,23},{8,24},{9,... | collective-permute-start | bytes 135176 | tf_op jit(solution)/shard_map/ppermute | solution.py:347
  58.8 3.8 %collective-permute-start.9 = (bf16[96,128]{1,0:T(8,128)(2,1)S(1)}, bf16[96,128]{1,0:T(8,128)(2,1)S(1)}, u32[]{:S(2)}, u32[]{:S(2)}) collective-permute-start(bf16[96,128]{1,0:T(8,128)(2,1)S(1)} %get-tuple-element.32), channel_id=1, source_target_pairs={{0,4},{4,0},{8,12},{12,8},{16,20},{20,16},{24,28},{28,24},{1,5},{5... | collective-permute-start | bytes 73736 | tf_op jit(solution)/shard_map/ppermute | solution.py:394
  60.2 2.4 %collective-permute-start.10 = (bf16[96,128]{1,0:T(8,128)(2,1)S(1)}, bf16[96,128]{1,0:T(8,128)(2,1)S(1)}, u32[]{:S(2)}, u32[]{:S(2)}) collective-permute-start(bf16[96,128]{1,0:T(8,128)(2,1)S(1)} %get-tuple-element.33), channel_id=1, source_target_pairs={{4,8},{8,4},{12,16},{16,12},{20,24},{24,20},{5,9},{9,5},{13,17},{1... | collective-permute-start | bytes 73736 | tf_op jit(solution)/shard_map/ppermute | solution.py:394
  64.1 9.6 %collective-permute-start.13 = (bf16[88,256]{1,0:T(8,128)(2,1)S(1)}, bf16[88,256]{1,0:T(8,128)(2,1)S(1)}, u32[]{:S(2)}, u32[]{:S(2)}) collective-permute-start(bf16[88,256]{1,0:T(8,128)(2,1)S(1)} %fusion.10), channel_id=1, source_target_pairs={{0,8},{1,9},{2,10},{3,11},{4,12},{5,13},{6,14},{7,15},{8,0},{9,1},... | collective-permute-start | bytes 135176 | tf_op jit(solution)/shard_map/ppermute | solution.py:347
  69.3 4.9 %collective-permute-start.12 = (bf16[88,256]{1,0:T(8,128)(2,1)S(1)}, bf16[88,256]{1,0:T(8,128)(2,1)S(1)}, u32[]{:S(2)}, u32[]{:S(2)}) collective-permute-start(bf16[88,256]{1,0:T(8,128)(2,1)S(1)} %fusion.10), channel_id=1, source_target_pairs={{0,16},{1,17},{2,18},{3,19},{4,20},{5,21},{6,22},{7,23},{8,24},{9,... | collective-permute-start | bytes 135176 | tf_op jit(solution)/shard_map/ppermute | solution.py:347
  69.6 5.9 %collective-permute-start.11 = (bf16[88,256]{1,0:T(8,128)(2,1)S(1)}, bf16[88,256]{1,0:T(8,128)(2,1)S(1)}, u32[]{:S(2)}, u32[]{:S(2)}) collective-permute-start(bf16[88,256]{1,0:T(8,128)(2,1)S(1)} %fusion.10), channel_id=1, source_target_pairs={{0,24},{1,25},{2,26},{3,27},{4,28},{5,29},{6,30},{7,31},{8,16},{9,... | collective-permute-start | bytes 135176 | tf_op jit(solution)/shard_map/ppermute | solution.py:347
  71.8 5.4 %collective-permute-start.14 = (bf16[192,256]{1,0:T(8,128)(2,1)S(1)}, bf16[192,256]{1,0:T(8,128)(2,1)S(1)}, u32[]{:S(2)}, u32[]{:S(2)}) collective-permute-start(bf16[192,256]{1,0:T(8,128)(2,1)S(1)} %bitcast.66), channel_id=1, source_target_pairs={{0,4},{1,5},{2,6},{3,7},{4,0},{5,1},{6,2},{7,3},{8,12},{9,13},{10,... | collective-permute-start | bytes 294920 | tf_op jit(solution)/shard_map/ppermute | solution.py:347
  77.2 6.4 %collective-permute-start.17 = (bf16[352,256]{1,0:T(8,128)(2,1)S(1)}, bf16[352,256]{1,0:T(8,128)(2,1)S(1)}, u32[]{:S(2)}, u32[]{:S(2)}) collective-permute-start(bf16[352,256]{1,0:T(8,128)(2,1)S(1)} %pad_maximum_fusion.2), channel_id=1, source_target_pairs={{0,2},{1,3},{2,0},{3,1},{4,6},{5,7},{6,4},{7,5},{8,10},{9,11},{10,... | collective-permute-start | bytes 540680 | tf_op jit(solution)/shard_map/ppermute | solution.py:347
  79.1 6.3 %collective-permute-start.16 = (bf16[352,256]{1,0:T(8,128)(2,1)S(1)}, bf16[352,256]{1,0:T(8,128)(2,1)S(1)}, u32[]{:S(2)}, u32[]{:S(2)}) collective-permute-start(bf16[352,256]{1,0:T(8,128)(2,1)S(1)} %pad_maximum_fusion.2), channel_id=1, source_target_pairs={{0,4},{1,5},{2,6},{3,7},{4,0},{5,1},{6,2},{7,3},{8,12},{9,13},{10,... | collective-permute-start | bytes 540680 | tf_op jit(solution)/shard_map/ppermute | solution.py:347
  80.9 6.4 %collective-permute-start.15 = (bf16[352,256]{1,0:T(8,128)(2,1)S(1)}, bf16[352,256]{1,0:T(8,128)(2,1)S(1)}, u32[]{:S(2)}, u32[]{:S(2)}) collective-permute-start(bf16[352,256]{1,0:T(8,128)(2,1)S(1)} %pad_maximum_fusion.2), channel_id=1, source_target_pairs={{0,6},{1,7},{2,4},{3,5},{4,2},{5,3},{6,0},{7,1},{8,14},{9,15},{10,... | collective-permute-start | bytes 540680 | tf_op jit(solution)/shard_map/ppermute | solution.py:347
  81.0 6.5 %collective-permute-start.20 = (bf16[96,256]{1,0:T(8,128)(2,1)S(1)}, bf16[96,256]{1,0:T(8,128)(2,1)S(1)}, u32[]{:S(2)}, u32[]{:S(2)}) collective-permute-start(bf16[96,256]{1,0:T(8,128)(2,1)S(1)} %get-tuple-element.54), channel_id=1, source_target_pairs={{0,24},{1,25},{2,26},{3,27},{4,28},{5,29},{6,30},{7,31},{8,16},{9,... | collective-permute-start | bytes 147464 | tf_op jit(solution)/shard_map/ppermute | solution.py:347
  82.5 5.6 %collective-permute-start.19 = (bf16[96,256]{1,0:T(8,128)(2,1)S(1)}, bf16[96,256]{1,0:T(8,128)(2,1)S(1)}, u32[]{:S(2)}, u32[]{:S(2)}) collective-permute-start(bf16[96,256]{1,0:T(8,128)(2,1)S(1)} %get-tuple-element.55), channel_id=1, source_target_pairs={{0,16},{1,17},{2,18},{3,19},{4,20},{5,21},{6,22},{7,23},{8,24},{9,... | collective-permute-start | bytes 147464 | tf_op jit(solution)/shard_map/ppermute | solution.py:347
  83.6 4.6 %copy-start.2 = (s32[1024]{0:T(1024)S(1)}, s32[1024]{0:T(1024)}, u32[]{:S(2)}) copy-start(s32[1024]{0:T(1024)} %param.9) | copy-start | bytes 12292
  83.6 4.6 %collective-permute-start.18 = (bf16[96,256]{1,0:T(8,128)(2,1)S(1)}, bf16[96,256]{1,0:T(8,128)(2,1)S(1)}, u32[]{:S(2)}, u32[]{:S(2)}) collective-permute-start(bf16[96,256]{1,0:T(8,128)(2,1)S(1)} %get-tuple-element.56), channel_id=1, source_target_pairs={{0,8},{1,9},{2,10},{3,11},{4,12},{5,13},{6,14},{7,15},{8,0},{9,1},... | collective-permute-start | bytes 147464 | tf_op jit(solution)/shard_map/ppermute | solution.py:347
  88.2 2.2 %collective-permute-start.21 = (bf16[1408,256]{1,0:T(8,128)(2,1)S(1)}, bf16[1408,256]{1,0:T(8,128)(2,1)S(1)}, u32[]{:S(2)}, u32[]{:S(2)}) collective-permute-start(bf16[1408,256]{1,0:T(8,128)(2,1)S(1)} %pad_maximum_fusion), channel_id=1, source_target_pairs={{0,1},{1,0},{2,3},{3,2},{4,5},{5,4},{6,7},{7,6},{8,9},{9,8},{10,11... | collective-permute-start | bytes 2162696 | tf_op jit(solution)/shard_map/ppermute | solution.py:347

commit v7 on v5

--- a/solution.py
+++ b/solution.py
@@ -12,9 +12,9 @@
 F32 = jnp.float32
 LOW = 256
 SHIFT = 8
-VMEM_LIMIT = 20 << 20
+VMEM_LIMIT = 53 << 20
 SMALL_LIMIT = 6 << 20
-FULL_LIMIT = 52 << 20
+FULL_LIMIT = 51 << 20
 ALL_LIMIT = 60 << 20
 AXES = ("brick", "group")
 
@@ -217,6 +217,13 @@
         out_ref[:, a * LOW : (a + 1) * LOW] = placed[a * channels : (a + 1) * channels].astype(BF)
 
 
+def halve_kernel(digit_ref, keep_ref, got_ref, *out_refs):
+    rows = out_refs[0].shape[0]
+    for d, out_ref in enumerate(out_refs):
+        at = pl.ds(pl.multiple_of((digit_ref[0] ^ d) * rows, 16), rows)
+        out_ref[...] = (keep_ref[at, :].astype(F32) + got_ref[at, :].astype(F32)).astype(out_ref.dtype)
+
+
 def whole(count):
     return [pl.BlockSpec(memory_space=pltpu.VMEM)] * count
 
@@ -252,7 +259,7 @@
         out_shape=(
             jax.ShapeDtypeStruct((voxels, c_out), BF),
             jax.ShapeDtypeStruct((padded // 2, c_out), BF),
-            jax.ShapeDtypeStruct((padded // 2, c_out), F32),
+            jax.ShapeDtypeStruct((padded // 2, c_out), BF),
         ),
         in_specs=[pl.BlockSpec(memory_space=pltpu.SMEM)] + whole(5) + [hbm] + whole(1) + [hbm],
         out_specs=(hbm,) + tuple(whole(2)),
@@ -330,6 +337,19 @@
     )(side, keep, came, order)
 
 
+def halve(digit, keep, got, radix):
+    rows, width = keep.shape
+    shapes = [jax.ShapeDtypeStruct((rows // radix, width), F32 if d == 0 else BF) for d in range(radix)]
+    return pl.pallas_call(
+        halve_kernel,
+        out_shape=tuple(shapes),
+        in_specs=[pl.BlockSpec(memory_space=pltpu.SMEM)] + whole(2),
+        out_specs=tuple(whole(radix)),
+        compiler_params=pltpu.CompilerParams(vmem_limit_bytes=SMALL_LIMIT),
+        cost_estimate=pl.CostEstimate(flops=rows * width, bytes_accessed=7 * rows * width, transcendentals=0),
+    )(digit, keep, got)
+
+
 def stages(count):
     plan, stride = [], 1
     while stride < count:
@@ -440,8 +460,17 @@
     output, give, keep = forward(flags, got, first, second, low, high, w, bias[None], cotangent, padded)
     packed = (bricks, count) == (8, 32) and per * 2 == LOW and channels % 16 == 0
     plan = stages(count)[1:]
-    total = (keep + swapped(give, count, 1, 2, 1).astype(F32)).astype(BF)
-    total = reduce_stage(total, flat, count, *plan[0])
+    taken = swapped(give, count, 1, 2, 1)
+    if plan[0][1] == 4 and padded % 128 == 0:
+        stride, radix = plan[0]
+        pieces = halve((flat // stride % radix).astype(jnp.int32)[None], keep, taken, radix)
+        total = pieces[0]
+        for d in range(1, radix):
+            total = total + swapped(pieces[d], count, stride, radix, d).astype(F32)
+        total = total.astype(BF)
+    else:
+        total = (keep.astype(F32) + taken.astype(F32)).astype(BF)
+        total = reduce_stage(total, flat, count, *plan[0])
     here, first, second = backward(packed, flags, output, cotangent, low, high, w, face)
     total, first, second = lax.optimization_barrier((total, first, second))
     first, second = meet(first, second)

time: 90 us -> 89.2 us (level)
  other arithmetic: 6.75 us -> 5.02 us
  Pallas kernels: 24.7 us -> 25.7 us
    pallas_call x1, Pallas kernels: 9.02 us -> 10.9 us  [backward(): pl.pallas_call(functools.partial(backward_kernel, packed), out_shape=(jax...]
    convert_element_type x1, other arithmetic: 1.71 us -> 0.08 us  [on_device(): total = total.astype(BF)]
    pallas_call x1, Pallas kernels: 11.8 us -> 10.7 us  [forward(): pl.pallas_call(forward_kernel, out_shape=(jax.ShapeDtypeStruct((voxels, c...]
  transfers between devices with their start and end apart: 19 -> 19, of which waited for: 11 -> 11; matrix products, arithmetic and copies ran while one was open for 4% -> 4% of each run, Pallas kernels for 12% -> 14%
where the time goes in v7:
time: 89.2 us; the launch traced here: 88.9 us
  starting transfers between devices  32.2 us (36%)
  Pallas kernels  25.7 us (29%)
  waiting for transfers between devices  22.9 us (26%)
  other arithmetic  5.02 us (6%)
  local copies, waits for them, and re-layouts  1.75 us (2%)
  between operations  1.06 us (1%)
    ppermute x14, starting transfers between devices, swapped(): return lax.ppermute(array, AXES, [(i, partner(i)) for i in range(count)])  19.1 us
    ppermute x14, waiting for transfers between devices, swapped(): return lax.ppermute(array, AXES, [(i, partner(i)) for i in range(count)])  15.2 us
    pallas_call x1, Pallas kernels, backward(): pl.pallas_call(functools.partial(backward_kernel, packed), out_shape=(jax...  10.9 us
    pallas_call x1, Pallas kernels, forward(): pl.pallas_call(forward_kernel, out_shape=(jax.ShapeDtypeStruct((voxels, c...  10.7 us
    all_to_all x1, starting transfers between devices, on_device(): got = lax.all_to_all(send, 'brick', split_axis=0, concat_axis=0)  7.26 us
    ppermute x4, starting transfers between devices, meet(): got.append(lax.ppermute(array, 'brick', pairs))  5.8 us
    all_to_all x1, waiting for transfers between devices, on_device(): got = lax.all_to_all(send, 'brick', split_axis=0, concat_axis=0)  4.21 us
    ppermute x4, waiting for transfers between devices, meet(): got.append(lax.ppermute(array, 'brick', pairs))  3.45 us
  transfers between devices with their start and end apart: 19, of which 11 were waited for; matrix products, arithmetic and copies ran while one was open for 4% of the time, Pallas kernels for 14%

profile of v7, /device:TPU:0, one launch (start us, length us, event | category | flops | bytes accessed | tf_op | source)
XLA Modules:
  0.0 88.9 jit_solution(16208477482048580874)
XLA Ops:
  0.7 2.1 %shard_map.103 = bf16[8,96,128]{2,1,0:T(8,128)(2,1)} custom-call(bf16[96,1024]{1,0:T(8,128)(2,1)} %bitcast.83, s32[1,1024]{1,0:T(1,128)} %bitcast.70), custom_call_target="tpu_custom_call" | custom-call | flops 201326592 | bytes 524288 | tf_op jit(solution)/shard_map/pallas_call | solution.py:234
  2.7 7.3 %all-to-all-start = ((bf16[8,96,128]{2,1,0:T(8,128)(2,1)}), bf16[8,96,128]{2,1,0:T(8,128)(2,1)S(1)}, u32[]{:S(2)}, u32[]{:S(2)}) async-start(bf16[8,96,128]{2,1,0:T(8,128)(2,1)} %shard_map.103), calls=%async_computation | async-start | bytes 393216 | tf_op jit(solution)/shard_map/all_to_all | solution.py:445
  10.0 1.3 %fusion.19 = (s32[1]{0:T(128)}, s32[1]{0:T(128)}) fusion(s32[2]{0:T(128)} %param.11), kind=kLoop, calls=%fused_computation.64 | loop fusion | bytes 16 | tf_op jit(solution)/shard_map/slice | solution.py:448
  11.3 0.9 %shift-right-logical_convert_fusion = (f32[27,1024]{1,0:T(8,128)S(1)}, f32[27,1024]{1,0:T(8,128)S(1)}) fusion(s32[27,1024]{1,0:T(8,128)} %param.12), kind=kLoop, calls=%fused_computation.18 | loop fusion | flops 110592 | bytes 331776 | tf_op jit(solution)/shard_map/convert_element_type | solution.py:459
  12.2 1.3 %select_select_fusion.9 = s32[256]{0:T(256)S(1)} fusion(s32[256]{0:T(256)S(1)} %copy-done.3, s32[]{:T(128)} %bitcast.3, s32[]{:T(128)} %bitcast.2), kind=kLoop, calls=%fused_computation.62 | loop fusion | flops 1536 | bytes 2056 | tf_op jit(solution)/shard_map/jit(_where)/select_n | solution.py:449
  13.7 4.2 %all-to-all-done.got_ref = bf16[8,96,128]{2,1,0:T(8,128)(2,1)S(1)} async-done(((bf16[8,96,128]{2,1,0:T(8,128)(2,1)}), bf16[8,96,128]{2,1,0:T(8,128)(2,1)S(1)}, u32[]{:S(2)}, u32[]{:S(2)}) %all-to-all-start) | async-done | bytes 196640 | tf_op jit(solution)/shard_map/all_to_all | solution.py:445
  18.3 0.7 collective-permute-start.1
  18.9 3.1 %collective-permute-start = (bf16[96,128]{1,0:T(8,128)(2,1)S(1)}, bf16[96,128]{1,0:T(8,128)(2,1)S(1)}, u32[]{:S(2)}, u32[]{:S(2)}) collective-permute-start(bf16[96,128]{1,0:T(8,128)(2,1)S(1)} %get-tuple-element.70), channel_id=1, source_target_pairs={{0,4},{4,0},{8,12},{12,8},{16,20},{20,16},{24,28},{28,24},{1,5},{5... | collective-permute-start | bytes 73736 | tf_op jit(solution)/shard_map/ppermute | solution.py:427
  22.1 1.7 %collective-permute-done.even_ref = bf16[96,128]{1,0:T(8,128)(2,1)S(1)} collective-permute-done((bf16[96,128]{1,0:T(8,128)(2,1)S(1)}, bf16[96,128]{1,0:T(8,128)(2,1)S(1)}, u32[]{:S(2)}, u32[]{:S(2)}) %collective-permute-start) | collective-permute-done | bytes 24608 | tf_op jit(solution)/shard_map/ppermute | solution.py:427
  23.8 10.7 %shard_map.104 = (bf16[1024,256]{1,0:T(8,128)(2,1)}, bf16[1408,256]{1,0:T(8,128)(2,1)S(1)}, bf16[1408,256]{1,0:T(8,128)(2,1)S(1)}) custom-call(s32[2]{0:T(128)S(1)} %pad_add_fusion.flag_ref, bf16[8,96,128]{2,1,0:T(8,128)(2,1)S(1)} %all-to-all-done.got_ref, bf16[96,128]{1,0:T(8,128)(2,1)S(1)} %collective-permute-done.even_ref, ...), custom_call_target="tpu_custom_call" | custom-call | flops 9512681472 | bytes 5242880 | tf_op jit(solution)/shard_map/pallas_call | solution.py:257
  34.6 2.1 %collective-permute-done.2.got_ref = bf16[1408,256]{1,0:T(8,128)(2,1)S(1)} collective-permute-done((bf16[1408,256]{1,0:T(8,128)(2,1)S(1)}, bf16[1408,256]{1,0:T(8,128)(2,1)S(1)}, u32[]{:S(2)}, u32[]{:S(2)}) %collective-permute-start.2) | collective-permute-done | bytes 720928 | tf_op jit(solution)/shard_map/ppermute | solution.py:371
  36.9 1.6 %collective-permute-start.3 = (bf16[352,256]{1,0:T(8,128)(2,1)S(1)}, bf16[352,256]{1,0:T(8,128)(2,1)S(1)}, u32[]{:S(2)}, u32[]{:S(2)}) collective-permute-start(bf16[352,256]{1,0:T(8,128)(2,1)S(1)} %get-tuple-element.28), channel_id=1, source_target_pairs={{0,2},{1,3},{2,0},{3,1},{4,6},{5,7},{6,4},{7,5},{8,10},{9,11},{10,... | collective-permute-start | bytes 540680 | tf_op jit(solution)/shard_map/ppermute | solution.py:371
  38.5 2.3 %collective-permute-start.4 = (bf16[352,256]{1,0:T(8,128)(2,1)S(1)}, bf16[352,256]{1,0:T(8,128)(2,1)S(1)}, u32[]{:S(2)}, u32[]{:S(2)}) collective-permute-start(bf16[352,256]{1,0:T(8,128)(2,1)S(1)} %get-tuple-element.29), channel_id=1, source_target_pairs={{0,4},{1,5},{2,6},{3,7},{4,0},{5,1},{6,2},{7,3},{8,12},{9,13},{10,... | collective-permute-start | bytes 540680 | tf_op jit(solution)/shard_map/ppermute | solution.py:371
  40.8 10.9 %shard_map.106 = (f32[384,256]{1,0:T(8,128)S(1)}, bf16[96,128]{1,0:T(8,128)(2,1)S(1)}, bf16[96,128]{1,0:T(8,128)(2,1)S(1)}) custom-call(s32[2]{0:T(128)S(1)} %pad_add_fusion.flag_ref, bf16[1024,256]{1,0:T(8,128)(2,1)} %get-tuple-element.19.out_hbm, bf16[1024,256]{1,0:T(8,128)(2,1)} %cot_hbm.3, f32[27,1024]{1,0:T(8,128)S(1)} %get-tuple-element.68.low_ref, ...), custom_call_target="tpu_custom_call" | custom-call | flops 8153726976 | bytes 3145728 | tf_op jit(solution)/shard_map/pallas_call | solution.py:290
  51.9 2.5 %collective-permute-start.6 = (bf16[88,256]{1,0:T(8,128)(2,1)S(1)}, bf16[88,256]{1,0:T(8,128)(2,1)S(1)}, u32[]{:S(2)}, u32[]{:S(2)}) collective-permute-start(bf16[88,256]{1,0:T(8,128)(2,1)S(1)} %get-tuple-element.64), channel_id=1, source_target_pairs={{0,8},{1,9},{2,10},{3,11},{4,12},{5,13},{6,14},{7,15},{8,0},{9,1},... | collective-permute-start | bytes 135176 | tf_op jit(solution)/shard_map/ppermute | solution.py:371
  54.4 1.2 %collective-permute-start.8 = (bf16[88,256]{1,0:T(8,128)(2,1)S(1)}, bf16[88,256]{1,0:T(8,128)(2,1)S(1)}, u32[]{:S(2)}, u32[]{:S(2)}) collective-permute-start(bf16[88,256]{1,0:T(8,128)(2,1)S(1)} %get-tuple-element.65), channel_id=1, source_target_pairs={{0,24},{1,25},{2,26},{3,27},{4,28},{5,29},{6,30},{7,31},{8,16},{9,... | collective-permute-start | bytes 135176 | tf_op jit(solution)/shard_map/ppermute | solution.py:371
  55.9 1.4 %collective-permute-start.9 = (bf16[96,128]{1,0:T(8,128)(2,1)S(1)}, bf16[96,128]{1,0:T(8,128)(2,1)S(1)}, u32[]{:S(2)}, u32[]{:S(2)}) collective-permute-start(bf16[96,128]{1,0:T(8,128)(2,1)S(1)} %get-tuple-element.35), channel_id=1, source_target_pairs={{0,4},{4,0},{8,12},{12,8},{16,20},{20,16},{24,28},{28,24},{1,5},{5... | collective-permute-start | bytes 73736 | tf_op jit(solution)/shard_map/ppermute | solution.py:427
  57.4 0.7 collective-permute-start.10
  58.1 1.7 %collective-permute-done.9.first_ref = bf16[96,128]{1,0:T(8,128)(2,1)S(1)} collective-permute-done((bf16[96,128]{1,0:T(8,128)(2,1)S(1)}, bf16[96,128]{1,0:T(8,128)(2,1)S(1)}, u32[]{:S(2)}, u32[]{:S(2)}) %collective-permute-start.9) | collective-permute-done | bytes 24608 | tf_op jit(solution)/shard_map/ppermute | solution.py:427
  59.8 0.8 shard_map.107
  60.6 0.6 collective-permute-done.7
  61.3 4.8 %collective-permute-start.11 = (bf16[184,256]{1,0:T(8,128)(2,1)S(1)}, bf16[184,256]{1,0:T(8,128)(2,1)S(1)}, u32[]{:S(2)}, u32[]{:S(2)}) collective-permute-start(bf16[184,256]{1,0:T(8,128)(2,1)S(1)} %get-tuple-element.71), channel_id=1, source_target_pairs={{0,24},{1,25},{2,26},{3,27},{4,28},{5,29},{6,30},{7,31},{8,16},{9,... | collective-permute-start | bytes 282632 | tf_op jit(solution)/shard_map/ppermute | solution.py:371
  66.1 2.1 %collective-permute-start.12 = (bf16[184,256]{1,0:T(8,128)(2,1)S(1)}, bf16[184,256]{1,0:T(8,128)(2,1)S(1)}, u32[]{:S(2)}, u32[]{:S(2)}) collective-permute-start(bf16[184,256]{1,0:T(8,128)(2,1)S(1)} %get-tuple-element.72), channel_id=1, source_target_pairs={{0,16},{1,17},{2,18},{3,19},{4,20},{5,21},{6,22},{7,23},{8,24},{9,... | collective-permute-start | bytes 282632 | tf_op jit(solution)/shard_map/ppermute | solution.py:371
  68.3 1.5 %collective-permute-done.11 = bf16[184,256]{1,0:T(8,128)(2,1)S(1)} collective-permute-done((bf16[184,256]{1,0:T(8,128)(2,1)S(1)}, bf16[184,256]{1,0:T(8,128)(2,1)S(1)}, u32[]{:S(2)}, u32[]{:S(2)}) %collective-permute-start.11) | collective-permute-done | bytes 94240 | tf_op jit(solution)/shard_map/ppermute | solution.py:371
  69.8 3.5 %collective-permute-done.12 = bf16[184,256]{1,0:T(8,128)(2,1)S(1)} collective-permute-done((bf16[184,256]{1,0:T(8,128)(2,1)S(1)}, bf16[184,256]{1,0:T(8,128)(2,1)S(1)}, u32[]{:S(2)}, u32[]{:S(2)}) %collective-permute-start.12) | collective-permute-done | bytes 94240 | tf_op jit(solution)/shard_map/ppermute | solution.py:371
  73.9 2.5 %collective-permute-start.15 = (bf16[544,256]{1,0:T(8,128)(2,1)S(1)}, bf16[544,256]{1,0:T(8,128)(2,1)S(1)}, u32[]{:S(2)}, u32[]{:S(2)}) collective-permute-start(bf16[544,256]{1,0:T(8,128)(2,1)S(1)} %constant_dynamic-update-slice_fusion), channel_id=1, source_target_pairs={{0,4},{1,5},{2,6},{3,7},{4,0},{5,1},{6,2},{7,3},{8,12},{9,13},{10,... | collective-permute-start | bytes 835592 | tf_op jit(solution)/shard_map/ppermute | solution.py:371
  76.5 1.3 %collective-permute-start.16 = (bf16[352,256]{1,0:T(8,128)(2,1)S(1)}, bf16[352,256]{1,0:T(8,128)(2,1)S(1)}, u32[]{:S(2)}, u32[]{:S(2)}) collective-permute-start(bf16[352,256]{1,0:T(8,128)(2,1)S(1)} %pad_maximum_fusion.2), channel_id=1, source_target_pairs={{0,2},{1,3},{2,0},{3,1},{4,6},{5,7},{6,4},{7,5},{8,10},{9,11},{10,... | collective-permute-start | bytes 540680 | tf_op jit(solution)/shard_map/ppermute | solution.py:371
  78.0 4.0 %collective-permute-done.16 = bf16[352,256]{1,0:T(8,128)(2,1)S(1)} collective-permute-done((bf16[352,256]{1,0:T(8,128)(2,1)S(1)}, bf16[352,256]{1,0:T(8,128)(2,1)S(1)}, u32[]{:S(2)}, u32[]{:S(2)}) %collective-permute-start.16) | collective-permute-done | bytes 180256 | tf_op jit(solution)/shard_map/ppermute | solution.py:371
  82.0 2.3 %collective-permute-done.14 = bf16[352,256]{1,0:T(8,128)(2,1)S(1)} collective-permute-done((bf16[352,256]{1,0:T(8,128)(2,1)S(1)}, bf16[352,256]{1,0:T(8,128)(2,1)S(1)}, u32[]{:S(2)}, u32[]{:S(2)}) %collective-permute-start.14) | collective-permute-done | bytes 180256 | tf_op jit(solution)/shard_map/ppermute | solution.py:371
  85.2 1.1 %shard_map.108 = bf16[96,1024]{1,0:T(8,128)(2,1)} custom-call(s32[1]{0:T(128)} %bitcast.9.side_ref, bf16[192,256]{1,0:T(8,128)(2,1)S(1)} %bitcast.69, bf16[192,256]{1,0:T(8,128)(2,1)S(1)} %slice.77.came_ref, s32[1,1024]{1,0:T(1,128)S(1)} %bitcast.71), custom_call_target="tpu_custom_call" | custom-call | flops 201326592 | bytes 1048576 | tf_op jit(solution)/shard_map/pallas_call | solution.py:329
  86.3 0.7 collective-permute-done.17
  87.1 1.7 %convert_multiply_fusion = f32[2592,256]{1,0:T(8,128)} fusion(bf16[1296,256]{1,0:T(8,128)(2,1)S(1)} %get-tuple-element.50, bf16[1296,256]{1,0:T(8,128)(2,1)S(1)} %get-tuple-element.49), kind=kLoop, calls=%fused_computation | loop fusion | flops 3317760 | bytes 3981312 | tf_op jit(solution)/shard_map/mul | solution.py:512
  (47 shorter events, 3.1 us)
Async XLA Ops:
  0.6 11.6 %copy-start.3 = (s32[256]{0:T(256)S(1)}, s32[256]{0:T(256)}, u32[]{:S(2)}) copy-start(s32[256]{0:T(256)} %param.10) | copy-start | bytes 3076
  0.6 23.2 %copy-start = (bf16[1024,256]{1,0:T(8,128)(2,1)S(1)}, bf16[1024,256]{1,0:T(8,128)(2,1)}, u32[]{:S(2)}) copy-start(bf16[1024,256]{1,0:T(8,128)(2,1)} %cot_hbm.3) | copy-start | bytes 1572868
  0.7 23.2 %copy-start.2 = (f32[256]{0:T(256)S(1)}, f32[256]{0:T(256)}, u32[]{:S(2)}) copy-start(f32[256]{0:T(256)} %param.14) | copy-start | bytes 3076
  2.7 15.2 %all-to-all-start = ((bf16[8,96,128]{2,1,0:T(8,128)(2,1)}), bf16[8,96,128]{2,1,0:T(8,128)(2,1)S(1)}, u32[]{:S(2)}, u32[]{:S(2)}) async-start(bf16[8,96,128]{2,1,0:T(8,128)(2,1)} %shard_map.103), calls=%async_computation | async-start | bytes 393216 | tf_op jit(solution)/shard_map/all_to_all | solution.py:445
  18.3 3.8 %collective-permute-start.1 = (bf16[96,128]{1,0:T(8,128)(2,1)S(1)}, bf16[96,128]{1,0:T(8,128)(2,1)S(1)}, u32[]{:S(2)}, u32[]{:S(2)}) collective-permute-start(bf16[96,128]{1,0:T(8,128)(2,1)S(1)} %get-tuple-element.69), channel_id=1, source_target_pairs={{4,8},{8,4},{12,16},{16,12},{20,24},{24,20},{5,9},{9,5},{13,17},{1... | collective-permute-start | bytes 73736 | tf_op jit(solution)/shard_map/ppermute | solution.py:427
  18.9 4.9 %collective-permute-start = (bf16[96,128]{1,0:T(8,128)(2,1)S(1)}, bf16[96,128]{1,0:T(8,128)(2,1)S(1)}, u32[]{:S(2)}, u32[]{:S(2)}) collective-permute-start(bf16[96,128]{1,0:T(8,128)(2,1)S(1)} %get-tuple-element.70), channel_id=1, source_target_pairs={{0,4},{4,0},{8,12},{12,8},{16,20},{20,16},{24,28},{28,24},{1,5},{5... | collective-permute-start | bytes 73736 | tf_op jit(solution)/shard_map/ppermute | solution.py:427
  34.5 2.3 %collective-permute-start.2 = (bf16[1408,256]{1,0:T(8,128)(2,1)S(1)}, bf16[1408,256]{1,0:T(8,128)(2,1)S(1)}, u32[]{:S(2)}, u32[]{:S(2)}) collective-permute-start(bf16[1408,256]{1,0:T(8,128)(2,1)S(1)} %get-tuple-element.26), channel_id=1, source_target_pairs={{0,1},{1,0},{2,3},{3,2},{4,5},{5,4},{6,7},{7,6},{8,9},{9,8},{10,11... | collective-permute-start | bytes 2162696 | tf_op jit(solution)/shard_map/ppermute | solution.py:371
  36.9 14.8 %collective-permute-start.3 = (bf16[352,256]{1,0:T(8,128)(2,1)S(1)}, bf16[352,256]{1,0:T(8,128)(2,1)S(1)}, u32[]{:S(2)}, u32[]{:S(2)}) collective-permute-start(bf16[352,256]{1,0:T(8,128)(2,1)S(1)} %get-tuple-element.28), channel_id=1, source_target_pairs={{0,2},{1,3},{2,0},{3,1},{4,6},{5,7},{6,4},{7,5},{8,10},{9,11},{10,... | collective-permute-start | bytes 540680 | tf_op jit(solution)/shard_map/ppermute | solution.py:371
  38.5 13.2 %collective-permute-start.4 = (bf16[352,256]{1,0:T(8,128)(2,1)S(1)}, bf16[352,256]{1,0:T(8,128)(2,1)S(1)}, u32[]{:S(2)}, u32[]{:S(2)}) collective-permute-start(bf16[352,256]{1,0:T(8,128)(2,1)S(1)} %get-tuple-element.29), channel_id=1, source_target_pairs={{0,4},{1,5},{2,6},{3,7},{4,0},{5,1},{6,2},{7,3},{8,12},{9,13},{10,... | collective-permute-start | bytes 540680 | tf_op jit(solution)/shard_map/ppermute | solution.py:371
  40.8 11.0 %collective-permute-start.5 = (bf16[352,256]{1,0:T(8,128)(2,1)S(1)}, bf16[352,256]{1,0:T(8,128)(2,1)S(1)}, u32[]{:S(2)}, u32[]{:S(2)}) collective-permute-start(bf16[352,256]{1,0:T(8,128)(2,1)S(1)} %get-tuple-element.30), channel_id=1, source_target_pairs={{0,6},{1,7},{2,4},{3,5},{4,2},{5,3},{6,0},{7,1},{8,14},{9,15},{10,... | collective-permute-start | bytes 540680 | tf_op jit(solution)/shard_map/ppermute | solution.py:371
  51.9 8.7 %collective-permute-start.6 = (bf16[88,256]{1,0:T(8,128)(2,1)S(1)}, bf16[88,256]{1,0:T(8,128)(2,1)S(1)}, u32[]{:S(2)}, u32[]{:S(2)}) collective-permute-start(bf16[88,256]{1,0:T(8,128)(2,1)S(1)} %get-tuple-element.64), channel_id=1, source_target_pairs={{0,8},{1,9},{2,10},{3,11},{4,12},{5,13},{6,14},{7,15},{8,0},{9,1},... | collective-permute-start | bytes 135176 | tf_op jit(solution)/shard_map/ppermute | solution.py:371
  54.4 6.2 %collective-permute-start.8 = (bf16[88,256]{1,0:T(8,128)(2,1)S(1)}, bf16[88,256]{1,0:T(8,128)(2,1)S(1)}, u32[]{:S(2)}, u32[]{:S(2)}) collective-permute-start(bf16[88,256]{1,0:T(8,128)(2,1)S(1)} %get-tuple-element.65), channel_id=1, source_target_pairs={{0,24},{1,25},{2,26},{3,27},{4,28},{5,29},{6,30},{7,31},{8,16},{9,... | collective-permute-start | bytes 135176 | tf_op jit(solution)/shard_map/ppermute | solution.py:371
  55.6 5.6 %collective-permute-start.7 = (bf16[88,256]{1,0:T(8,128)(2,1)S(1)}, bf16[88,256]{1,0:T(8,128)(2,1)S(1)}, u32[]{:S(2)}, u32[]{:S(2)}) collective-permute-start(bf16[88,256]{1,0:T(8,128)(2,1)S(1)} %get-tuple-element.66), channel_id=1, source_target_pairs={{0,16},{1,17},{2,18},{3,19},{4,20},{5,21},{6,22},{7,23},{8,24},{9,... | collective-permute-start | bytes 135176 | tf_op jit(solution)/shard_map/ppermute | solution.py:371
  55.9 3.8 %collective-permute-start.9 = (bf16[96,128]{1,0:T(8,128)(2,1)S(1)}, bf16[96,128]{1,0:T(8,128)(2,1)S(1)}, u32[]{:S(2)}, u32[]{:S(2)}) collective-permute-start(bf16[96,128]{1,0:T(8,128)(2,1)S(1)} %get-tuple-element.35), channel_id=1, source_target_pairs={{0,4},{4,0},{8,12},{12,8},{16,20},{20,16},{24,28},{28,24},{1,5},{5... | collective-permute-start | bytes 73736 | tf_op jit(solution)/shard_map/ppermute | solution.py:427
  57.4 2.4 %collective-permute-start.10 = (bf16[96,128]{1,0:T(8,128)(2,1)S(1)}, bf16[96,128]{1,0:T(8,128)(2,1)S(1)}, u32[]{:S(2)}, u32[]{:S(2)}) collective-permute-start(bf16[96,128]{1,0:T(8,128)(2,1)S(1)} %get-tuple-element.36), channel_id=1, source_target_pairs={{4,8},{8,4},{12,16},{16,12},{20,24},{24,20},{5,9},{9,5},{13,17},{1... | collective-permute-start | bytes 73736 | tf_op jit(solution)/shard_map/ppermute | solution.py:427
  61.3 8.5 %collective-permute-start.11 = (bf16[184,256]{1,0:T(8,128)(2,1)S(1)}, bf16[184,256]{1,0:T(8,128)(2,1)S(1)}, u32[]{:S(2)}, u32[]{:S(2)}) collective-permute-start(bf16[184,256]{1,0:T(8,128)(2,1)S(1)} %get-tuple-element.71), channel_id=1, source_target_pairs={{0,24},{1,25},{2,26},{3,27},{4,28},{5,29},{6,30},{7,31},{8,16},{9,... | collective-permute-start | bytes 282632 | tf_op jit(solution)/shard_map/ppermute | solution.py:371
  66.1 7.1 %collective-permute-start.12 = (bf16[184,256]{1,0:T(8,128)(2,1)S(1)}, bf16[184,256]{1,0:T(8,128)(2,1)S(1)}, u32[]{:S(2)}, u32[]{:S(2)}) collective-permute-start(bf16[184,256]{1,0:T(8,128)(2,1)S(1)} %get-tuple-element.72), channel_id=1, source_target_pairs={{0,16},{1,17},{2,18},{3,19},{4,20},{5,21},{6,22},{7,23},{8,24},{9,... | collective-permute-start | bytes 282632 | tf_op jit(solution)/shard_map/ppermute | solution.py:371
  68.3 5.4 %collective-permute-start.13 = (bf16[184,256]{1,0:T(8,128)(2,1)S(1)}, bf16[184,256]{1,0:T(8,128)(2,1)S(1)}, u32[]{:S(2)}, u32[]{:S(2)}) collective-permute-start(bf16[184,256]{1,0:T(8,128)(2,1)S(1)} %get-tuple-element.73), channel_id=1, source_target_pairs={{0,8},{1,9},{2,10},{3,11},{4,12},{5,13},{6,14},{7,15},{8,0},{9,1},... | collective-permute-start | bytes 282632 | tf_op jit(solution)/shard_map/ppermute | solution.py:371
  73.9 10.4 %collective-permute-start.15 = (bf16[544,256]{1,0:T(8,128)(2,1)S(1)}, bf16[544,256]{1,0:T(8,128)(2,1)S(1)}, u32[]{:S(2)}, u32[]{:S(2)}) collective-permute-start(bf16[544,256]{1,0:T(8,128)(2,1)S(1)} %constant_dynamic-update-slice_fusion), channel_id=1, source_target_pairs={{0,4},{1,5},{2,6},{3,7},{4,0},{5,1},{6,2},{7,3},{8,12},{9,13},{10,... | collective-permute-start | bytes 835592 | tf_op jit(solution)/shard_map/ppermute | solution.py:371
  76.5 5.6 %collective-permute-start.16 = (bf16[352,256]{1,0:T(8,128)(2,1)S(1)}, bf16[352,256]{1,0:T(8,128)(2,1)S(1)}, u32[]{:S(2)}, u32[]{:S(2)}) collective-permute-start(bf16[352,256]{1,0:T(8,128)(2,1)S(1)} %pad_maximum_fusion.2), channel_id=1, source_target_pairs={{0,2},{1,3},{2,0},{3,1},{4,6},{5,7},{6,4},{7,5},{8,10},{9,11},{10,... | collective-permute-start | bytes 540680 | tf_op jit(solution)/shard_map/ppermute | solution.py:371
  77.8 6.6 %collective-permute-start.14 = (bf16[352,256]{1,0:T(8,128)(2,1)S(1)}, bf16[352,256]{1,0:T(8,128)(2,1)S(1)}, u32[]{:S(2)}, u32[]{:S(2)}) collective-permute-start(bf16[352,256]{1,0:T(8,128)(2,1)S(1)} %pad_maximum_fusion.2), channel_id=1, source_target_pairs={{0,6},{1,7},{2,4},{3,5},{4,2},{5,3},{6,0},{7,1},{8,14},{9,15},{10,... | collective-permute-start | bytes 540680 | tf_op jit(solution)/shard_map/ppermute | solution.py:371
  84.5 0.7 copy-start.1
  84.8 2.3 %collective-permute-start.17 = (bf16[1408,256]{1,0:T(8,128)(2,1)S(1)}, bf16[1408,256]{1,0:T(8,128)(2,1)S(1)}, u32[]{:S(2)}, u32[]{:S(2)}) collective-permute-start(bf16[1408,256]{1,0:T(8,128)(2,1)S(1)} %pad_maximum_fusion), channel_id=1, source_target_pairs={{0,1},{1,0},{2,3},{3,2},{4,5},{5,4},{6,7},{7,6},{8,9},{9,8},{10,11... | collective-permute-start | bytes 2162696 | tf_op jit(solution)/shard_map/ppermute | solution.py:371

commit v8 on v7

--- a/solution.py
+++ b/solution.py
@@ -127,8 +127,8 @@
 
 
 def backward_kernel(
-    packed, flag_ref, out_hbm, cot_hbm, low_ref, high_ref, w_ref, here_ref, first_ref, second_ref,
-    c_ref, acc_ref, pg_ref, out_ref, cot_ref, out_sem, cot_sem,
+    packed, flag_ref, out_hbm, cot_hbm, low_ref, high_ref, w_hbm, here_ref, first_ref, second_ref,
+    c_ref, acc_ref, pg_ref, out_ref, cot_ref, w_ref, out_sem, cot_sem, w_sems,
 ):
     fetch_out = pltpu.make_async_copy(out_hbm, out_ref, out_sem)
     fetch_out.start()
@@ -136,15 +136,21 @@
     fetch_cot.start()
     offsets, voxels = low_ref.shape
     depth = w_ref.shape[0]
+    step = depth // 9
+    fetch_w = []
+    for m in range(9):
+        sl = slice(m * step, (m + 1) * step)
+        fetch_w.append(pltpu.make_async_copy(w_hbm.at[sl, :], w_ref.at[sl, :], w_sems.at[m]))
+        fetch_w[m].start()
     channels = depth // offsets
     here = voxels // LOW
     blocks = acc_ref.shape[0] // channels
     fetch_out.wait()
     fetch_cot.wait()
     pg_ref[...] = jnp.where(out_ref[...] > 0, cot_ref[...], jnp.zeros((), BF))
-    step = depth // 9
     for m in range(9):
         sl = slice(m * step, (m + 1) * step)
+        fetch_w[m].wait()
         c_ref[sl, :] = dot(w_ref[sl, :], pg_ref[...], 1, 1).astype(BF)
     center = offsets // 2
     for a in range(here):
@@ -294,7 +300,7 @@
             jax.ShapeDtypeStruct((channels, face), BF),
             jax.ShapeDtypeStruct((channels, face), BF),
         ),
-        in_specs=[pl.BlockSpec(memory_space=pltpu.SMEM), hbm, hbm] + whole(3),
+        in_specs=[pl.BlockSpec(memory_space=pltpu.SMEM), hbm, hbm] + whole(2) + [hbm],
         out_specs=tuple(whole(3)),
         scratch_shapes=[
             pltpu.VMEM((depth, voxels), BF),
@@ -302,8 +308,10 @@
             pltpu.VMEM((voxels, c_out), BF),
             pltpu.VMEM((voxels, c_out), BF),
             pltpu.VMEM((voxels, c_out), BF),
-            pltpu.SemaphoreType.DMA,
-            pltpu.SemaphoreType.DMA,
+            pltpu.VMEM((depth, c_out), BF),
+            pltpu.SemaphoreType.DMA,
+            pltpu.SemaphoreType.DMA,
+            pltpu.SemaphoreType.DMA((9,)),
         ],
         compiler_params=pltpu.CompilerParams(vmem_limit_bytes=VMEM_LIMIT),
         cost_estimate=pl.CostEstimate(flops=2 * macs, bytes_accessed=3 << 20, transcendentals=0),

time: 89.2 us -> 90.6 us (1.016)
  Pallas kernels: 25.7 us -> 27.1 us
    pallas_call x1, Pallas kernels: 10.9 us -> 12.3 us  [backward(): pl.pallas_call(functools.partial(backward_kernel, packed), out_shape=(jax...]
  transfers between devices with their start and end apart: 19 -> 19, of which waited for: 11 -> 11; matrix products, arithmetic and copies ran while one was open for 4% -> 4% of each run, Pallas kernels for 14% -> 16%
where the time goes in v8:
time: 90.6 us; the launch traced here: 90.2 us
  starting transfers between devices  32.1 us (35%)
  Pallas kernels  27.1 us (30%)
  waiting for transfers between devices  22.9 us (25%)
  other arithmetic  5.02 us (6%)
  local copies, waits for them, and re-layouts  1.75 us (2%)
  between operations  1.06 us (1%)
    ppermute x14, starting transfers between devices, swapped(): return lax.ppermute(array, AXES, [(i, partner(i)) for i in range(count)])  19.1 us
    ppermute x14, waiting for transfers between devices, swapped(): return lax.ppermute(array, AXES, [(i, partner(i)) for i in range(count)])  15.2 us
    pallas_call x1, Pallas kernels, backward(): pl.pallas_call(functools.partial(backward_kernel, packed), out_shape=(jax...  12.3 us
    pallas_call x1, Pallas kernels, forward(): pl.pallas_call(forward_kernel, out_shape=(jax.ShapeDtypeStruct((voxels, c...  10.7 us
    all_to_all x1, starting transfers between devices, on_device(): got = lax.all_to_all(send, 'brick', split_axis=0, concat_axis=0)  7.26 us
    ppermute x4, starting transfers between devices, meet(): got.append(lax.ppermute(array, 'brick', pairs))  5.75 us
    all_to_all x1, waiting for transfers between devices, on_device(): got = lax.all_to_all(send, 'brick', split_axis=0, concat_axis=0)  4.21 us
    ppermute x4, waiting for transfers between devices, meet(): got.append(lax.ppermute(array, 'brick', pairs))  3.49 us
  transfers between devices with their start and end apart: 19, of which 11 were waited for; matrix products, arithmetic and copies ran while one was open for 4% of the time, Pallas kernels for 16%

profile of v8, /device:TPU:0, one launch (start us, length us, event | category | flops | bytes accessed | tf_op | source)
XLA Modules:
  0.0 90.2 jit_solution(548085737676555458)
XLA Ops:
  0.7 2.1 %shard_map.103 = bf16[8,96,128]{2,1,0:T(8,128)(2,1)} custom-call(bf16[96,1024]{1,0:T(8,128)(2,1)} %bitcast.83, s32[1,1024]{1,0:T(1,128)} %bitcast.70), custom_call_target="tpu_custom_call" | custom-call | flops 201326592 | bytes 524288 | tf_op jit(solution)/shard_map/pallas_call | solution.py:240
  2.7 7.3 %all-to-all-start = ((bf16[8,96,128]{2,1,0:T(8,128)(2,1)}), bf16[8,96,128]{2,1,0:T(8,128)(2,1)S(1)}, u32[]{:S(2)}, u32[]{:S(2)}) async-start(bf16[8,96,128]{2,1,0:T(8,128)(2,1)} %shard_map.103), calls=%async_computation | async-start | bytes 393216 | tf_op jit(solution)/shard_map/all_to_all | solution.py:453
  10.0 1.3 %fusion.19 = (s32[1]{0:T(128)}, s32[1]{0:T(128)}) fusion(s32[2]{0:T(128)} %param.11), kind=kLoop, calls=%fused_computation.64 | loop fusion | bytes 16 | tf_op jit(solution)/shard_map/slice | solution.py:456
  11.3 0.9 %shift-right-logical_convert_fusion = (f32[27,1024]{1,0:T(8,128)S(1)}, f32[27,1024]{1,0:T(8,128)S(1)}) fusion(s32[27,1024]{1,0:T(8,128)} %param.12), kind=kLoop, calls=%fused_computation.18 | loop fusion | flops 110592 | bytes 331776 | tf_op jit(solution)/shard_map/convert_element_type | solution.py:467
  12.2 1.3 %select_select_fusion.9 = s32[256]{0:T(256)S(1)} fusion(s32[256]{0:T(256)S(1)} %copy-done.3, s32[]{:T(128)} %bitcast.3, s32[]{:T(128)} %bitcast.2), kind=kLoop, calls=%fused_computation.62 | loop fusion | flops 1536 | bytes 2056 | tf_op jit(solution)/shard_map/jit(_where)/select_n | solution.py:457
  13.7 4.2 %all-to-all-done.got_ref = bf16[8,96,128]{2,1,0:T(8,128)(2,1)S(1)} async-done(((bf16[8,96,128]{2,1,0:T(8,128)(2,1)}), bf16[8,96,128]{2,1,0:T(8,128)(2,1)S(1)}, u32[]{:S(2)}, u32[]{:S(2)}) %all-to-all-start) | async-done | bytes 196640 | tf_op jit(solution)/shard_map/all_to_all | solution.py:453
  18.3 0.7 collective-permute-start.1
  18.9 3.1 %collective-permute-start = (bf16[96,128]{1,0:T(8,128)(2,1)S(1)}, bf16[96,128]{1,0:T(8,128)(2,1)S(1)}, u32[]{:S(2)}, u32[]{:S(2)}) collective-permute-start(bf16[96,128]{1,0:T(8,128)(2,1)S(1)} %get-tuple-element.70), channel_id=1, source_target_pairs={{0,4},{4,0},{8,12},{12,8},{16,20},{20,16},{24,28},{28,24},{1,5},{5... | collective-permute-start | bytes 73736 | tf_op jit(solution)/shard_map/ppermute | solution.py:435
  22.1 1.7 %collective-permute-done.even_ref = bf16[96,128]{1,0:T(8,128)(2,1)S(1)} collective-permute-done((bf16[96,128]{1,0:T(8,128)(2,1)S(1)}, bf16[96,128]{1,0:T(8,128)(2,1)S(1)}, u32[]{:S(2)}, u32[]{:S(2)}) %collective-permute-start) | collective-permute-done | bytes 24608 | tf_op jit(solution)/shard_map/ppermute | solution.py:435
  23.8 10.7 %shard_map.104 = (bf16[1024,256]{1,0:T(8,128)(2,1)}, bf16[1408,256]{1,0:T(8,128)(2,1)S(1)}, bf16[1408,256]{1,0:T(8,128)(2,1)S(1)}) custom-call(s32[2]{0:T(128)S(1)} %pad_add_fusion.flag_ref, bf16[8,96,128]{2,1,0:T(8,128)(2,1)S(1)} %all-to-all-done.got_ref, bf16[96,128]{1,0:T(8,128)(2,1)S(1)} %collective-permute-done.even_ref, ...), custom_call_target="tpu_custom_call" | custom-call | flops 9512681472 | bytes 5242880 | tf_op jit(solution)/shard_map/pallas_call | solution.py:263
  34.6 2.1 %collective-permute-done.2.got_ref = bf16[1408,256]{1,0:T(8,128)(2,1)S(1)} collective-permute-done((bf16[1408,256]{1,0:T(8,128)(2,1)S(1)}, bf16[1408,256]{1,0:T(8,128)(2,1)S(1)}, u32[]{:S(2)}, u32[]{:S(2)}) %collective-permute-start.2) | collective-permute-done | bytes 720928 | tf_op jit(solution)/shard_map/ppermute | solution.py:379
  36.9 1.6 %collective-permute-start.3 = (bf16[352,256]{1,0:T(8,128)(2,1)S(1)}, bf16[352,256]{1,0:T(8,128)(2,1)S(1)}, u32[]{:S(2)}, u32[]{:S(2)}) collective-permute-start(bf16[352,256]{1,0:T(8,128)(2,1)S(1)} %get-tuple-element.28), channel_id=1, source_target_pairs={{0,2},{1,3},{2,0},{3,1},{4,6},{5,7},{6,4},{7,5},{8,10},{9,11},{10,... | collective-permute-start | bytes 540680 | tf_op jit(solution)/shard_map/ppermute | solution.py:379
  38.5 2.3 %collective-permute-start.4 = (bf16[352,256]{1,0:T(8,128)(2,1)S(1)}, bf16[352,256]{1,0:T(8,128)(2,1)S(1)}, u32[]{:S(2)}, u32[]{:S(2)}) collective-permute-start(bf16[352,256]{1,0:T(8,128)(2,1)S(1)} %get-tuple-element.29), channel_id=1, source_target_pairs={{0,4},{1,5},{2,6},{3,7},{4,0},{5,1},{6,2},{7,3},{8,12},{9,13},{10,... | collective-permute-start | bytes 540680 | tf_op jit(solution)/shard_map/ppermute | solution.py:379
  40.8 12.3 %shard_map.106 = (f32[384,256]{1,0:T(8,128)S(1)}, bf16[96,128]{1,0:T(8,128)(2,1)S(1)}, bf16[96,128]{1,0:T(8,128)(2,1)S(1)}) custom-call(s32[2]{0:T(128)S(1)} %pad_add_fusion.flag_ref, bf16[1024,256]{1,0:T(8,128)(2,1)} %get-tuple-element.19.out_hbm, bf16[1024,256]{1,0:T(8,128)(2,1)} %cot_hbm.3, f32[27,1024]{1,0:T(8,128)S(1)} %get-tuple-element.68.low_ref, ...), custom_call_target="tpu_custom_call" | custom-call | flops 8153726976 | bytes 3145728 | tf_op jit(solution)/shard_map/pallas_call | solution.py:296
  53.3 2.6 %collective-permute-start.6 = (bf16[88,256]{1,0:T(8,128)(2,1)S(1)}, bf16[88,256]{1,0:T(8,128)(2,1)S(1)}, u32[]{:S(2)}, u32[]{:S(2)}) collective-permute-start(bf16[88,256]{1,0:T(8,128)(2,1)S(1)} %get-tuple-element.64), channel_id=1, source_target_pairs={{0,8},{1,9},{2,10},{3,11},{4,12},{5,13},{6,14},{7,15},{8,0},{9,1},... | collective-permute-start | bytes 135176 | tf_op jit(solution)/shard_map/ppermute | solution.py:379
  55.8 1.2 %collective-permute-start.8 = (bf16[88,256]{1,0:T(8,128)(2,1)S(1)}, bf16[88,256]{1,0:T(8,128)(2,1)S(1)}, u32[]{:S(2)}, u32[]{:S(2)}) collective-permute-start(bf16[88,256]{1,0:T(8,128)(2,1)S(1)} %get-tuple-element.65), channel_id=1, source_target_pairs={{0,24},{1,25},{2,26},{3,27},{4,28},{5,29},{6,30},{7,31},{8,16},{9,... | collective-permute-start | bytes 135176 | tf_op jit(solution)/shard_map/ppermute | solution.py:379
  57.4 1.4 %collective-permute-start.9 = (bf16[96,128]{1,0:T(8,128)(2,1)S(1)}, bf16[96,128]{1,0:T(8,128)(2,1)S(1)}, u32[]{:S(2)}, u32[]{:S(2)}) collective-permute-start(bf16[96,128]{1,0:T(8,128)(2,1)S(1)} %get-tuple-element.35), channel_id=1, source_target_pairs={{0,4},{4,0},{8,12},{12,8},{16,20},{20,16},{24,28},{28,24},{1,5},{5... | collective-permute-start | bytes 73736 | tf_op jit(solution)/shard_map/ppermute | solution.py:435
  58.8 0.7 collective-permute-start.10
  59.4 1.8 %collective-permute-done.9.first_ref = bf16[96,128]{1,0:T(8,128)(2,1)S(1)} collective-permute-done((bf16[96,128]{1,0:T(8,128)(2,1)S(1)}, bf16[96,128]{1,0:T(8,128)(2,1)S(1)}, u32[]{:S(2)}, u32[]{:S(2)}) %collective-permute-start.9) | collective-permute-done | bytes 24608 | tf_op jit(solution)/shard_map/ppermute | solution.py:435
  61.2 0.8 shard_map.107
  62.0 0.6 collective-permute-done.7
  62.7 4.8 %collective-permute-start.11 = (bf16[184,256]{1,0:T(8,128)(2,1)S(1)}, bf16[184,256]{1,0:T(8,128)(2,1)S(1)}, u32[]{:S(2)}, u32[]{:S(2)}) collective-permute-start(bf16[184,256]{1,0:T(8,128)(2,1)S(1)} %get-tuple-element.71), channel_id=1, source_target_pairs={{0,24},{1,25},{2,26},{3,27},{4,28},{5,29},{6,30},{7,31},{8,16},{9,... | collective-permute-start | bytes 282632 | tf_op jit(solution)/shard_map/ppermute | solution.py:379
  67.5 2.2 %collective-permute-start.12 = (bf16[184,256]{1,0:T(8,128)(2,1)S(1)}, bf16[184,256]{1,0:T(8,128)(2,1)S(1)}, u32[]{:S(2)}, u32[]{:S(2)}) collective-permute-start(bf16[184,256]{1,0:T(8,128)(2,1)S(1)} %get-tuple-element.72), channel_id=1, source_target_pairs={{0,16},{1,17},{2,18},{3,19},{4,20},{5,21},{6,22},{7,23},{8,24},{9,... | collective-permute-start | bytes 282632 | tf_op jit(solution)/shard_map/ppermute | solution.py:379
  69.7 1.4 %collective-permute-done.11 = bf16[184,256]{1,0:T(8,128)(2,1)S(1)} collective-permute-done((bf16[184,256]{1,0:T(8,128)(2,1)S(1)}, bf16[184,256]{1,0:T(8,128)(2,1)S(1)}, u32[]{:S(2)}, u32[]{:S(2)}) %collective-permute-start.11) | collective-permute-done | bytes 94240 | tf_op jit(solution)/shard_map/ppermute | solution.py:379
  71.2 3.5 %collective-permute-done.12 = bf16[184,256]{1,0:T(8,128)(2,1)S(1)} collective-permute-done((bf16[184,256]{1,0:T(8,128)(2,1)S(1)}, bf16[184,256]{1,0:T(8,128)(2,1)S(1)}, u32[]{:S(2)}, u32[]{:S(2)}) %collective-permute-start.12) | collective-permute-done | bytes 94240 | tf_op jit(solution)/shard_map/ppermute | solution.py:379
  75.4 2.5 %collective-permute-start.15 = (bf16[544,256]{1,0:T(8,128)(2,1)S(1)}, bf16[544,256]{1,0:T(8,128)(2,1)S(1)}, u32[]{:S(2)}, u32[]{:S(2)}) collective-permute-start(bf16[544,256]{1,0:T(8,128)(2,1)S(1)} %constant_dynamic-update-slice_fusion), channel_id=1, source_target_pairs={{0,4},{1,5},{2,6},{3,7},{4,0},{5,1},{6,2},{7,3},{8,12},{9,13},{10,... | collective-permute-start | bytes 835592 | tf_op jit(solution)/shard_map/ppermute | solution.py:379
  77.9 1.2 %collective-permute-start.16 = (bf16[352,256]{1,0:T(8,128)(2,1)S(1)}, bf16[352,256]{1,0:T(8,128)(2,1)S(1)}, u32[]{:S(2)}, u32[]{:S(2)}) collective-permute-start(bf16[352,256]{1,0:T(8,128)(2,1)S(1)} %pad_maximum_fusion.2), channel_id=1, source_target_pairs={{0,2},{1,3},{2,0},{3,1},{4,6},{5,7},{6,4},{7,5},{8,10},{9,11},{10,... | collective-permute-start | bytes 540680 | tf_op jit(solution)/shard_map/ppermute | solution.py:379
  79.4 4.0 %collective-permute-done.16 = bf16[352,256]{1,0:T(8,128)(2,1)S(1)} collective-permute-done((bf16[352,256]{1,0:T(8,128)(2,1)S(1)}, bf16[352,256]{1,0:T(8,128)(2,1)S(1)}, u32[]{:S(2)}, u32[]{:S(2)}) %collective-permute-start.16) | collective-permute-done | bytes 180256 | tf_op jit(solution)/shard_map/ppermute | solution.py:379
  83.4 2.3 %collective-permute-done.14 = bf16[352,256]{1,0:T(8,128)(2,1)S(1)} collective-permute-done((bf16[352,256]{1,0:T(8,128)(2,1)S(1)}, bf16[352,256]{1,0:T(8,128)(2,1)S(1)}, u32[]{:S(2)}, u32[]{:S(2)}) %collective-permute-start.14) | collective-permute-done | bytes 180256 | tf_op jit(solution)/shard_map/ppermute | solution.py:379
  86.6 1.1 %shard_map.108 = bf16[96,1024]{1,0:T(8,128)(2,1)} custom-call(s32[1]{0:T(128)} %bitcast.9.side_ref, bf16[192,256]{1,0:T(8,128)(2,1)S(1)} %bitcast.69, bf16[192,256]{1,0:T(8,128)(2,1)S(1)} %slice.77.came_ref, s32[1,1024]{1,0:T(1,128)S(1)} %bitcast.71), custom_call_target="tpu_custom_call" | custom-call | flops 201326592 | bytes 1048576 | tf_op jit(solution)/shard_map/pallas_call | solution.py:337
  87.7 0.7 collective-permute-done.17
  88.5 1.7 %convert_multiply_fusion = f32[2592,256]{1,0:T(8,128)} fusion(bf16[1296,256]{1,0:T(8,128)(2,1)S(1)} %get-tuple-element.50, bf16[1296,256]{1,0:T(8,128)(2,1)S(1)} %get-tuple-element.49), kind=kLoop, calls=%fused_computation | loop fusion | flops 3317760 | bytes 3981312 | tf_op jit(solution)/shard_map/mul | solution.py:520
  (47 shorter events, 3.3 us)
Async XLA Ops:
  0.6 11.6 %copy-start.3 = (s32[256]{0:T(256)S(1)}, s32[256]{0:T(256)}, u32[]{:S(2)}) copy-start(s32[256]{0:T(256)} %param.10) | copy-start | bytes 3076
  0.6 23.2 %copy-start = (bf16[1024,256]{1,0:T(8,128)(2,1)S(1)}, bf16[1024,256]{1,0:T(8,128)(2,1)}, u32[]{:S(2)}) copy-start(bf16[1024,256]{1,0:T(8,128)(2,1)} %cot_hbm.3) | copy-start | bytes 1572868
  0.7 23.2 %copy-start.2 = (f32[256]{0:T(256)S(1)}, f32[256]{0:T(256)}, u32[]{:S(2)}) copy-start(f32[256]{0:T(256)} %param.14) | copy-start | bytes 3076
  2.7 15.2 %all-to-all-start = ((bf16[8,96,128]{2,1,0:T(8,128)(2,1)}), bf16[8,96,128]{2,1,0:T(8,128)(2,1)S(1)}, u32[]{:S(2)}, u32[]{:S(2)}) async-start(bf16[8,96,128]{2,1,0:T(8,128)(2,1)} %shard_map.103), calls=%async_computation | async-start | bytes 393216 | tf_op jit(solution)/shard_map/all_to_all | solution.py:453
  18.3 3.8 %collective-permute-start.1 = (bf16[96,128]{1,0:T(8,128)(2,1)S(1)}, bf16[96,128]{1,0:T(8,128)(2,1)S(1)}, u32[]{:S(2)}, u32[]{:S(2)}) collective-permute-start(bf16[96,128]{1,0:T(8,128)(2,1)S(1)} %get-tuple-element.69), channel_id=1, source_target_pairs={{4,8},{8,4},{12,16},{16,12},{20,24},{24,20},{5,9},{9,5},{13,17},{1... | collective-permute-start | bytes 73736 | tf_op jit(solution)/shard_map/ppermute | solution.py:435
  18.9 4.9 %collective-permute-start = (bf16[96,128]{1,0:T(8,128)(2,1)S(1)}, bf16[96,128]{1,0:T(8,128)(2,1)S(1)}, u32[]{:S(2)}, u32[]{:S(2)}) collective-permute-start(bf16[96,128]{1,0:T(8,128)(2,1)S(1)} %get-tuple-element.70), channel_id=1, source_target_pairs={{0,4},{4,0},{8,12},{12,8},{16,20},{20,16},{24,28},{28,24},{1,5},{5... | collective-permute-start | bytes 73736 | tf_op jit(solution)/shard_map/ppermute | solution.py:435
  34.5 2.3 %collective-permute-start.2 = (bf16[1408,256]{1,0:T(8,128)(2,1)S(1)}, bf16[1408,256]{1,0:T(8,128)(2,1)S(1)}, u32[]{:S(2)}, u32[]{:S(2)}) collective-permute-start(bf16[1408,256]{1,0:T(8,128)(2,1)S(1)} %get-tuple-element.26), channel_id=1, source_target_pairs={{0,1},{1,0},{2,3},{3,2},{4,5},{5,4},{6,7},{7,6},{8,9},{9,8},{10,11... | collective-permute-start | bytes 2162696 | tf_op jit(solution)/shard_map/ppermute | solution.py:379
  36.9 16.2 %collective-permute-start.3 = (bf16[352,256]{1,0:T(8,128)(2,1)S(1)}, bf16[352,256]{1,0:T(8,128)(2,1)S(1)}, u32[]{:S(2)}, u32[]{:S(2)}) collective-permute-start(bf16[352,256]{1,0:T(8,128)(2,1)S(1)} %get-tuple-element.28), channel_id=1, source_target_pairs={{0,2},{1,3},{2,0},{3,1},{4,6},{5,7},{6,4},{7,5},{8,10},{9,11},{10,... | collective-permute-start | bytes 540680 | tf_op jit(solution)/shard_map/ppermute | solution.py:379
  38.5 14.7 %collective-permute-start.4 = (bf16[352,256]{1,0:T(8,128)(2,1)S(1)}, bf16[352,256]{1,0:T(8,128)(2,1)S(1)}, u32[]{:S(2)}, u32[]{:S(2)}) collective-permute-start(bf16[352,256]{1,0:T(8,128)(2,1)S(1)} %get-tuple-element.29), channel_id=1, source_target_pairs={{0,4},{1,5},{2,6},{3,7},{4,0},{5,1},{6,2},{7,3},{8,12},{9,13},{10,... | collective-permute-start | bytes 540680 | tf_op jit(solution)/shard_map/ppermute | solution.py:379
  40.8 12.4 %collective-permute-start.5 = (bf16[352,256]{1,0:T(8,128)(2,1)S(1)}, bf16[352,256]{1,0:T(8,128)(2,1)S(1)}, u32[]{:S(2)}, u32[]{:S(2)}) collective-permute-start(bf16[352,256]{1,0:T(8,128)(2,1)S(1)} %get-tuple-element.30), channel_id=1, source_target_pairs={{0,6},{1,7},{2,4},{3,5},{4,2},{5,3},{6,0},{7,1},{8,14},{9,15},{10,... | collective-permute-start | bytes 540680 | tf_op jit(solution)/shard_map/ppermute | solution.py:379
  53.3 8.7 %collective-permute-start.6 = (bf16[88,256]{1,0:T(8,128)(2,1)S(1)}, bf16[88,256]{1,0:T(8,128)(2,1)S(1)}, u32[]{:S(2)}, u32[]{:S(2)}) collective-permute-start(bf16[88,256]{1,0:T(8,128)(2,1)S(1)} %get-tuple-element.64), channel_id=1, source_target_pairs={{0,8},{1,9},{2,10},{3,11},{4,12},{5,13},{6,14},{7,15},{8,0},{9,1},... | collective-permute-start | bytes 135176 | tf_op jit(solution)/shard_map/ppermute | solution.py:379
  55.8 6.2 %collective-permute-start.8 = (bf16[88,256]{1,0:T(8,128)(2,1)S(1)}, bf16[88,256]{1,0:T(8,128)(2,1)S(1)}, u32[]{:S(2)}, u32[]{:S(2)}) collective-permute-start(bf16[88,256]{1,0:T(8,128)(2,1)S(1)} %get-tuple-element.65), channel_id=1, source_target_pairs={{0,24},{1,25},{2,26},{3,27},{4,28},{5,29},{6,30},{7,31},{8,16},{9,... | collective-permute-start | bytes 135176 | tf_op jit(solution)/shard_map/ppermute | solution.py:379
  57.0 5.6 %collective-permute-start.7 = (bf16[88,256]{1,0:T(8,128)(2,1)S(1)}, bf16[88,256]{1,0:T(8,128)(2,1)S(1)}, u32[]{:S(2)}, u32[]{:S(2)}) collective-permute-start(bf16[88,256]{1,0:T(8,128)(2,1)S(1)} %get-tuple-element.66), channel_id=1, source_target_pairs={{0,16},{1,17},{2,18},{3,19},{4,20},{5,21},{6,22},{7,23},{8,24},{9,... | collective-permute-start | bytes 135176 | tf_op jit(solution)/shard_map/ppermute | solution.py:379
  57.4 3.8 %collective-permute-start.9 = (bf16[96,128]{1,0:T(8,128)(2,1)S(1)}, bf16[96,128]{1,0:T(8,128)(2,1)S(1)}, u32[]{:S(2)}, u32[]{:S(2)}) collective-permute-start(bf16[96,128]{1,0:T(8,128)(2,1)S(1)} %get-tuple-element.35), channel_id=1, source_target_pairs={{0,4},{4,0},{8,12},{12,8},{16,20},{20,16},{24,28},{28,24},{1,5},{5... | collective-permute-start | bytes 73736 | tf_op jit(solution)/shard_map/ppermute | solution.py:435
  58.8 2.5 %collective-permute-start.10 = (bf16[96,128]{1,0:T(8,128)(2,1)S(1)}, bf16[96,128]{1,0:T(8,128)(2,1)S(1)}, u32[]{:S(2)}, u32[]{:S(2)}) collective-permute-start(bf16[96,128]{1,0:T(8,128)(2,1)S(1)} %get-tuple-element.36), channel_id=1, source_target_pairs={{4,8},{8,4},{12,16},{16,12},{20,24},{24,20},{5,9},{9,5},{13,17},{1... | collective-permute-start | bytes 73736 | tf_op jit(solution)/shard_map/ppermute | solution.py:435
  62.7 8.4 %collective-permute-start.11 = (bf16[184,256]{1,0:T(8,128)(2,1)S(1)}, bf16[184,256]{1,0:T(8,128)(2,1)S(1)}, u32[]{:S(2)}, u32[]{:S(2)}) collective-permute-start(bf16[184,256]{1,0:T(8,128)(2,1)S(1)} %get-tuple-element.71), channel_id=1, source_target_pairs={{0,24},{1,25},{2,26},{3,27},{4,28},{5,29},{6,30},{7,31},{8,16},{9,... | collective-permute-start | bytes 282632 | tf_op jit(solution)/shard_map/ppermute | solution.py:379
  67.5 7.1 %collective-permute-start.12 = (bf16[184,256]{1,0:T(8,128)(2,1)S(1)}, bf16[184,256]{1,0:T(8,128)(2,1)S(1)}, u32[]{:S(2)}, u32[]{:S(2)}) collective-permute-start(bf16[184,256]{1,0:T(8,128)(2,1)S(1)} %get-tuple-element.72), channel_id=1, source_target_pairs={{0,16},{1,17},{2,18},{3,19},{4,20},{5,21},{6,22},{7,23},{8,24},{9,... | collective-permute-start | bytes 282632 | tf_op jit(solution)/shard_map/ppermute | solution.py:379
  69.7 5.4 %collective-permute-start.13 = (bf16[184,256]{1,0:T(8,128)(2,1)S(1)}, bf16[184,256]{1,0:T(8,128)(2,1)S(1)}, u32[]{:S(2)}, u32[]{:S(2)}) collective-permute-start(bf16[184,256]{1,0:T(8,128)(2,1)S(1)} %get-tuple-element.73), channel_id=1, source_target_pairs={{0,8},{1,9},{2,10},{3,11},{4,12},{5,13},{6,14},{7,15},{8,0},{9,1},... | collective-permute-start | bytes 282632 | tf_op jit(solution)/shard_map/ppermute | solution.py:379
  75.4 10.3 %collective-permute-start.15 = (bf16[544,256]{1,0:T(8,128)(2,1)S(1)}, bf16[544,256]{1,0:T(8,128)(2,1)S(1)}, u32[]{:S(2)}, u32[]{:S(2)}) collective-permute-start(bf16[544,256]{1,0:T(8,128)(2,1)S(1)} %constant_dynamic-update-slice_fusion), channel_id=1, source_target_pairs={{0,4},{1,5},{2,6},{3,7},{4,0},{5,1},{6,2},{7,3},{8,12},{9,13},{10,... | collective-permute-start | bytes 835592 | tf_op jit(solution)/shard_map/ppermute | solution.py:379
  77.9 5.6 %collective-permute-start.16 = (bf16[352,256]{1,0:T(8,128)(2,1)S(1)}, bf16[352,256]{1,0:T(8,128)(2,1)S(1)}, u32[]{:S(2)}, u32[]{:S(2)}) collective-permute-start(bf16[352,256]{1,0:T(8,128)(2,1)S(1)} %pad_maximum_fusion.2), channel_id=1, source_target_pairs={{0,2},{1,3},{2,0},{3,1},{4,6},{5,7},{6,4},{7,5},{8,10},{9,11},{10,... | collective-permute-start | bytes 540680 | tf_op jit(solution)/shard_map/ppermute | solution.py:379
  79.1 6.6 %collective-permute-start.14 = (bf16[352,256]{1,0:T(8,128)(2,1)S(1)}, bf16[352,256]{1,0:T(8,128)(2,1)S(1)}, u32[]{:S(2)}, u32[]{:S(2)}) collective-permute-start(bf16[352,256]{1,0:T(8,128)(2,1)S(1)} %pad_maximum_fusion.2), channel_id=1, source_target_pairs={{0,6},{1,7},{2,4},{3,5},{4,2},{5,3},{6,0},{7,1},{8,14},{9,15},{10,... | collective-permute-start | bytes 540680 | tf_op jit(solution)/shard_map/ppermute | solution.py:379
  85.9 0.7 copy-start.1
  86.1 2.3 %collective-permute-start.17 = (bf16[1408,256]{1,0:T(8,128)(2,1)S(1)}, bf16[1408,256]{1,0:T(8,128)(2,1)S(1)}, u32[]{:S(2)}, u32[]{:S(2)}) collective-permute-start(bf16[1408,256]{1,0:T(8,128)(2,1)S(1)} %pad_maximum_fusion), channel_id=1, source_target_pairs={{0,1},{1,0},{2,3},{3,2},{4,5},{5,4},{6,7},{7,6},{8,9},{9,8},{10,11... | collective-permute-start | bytes 2162696 | tf_op jit(solution)/shard_map/ppermute | solution.py:379

commit v9 on v7

--- a/solution.py
+++ b/solution.py
@@ -12,9 +12,9 @@
 F32 = jnp.float32
 LOW = 256
 SHIFT = 8
-VMEM_LIMIT = 53 << 20
+VMEM_LIMIT = 20 << 20
 SMALL_LIMIT = 6 << 20
-FULL_LIMIT = 51 << 20
+FULL_LIMIT = 50 << 20
 ALL_LIMIT = 60 << 20
 AXES = ("brick", "group")
 
@@ -127,20 +127,13 @@
 
 
 def backward_kernel(
-    packed, flag_ref, out_hbm, cot_hbm, low_ref, high_ref, w_ref, here_ref, first_ref, second_ref,
-    c_ref, acc_ref, pg_ref, out_ref, cot_ref, out_sem, cot_sem,
+    packed, flag_ref, out_ref, cot_ref, low_ref, high_ref, w_ref, here_ref, first_ref, second_ref, c_ref, acc_ref, pg_ref
 ):
-    fetch_out = pltpu.make_async_copy(out_hbm, out_ref, out_sem)
-    fetch_out.start()
-    fetch_cot = pltpu.make_async_copy(cot_hbm, cot_ref, cot_sem)
-    fetch_cot.start()
     offsets, voxels = low_ref.shape
     depth = w_ref.shape[0]
     channels = depth // offsets
     here = voxels // LOW
     blocks = acc_ref.shape[0] // channels
-    fetch_out.wait()
-    fetch_cot.wait()
     pg_ref[...] = jnp.where(out_ref[...] > 0, cot_ref[...], jnp.zeros((), BF))
     step = depth // 9
     for m in range(9):
@@ -176,7 +169,7 @@
     second_ref[...] = jnp.where(odd == 1, up, down).astype(BF)
 
 
-def finish_kernel(packed, flag_ref, here_ref, first_ref, second_ref, pick_ref, out_ref, from_ref):
+def finish_kernel(packed, flag_ref, here_ref, first_ref, second_ref, row_ref, out_ref, from_ref):
     channels, face = first_ref.shape
     blocks = here_ref.shape[0] // channels
     prev, after = sides(flag_ref[1], first_ref, second_ref)
@@ -184,7 +177,9 @@
     from_ref[:, face:] = after
     part, per = channels // 2, LOW // 2
     for a in range(blocks):
-        added = dot(from_ref[...], pick_ref[:, a * LOW : (a + 1) * LOW], 1, 0)
+        rows = lax.broadcasted_iota(jnp.int32, (LOW, 2 * face), 0) + a * LOW
+        hot = jnp.where(rows == row_ref[...], 1.0, 0.0).astype(BF)
+        added = dot(from_ref[...], hot, 1, 1)
         if not packed:
             at = slice(a * channels, (a + 1) * channels)
             out_ref[at, :] = (here_ref[at, :] + added).astype(BF)
@@ -281,7 +276,6 @@
 
 
 def backward(packed, flags, out, cot, low, high, w, face):
-    hbm = pl.BlockSpec(memory_space=pltpu.HBM)
     offsets, voxels = low.shape
     depth, c_out = w.shape
     channels = depth // offsets
@@ -294,23 +288,19 @@
             jax.ShapeDtypeStruct((channels, face), BF),
             jax.ShapeDtypeStruct((channels, face), BF),
         ),
-        in_specs=[pl.BlockSpec(memory_space=pltpu.SMEM), hbm, hbm] + whole(3),
+        in_specs=[pl.BlockSpec(memory_space=pltpu.SMEM)] + whole(5),
         out_specs=tuple(whole(3)),
         scratch_shapes=[
             pltpu.VMEM((depth, voxels), BF),
             pltpu.VMEM((rows, LOW), F32),
             pltpu.VMEM((voxels, c_out), BF),
-            pltpu.VMEM((voxels, c_out), BF),
-            pltpu.VMEM((voxels, c_out), BF),
-            pltpu.SemaphoreType.DMA,
-            pltpu.SemaphoreType.DMA,
         ],
         compiler_params=pltpu.CompilerParams(vmem_limit_bytes=VMEM_LIMIT),
         cost_estimate=pl.CostEstimate(flops=2 * macs, bytes_accessed=3 << 20, transcendentals=0),
     )(flags, out, cot, low, high, w)
 
 
-def finish(packed, flags, here, first, second, pick):
+def finish(packed, flags, here, first, second, face_rows):
     rows, _ = here.shape
     channels, face = first.shape
     return pl.pallas_call(
@@ -321,7 +311,7 @@
         scratch_shapes=[pltpu.VMEM((channels, 2 * face), BF)],
         compiler_params=pltpu.CompilerParams(vmem_limit_bytes=SMALL_LIMIT),
         cost_estimate=pl.CostEstimate(flops=4 * rows * LOW * face, bytes_accessed=1 << 20, transcendentals=0),
-    )(flags, here, first, second, pick)
+    )(flags, here, first, second, face_rows)
 
 
 def place(side, keep, came, order, channels):
@@ -446,7 +436,8 @@
 
     slots = jnp.arange(2 * face, dtype=jnp.int32)
     live = jnp.where(slots < face, slots < face_count[0], slots - face < face_count[1])
-    pick = one_hot_rows(jnp.where(live, face_list, -1), rows)
+    face_rows = jnp.where(live, face_list, -1)
+    pick = one_hot_rows(face_rows, rows)
     pick, got = lax.optimization_barrier((pick, got))
     local = got.transpose(1, 0, 2).reshape(channels, rows)
     shown = dot(local, pick, 1, 1).astype(BF)
@@ -477,7 +468,7 @@
     for stride, radix in plan[1:]:
         total = reduce_stage(total, flat, count, stride, radix)
 
-    local_grad = finish(packed, flags, here, first, second, pick)
+    local_grad = finish(packed, flags, here, first, second, face_rows[None])
     if packed:
         part = channels // 2
         total, local_grad = lax.optimization_barrier((total, local_grad))

time: 89.2 us -> 89.1 us (level)
    pallas_call x1, Pallas kernels: 10.9 us -> 8.95 us  [backward(): pl.pallas_call(functools.partial(backward_kernel, packed), out_shape=(jax...]
    pallas_call x1, Pallas kernels: 10.7 us -> 12.1 us  [forward(): pl.pallas_call(forward_kernel, out_shape=(jax.ShapeDtypeStruct((voxels, c...]
  transfers between devices with their start and end apart: 19 -> 19, of which waited for: 11 -> 11; matrix products, arithmetic and copies ran while one was open for 4% -> 4% of each run, Pallas kernels for 14% -> 12%
where the time goes in v9:
time: 89.1 us; the launch traced here: 88.8 us
  starting transfers between devices  32.4 us (36%)
  Pallas kernels  25.3 us (28%)
  waiting for transfers between devices  22.8 us (26%)
  other arithmetic  5.04 us (6%)
  local copies, waits for them, and re-layouts  1.76 us (2%)
  between operations  1.09 us (1%)
    ppermute x14, starting transfers between devices, swapped(): return lax.ppermute(array, AXES, [(i, partner(i)) for i in range(count)])  19.3 us
    ppermute x14, waiting for transfers between devices, swapped(): return lax.ppermute(array, AXES, [(i, partner(i)) for i in range(count)])  15.2 us
    pallas_call x1, Pallas kernels, forward(): pl.pallas_call(forward_kernel, out_shape=(jax.ShapeDtypeStruct((voxels, c...  12.1 us
    pallas_call x1, Pallas kernels, backward(): pl.pallas_call(functools.partial(backward_kernel, packed), out_shape=(jax...  8.95 us
    all_to_all x1, starting transfers between devices, on_device(): got = lax.all_to_all(send, 'brick', split_axis=0, concat_axis=0)  7.26 us
    ppermute x4, starting transfers between devices, meet(): got.append(lax.ppermute(array, 'brick', pairs))  5.79 us
    all_to_all x1, waiting for transfers between devices, on_device(): got = lax.all_to_all(send, 'brick', split_axis=0, concat_axis=0)  4.21 us
    ppermute x4, waiting for transfers between devices, meet(): got.append(lax.ppermute(array, 'brick', pairs))  3.45 us
  transfers between devices with their start and end apart: 19, of which 11 were waited for; matrix products, arithmetic and copies ran while one was open for 4% of the time, Pallas kernels for 12%

profile of v9, /device:TPU:0, one launch (start us, length us, event | category | flops | bytes accessed | tf_op | source)
XLA Modules:
  0.0 88.8 jit_solution(512477205844605278)
XLA Ops:
  0.7 2.1 %shard_map.103 = bf16[8,96,128]{2,1,0:T(8,128)(2,1)} custom-call(bf16[96,1024]{1,0:T(8,128)(2,1)} %bitcast.85, s32[1,1024]{1,0:T(1,128)} %bitcast.74), custom_call_target="tpu_custom_call" | custom-call | flops 201326592 | bytes 524288 | tf_op jit(solution)/shard_map/pallas_call | solution.py:229
  2.8 7.3 %all-to-all-start = ((bf16[8,96,128]{2,1,0:T(8,128)(2,1)}), bf16[8,96,128]{2,1,0:T(8,128)(2,1)S(1)}, u32[]{:S(2)}, u32[]{:S(2)}) async-start(bf16[8,96,128]{2,1,0:T(8,128)(2,1)} %shard_map.103), calls=%async_computation | async-start | bytes 393216 | tf_op jit(solution)/shard_map/all_to_all | solution.py:435
  10.1 1.3 %fusion.19 = (s32[1]{0:T(128)}, s32[1]{0:T(128)}) fusion(s32[2]{0:T(128)} %param.11), kind=kLoop, calls=%fused_computation.64 | loop fusion | bytes 16 | tf_op jit(solution)/shard_map/slice | solution.py:438
  11.4 0.9 %shift-right-logical_convert_fusion = (f32[27,1024]{1,0:T(8,128)S(1)}, f32[27,1024]{1,0:T(8,128)S(1)}) fusion(s32[27,1024]{1,0:T(8,128)} %param.12), kind=kLoop, calls=%fused_computation.18 | loop fusion | flops 110592 | bytes 331776 | tf_op jit(solution)/shard_map/convert_element_type | solution.py:450
  12.3 1.3 %select_select_fusion.9 = s32[256]{0:T(256)S(1)} fusion(s32[256]{0:T(256)S(1)} %copy-done.6, s32[]{:T(128)} %bitcast.3, s32[]{:T(128)} %bitcast.2), kind=kLoop, calls=%fused_computation.62 | loop fusion | flops 1536 | bytes 2056 | tf_op jit(solution)/shard_map/jit(_where)/select_n | solution.py:439
  13.8 4.2 %all-to-all-done.got_ref = bf16[8,96,128]{2,1,0:T(8,128)(2,1)S(1)} async-done(((bf16[8,96,128]{2,1,0:T(8,128)(2,1)}), bf16[8,96,128]{2,1,0:T(8,128)(2,1)S(1)}, u32[]{:S(2)}, u32[]{:S(2)}) %all-to-all-start) | async-done | bytes 196640 | tf_op jit(solution)/shard_map/all_to_all | solution.py:435
  18.4 0.7 collective-permute-start.1
  19.0 3.1 %collective-permute-start = (bf16[96,128]{1,0:T(8,128)(2,1)S(1)}, bf16[96,128]{1,0:T(8,128)(2,1)S(1)}, u32[]{:S(2)}, u32[]{:S(2)}) collective-permute-start(bf16[96,128]{1,0:T(8,128)(2,1)S(1)} %get-tuple-element.70), channel_id=1, source_target_pairs={{0,4},{4,0},{8,12},{12,8},{16,20},{20,16},{24,28},{28,24},{1,5},{5... | collective-permute-start | bytes 73736 | tf_op jit(solution)/shard_map/ppermute | solution.py:417
  22.2 1.7 %collective-permute-done.even_ref = bf16[96,128]{1,0:T(8,128)(2,1)S(1)} collective-permute-done((bf16[96,128]{1,0:T(8,128)(2,1)S(1)}, bf16[96,128]{1,0:T(8,128)(2,1)S(1)}, u32[]{:S(2)}, u32[]{:S(2)}) %collective-permute-start) | collective-permute-done | bytes 24608 | tf_op jit(solution)/shard_map/ppermute | solution.py:417
  23.9 12.1 %shard_map.104 = (bf16[1024,256]{1,0:T(8,128)(2,1)}, bf16[1408,256]{1,0:T(8,128)(2,1)}, bf16[1408,256]{1,0:T(8,128)(2,1)S(1)}) custom-call(s32[2]{0:T(128)S(1)} %pad_add_fusion.flag_ref, bf16[8,96,128]{2,1,0:T(8,128)(2,1)S(1)} %all-to-all-done.got_ref, bf16[96,128]{1,0:T(8,128)(2,1)S(1)} %collective-permute-done.even_ref, ...), custom_call_target="tpu_custom_call" | custom-call | flops 9512681472 | bytes 5242880 | tf_op jit(solution)/shard_map/pallas_call | solution.py:252
  36.2 2.3 %collective-permute-done.2.got_ref = bf16[1408,256]{1,0:T(8,128)(2,1)S(1)} collective-permute-done((bf16[1408,256]{1,0:T(8,128)(2,1)}, bf16[1408,256]{1,0:T(8,128)(2,1)S(1)}, u32[]{:S(2)}, u32[]{:S(2)}) %collective-permute-start.2) | collective-permute-done | bytes 720928 | tf_op jit(solution)/shard_map/ppermute | solution.py:361
  38.7 1.6 %collective-permute-start.3 = (bf16[352,256]{1,0:T(8,128)(2,1)S(1)}, bf16[352,256]{1,0:T(8,128)(2,1)S(1)}, u32[]{:S(2)}, u32[]{:S(2)}) collective-permute-start(bf16[352,256]{1,0:T(8,128)(2,1)S(1)} %get-tuple-element.28), channel_id=1, source_target_pairs={{0,2},{1,3},{2,0},{3,1},{4,6},{5,7},{6,4},{7,5},{8,10},{9,11},{10,... | collective-permute-start | bytes 540680 | tf_op jit(solution)/shard_map/ppermute | solution.py:361
  40.2 2.3 %collective-permute-start.4 = (bf16[352,256]{1,0:T(8,128)(2,1)S(1)}, bf16[352,256]{1,0:T(8,128)(2,1)S(1)}, u32[]{:S(2)}, u32[]{:S(2)}) collective-permute-start(bf16[352,256]{1,0:T(8,128)(2,1)S(1)} %get-tuple-element.29), channel_id=1, source_target_pairs={{0,4},{1,5},{2,6},{3,7},{4,0},{5,1},{6,2},{7,3},{8,12},{9,13},{10,... | collective-permute-start | bytes 540680 | tf_op jit(solution)/shard_map/ppermute | solution.py:361
  42.5 8.9 %shard_map.106 = (f32[384,256]{1,0:T(8,128)S(1)}, bf16[96,128]{1,0:T(8,128)(2,1)S(1)}, bf16[96,128]{1,0:T(8,128)(2,1)S(1)}) custom-call(s32[2]{0:T(128)S(1)} %pad_add_fusion.flag_ref, bf16[1024,256]{1,0:T(8,128)(2,1)S(1)} %copy-done.5, bf16[1024,256]{1,0:T(8,128)(2,1)S(1)} %copy-done.2, f32[27,1024]{1,0:T(8,128)S(1)} %get-tuple-element.68.low_ref, ...), custom_call_target="tpu_custom_call" | custom-call | flops 8153726976 | bytes 3145728 | tf_op jit(solution)/shard_map/pallas_call | solution.py:284
  51.7 2.6 %collective-permute-start.6 = (bf16[88,256]{1,0:T(8,128)(2,1)S(1)}, bf16[88,256]{1,0:T(8,128)(2,1)S(1)}, u32[]{:S(2)}, u32[]{:S(2)}) collective-permute-start(bf16[88,256]{1,0:T(8,128)(2,1)S(1)} %get-tuple-element.64), channel_id=1, source_target_pairs={{0,8},{1,9},{2,10},{3,11},{4,12},{5,13},{6,14},{7,15},{8,0},{9,1},... | collective-permute-start | bytes 135176 | tf_op jit(solution)/shard_map/ppermute | solution.py:361
  54.2 1.2 %collective-permute-start.8 = (bf16[88,256]{1,0:T(8,128)(2,1)S(1)}, bf16[88,256]{1,0:T(8,128)(2,1)S(1)}, u32[]{:S(2)}, u32[]{:S(2)}) collective-permute-start(bf16[88,256]{1,0:T(8,128)(2,1)S(1)} %get-tuple-element.65), channel_id=1, source_target_pairs={{0,24},{1,25},{2,26},{3,27},{4,28},{5,29},{6,30},{7,31},{8,16},{9,... | collective-permute-start | bytes 135176 | tf_op jit(solution)/shard_map/ppermute | solution.py:361
  55.8 1.4 %collective-permute-start.9 = (bf16[96,128]{1,0:T(8,128)(2,1)S(1)}, bf16[96,128]{1,0:T(8,128)(2,1)S(1)}, u32[]{:S(2)}, u32[]{:S(2)}) collective-permute-start(bf16[96,128]{1,0:T(8,128)(2,1)S(1)} %get-tuple-element.35), channel_id=1, source_target_pairs={{0,4},{4,0},{8,12},{12,8},{16,20},{20,16},{24,28},{28,24},{1,5},{5... | collective-permute-start | bytes 73736 | tf_op jit(solution)/shard_map/ppermute | solution.py:417
  57.2 0.7 collective-permute-start.10
  57.9 1.7 %collective-permute-done.9.first_ref = bf16[96,128]{1,0:T(8,128)(2,1)S(1)} collective-permute-done((bf16[96,128]{1,0:T(8,128)(2,1)S(1)}, bf16[96,128]{1,0:T(8,128)(2,1)S(1)}, u32[]{:S(2)}, u32[]{:S(2)}) %collective-permute-start.9) | collective-permute-done | bytes 24608 | tf_op jit(solution)/shard_map/ppermute | solution.py:417
  59.6 0.9 shard_map.107
  60.5 0.5 collective-permute-done.7
  61.1 4.9 %collective-permute-start.11 = (bf16[184,256]{1,0:T(8,128)(2,1)S(1)}, bf16[184,256]{1,0:T(8,128)(2,1)S(1)}, u32[]{:S(2)}, u32[]{:S(2)}) collective-permute-start(bf16[184,256]{1,0:T(8,128)(2,1)S(1)} %get-tuple-element.71), channel_id=1, source_target_pairs={{0,24},{1,25},{2,26},{3,27},{4,28},{5,29},{6,30},{7,31},{8,16},{9,... | collective-permute-start | bytes 282632 | tf_op jit(solution)/shard_map/ppermute | solution.py:361
  66.0 2.2 %collective-permute-start.12 = (bf16[184,256]{1,0:T(8,128)(2,1)S(1)}, bf16[184,256]{1,0:T(8,128)(2,1)S(1)}, u32[]{:S(2)}, u32[]{:S(2)}) collective-permute-start(bf16[184,256]{1,0:T(8,128)(2,1)S(1)} %get-tuple-element.72), channel_id=1, source_target_pairs={{0,16},{1,17},{2,18},{3,19},{4,20},{5,21},{6,22},{7,23},{8,24},{9,... | collective-permute-start | bytes 282632 | tf_op jit(solution)/shard_map/ppermute | solution.py:361
  68.2 1.4 %collective-permute-done.11 = bf16[184,256]{1,0:T(8,128)(2,1)S(1)} collective-permute-done((bf16[184,256]{1,0:T(8,128)(2,1)S(1)}, bf16[184,256]{1,0:T(8,128)(2,1)S(1)}, u32[]{:S(2)}, u32[]{:S(2)}) %collective-permute-start.11) | collective-permute-done | bytes 94240 | tf_op jit(solution)/shard_map/ppermute | solution.py:361
  69.6 3.5 %collective-permute-done.12 = bf16[184,256]{1,0:T(8,128)(2,1)S(1)} collective-permute-done((bf16[184,256]{1,0:T(8,128)(2,1)S(1)}, bf16[184,256]{1,0:T(8,128)(2,1)S(1)}, u32[]{:S(2)}, u32[]{:S(2)}) %collective-permute-start.12) | collective-permute-done | bytes 94240 | tf_op jit(solution)/shard_map/ppermute | solution.py:361
  73.9 2.6 %collective-permute-start.15 = (bf16[544,256]{1,0:T(8,128)(2,1)S(1)}, bf16[544,256]{1,0:T(8,128)(2,1)S(1)}, u32[]{:S(2)}, u32[]{:S(2)}) collective-permute-start(bf16[544,256]{1,0:T(8,128)(2,1)S(1)} %constant_dynamic-update-slice_fusion), channel_id=1, source_target_pairs={{0,4},{1,5},{2,6},{3,7},{4,0},{5,1},{6,2},{7,3},{8,12},{9,13},{10,... | collective-permute-start | bytes 835592 | tf_op jit(solution)/shard_map/ppermute | solution.py:361
  76.5 1.3 %collective-permute-start.16 = (bf16[352,256]{1,0:T(8,128)(2,1)S(1)}, bf16[352,256]{1,0:T(8,128)(2,1)S(1)}, u32[]{:S(2)}, u32[]{:S(2)}) collective-permute-start(bf16[352,256]{1,0:T(8,128)(2,1)S(1)} %pad_maximum_fusion.2), channel_id=1, source_target_pairs={{0,2},{1,3},{2,0},{3,1},{4,6},{5,7},{6,4},{7,5},{8,10},{9,11},{10,... | collective-permute-start | bytes 540680 | tf_op jit(solution)/shard_map/ppermute | solution.py:361
  78.0 4.8 %collective-permute-done.16 = bf16[352,256]{1,0:T(8,128)(2,1)S(1)} collective-permute-done((bf16[352,256]{1,0:T(8,128)(2,1)S(1)}, bf16[352,256]{1,0:T(8,128)(2,1)S(1)}, u32[]{:S(2)}, u32[]{:S(2)}) %collective-permute-start.16) | collective-permute-done | bytes 180256 | tf_op jit(solution)/shard_map/ppermute | solution.py:361
  82.8 1.5 %collective-permute-done.14 = bf16[352,256]{1,0:T(8,128)(2,1)S(1)} collective-permute-done((bf16[352,256]{1,0:T(8,128)(2,1)S(1)}, bf16[352,256]{1,0:T(8,128)(2,1)S(1)}, u32[]{:S(2)}, u32[]{:S(2)}) %collective-permute-start.14) | collective-permute-done | bytes 180256 | tf_op jit(solution)/shard_map/ppermute | solution.py:361
  85.1 1.1 %shard_map.108 = bf16[96,1024]{1,0:T(8,128)(2,1)} custom-call(s32[1]{0:T(128)} %bitcast.9.side_ref, bf16[192,256]{1,0:T(8,128)(2,1)S(1)} %bitcast.70, bf16[192,256]{1,0:T(8,128)(2,1)S(1)} %slice.77.came_ref, s32[1,1024]{1,0:T(1,128)S(1)} %bitcast.75), custom_call_target="tpu_custom_call" | custom-call | flops 201326592 | bytes 1048576 | tf_op jit(solution)/shard_map/pallas_call | solution.py:319
  86.2 0.7 collective-permute-done.17
  87.0 1.7 %convert_multiply_fusion = f32[2592,256]{1,0:T(8,128)} fusion(bf16[1296,256]{1,0:T(8,128)(2,1)S(1)} %get-tuple-element.50, bf16[1296,256]{1,0:T(8,128)(2,1)S(1)} %get-tuple-element.49), kind=kLoop, calls=%fused_computation | loop fusion | flops 3317760 | bytes 3981312 | tf_op jit(solution)/shard_map/mul | solution.py:503
  (53 shorter events, 3.1 us)
Async XLA Ops:
  0.6 11.7 %copy-start.6 = (s32[256]{0:T(256)S(1)}, s32[256]{0:T(256)}, u32[]{:S(2)}) copy-start(s32[256]{0:T(256)} %param.10) | copy-start | bytes 3076
  0.6 23.2 %copy-start = (bf16[27,96,256]{2,1,0:T(8,128)(2,1)S(1)}, bf16[27,96,256]{2,1,0:T(8,128)(2,1)}, u32[]{:S(2)}) copy-start(bf16[27,96,256]{2,1,0:T(8,128)(2,1)} %param.13) | copy-start | bytes 3981316
  0.7 23.2 %copy-start.1 = (bf16[1024,256]{1,0:T(8,128)(2,1)S(1)}, bf16[1024,256]{1,0:T(8,128)(2,1)}, u32[]{:S(2)}) copy-start(bf16[1024,256]{1,0:T(8,128)(2,1)} %cot_ref.1) | copy-start | bytes 1572868
  0.7 23.2 %copy-start.4 = (f32[256]{0:T(256)S(1)}, f32[256]{0:T(256)}, u32[]{:S(2)}) copy-start(f32[256]{0:T(256)} %param.14) | copy-start | bytes 3076
  2.8 15.2 %all-to-all-start = ((bf16[8,96,128]{2,1,0:T(8,128)(2,1)}), bf16[8,96,128]{2,1,0:T(8,128)(2,1)S(1)}, u32[]{:S(2)}, u32[]{:S(2)}) async-start(bf16[8,96,128]{2,1,0:T(8,128)(2,1)} %shard_map.103), calls=%async_computation | async-start | bytes 393216 | tf_op jit(solution)/shard_map/all_to_all | solution.py:435
  18.4 3.8 %collective-permute-start.1 = (bf16[96,128]{1,0:T(8,128)(2,1)S(1)}, bf16[96,128]{1,0:T(8,128)(2,1)S(1)}, u32[]{:S(2)}, u32[]{:S(2)}) collective-permute-start(bf16[96,128]{1,0:T(8,128)(2,1)S(1)} %get-tuple-element.69), channel_id=1, source_target_pairs={{4,8},{8,4},{12,16},{16,12},{20,24},{24,20},{5,9},{9,5},{13,17},{1... | collective-permute-start | bytes 73736 | tf_op jit(solution)/shard_map/ppermute | solution.py:417
  19.0 4.9 %collective-permute-start = (bf16[96,128]{1,0:T(8,128)(2,1)S(1)}, bf16[96,128]{1,0:T(8,128)(2,1)S(1)}, u32[]{:S(2)}, u32[]{:S(2)}) collective-permute-start(bf16[96,128]{1,0:T(8,128)(2,1)S(1)} %get-tuple-element.70), channel_id=1, source_target_pairs={{0,4},{4,0},{8,12},{12,8},{16,20},{20,16},{24,28},{28,24},{1,5},{5... | collective-permute-start | bytes 73736 | tf_op jit(solution)/shard_map/ppermute | solution.py:417
  36.0 2.5 %collective-permute-start.2 = (bf16[1408,256]{1,0:T(8,128)(2,1)}, bf16[1408,256]{1,0:T(8,128)(2,1)S(1)}, u32[]{:S(2)}, u32[]{:S(2)}) collective-permute-start(bf16[1408,256]{1,0:T(8,128)(2,1)} %get-tuple-element.26), channel_id=1, source_target_pairs={{0,1},{1,0},{2,3},{3,2},{4,5},{5,4},{6,7},{7,6},{8,9},{9,8},{10,11... | collective-permute-start | bytes 2162696 | tf_op jit(solution)/shard_map/ppermute | solution.py:361
  36.2 6.4 %copy-start.2 = (bf16[1024,256]{1,0:T(8,128)(2,1)S(1)}, bf16[1024,256]{1,0:T(8,128)(2,1)}, u32[]{:S(2)}) copy-start(bf16[1024,256]{1,0:T(8,128)(2,1)} %cot_ref.1) | copy-start | bytes 1572868
  36.2 6.3 %copy-start.5 = (bf16[1024,256]{1,0:T(8,128)(2,1)S(1)}, bf16[1024,256]{1,0:T(8,128)(2,1)}, u32[]{:S(2)}) copy-start(bf16[1024,256]{1,0:T(8,128)(2,1)} %get-tuple-element.19.out_ref) | copy-start | bytes 1572868
  38.7 12.8 %collective-permute-start.3 = (bf16[352,256]{1,0:T(8,128)(2,1)S(1)}, bf16[352,256]{1,0:T(8,128)(2,1)S(1)}, u32[]{:S(2)}, u32[]{:S(2)}) collective-permute-start(bf16[352,256]{1,0:T(8,128)(2,1)S(1)} %get-tuple-element.28), channel_id=1, source_target_pairs={{0,2},{1,3},{2,0},{3,1},{4,6},{5,7},{6,4},{7,5},{8,10},{9,11},{10,... | collective-permute-start | bytes 540680 | tf_op jit(solution)/shard_map/ppermute | solution.py:361
  40.2 11.3 %collective-permute-start.4 = (bf16[352,256]{1,0:T(8,128)(2,1)S(1)}, bf16[352,256]{1,0:T(8,128)(2,1)S(1)}, u32[]{:S(2)}, u32[]{:S(2)}) collective-permute-start(bf16[352,256]{1,0:T(8,128)(2,1)S(1)} %get-tuple-element.29), channel_id=1, source_target_pairs={{0,4},{1,5},{2,6},{3,7},{4,0},{5,1},{6,2},{7,3},{8,12},{9,13},{10,... | collective-permute-start | bytes 540680 | tf_op jit(solution)/shard_map/ppermute | solution.py:361
  42.5 9.0 %collective-permute-start.5 = (bf16[352,256]{1,0:T(8,128)(2,1)S(1)}, bf16[352,256]{1,0:T(8,128)(2,1)S(1)}, u32[]{:S(2)}, u32[]{:S(2)}) collective-permute-start(bf16[352,256]{1,0:T(8,128)(2,1)S(1)} %get-tuple-element.30), channel_id=1, source_target_pairs={{0,6},{1,7},{2,4},{3,5},{4,2},{5,3},{6,0},{7,1},{8,14},{9,15},{10,... | collective-permute-start | bytes 540680 | tf_op jit(solution)/shard_map/ppermute | solution.py:361
  51.7 8.8 %collective-permute-start.6 = (bf16[88,256]{1,0:T(8,128)(2,1)S(1)}, bf16[88,256]{1,0:T(8,128)(2,1)S(1)}, u32[]{:S(2)}, u32[]{:S(2)}) collective-permute-start(bf16[88,256]{1,0:T(8,128)(2,1)S(1)} %get-tuple-element.64), channel_id=1, source_target_pairs={{0,8},{1,9},{2,10},{3,11},{4,12},{5,13},{6,14},{7,15},{8,0},{9,1},... | collective-permute-start | bytes 135176 | tf_op jit(solution)/shard_map/ppermute | solution.py:361
  54.2 6.3 %collective-permute-start.8 = (bf16[88,256]{1,0:T(8,128)(2,1)S(1)}, bf16[88,256]{1,0:T(8,128)(2,1)S(1)}, u32[]{:S(2)}, u32[]{:S(2)}) collective-permute-start(bf16[88,256]{1,0:T(8,128)(2,1)S(1)} %get-tuple-element.65), channel_id=1, source_target_pairs={{0,24},{1,25},{2,26},{3,27},{4,28},{5,29},{6,30},{7,31},{8,16},{9,... | collective-permute-start | bytes 135176 | tf_op jit(solution)/shard_map/ppermute | solution.py:361
  55.4 5.6 %collective-permute-start.7 = (bf16[88,256]{1,0:T(8,128)(2,1)S(1)}, bf16[88,256]{1,0:T(8,128)(2,1)S(1)}, u32[]{:S(2)}, u32[]{:S(2)}) collective-permute-start(bf16[88,256]{1,0:T(8,128)(2,1)S(1)} %get-tuple-element.66), channel_id=1, source_target_pairs={{0,16},{1,17},{2,18},{3,19},{4,20},{5,21},{6,22},{7,23},{8,24},{9,... | collective-permute-start | bytes 135176 | tf_op jit(solution)/shard_map/ppermute | solution.py:361
  55.8 3.8 %collective-permute-start.9 = (bf16[96,128]{1,0:T(8,128)(2,1)S(1)}, bf16[96,128]{1,0:T(8,128)(2,1)S(1)}, u32[]{:S(2)}, u32[]{:S(2)}) collective-permute-start(bf16[96,128]{1,0:T(8,128)(2,1)S(1)} %get-tuple-element.35), channel_id=1, source_target_pairs={{0,4},{4,0},{8,12},{12,8},{16,20},{20,16},{24,28},{28,24},{1,5},{5... | collective-permute-start | bytes 73736 | tf_op jit(solution)/shard_map/ppermute | solution.py:417
  57.2 2.4 %collective-permute-start.10 = (bf16[96,128]{1,0:T(8,128)(2,1)S(1)}, bf16[96,128]{1,0:T(8,128)(2,1)S(1)}, u32[]{:S(2)}, u32[]{:S(2)}) collective-permute-start(bf16[96,128]{1,0:T(8,128)(2,1)S(1)} %get-tuple-element.36), channel_id=1, source_target_pairs={{4,8},{8,4},{12,16},{16,12},{20,24},{24,20},{5,9},{9,5},{13,17},{1... | collective-permute-start | bytes 73736 | tf_op jit(solution)/shard_map/ppermute | solution.py:417
  61.1 8.5 %collective-permute-start.11 = (bf16[184,256]{1,0:T(8,128)(2,1)S(1)}, bf16[184,256]{1,0:T(8,128)(2,1)S(1)}, u32[]{:S(2)}, u32[]{:S(2)}) collective-permute-start(bf16[184,256]{1,0:T(8,128)(2,1)S(1)} %get-tuple-element.71), channel_id=1, source_target_pairs={{0,24},{1,25},{2,26},{3,27},{4,28},{5,29},{6,30},{7,31},{8,16},{9,... | collective-permute-start | bytes 282632 | tf_op jit(solution)/shard_map/ppermute | solution.py:361
  66.0 7.1 %collective-permute-start.12 = (bf16[184,256]{1,0:T(8,128)(2,1)S(1)}, bf16[184,256]{1,0:T(8,128)(2,1)S(1)}, u32[]{:S(2)}, u32[]{:S(2)}) collective-permute-start(bf16[184,256]{1,0:T(8,128)(2,1)S(1)} %get-tuple-element.72), channel_id=1, source_target_pairs={{0,16},{1,17},{2,18},{3,19},{4,20},{5,21},{6,22},{7,23},{8,24},{9,... | collective-permute-start | bytes 282632 | tf_op jit(solution)/shard_map/ppermute | solution.py:361
  68.2 5.4 %collective-permute-start.13 = (bf16[184,256]{1,0:T(8,128)(2,1)S(1)}, bf16[184,256]{1,0:T(8,128)(2,1)S(1)}, u32[]{:S(2)}, u32[]{:S(2)}) collective-permute-start(bf16[184,256]{1,0:T(8,128)(2,1)S(1)} %get-tuple-element.73), channel_id=1, source_target_pairs={{0,8},{1,9},{2,10},{3,11},{4,12},{5,13},{6,14},{7,15},{8,0},{9,1},... | collective-permute-start | bytes 282632 | tf_op jit(solution)/shard_map/ppermute | solution.py:361
  73.9 10.4 %collective-permute-start.15 = (bf16[544,256]{1,0:T(8,128)(2,1)S(1)}, bf16[544,256]{1,0:T(8,128)(2,1)S(1)}, u32[]{:S(2)}, u32[]{:S(2)}) collective-permute-start(bf16[544,256]{1,0:T(8,128)(2,1)S(1)} %constant_dynamic-update-slice_fusion), channel_id=1, source_target_pairs={{0,4},{1,5},{2,6},{3,7},{4,0},{5,1},{6,2},{7,3},{8,12},{9,13},{10,... | collective-permute-start | bytes 835592 | tf_op jit(solution)/shard_map/ppermute | solution.py:361
  76.5 6.3 %collective-permute-start.16 = (bf16[352,256]{1,0:T(8,128)(2,1)S(1)}, bf16[352,256]{1,0:T(8,128)(2,1)S(1)}, u32[]{:S(2)}, u32[]{:S(2)}) collective-permute-start(bf16[352,256]{1,0:T(8,128)(2,1)S(1)} %pad_maximum_fusion.2), channel_id=1, source_target_pairs={{0,2},{1,3},{2,0},{3,1},{4,6},{5,7},{6,4},{7,5},{8,10},{9,11},{10,... | collective-permute-start | bytes 540680 | tf_op jit(solution)/shard_map/ppermute | solution.py:361
  77.8 6.4 %collective-permute-start.14 = (bf16[352,256]{1,0:T(8,128)(2,1)S(1)}, bf16[352,256]{1,0:T(8,128)(2,1)S(1)}, u32[]{:S(2)}, u32[]{:S(2)}) collective-permute-start(bf16[352,256]{1,0:T(8,128)(2,1)S(1)} %pad_maximum_fusion.2), channel_id=1, source_target_pairs={{0,6},{1,7},{2,4},{3,5},{4,2},{5,3},{6,0},{7,1},{8,14},{9,15},{10,... | collective-permute-start | bytes 540680 | tf_op jit(solution)/shard_map/ppermute | solution.py:361
  84.4 0.7 copy-start.3
  84.7 2.3 %collective-permute-start.17 = (bf16[1408,256]{1,0:T(8,128)(2,1)S(1)}, bf16[1408,256]{1,0:T(8,128)(2,1)S(1)}, u32[]{:S(2)}, u32[]{:S(2)}) collective-permute-start(bf16[1408,256]{1,0:T(8,128)(2,1)S(1)} %pad_maximum_fusion), channel_id=1, source_target_pairs={{0,1},{1,0},{2,3},{3,2},{4,5},{5,4},{6,7},{7,6},{8,9},{9,8},{10,11... | collective-permute-start | bytes 2162696 | tf_op jit(solution)/shard_map/ppermute | solution.py:361

commit v10 on v9

--- a/solution.py
+++ b/solution.py
@@ -12,9 +12,9 @@
 F32 = jnp.float32
 LOW = 256
 SHIFT = 8
-VMEM_LIMIT = 20 << 20
+VMEM_LIMIT = 52 << 20
 SMALL_LIMIT = 6 << 20
-FULL_LIMIT = 50 << 20
+FULL_LIMIT = 51 << 20
 ALL_LIMIT = 60 << 20
 AXES = ("brick", "group")
 

time: 89.1 us -> 88.2 us (0.990)
    pallas_call x1, Pallas kernels: 12.1 us -> 10.7 us  [forward(): pl.pallas_call(forward_kernel, out_shape=(jax.ShapeDtypeStruct((voxels, c...]
  transfers between devices with their start and end apart: 19 -> 19, of which waited for: 11 -> 11; matrix products, arithmetic and copies ran while one was open for 4% -> 4% of each run, Pallas kernels for 12% -> 13%
where the time goes in v10:
time: 88.2 us; the launch traced here: 87.8 us
  starting transfers between devices  32.4 us (37%)
  Pallas kernels  24.6 us (28%)
  waiting for transfers between devices  22.6 us (26%)
  other arithmetic  5.03 us (6%)
  local copies, waits for them, and re-layouts  1.76 us (2%)
  between operations  1.07 us (1%)
    ppermute x14, starting transfers between devices, swapped(): return lax.ppermute(array, AXES, [(i, partner(i)) for i in range(count)])  19.3 us
    ppermute x14, waiting for transfers between devices, swapped(): return lax.ppermute(array, AXES, [(i, partner(i)) for i in range(count)])  15 us
    pallas_call x1, Pallas kernels, forward(): pl.pallas_call(forward_kernel, out_shape=(jax.ShapeDtypeStruct((voxels, c...  10.7 us
    pallas_call x1, Pallas kernels, backward(): pl.pallas_call(functools.partial(backward_kernel, packed), out_shape=(jax...  9.72 us
    all_to_all x1, starting transfers between devices, on_device(): got = lax.all_to_all(send, 'brick', split_axis=0, concat_axis=0)  7.27 us
    ppermute x4, starting transfers between devices, meet(): got.append(lax.ppermute(array, 'brick', pairs))  5.8 us
    all_to_all x1, waiting for transfers between devices, on_device(): got = lax.all_to_all(send, 'brick', split_axis=0, concat_axis=0)  4.21 us
    ppermute x4, waiting for transfers between devices, meet(): got.append(lax.ppermute(array, 'brick', pairs))  3.45 us
  transfers between devices with their start and end apart: 19, of which 11 were waited for; matrix products, arithmetic and copies ran while one was open for 4% of the time, Pallas kernels for 13%

profile of v10, /device:TPU:0, one launch (start us, length us, event | category | flops | bytes accessed | tf_op | source)
XLA Modules:
  0.0 87.8 jit_solution(15698059443942452122)
XLA Ops:
  0.7 2.1 %shard_map.103 = bf16[8,96,128]{2,1,0:T(8,128)(2,1)} custom-call(bf16[96,1024]{1,0:T(8,128)(2,1)} %bitcast.85, s32[1,1024]{1,0:T(1,128)} %bitcast.72), custom_call_target="tpu_custom_call" | custom-call | flops 201326592 | bytes 524288 | tf_op jit(solution)/shard_map/pallas_call | solution.py:229
  2.7 7.3 %all-to-all-start = ((bf16[8,96,128]{2,1,0:T(8,128)(2,1)}), bf16[8,96,128]{2,1,0:T(8,128)(2,1)S(1)}, u32[]{:S(2)}, u32[]{:S(2)}) async-start(bf16[8,96,128]{2,1,0:T(8,128)(2,1)} %shard_map.103), calls=%async_computation | async-start | bytes 393216 | tf_op jit(solution)/shard_map/all_to_all | solution.py:435
  10.0 1.3 %fusion.19 = (s32[1]{0:T(128)}, s32[1]{0:T(128)}) fusion(s32[2]{0:T(128)} %param.11), kind=kLoop, calls=%fused_computation.64 | loop fusion | bytes 16 | tf_op jit(solution)/shard_map/slice | solution.py:438
  11.3 0.9 %shift-right-logical_convert_fusion = (f32[27,1024]{1,0:T(8,128)S(1)}, f32[27,1024]{1,0:T(8,128)S(1)}) fusion(s32[27,1024]{1,0:T(8,128)} %param.12), kind=kLoop, calls=%fused_computation.18 | loop fusion | flops 110592 | bytes 331776 | tf_op jit(solution)/shard_map/convert_element_type | solution.py:450
  12.2 1.3 %select_select_fusion.9 = s32[256]{0:T(256)S(1)} fusion(s32[256]{0:T(256)S(1)} %copy-done.4, s32[]{:T(128)} %bitcast.3, s32[]{:T(128)} %bitcast.2), kind=kLoop, calls=%fused_computation.62 | loop fusion | flops 1536 | bytes 2056 | tf_op jit(solution)/shard_map/jit(_where)/select_n | solution.py:439
  13.7 4.2 %all-to-all-done.got_ref = bf16[8,96,128]{2,1,0:T(8,128)(2,1)S(1)} async-done(((bf16[8,96,128]{2,1,0:T(8,128)(2,1)}), bf16[8,96,128]{2,1,0:T(8,128)(2,1)S(1)}, u32[]{:S(2)}, u32[]{:S(2)}) %all-to-all-start) | async-done | bytes 196640 | tf_op jit(solution)/shard_map/all_to_all | solution.py:435
  18.3 0.7 collective-permute-start.1
  18.9 3.1 %collective-permute-start = (bf16[96,128]{1,0:T(8,128)(2,1)S(1)}, bf16[96,128]{1,0:T(8,128)(2,1)S(1)}, u32[]{:S(2)}, u32[]{:S(2)}) collective-permute-start(bf16[96,128]{1,0:T(8,128)(2,1)S(1)} %get-tuple-element.70), channel_id=1, source_target_pairs={{0,4},{4,0},{8,12},{12,8},{16,20},{20,16},{24,28},{28,24},{1,5},{5... | collective-permute-start | bytes 73736 | tf_op jit(solution)/shard_map/ppermute | solution.py:417
  22.1 1.7 %collective-permute-done.even_ref = bf16[96,128]{1,0:T(8,128)(2,1)S(1)} collective-permute-done((bf16[96,128]{1,0:T(8,128)(2,1)S(1)}, bf16[96,128]{1,0:T(8,128)(2,1)S(1)}, u32[]{:S(2)}, u32[]{:S(2)}) %collective-permute-start) | collective-permute-done | bytes 24608 | tf_op jit(solution)/shard_map/ppermute | solution.py:417
  23.8 10.7 %shard_map.104 = (bf16[1024,256]{1,0:T(8,128)(2,1)}, bf16[1408,256]{1,0:T(8,128)(2,1)S(1)}, bf16[1408,256]{1,0:T(8,128)(2,1)S(1)}) custom-call(s32[2]{0:T(128)S(1)} %pad_add_fusion.flag_ref, bf16[8,96,128]{2,1,0:T(8,128)(2,1)S(1)} %all-to-all-done.got_ref, bf16[96,128]{1,0:T(8,128)(2,1)S(1)} %collective-permute-done.even_ref, ...), custom_call_target="tpu_custom_call" | custom-call | flops 9512681472 | bytes 5242880 | tf_op jit(solution)/shard_map/pallas_call | solution.py:252
  34.7 2.1 %collective-permute-done.2.got_ref = bf16[1408,256]{1,0:T(8,128)(2,1)S(1)} collective-permute-done((bf16[1408,256]{1,0:T(8,128)(2,1)S(1)}, bf16[1408,256]{1,0:T(8,128)(2,1)S(1)}, u32[]{:S(2)}, u32[]{:S(2)}) %collective-permute-start.2) | collective-permute-done | bytes 720928 | tf_op jit(solution)/shard_map/ppermute | solution.py:361
  37.0 1.6 %collective-permute-start.3 = (bf16[352,256]{1,0:T(8,128)(2,1)S(1)}, bf16[352,256]{1,0:T(8,128)(2,1)S(1)}, u32[]{:S(2)}, u32[]{:S(2)}) collective-permute-start(bf16[352,256]{1,0:T(8,128)(2,1)S(1)} %get-tuple-element.28), channel_id=1, source_target_pairs={{0,2},{1,3},{2,0},{3,1},{4,6},{5,7},{6,4},{7,5},{8,10},{9,11},{10,... | collective-permute-start | bytes 540680 | tf_op jit(solution)/shard_map/ppermute | solution.py:361
  38.5 2.3 %collective-permute-start.4 = (bf16[352,256]{1,0:T(8,128)(2,1)S(1)}, bf16[352,256]{1,0:T(8,128)(2,1)S(1)}, u32[]{:S(2)}, u32[]{:S(2)}) collective-permute-start(bf16[352,256]{1,0:T(8,128)(2,1)S(1)} %get-tuple-element.29), channel_id=1, source_target_pairs={{0,4},{1,5},{2,6},{3,7},{4,0},{5,1},{6,2},{7,3},{8,12},{9,13},{10,... | collective-permute-start | bytes 540680 | tf_op jit(solution)/shard_map/ppermute | solution.py:361
  40.8 9.7 %shard_map.106 = (f32[384,256]{1,0:T(8,128)S(1)}, bf16[96,128]{1,0:T(8,128)(2,1)S(1)}, bf16[96,128]{1,0:T(8,128)(2,1)S(1)}) custom-call(s32[2]{0:T(128)S(1)} %pad_add_fusion.flag_ref, bf16[1024,256]{1,0:T(8,128)(2,1)S(1)} %copy-done.3, bf16[1024,256]{1,0:T(8,128)(2,1)S(1)} %copy-done, f32[27,1024]{1,0:T(8,128)S(1)} %get-tuple-element.68.low_ref, ...), custom_call_target="tpu_custom_call" | custom-call | flops 8153726976 | bytes 3145728 | tf_op jit(solution)/shard_map/pallas_call | solution.py:284
  50.7 2.6 %collective-permute-start.6 = (bf16[88,256]{1,0:T(8,128)(2,1)S(1)}, bf16[88,256]{1,0:T(8,128)(2,1)S(1)}, u32[]{:S(2)}, u32[]{:S(2)}) collective-permute-start(bf16[88,256]{1,0:T(8,128)(2,1)S(1)} %get-tuple-element.64), channel_id=1, source_target_pairs={{0,8},{1,9},{2,10},{3,11},{4,12},{5,13},{6,14},{7,15},{8,0},{9,1},... | collective-permute-start | bytes 135176 | tf_op jit(solution)/shard_map/ppermute | solution.py:361
  53.3 1.2 %collective-permute-start.8 = (bf16[88,256]{1,0:T(8,128)(2,1)S(1)}, bf16[88,256]{1,0:T(8,128)(2,1)S(1)}, u32[]{:S(2)}, u32[]{:S(2)}) collective-permute-start(bf16[88,256]{1,0:T(8,128)(2,1)S(1)} %get-tuple-element.65), channel_id=1, source_target_pairs={{0,24},{1,25},{2,26},{3,27},{4,28},{5,29},{6,30},{7,31},{8,16},{9,... | collective-permute-start | bytes 135176 | tf_op jit(solution)/shard_map/ppermute | solution.py:361
  54.8 1.4 %collective-permute-start.9 = (bf16[96,128]{1,0:T(8,128)(2,1)S(1)}, bf16[96,128]{1,0:T(8,128)(2,1)S(1)}, u32[]{:S(2)}, u32[]{:S(2)}) collective-permute-start(bf16[96,128]{1,0:T(8,128)(2,1)S(1)} %get-tuple-element.35), channel_id=1, source_target_pairs={{0,4},{4,0},{8,12},{12,8},{16,20},{20,16},{24,28},{28,24},{1,5},{5... | collective-permute-start | bytes 73736 | tf_op jit(solution)/shard_map/ppermute | solution.py:417
  56.2 0.7 collective-permute-start.10
  56.9 1.7 %collective-permute-done.9.first_ref = bf16[96,128]{1,0:T(8,128)(2,1)S(1)} collective-permute-done((bf16[96,128]{1,0:T(8,128)(2,1)S(1)}, bf16[96,128]{1,0:T(8,128)(2,1)S(1)}, u32[]{:S(2)}, u32[]{:S(2)}) %collective-permute-start.9) | collective-permute-done | bytes 24608 | tf_op jit(solution)/shard_map/ppermute | solution.py:417
  58.6 0.9 shard_map.107
  59.5 0.5 collective-permute-done.7
  60.2 4.9 %collective-permute-start.11 = (bf16[184,256]{1,0:T(8,128)(2,1)S(1)}, bf16[184,256]{1,0:T(8,128)(2,1)S(1)}, u32[]{:S(2)}, u32[]{:S(2)}) collective-permute-start(bf16[184,256]{1,0:T(8,128)(2,1)S(1)} %get-tuple-element.71), channel_id=1, source_target_pairs={{0,24},{1,25},{2,26},{3,27},{4,28},{5,29},{6,30},{7,31},{8,16},{9,... | collective-permute-start | bytes 282632 | tf_op jit(solution)/shard_map/ppermute | solution.py:361
  65.1 2.2 %collective-permute-start.12 = (bf16[184,256]{1,0:T(8,128)(2,1)S(1)}, bf16[184,256]{1,0:T(8,128)(2,1)S(1)}, u32[]{:S(2)}, u32[]{:S(2)}) collective-permute-start(bf16[184,256]{1,0:T(8,128)(2,1)S(1)} %get-tuple-element.72), channel_id=1, source_target_pairs={{0,16},{1,17},{2,18},{3,19},{4,20},{5,21},{6,22},{7,23},{8,24},{9,... | collective-permute-start | bytes 282632 | tf_op jit(solution)/shard_map/ppermute | solution.py:361
  67.3 1.4 %collective-permute-done.11 = bf16[184,256]{1,0:T(8,128)(2,1)S(1)} collective-permute-done((bf16[184,256]{1,0:T(8,128)(2,1)S(1)}, bf16[184,256]{1,0:T(8,128)(2,1)S(1)}, u32[]{:S(2)}, u32[]{:S(2)}) %collective-permute-start.11) | collective-permute-done | bytes 94240 | tf_op jit(solution)/shard_map/ppermute | solution.py:361
  68.7 3.5 %collective-permute-done.12 = bf16[184,256]{1,0:T(8,128)(2,1)S(1)} collective-permute-done((bf16[184,256]{1,0:T(8,128)(2,1)S(1)}, bf16[184,256]{1,0:T(8,128)(2,1)S(1)}, u32[]{:S(2)}, u32[]{:S(2)}) %collective-permute-start.12) | collective-permute-done | bytes 94240 | tf_op jit(solution)/shard_map/ppermute | solution.py:361
  72.9 2.6 %collective-permute-start.15 = (bf16[544,256]{1,0:T(8,128)(2,1)S(1)}, bf16[544,256]{1,0:T(8,128)(2,1)S(1)}, u32[]{:S(2)}, u32[]{:S(2)}) collective-permute-start(bf16[544,256]{1,0:T(8,128)(2,1)S(1)} %constant_dynamic-update-slice_fusion), channel_id=1, source_target_pairs={{0,4},{1,5},{2,6},{3,7},{4,0},{5,1},{6,2},{7,3},{8,12},{9,13},{10,... | collective-permute-start | bytes 835592 | tf_op jit(solution)/shard_map/ppermute | solution.py:361
  75.5 1.3 %collective-permute-start.16 = (bf16[352,256]{1,0:T(8,128)(2,1)S(1)}, bf16[352,256]{1,0:T(8,128)(2,1)S(1)}, u32[]{:S(2)}, u32[]{:S(2)}) collective-permute-start(bf16[352,256]{1,0:T(8,128)(2,1)S(1)} %pad_maximum_fusion.2), channel_id=1, source_target_pairs={{0,2},{1,3},{2,0},{3,1},{4,6},{5,7},{6,4},{7,5},{8,10},{9,11},{10,... | collective-permute-start | bytes 540680 | tf_op jit(solution)/shard_map/ppermute | solution.py:361
  77.1 4.0 %collective-permute-done.16 = bf16[352,256]{1,0:T(8,128)(2,1)S(1)} collective-permute-done((bf16[352,256]{1,0:T(8,128)(2,1)S(1)}, bf16[352,256]{1,0:T(8,128)(2,1)S(1)}, u32[]{:S(2)}, u32[]{:S(2)}) %collective-permute-start.16) | collective-permute-done | bytes 180256 | tf_op jit(solution)/shard_map/ppermute | solution.py:361
  81.1 2.2 %collective-permute-done.14 = bf16[352,256]{1,0:T(8,128)(2,1)S(1)} collective-permute-done((bf16[352,256]{1,0:T(8,128)(2,1)S(1)}, bf16[352,256]{1,0:T(8,128)(2,1)S(1)}, u32[]{:S(2)}, u32[]{:S(2)}) %collective-permute-start.14) | collective-permute-done | bytes 180256 | tf_op jit(solution)/shard_map/ppermute | solution.py:361
  84.2 1.1 %shard_map.108 = bf16[96,1024]{1,0:T(8,128)(2,1)} custom-call(s32[1]{0:T(128)} %bitcast.9.side_ref, bf16[192,256]{1,0:T(8,128)(2,1)S(1)} %bitcast.70, bf16[192,256]{1,0:T(8,128)(2,1)S(1)} %slice.77.came_ref, s32[1,1024]{1,0:T(1,128)S(1)} %bitcast.73), custom_call_target="tpu_custom_call" | custom-call | flops 201326592 | bytes 1048576 | tf_op jit(solution)/shard_map/pallas_call | solution.py:319
  85.3 0.7 collective-permute-done.17
  86.1 1.7 %convert_multiply_fusion = f32[2592,256]{1,0:T(8,128)} fusion(bf16[1296,256]{1,0:T(8,128)(2,1)S(1)} %get-tuple-element.50, bf16[1296,256]{1,0:T(8,128)(2,1)S(1)} %get-tuple-element.49), kind=kLoop, calls=%fused_computation | loop fusion | flops 3317760 | bytes 3981312 | tf_op jit(solution)/shard_map/mul | solution.py:503
  (49 shorter events, 3.2 us)
Async XLA Ops:
  0.6 11.6 %copy-start.4 = (s32[256]{0:T(256)S(1)}, s32[256]{0:T(256)}, u32[]{:S(2)}) copy-start(s32[256]{0:T(256)} %param.10) | copy-start | bytes 3076
  0.6 23.2 %copy-start = (bf16[1024,256]{1,0:T(8,128)(2,1)S(1)}, bf16[1024,256]{1,0:T(8,128)(2,1)}, u32[]{:S(2)}) copy-start(bf16[1024,256]{1,0:T(8,128)(2,1)} %cot_ref.1) | copy-start | bytes 1572868
  0.7 23.2 %copy-start.2 = (f32[256]{0:T(256)S(1)}, f32[256]{0:T(256)}, u32[]{:S(2)}) copy-start(f32[256]{0:T(256)} %param.14) | copy-start | bytes 3076
  2.7 15.2 %all-to-all-start = ((bf16[8,96,128]{2,1,0:T(8,128)(2,1)}), bf16[8,96,128]{2,1,0:T(8,128)(2,1)S(1)}, u32[]{:S(2)}, u32[]{:S(2)}) async-start(bf16[8,96,128]{2,1,0:T(8,128)(2,1)} %shard_map.103), calls=%async_computation | async-start | bytes 393216 | tf_op jit(solution)/shard_map/all_to_all | solution.py:435
  18.3 3.8 %collective-permute-start.1 = (bf16[96,128]{1,0:T(8,128)(2,1)S(1)}, bf16[96,128]{1,0:T(8,128)(2,1)S(1)}, u32[]{:S(2)}, u32[]{:S(2)}) collective-permute-start(bf16[96,128]{1,0:T(8,128)(2,1)S(1)} %get-tuple-element.69), channel_id=1, source_target_pairs={{4,8},{8,4},{12,16},{16,12},{20,24},{24,20},{5,9},{9,5},{13,17},{1... | collective-permute-start | bytes 73736 | tf_op jit(solution)/shard_map/ppermute | solution.py:417
  18.9 4.9 %collective-permute-start = (bf16[96,128]{1,0:T(8,128)(2,1)S(1)}, bf16[96,128]{1,0:T(8,128)(2,1)S(1)}, u32[]{:S(2)}, u32[]{:S(2)}) collective-permute-start(bf16[96,128]{1,0:T(8,128)(2,1)S(1)} %get-tuple-element.70), channel_id=1, source_target_pairs={{0,4},{4,0},{8,12},{12,8},{16,20},{20,16},{24,28},{28,24},{1,5},{5... | collective-permute-start | bytes 73736 | tf_op jit(solution)/shard_map/ppermute | solution.py:417
  34.5 2.3 %collective-permute-start.2 = (bf16[1408,256]{1,0:T(8,128)(2,1)S(1)}, bf16[1408,256]{1,0:T(8,128)(2,1)S(1)}, u32[]{:S(2)}, u32[]{:S(2)}) collective-permute-start(bf16[1408,256]{1,0:T(8,128)(2,1)S(1)} %get-tuple-element.26), channel_id=1, source_target_pairs={{0,1},{1,0},{2,3},{3,2},{4,5},{5,4},{6,7},{7,6},{8,9},{9,8},{10,11... | collective-permute-start | bytes 2162696 | tf_op jit(solution)/shard_map/ppermute | solution.py:361
  34.7 6.1 %copy-start.3 = (bf16[1024,256]{1,0:T(8,128)(2,1)S(1)}, bf16[1024,256]{1,0:T(8,128)(2,1)}, u32[]{:S(2)}) copy-start(bf16[1024,256]{1,0:T(8,128)(2,1)} %get-tuple-element.19.out_ref) | copy-start | bytes 1572868
  37.0 13.6 %collective-permute-start.3 = (bf16[352,256]{1,0:T(8,128)(2,1)S(1)}, bf16[352,256]{1,0:T(8,128)(2,1)S(1)}, u32[]{:S(2)}, u32[]{:S(2)}) collective-permute-start(bf16[352,256]{1,0:T(8,128)(2,1)S(1)} %get-tuple-element.28), channel_id=1, source_target_pairs={{0,2},{1,3},{2,0},{3,1},{4,6},{5,7},{6,4},{7,5},{8,10},{9,11},{10,... | collective-permute-start | bytes 540680 | tf_op jit(solution)/shard_map/ppermute | solution.py:361
  38.5 12.0 %collective-permute-start.4 = (bf16[352,256]{1,0:T(8,128)(2,1)S(1)}, bf16[352,256]{1,0:T(8,128)(2,1)S(1)}, u32[]{:S(2)}, u32[]{:S(2)}) collective-permute-start(bf16[352,256]{1,0:T(8,128)(2,1)S(1)} %get-tuple-element.29), channel_id=1, source_target_pairs={{0,4},{1,5},{2,6},{3,7},{4,0},{5,1},{6,2},{7,3},{8,12},{9,13},{10,... | collective-permute-start | bytes 540680 | tf_op jit(solution)/shard_map/ppermute | solution.py:361
  40.8 9.8 %collective-permute-start.5 = (bf16[352,256]{1,0:T(8,128)(2,1)S(1)}, bf16[352,256]{1,0:T(8,128)(2,1)S(1)}, u32[]{:S(2)}, u32[]{:S(2)}) collective-permute-start(bf16[352,256]{1,0:T(8,128)(2,1)S(1)} %get-tuple-element.30), channel_id=1, source_target_pairs={{0,6},{1,7},{2,4},{3,5},{4,2},{5,3},{6,0},{7,1},{8,14},{9,15},{10,... | collective-permute-start | bytes 540680 | tf_op jit(solution)/shard_map/ppermute | solution.py:361
  50.7 8.8 %collective-permute-start.6 = (bf16[88,256]{1,0:T(8,128)(2,1)S(1)}, bf16[88,256]{1,0:T(8,128)(2,1)S(1)}, u32[]{:S(2)}, u32[]{:S(2)}) collective-permute-start(bf16[88,256]{1,0:T(8,128)(2,1)S(1)} %get-tuple-element.64), channel_id=1, source_target_pairs={{0,8},{1,9},{2,10},{3,11},{4,12},{5,13},{6,14},{7,15},{8,0},{9,1},... | collective-permute-start | bytes 135176 | tf_op jit(solution)/shard_map/ppermute | solution.py:361
  53.3 6.3 %collective-permute-start.8 = (bf16[88,256]{1,0:T(8,128)(2,1)S(1)}, bf16[88,256]{1,0:T(8,128)(2,1)S(1)}, u32[]{:S(2)}, u32[]{:S(2)}) collective-permute-start(bf16[88,256]{1,0:T(8,128)(2,1)S(1)} %get-tuple-element.65), channel_id=1, source_target_pairs={{0,24},{1,25},{2,26},{3,27},{4,28},{5,29},{6,30},{7,31},{8,16},{9,... | collective-permute-start | bytes 135176 | tf_op jit(solution)/shard_map/ppermute | solution.py:361
  54.5 5.6 %collective-permute-start.7 = (bf16[88,256]{1,0:T(8,128)(2,1)S(1)}, bf16[88,256]{1,0:T(8,128)(2,1)S(1)}, u32[]{:S(2)}, u32[]{:S(2)}) collective-permute-start(bf16[88,256]{1,0:T(8,128)(2,1)S(1)} %get-tuple-element.66), channel_id=1, source_target_pairs={{0,16},{1,17},{2,18},{3,19},{4,20},{5,21},{6,22},{7,23},{8,24},{9,... | collective-permute-start | bytes 135176 | tf_op jit(solution)/shard_map/ppermute | solution.py:361
  54.8 3.8 %collective-permute-start.9 = (bf16[96,128]{1,0:T(8,128)(2,1)S(1)}, bf16[96,128]{1,0:T(8,128)(2,1)S(1)}, u32[]{:S(2)}, u32[]{:S(2)}) collective-permute-start(bf16[96,128]{1,0:T(8,128)(2,1)S(1)} %get-tuple-element.35), channel_id=1, source_target_pairs={{0,4},{4,0},{8,12},{12,8},{16,20},{20,16},{24,28},{28,24},{1,5},{5... | collective-permute-start | bytes 73736 | tf_op jit(solution)/shard_map/ppermute | solution.py:417
  56.2 2.4 %collective-permute-start.10 = (bf16[96,128]{1,0:T(8,128)(2,1)S(1)}, bf16[96,128]{1,0:T(8,128)(2,1)S(1)}, u32[]{:S(2)}, u32[]{:S(2)}) collective-permute-start(bf16[96,128]{1,0:T(8,128)(2,1)S(1)} %get-tuple-element.36), channel_id=1, source_target_pairs={{4,8},{8,4},{12,16},{16,12},{20,24},{24,20},{5,9},{9,5},{13,17},{1... | collective-permute-start | bytes 73736 | tf_op jit(solution)/shard_map/ppermute | solution.py:417
  60.2 8.5 %collective-permute-start.11 = (bf16[184,256]{1,0:T(8,128)(2,1)S(1)}, bf16[184,256]{1,0:T(8,128)(2,1)S(1)}, u32[]{:S(2)}, u32[]{:S(2)}) collective-permute-start(bf16[184,256]{1,0:T(8,128)(2,1)S(1)} %get-tuple-element.71), channel_id=1, source_target_pairs={{0,24},{1,25},{2,26},{3,27},{4,28},{5,29},{6,30},{7,31},{8,16},{9,... | collective-permute-start | bytes 282632 | tf_op jit(solution)/shard_map/ppermute | solution.py:361
  65.1 7.1 %collective-permute-start.12 = (bf16[184,256]{1,0:T(8,128)(2,1)S(1)}, bf16[184,256]{1,0:T(8,128)(2,1)S(1)}, u32[]{:S(2)}, u32[]{:S(2)}) collective-permute-start(bf16[184,256]{1,0:T(8,128)(2,1)S(1)} %get-tuple-element.72), channel_id=1, source_target_pairs={{0,16},{1,17},{2,18},{3,19},{4,20},{5,21},{6,22},{7,23},{8,24},{9,... | collective-permute-start | bytes 282632 | tf_op jit(solution)/shard_map/ppermute | solution.py:361
  67.3 5.4 %collective-permute-start.13 = (bf16[184,256]{1,0:T(8,128)(2,1)S(1)}, bf16[184,256]{1,0:T(8,128)(2,1)S(1)}, u32[]{:S(2)}, u32[]{:S(2)}) collective-permute-start(bf16[184,256]{1,0:T(8,128)(2,1)S(1)} %get-tuple-element.73), channel_id=1, source_target_pairs={{0,8},{1,9},{2,10},{3,11},{4,12},{5,13},{6,14},{7,15},{8,0},{9,1},... | collective-permute-start | bytes 282632 | tf_op jit(solution)/shard_map/ppermute | solution.py:361
  72.9 10.4 %collective-permute-start.15 = (bf16[544,256]{1,0:T(8,128)(2,1)S(1)}, bf16[544,256]{1,0:T(8,128)(2,1)S(1)}, u32[]{:S(2)}, u32[]{:S(2)}) collective-permute-start(bf16[544,256]{1,0:T(8,128)(2,1)S(1)} %constant_dynamic-update-slice_fusion), channel_id=1, source_target_pairs={{0,4},{1,5},{2,6},{3,7},{4,0},{5,1},{6,2},{7,3},{8,12},{9,13},{10,... | collective-permute-start | bytes 835592 | tf_op jit(solution)/shard_map/ppermute | solution.py:361
  75.5 5.6 %collective-permute-start.16 = (bf16[352,256]{1,0:T(8,128)(2,1)S(1)}, bf16[352,256]{1,0:T(8,128)(2,1)S(1)}, u32[]{:S(2)}, u32[]{:S(2)}) collective-permute-start(bf16[352,256]{1,0:T(8,128)(2,1)S(1)} %pad_maximum_fusion.2), channel_id=1, source_target_pairs={{0,2},{1,3},{2,0},{3,1},{4,6},{5,7},{6,4},{7,5},{8,10},{9,11},{10,... | collective-permute-start | bytes 540680 | tf_op jit(solution)/shard_map/ppermute | solution.py:361
  76.9 6.5 %collective-permute-start.14 = (bf16[352,256]{1,0:T(8,128)(2,1)S(1)}, bf16[352,256]{1,0:T(8,128)(2,1)S(1)}, u32[]{:S(2)}, u32[]{:S(2)}) collective-permute-start(bf16[352,256]{1,0:T(8,128)(2,1)S(1)} %pad_maximum_fusion.2), channel_id=1, source_target_pairs={{0,6},{1,7},{2,4},{3,5},{4,2},{5,3},{6,0},{7,1},{8,14},{9,15},{10,... | collective-permute-start | bytes 540680 | tf_op jit(solution)/shard_map/ppermute | solution.py:361
  83.5 0.7 copy-start.1
  83.8 2.3 %collective-permute-start.17 = (bf16[1408,256]{1,0:T(8,128)(2,1)S(1)}, bf16[1408,256]{1,0:T(8,128)(2,1)S(1)}, u32[]{:S(2)}, u32[]{:S(2)}) collective-permute-start(bf16[1408,256]{1,0:T(8,128)(2,1)S(1)} %pad_maximum_fusion), channel_id=1, source_target_pairs={{0,1},{1,0},{2,3},{3,2},{4,5},{5,4},{6,7},{7,6},{8,9},{9,8},{10,11... | collective-permute-start | bytes 2162696 | tf_op jit(solution)/shard_map/ppermute | solution.py:361
